TPU v7x, 128 devices: a whole 4x4x4 slice. The times are simulated.
128 devices in a mesh: pos: 64 (over z, y, x), head: 2 (over core).
Axes of the slice: x: 4, y: 4, z: 4, core: 2. Of those that a mesh axis runs over, the one named last changes fastest.
Arguments:
- inputs: bfloat16 [65536, 1024], P('pos'), may hold values from -400 to 400
- valid_blocks: int32 [512], P('pos'), may hold values from 0 to 1, as said below
- latents: bfloat16 [2048, 1024], P('pos'), may hold values from -6 to 6
- w_query: bfloat16 [1024, 1024], P(None, 'head'), may hold values from -0.1875 to 0.1875
- w_key: bfloat16 [1024, 1024], P(None, 'head'), may hold values from -0.1875 to 0.1875
- w_value: bfloat16 [1024, 1024], P(None, 'head'), may hold values from -0.1875 to 0.1875
- w_out: bfloat16 [1024, 1024], P('head'), may hold values from -0.1875 to 0.1875
- w_mlp: bfloat16 [1024, 1024], replicated, may hold values from -0.1875 to 0.1875
- w_lkey: bfloat16 [1024, 1024], P(None, 'head'), may hold values from -0.1875 to 0.1875
- w_lvalue: bfloat16 [1024, 1024], P(None, 'head'), may hold values from -0.1875 to 0.1875
- w_pquery: bfloat16 [1024, 1024], P(None, 'head'), may hold values from -0.1875 to 0.1875
- w_pout: bfloat16 [1024, 1024], P('head'), may hold values from -0.1875 to 0.1875
Outputs:
- decoded: bfloat16 [65536, 1024], P(('pos', 'head'))
Inputs may be any that keep to these rules, and one draw needn't show every extreme that they name: `valid_blocks`: within the 1024 positions of each device the blocks marked 1 come first; every device has at least one block marked 1, and some device has all its blocks marked 1.
All inputs are finite; a program needn't handle non-finite values.
Results may differ from a plain program's by a relative error of at most 0.017.
The roundings to bfloat16 on the way count: a program that leaves them out, or rounds other values in their place, can miss the bound.
Values may be sent and summed in bfloat16 or wider, within the bound.
No kernel may reach another device: no remote copies, remote signals or barrier semaphores. Data moves between devices by JAX's collectives and lax.ppermute only.
A program may use at most 128 MiB of HBM per device.

v0:
```python
import jax
import jax.numpy as jnp
from jax import lax
from jax.sharding import PartitionSpec as P

HEAD_DIM = 128
LAT = 2048
BLK = 128


masked_score = -1e30
epsilon = 1e-05


def rms_norm(values):
    return values * lax.rsqrt(jnp.mean(values * values, axis=-1, keepdims=True) + epsilon)


def per_device(
    inputs,
    valid_blocks,
    latents,
    w_query,
    w_key,
    w_value,
    w_out,
    w_mlp,
    w_lkey,
    w_lvalue,
    w_pquery,
    w_pout,
):
    scaling = HEAD_DIM ** (-0.5)
    pos_local = inputs.shape[0]
    lat_local = latents.shape[0]
    heads_local = w_key.shape[1] // HEAD_DIM
    columns = heads_local * HEAD_DIM
    pos_keys = (
        jnp.dot(inputs, w_key, preferred_element_type=jnp.float32)
        .astype(jnp.bfloat16)
        .reshape(pos_local, heads_local, HEAD_DIM)
    )
    pos_values = (
        jnp.dot(inputs, w_value, preferred_element_type=jnp.float32)
        .astype(jnp.bfloat16)
        .reshape(pos_local, heads_local, HEAD_DIM)
    )
    own_queries = jnp.dot(latents, w_query, preferred_element_type=jnp.float32).astype(jnp.bfloat16)
    lat_queries = lax.all_gather(own_queries, "pos", axis=0, tiled=True).reshape(
        LAT, heads_local, HEAD_DIM
    )
    alive_mask = jnp.repeat(valid_blocks, BLK) > 0
    lat_block = min(LAT, 1024)

    def cross_block(query_rows):
        scores = (
            jnp.einsum("lhe,phe->lhp", query_rows, pos_keys, preferred_element_type=jnp.float32)
            * scaling
        )
        scores = jnp.where(alive_mask[None, None, :], scores, masked_score)
        row_max = jnp.max(scores, axis=-1)
        exponent = jnp.exp(scores - row_max[..., None])
        totals = jnp.sum(exponent, axis=-1)
        sums = jnp.einsum(
            "lhp,phe->lhe",
            exponent.astype(jnp.bfloat16),
            pos_values,
            preferred_element_type=jnp.float32,
        )
        return (row_max, totals, sums)

    row_max, totals, sums = lax.map(
        cross_block, lat_queries.reshape(LAT // lat_block, lat_block, heads_local, HEAD_DIM)
    )
    row_max = row_max.reshape(LAT, heads_local)
    totals = totals.reshape(LAT, heads_local)
    sums = sums.reshape(LAT, heads_local, HEAD_DIM)
    global_max = lax.pmax(row_max.astype(jnp.bfloat16), "pos").astype(row_max.dtype)
    factor = jnp.exp(row_max - global_max)
    scaled_totals = totals * factor
    scaled_sums = sums * factor[..., None]
    all_totals, all_sums = lax.psum((scaled_totals, scaled_sums), "pos")
    offset = lax.axis_index("pos") * lat_local
    own_totals = lax.dynamic_slice_in_dim(all_totals, offset, lat_local, 0)
    own_sums = lax.dynamic_slice_in_dim(all_sums, offset, lat_local, 0)
    attended = (own_sums / own_totals[..., None]).astype(jnp.bfloat16).reshape(lat_local, columns)
    partial_terms = jnp.dot(attended, w_out, preferred_element_type=jnp.float32)
    merged = lax.psum(partial_terms.astype(jnp.bfloat16), "head").astype(jnp.float32)
    normed = rms_norm(merged)
    hidden = jax.nn.gelu(
        jnp.dot(normed.astype(jnp.bfloat16), w_mlp, preferred_element_type=jnp.float32)
    )
    lat_rows = (normed + hidden).astype(jnp.bfloat16)
    lat_keys = jnp.dot(lat_rows, w_lkey, preferred_element_type=jnp.float32).astype(jnp.bfloat16)
    lat_values = jnp.dot(lat_rows, w_lvalue, preferred_element_type=jnp.float32).astype(
        jnp.bfloat16
    )
    query_block = min(pos_local, 512)
    pos_queries = jnp.dot(inputs, w_pquery, preferred_element_type=jnp.float32).astype(jnp.bfloat16)
    pos_queries = pos_queries.reshape(pos_local // query_block, query_block, heads_local, HEAD_DIM)
    shape_rows = (pos_local // query_block, query_block, heads_local)
    initial = (
        jnp.full(shape_rows, masked_score, jnp.float32),
        jnp.zeros(shape_rows, jnp.float32),
        jnp.zeros(shape_rows + (HEAD_DIM,), jnp.float32),
    )
    piece_keys = lax.all_gather(lat_keys, "pos", axis=0, tiled=True).reshape(
        -1, heads_local, HEAD_DIM
    )
    piece_values = lax.all_gather(lat_values, "pos", axis=0, tiled=True).reshape(
        -1, heads_local, HEAD_DIM
    )

    def one_block(operands):
        query_rows, old_max, old_totals, old_sums = operands
        scores = (
            jnp.einsum("phe,lhe->phl", query_rows, piece_keys, preferred_element_type=jnp.float32)
            * scaling
        )
        new_max = jnp.maximum(old_max, jnp.max(scores, axis=-1))
        keeping = jnp.exp(old_max - new_max)
        exponent = jnp.exp(scores - new_max[..., None])
        new_totals = old_totals * keeping + jnp.sum(exponent, axis=-1)
        new_sums = old_sums * keeping[..., None] + jnp.einsum(
            "phl,lhe->phe",
            exponent.astype(jnp.bfloat16),
            piece_values,
            preferred_element_type=jnp.float32,
        )
        return (new_max, new_totals, new_sums)

    final_max, final_totals, final_sums = lax.map(
        one_block, (pos_queries, initial[0], initial[1], initial[2])
    )
    pos_attended = (
        (final_sums / final_totals[..., None]).astype(jnp.bfloat16).reshape(pos_local, columns)
    )
    terms = jnp.dot(pos_attended, w_pout, preferred_element_type=jnp.float32)
    own_rows = lax.psum_scatter(
        terms.astype(jnp.bfloat16), "head", scatter_dimension=0, tiled=True
    ).astype(jnp.float32)
    return rms_norm(own_rows).astype(jnp.bfloat16)


def solution(mesh):
    placed = (
        P("pos", None),
        P("pos"),
        P("pos", None),
        P(None, "head"),
        P(None, "head"),
        P(None, "head"),
        P("head", None),
        P(),
        P(None, "head"),
        P(None, "head"),
        P(None, "head"),
        P("head", None),
    )
    return jax.shard_map(
        per_device, mesh=mesh, in_specs=placed, out_specs=P(("pos", "head"), None), check_vma=False
    )
```

profile of v0, /device:TPU:1, one launch (start us, length us, event | category | flops | bytes accessed | tf_op | source)
XLA Modules:
  0.0 1036.8 jit_solution(1625358835715837680)
XLA Ops:
  6.5 0.0 copy-start
  6.5 2.3 convolution_convert_fusion.7
  8.9 0.0 all-gather.4.cloned.1.call-update
  8.9 0.0 all-reduce.3.cloned.1.call-start
  9.0 3.5 convolution_convert_fusion.2
  12.5 1.6 copy.31
  14.1 0.0 copy-start.7
  14.1 3.5 convolution_convert_fusion.1
  17.6 2.3 copy.32
  19.9 57.2 %all-gather.4.cloned.1.call-done = bf16[2048,512]{1,0:T(8,128)(2,1)} async-done(((bf16[32,512]{1,0:T(8,128)(2,1)}), bf16[2048,512]{1,0:T(8,128)(2,1)}) %all-gather.4.cloned.1.call-update) | async-done | bytes 2097168 | tf_op jit(solution)/shard_map/all_gather | solution.py:49
  77.1 4.0 reshape_reshape.3
  81.1 57.6 %while.28 = (s32[]{:T(128)}, f32[2,1024,4]{1,2,0:T(4,128)S(1)}, f32[2,1024,4]{1,2,0:T(4,128)S(1)}, f32[2,1024,4,128]{3,1,0,2:T(8,128)}, bf16[2,1024,4,128]{3,2,1...) while((s32[]{:T(128)}, f32[2,1024,4]{1,2,0:T(4,128)S(1)}, ...), condition=%wide.region_3.4_spmd.clone, body=%wide.region_0.3_spmd.clone.sunk | while | flops 2193612800 | bytes 57807468 | solution.py:72
  81.1 1.6 constant_dynamic-slice_fusion.6
  82.7 0.1 broadcast_bitcast_fusion.2
  82.8 7.2 bitcast_reduce_fusion.5
  90.0 12.0 %bitcast_dynamic-update-slice_fusion.9 = f32[2,1024,4,128]{3,1,0,2:T(8,128)} fusion(f32[2,1024,4,128]{3,1,0,2:T(8,128)} %get-tuple-element.300, s32[]{:T(128)} %get-tuple-element.297, bf16[1024,4,128]{2,0,1:T(8,128)(2,1)} %get-tuple-element.312, f32[4,1024,1024]{1,2,0:T(8,128)} %get-tuple-element.284, f32[1024,4]{0,1:T(4,128)S(1)} %get-tuple-element.285, ...), kind=kOutput, calls=%fused_computation.28.clone.1 | convolution fusion | flops 1090519040 | bytes 19940864 | tf_op jit(solution)/shard_map/while/body/eval_jaxpr/lhp,phe->lhe/dot_general | solution.py:64
  102.0 7.9 fusion.98
  109.9 1.6 constant_dynamic-slice_fusion.6
  111.5 0.1 broadcast_bitcast_fusion.2
  111.6 7.2 bitcast_reduce_fusion.5
  118.8 12.0 %bitcast_dynamic-update-slice_fusion.9 = f32[2,1024,4,128]{3,1,0,2:T(8,128)} fusion(f32[2,1024,4,128]{3,1,0,2:T(8,128)} %get-tuple-element.300, s32[]{:T(128)} %get-tuple-element.297, bf16[1024,4,128]{2,0,1:T(8,128)(2,1)} %get-tuple-element.312, f32[4,1024,1024]{1,2,0:T(8,128)} %get-tuple-element.284, f32[1024,4]{0,1:T(4,128)S(1)} %get-tuple-element.285, ...), kind=kOutput, calls=%fused_computation.28.clone.1 | convolution fusion | flops 1090519040 | bytes 19940864 | tf_op jit(solution)/shard_map/while/body/eval_jaxpr/lhp,phe->lhe/dot_general | solution.py:64
  130.8 7.9 fusion.98
  138.7 290.1 %pmax.7 = bf16[2048,4]{0,1:T(4,128)(2,1)S(1)} all-reduce(bf16[2048,4]{0,1:T(4,128)(2,1)S(1)} %convert_element_type.61), channel_id=1, replica_groups=mesh['pos'=64,'head'=2] {'pos'}, use_global_device_ids=true, to_apply=%region_4.5 | all-reduce | flops 8192 | bytes 32768 | tf_op jit(solution)/shard_map/pmax | solution.py:78
  428.9 4.2 bitcast_multiply_fusion
  433.0 0.0 all-reduce.3.cloned.1.call-update
  433.1 0.0 all-reduce.5.cloned.1.call-start
  433.1 287.4 %psum.22 = f32[2048,4]{0,1:T(4,128)S(1)} all-reduce(f32[2048,4]{0,1:T(4,128)S(1)} %get-tuple-element.176), channel_id=1, replica_groups=mesh['pos'=64,'head'=2] {'pos'}, use_global_device_ids=true, to_apply=%region_6.7 | all-reduce | flops 8192 | bytes 65536 | tf_op jit(solution)/shard_map/psum | solution.py:82
  720.5 0.1 constant_dynamic-slice_fusion.2
  720.6 1.8 convolution_convert_fusion.4
  722.4 0.0 all-reduce.5.cloned.1.call-update
  722.4 0.0 all-gather.8.cloned.1.call-start
  722.5 128.8 %all-reduce.5.cloned.1.call-done = bf16[32,1024]{1,0:T(8,128)(2,1)} async-done(((bf16[32,1024]{1,0:T(8,128)(2,1)}), bf16[32,1024]{1,0:T(8,128)(2,1)}) %all-reduce.5.cloned.1.call-update) | async-done | bytes 65552 | tf_op jit(solution)/shard_map/psum | solution.py:88
  851.2 1.0 fusion.41
  852.2 2.1 fusion.40
  854.4 2.1 convolution_convert_fusion.5
  856.5 0.0 all-gather.8.cloned.1.call-update
  856.5 0.0 all-gather.6.cloned.1.call-start
  856.6 2.1 convolution_convert_fusion.6
  858.7 0.0 all-gather.6.cloned.1.call-update
  858.7 0.0 reduce-scatter.2.cloned.1.call-start
  858.8 3.4 convolution_convert_fusion.3
  862.2 1.3 reshape.91
  863.6 57.7 %all-gather.8.cloned.1.call-done = bf16[2048,512]{1,0:T(8,128)(2,1)} async-done(((bf16[32,512]{1,0:T(8,128)(2,1)}), bf16[2048,512]{1,0:T(8,128)(2,1)}) %all-gather.8.cloned.1.call-update) | async-done | bytes 2097168 | tf_op jit(solution)/shard_map/all_gather | solution.py:110
  921.3 3.3 copy_bitcast_fusion.4
  924.6 62.4 %all-gather.6.cloned.1.call-done = bf16[2048,512]{1,0:T(8,128)(2,1)} async-done(((bf16[32,512]{1,0:T(8,128)(2,1)}), bf16[2048,512]{1,0:T(8,128)(2,1)}) %all-gather.6.cloned.1.call-update) | async-done | bytes 2097168 | tf_op jit(solution)/shard_map/all_gather | solution.py:107
  987.0 2.0 copy_bitcast_fusion.5
  988.9 19.4 %while.27 = (s32[]{:T(128)}, f32[2,512,4]{1,2,0:T(4,128)S(1)}, f32[2,512,4,128]{3,1,2,0:T(8,128)}, bf16[2,512,4,128]{3,2,1,0:T(4,128)(2,1)S(1)}, bf16[2048,4,128...) while((s32[]{:T(128)}, f32[2,512,4]{1,2,0:T(4,128)S(1)}, ...), condition=%wide.region_12.13_spmd, body=%wide.region_9.12_spmd.sunk | while | flops 2181310464 | bytes 82403496 | solution.py:132
  989.0 0.2 constant_dynamic-slice_fusion.5
  989.2 2.4 bitcast_reduce_fusion.4
  991.7 3.7 fusion.94
  995.3 3.3 fusion.93
  998.7 0.2 constant_dynamic-slice_fusion.5
  998.9 2.4 bitcast_reduce_fusion.4
  1001.4 3.7 fusion.94
  1005.0 3.3 fusion.93
  1008.4 0.0 copy-start.6
  1008.4 2.0 divide_convert_fusion
  1010.4 0.8 copy.38
  1011.3 0.0 copy-start.1
  1011.3 2.6 convolution_convert_fusion
  1013.9 0.0 reduce-scatter.2.cloned.1.call-update
  1013.9 12.1 %reduce-scatter.2.cloned.1.call-done = bf16[512,1024]{1,0:T(8,128)(2,1)} async-done(((bf16[1024,1024]{1,0:T(8,128)(2,1)}), bf16[512,1024]{1,0:T(8,128)(2,1)}) %reduce-scatter.2.cloned.1.call-update) | async-done | bytes 1048592 | tf_op jit(solution)/shard_map/reduce_scatter | solution.py:139
  1026.0 1.5 fusion.34
  1027.5 2.4 fusion.35
  (36 shorter events, 0.2 us)
Async XLA Ops:
  6.5 2.4 copy-start
  6.5 70.6 %all-gather.4.cloned.1.call-start = ((), (), s32[]{:S(2)}) async-start(), calls=%async_computation.1 | async-start | bytes 2129920 | tf_op jit(solution)/shard_map/all_gather | solution.py:49
  8.9 711.7 %all-reduce.3.cloned.1.call-start = ((), (), s32[]{:S(2)}) async-start(), calls=%async_computation.2 | async-start | bytes 8388608 | tf_op jit(solution)/shard_map/psum | solution.py:82
  14.1 5.8 copy-start.7
  433.0 287.6 %copy-start.5 = (bf16[512,1024]{1,0:T(8,128)(2,1)S(1)}, bf16[512,1024]{1,0:T(8,128)(2,1)}, u32[]{:S(2)}) copy-start(bf16[512,1024]{1,0:T(8,128)(2,1)} %param.22) | copy-start | bytes 3145732
  433.1 418.2 %all-reduce.5.cloned.1.call-start = ((), (), s32[]{:S(2)}) async-start(), calls=%async_computation.3 | async-start | bytes 131072 | tf_op jit(solution)/shard_map/psum | solution.py:88
  722.4 198.9 %all-gather.8.cloned.1.call-start = ((), (), s32[]{:S(2)}) async-start(), calls=%async_computation.5 | async-start | bytes 2129920 | tf_op jit(solution)/shard_map/all_gather | solution.py:110
  856.5 130.5 %all-gather.6.cloned.1.call-start = ((), (), s32[]{:S(2)}) async-start(), calls=%async_computation.4 | async-start | bytes 2129920 | tf_op jit(solution)/shard_map/all_gather | solution.py:107
  858.7 167.3 %reduce-scatter.2.cloned.1.call-start = ((), (), s32[]{:S(2)}) async-start(), calls=%async_computation.6 | async-start | bytes 3145728 | tf_op jit(solution)/shard_map/reduce_scatter | solution.py:139
  989.2 2.5 copy-start.2
  989.2 2.5 copy-start.4
  995.3 3.3 copy-start.3
  998.9 2.5 copy-start.2
  998.9 2.5 copy-start.4
  1005.0 3.3 copy-start.3
  1008.4 2.9 copy-start.6
  1011.3 18.7 %copy-start.1 = (bf16[1024,1024]{1,0:T(8,128)(2,1)S(1)}, bf16[1024,1024]{1,0:T(8,128)(2,1)}, u32[]{:S(2)}) copy-start(bf16[1024,1024]{1,0:T(8,128)(2,1)} %param.16) | copy-start | bytes 6291460
Sparse Core Ops, SparseCore 0:
  10.2 66.8 all-gather.3
  433.2 187.4 all-reduce.2
  722.6 128.6 all-reduce.4
  856.6 64.6 all-gather.7
  924.0 62.9 all-gather.5
  1014.0 11.9 reduce-scatter.1
where the time goes:
time: 1040 us
  blocking collectives  578 us (56%)
  waiting for transfers between devices  318 us (31%)
  matrix products  74.2 us (7%)
  other arithmetic  33.5 us (3%)
  local copies, waits for them, and re-layouts  19.1 us (2%)
  between operations  13.6 us (1%)
    pmax x1, blocking collectives, per_device(): lax.pmax(row_max.astype(jnp.bfloat16), 'pos').astype(row_max.dtype)  290 us
    psum x1, blocking collectives, per_device(): all_totals, all_sums = lax.psum((scaled_totals, scaled_sums), 'pos')  287 us
    psum x1, waiting for transfers between devices, per_device(): lax.psum(partial_terms.astype(jnp.bfloat16), 'head').astype(jnp.float32)  129 us
    all_gather x1, waiting for transfers between devices, per_device(): lax.all_gather(lat_keys, 'pos', axis=0, tiled=True)  62.4 us
    all_gather x1, waiting for transfers between devices, per_device(): lax.all_gather(lat_values, 'pos', axis=0, tiled=True)  57.7 us
    all_gather x1, waiting for transfers between devices, per_device(): lax.all_gather(own_queries, 'pos', axis=0, tiled=True)  57.2 us
    dot_general x2, matrix products, cross_block(): jnp.einsum('lhp,phe->lhe', exponent.astype(jnp.bfloat16), pos_values, pre...  24 us
  transfers between devices with their start and end apart: 6, of which 5 were waited for; matrix products, arithmetic and copies ran while one was open for 2% of the time, Pallas kernels for 0%

commit v1 on v0

v1 whole, which is shorter than its diff:
```python
import functools

import jax
import jax.numpy as jnp
from jax import lax
from jax.experimental import pallas as pl
from jax.experimental.pallas import tpu as pltpu
from jax.sharding import PartitionSpec as P

HEAD_DIM = 128
BLK = 128
SCALE = HEAD_DIM ** (-0.5)
LOG2E = 1.4426950408889634
MASKED = -1e30
EPS = 1e-05
F32 = jnp.float32
BF16 = jnp.bfloat16
ROW_BLOCK = 256
LSE_ROWS = 8


def rms_norm(values):
    return values * lax.rsqrt(jnp.mean(values * values, axis=-1, keepdims=True) + EPS)


def nt_dot(a, b):
    return lax.dot_general(a, b, (((1,), (1,)), ((), ())), preferred_element_type=F32)


def cross_kernel(count_ref, q_ref, k_ref, v_ref, out_ref, *, lat_local):
    heads = q_ref.shape[1] // HEAD_DIM
    rows = q_ref.shape[0]
    owners = rows // lat_local
    span = heads * lat_local
    keys = k_ref.shape[0]
    valid = count_ref[0] * BLK

    def run(masked):
        columns = []
        for h in range(heads):
            cols = slice(h * HEAD_DIM, (h + 1) * HEAD_DIM)
            s = nt_dot(q_ref[:, cols], k_ref[:, cols])
            if masked:
                where = lax.broadcasted_iota(jnp.int32, s.shape, 1) < valid
                s = jnp.where(where, s, MASKED)
            m = jnp.max(s, axis=1, keepdims=True)
            p = jnp.exp2((s - m) * (SCALE * LOG2E))
            total = jnp.sum(p, axis=1, keepdims=True)
            o = jnp.dot(p.astype(BF16), v_ref[:, cols], preferred_element_type=F32)
            o = (o / total).astype(BF16)
            out_ref[:, h * lat_local : (h + 1) * lat_local, :] = o.reshape(owners, lat_local, HEAD_DIM)
            columns.append(m * SCALE + jnp.log(total))
        for d in range(owners):
            part = jnp.concatenate(
                [c[d * lat_local : (d + 1) * lat_local] for c in columns], axis=0
            )
            row = jnp.transpose(jnp.broadcast_to(part, (span, HEAD_DIM)))[:LSE_ROWS]
            hi = row.astype(BF16).astype(F32)
            mid = (row - hi).astype(BF16).astype(F32)
            low = (row - hi - mid).astype(BF16).astype(F32)
            place = lax.broadcasted_iota(jnp.int32, row.shape, 0)
            packed = jnp.where(place == 0, hi, jnp.where(place == 1, mid, jnp.where(place == 2, low, 0.0)))
            out_ref[d, span : span + LSE_ROWS, :] = packed.astype(BF16)

    full = valid == keys

    @pl.when(full)
    def _():
        run(False)

    @pl.when(jnp.logical_not(full))
    def _():
        run(True)


def combine_kernel(core_ref, r_ref, w_ref, own_ref, other_ref, terms_ref, *, lat_local):
    devices, tall, _ = r_ref.shape
    span = tall - LSE_ROWS
    heads = span // lat_local
    lse = jnp.sum(r_ref[:, span : span + LSE_ROWS, :].astype(F32), axis=1)
    w = jnp.exp(lse - jnp.max(lse, axis=0, keepdims=True))
    w = w / jnp.sum(w, axis=0, keepdims=True)
    wt = jnp.transpose(w)
    acc = jnp.zeros((span, HEAD_DIM), F32)
    for d in range(devices):
        acc = acc + wt[:, d : d + 1] * r_ref[d, :span, :].astype(F32)
    attended = acc.astype(BF16)
    terms = jnp.zeros((lat_local, w_ref.shape[1]), F32)
    for h in range(heads):
        terms = terms + jnp.dot(
            attended[h * lat_local : (h + 1) * lat_local],
            w_ref[h * HEAD_DIM : (h + 1) * HEAD_DIM, :],
            preferred_element_type=F32,
        )
    half = lat_local // 2
    terms_ref[...] = terms.reshape(2, half, w_ref.shape[1])
    own_ref[...] = terms_ref[core_ref[0]]
    other_ref[...] = terms_ref[1 - core_ref[0]].astype(BF16)


def latent_kernel(own_ref, recv_ref, w_ref, out_ref):
    normed = rms_norm(own_ref[...] + recv_ref[...].astype(F32))
    hidden = jax.nn.gelu(jnp.dot(normed.astype(BF16), w_ref[...], preferred_element_type=F32))
    rows = (normed + hidden).astype(BF16)
    out_ref[...] = jnp.broadcast_to(rows[None], out_ref.shape)


def decode_kernel(base_ref, q_ref, ka_ref, va_ref, kb_ref, vb_ref, w_ref, out_ref):
    heads = q_ref.shape[1] // HEAD_DIM
    outs = []
    for h in range(heads):
        cols = slice(h * HEAD_DIM, (h + 1) * HEAD_DIM)
        q = q_ref[:, cols]
        sa = nt_dot(q, ka_ref[:, cols])
        sb = nt_dot(q, kb_ref[:, cols])
        m = jnp.maximum(jnp.max(sa, axis=1, keepdims=True), jnp.max(sb, axis=1, keepdims=True))
        pa = jnp.exp2((sa - m) * (SCALE * LOG2E))
        pb = jnp.exp2((sb - m) * (SCALE * LOG2E))
        total = jnp.sum(pa, axis=1, keepdims=True) + jnp.sum(pb, axis=1, keepdims=True)
        o = jnp.dot(pa.astype(BF16), va_ref[:, cols], preferred_element_type=F32)
        o = o + jnp.dot(pb.astype(BF16), vb_ref[:, cols], preferred_element_type=F32)
        outs.append((o / total).astype(BF16))
    attended = jnp.concatenate(outs, axis=1)
    out_ref[...] = jnp.dot(attended, w_ref[...], preferred_element_type=F32).astype(out_ref.dtype)


def final_kernel(own_ref, recv_ref, out_ref):
    out_ref[...] = rms_norm(own_ref[...] + recv_ref[...].astype(F32)).astype(out_ref.dtype)


def full_spec(array):
    return pl.BlockSpec(array.shape, lambda *_: (0,) * array.ndim)


def params(limit=56 << 20):
    return pltpu.CompilerParams(vmem_limit_bytes=limit)


def cross(count, q, k, v, lat_local):
    lat, columns = q.shape
    heads = columns // HEAD_DIM
    tall = heads * lat_local + LSE_ROWS
    block = min(ROW_BLOCK, lat)
    return pl.pallas_call(
        functools.partial(cross_kernel, lat_local=lat_local),
        out_shape=jax.ShapeDtypeStruct((lat // lat_local, tall, HEAD_DIM), BF16),
        grid_spec=pltpu.PrefetchScalarGridSpec(
            num_scalar_prefetch=1,
            grid=(lat // block,),
            in_specs=[
                pl.BlockSpec((block, columns), lambda i, c: (i, 0)),
                full_spec(k),
                full_spec(v),
            ],
            out_specs=pl.BlockSpec((block // lat_local, tall, HEAD_DIM), lambda i, c: (i, 0, 0)),
        ),
        compiler_params=params(),
        name="cross",
    )(count, q, k, v)


def combine(core, r, w_out, lat_local):
    width = w_out.shape[1]
    half = lat_local // 2
    vmem = pl.BlockSpec(memory_space=pltpu.VMEM)
    return pl.pallas_call(
        functools.partial(combine_kernel, lat_local=lat_local),
        out_shape=(
            jax.ShapeDtypeStruct((half, width), F32),
            jax.ShapeDtypeStruct((half, width), BF16),
        ),
        in_specs=[pl.BlockSpec(memory_space=pltpu.SMEM), vmem, vmem],
        out_specs=(vmem, vmem),
        scratch_shapes=[pltpu.VMEM((2, half, width), F32)],
        compiler_params=params(24 << 20),
        name="combine",
    )(core, r, w_out)


def latent_rows(own, recv, w_mlp, devices):
    vmem = pl.BlockSpec(memory_space=pltpu.VMEM)
    return pl.pallas_call(
        latent_kernel,
        out_shape=jax.ShapeDtypeStruct((devices,) + own.shape, BF16),
        in_specs=[vmem] * 3,
        out_specs=vmem,
        compiler_params=params(24 << 20),
        name="latent",
    )(own, recv, w_mlp)


def decode(base, q, ka, va, kb, vb, w_pout, dtype):
    rows, columns = q.shape[0] // 2, q.shape[1]
    width = w_pout.shape[1]
    block = min(ROW_BLOCK, rows)
    return pl.pallas_call(
        decode_kernel,
        out_shape=jax.ShapeDtypeStruct((rows, width), dtype),
        grid_spec=pltpu.PrefetchScalarGridSpec(
            num_scalar_prefetch=1,
            grid=(rows // block,),
            in_specs=[
                pl.BlockSpec((block, columns), lambda i, b: (b[0] * (rows // block) + i, 0)),
                *[full_spec(x) for x in (ka, va, kb, vb, w_pout)],
            ],
            out_specs=pl.BlockSpec((block, width), lambda i, b: (i, 0)),
        ),
        compiler_params=params(),
        cost_estimate=pl.CostEstimate(
            flops=4 * rows * columns * 2 * ka.shape[0], bytes_accessed=8 << 20, transcendentals=1 << 22
        ),
        name="decode",
    )(base, q, ka, va, kb, vb, w_pout)


def finish(own, recv):
    rows, width = own.shape
    block = min(256, rows)
    spec = pl.BlockSpec((block, width), lambda i: (i, 0))
    return pl.pallas_call(
        final_kernel,
        out_shape=jax.ShapeDtypeStruct((rows, width), BF16),
        grid=(rows // block,),
        in_specs=[spec, spec],
        out_specs=spec,
        compiler_params=params(24 << 20),
        name="finish",
    )(own, recv)


def project(a, w):
    return jnp.dot(a, w, preferred_element_type=F32).astype(BF16)


def per_device(
    devices,
    inputs,
    valid_blocks,
    latents,
    w_query,
    w_key,
    w_value,
    w_out,
    w_mlp,
    w_lkey,
    w_lvalue,
    w_pquery,
    w_pout,
):
    lat_local = latents.shape[0]
    columns = w_key.shape[1]
    width = inputs.shape[1]
    core = lax.axis_index("head").astype(jnp.int32).reshape(1)
    swap = [(0, 1), (1, 0)]

    own_queries = project(latents, w_query)
    spread = jnp.broadcast_to(own_queries[None], (devices,) + own_queries.shape)
    lat_queries = lax.all_to_all(spread, "pos", 0, 0).reshape(devices * lat_local, columns)
    keys = project(inputs, w_key)
    values = project(inputs, w_value)
    pos_queries = project(inputs, w_pquery)

    count = jnp.sum(valid_blocks).astype(jnp.int32).reshape(1)
    partial = cross(count, lat_queries, keys, values, lat_local)
    gathered = lax.all_to_all(partial, "pos", 0, 0)
    own, other = combine(core, gathered, w_out, lat_local)
    recv = lax.ppermute(other, "head", swap)
    rows = latent_rows(own, recv, w_mlp, devices)
    rows_a = lax.all_to_all(rows, "pos", 0, 0).reshape(devices * lat_local // 2, width)
    rows_b = lax.ppermute(rows_a, "head", swap)
    ka, va = project(rows_a, w_lkey), project(rows_a, w_lvalue)
    kb, vb = project(rows_b, w_lkey), project(rows_b, w_lvalue)
    away = decode(1 - core, pos_queries, ka, va, kb, vb, w_pout, BF16)
    arrived = lax.ppermute(away, "head", swap)
    home = decode(core, pos_queries, ka, va, kb, vb, w_pout, F32)
    return finish(home, arrived)


def solution(mesh):
    placed = (
        P("pos", None),
        P("pos"),
        P("pos", None),
        P(None, "head"),
        P(None, "head"),
        P(None, "head"),
        P("head", None),
        P(),
        P(None, "head"),
        P(None, "head"),
        P(None, "head"),
        P("head", None),
    )
    return jax.shard_map(
        functools.partial(per_device, mesh.shape["pos"]),
        mesh=mesh,
        in_specs=placed,
        out_specs=P(("pos", "head"), None),
        check_vma=False,
    )
```

time: 1040 us -> 183 us (0.18)
  blocking collectives: 578 us -> 34.7 us
  waiting for transfers between devices: 318 us -> 53.7 us
  matrix products: 74.2 us -> 17.3 us
  Pallas kernels: 0 us -> 48.9 us
  other arithmetic: 33.5 us -> 0.71 us
  starting transfers between devices: 0.21 us -> 24.7 us
  local copies, waits for them, and re-layouts: 19.1 us -> 3.23 us
  between operations: 13.6 us -> 0.08 us
    pmax x1 -> x0, blocking collectives: 290 us -> none  [per_device(): lax.pmax(row_max.astype(jnp.bfloat16), 'pos').astype(row_max.dtype)]
    psum x1 -> x0, blocking collectives: 287 us -> none  [per_device(): all_totals, all_sums = lax.psum((scaled_totals, scaled_sums), 'pos')]
    all_gather x3 -> x0, waiting for transfers between devices: 177 us -> none  [the longest x1 62.4 us: per_device(): lax.all_gather(lat_keys, 'pos', axis=0, tiled=True)]
    psum x2 -> x0, waiting for transfers between devices: 129 us -> none  [the longest x1 129 us: per_device(): lax.psum(partial_terms.astype(jnp.bfloat16), 'head').astype(jnp.float32)]
    dot_general x17 -> x8, matrix products: 74.2 us -> 17.3 us  [project(): return jnp.dot(a, w, preferred_element_type=F32).astype(BF16)]
    all_to_all x0 -> x2, waiting for transfers between devices: none -> 52.9 us  [the longest x1 29.8 us: per_device(): gathered = lax.all_to_all(partial, 'pos', 0, 0)]
    pallas_call x0 -> x6, Pallas kernels: none -> 48.9 us  [the longest x2 21.8 us: decode(): pl.pallas_call(decode_kernel, out_shape=jax.ShapeDtypeStruct((rows, width...]
    all_to_all x0 -> x1, blocking collectives: none -> 34.7 us  [per_device(): lax.all_to_all(rows, 'pos', 0, 0).reshape(devices * lat_local // 2, width)]
  transfers between devices with their start and end apart: 6 -> 5, of which waited for: 5 -> 3; matrix products, arithmetic and copies ran while one was open for 2% -> 6% of each run, Pallas kernels for 0% -> 6%
where the time goes in v1:
time: 183 us
  waiting for transfers between devices  53.7 us (29%)
  Pallas kernels  48.9 us (27%)
  blocking collectives  34.7 us (19%)
  starting transfers between devices  24.7 us (13%)
  matrix products  17.3 us (9%)
  local copies, waits for them, and re-layouts  3.23 us (2%)
    all_to_all x1, blocking collectives, per_device(): lax.all_to_all(rows, 'pos', 0, 0).reshape(devices * lat_local // 2, width)  34.7 us
    all_to_all x1, waiting for transfers between devices, per_device(): gathered = lax.all_to_all(partial, 'pos', 0, 0)  29.8 us
    all_to_all x1, waiting for transfers between devices, per_device(): lax.all_to_all(spread, 'pos', 0, 0).reshape(devices * lat_local, columns)  23.1 us
    pallas_call x2, Pallas kernels, decode(): pl.pallas_call(decode_kernel, out_shape=jax.ShapeDtypeStruct((rows, width...  21.8 us
    pallas_call x1, Pallas kernels, cross(): pl.pallas_call(functools.partial(cross_kernel, lat_local=lat_local), out_...  21.6 us
    dot_general x8, matrix products, project(): return jnp.dot(a, w, preferred_element_type=F32).astype(BF16)  17.3 us
    all_to_all x1, starting transfers between devices, per_device(): lax.all_to_all(spread, 'pos', 0, 0).reshape(devices * lat_local, columns)  12.3 us
    all_to_all x1, starting transfers between devices, per_device(): gathered = lax.all_to_all(partial, 'pos', 0, 0)  7.74 us
  transfers between devices with their start and end apart: 5, of which 3 were waited for; matrix products, arithmetic and copies ran while one was open for 6% of the time, Pallas kernels for 6%

profile of v1, /device:TPU:1, one launch (start us, length us, event | category | flops | bytes accessed | tf_op | source)
XLA Modules:
  0.0 183.3 jit_solution(6070786367735255321)
XLA Ops:
  0.0 0.0 copy-start
  0.0 1.7 convolution_convert_fusion.7
  1.7 1.6 broadcast_in_dim.2
  3.3 0.0 copy-start.9
  3.3 0.0 copy-start.4
  3.3 12.3 %all-to-all-start = ((bf16[64,32,512]{2,1,0:T(8,128)(2,1)}), bf16[64,32,512]{2,1,0:T(8,128)(2,1)}, u32[]{:S(2)}, u32[]{:S(2)}) async-start(bf16[64,32,512]{2,1,0:T(8,128)(2,1)} %broadcast_in_dim.2), calls=%async_computation | async-start | bytes 4194304 | tf_op jit(solution)/shard_map/all_to_all | solution.py:258
  15.6 0.0 copy-done.9
  15.7 0.7 reduce_sum.9
  16.4 0.0 copy-done
  16.4 0.0 copy-done.4
  16.4 0.0 copy-start.5
  16.4 2.2 %convolution_convert_fusion.5.k_ref = bf16[1024,512]{1,0:T(8,128)(2,1)} fusion(bf16[1024,1024]{1,0:T(8,128)(2,1)S(1)} %copy-done, bf16[1024,512]{1,0:T(8,128)(2,1)S(1)} %copy-done.4), kind=kOutput, calls=%fused_computation.5 | convolution fusion | flops 1074266112 | bytes 4194304 | tf_op jit(solution)/shard_map/dot_general | solution.py:232
  18.6 0.0 copy-done.5
  18.6 2.2 %convolution_convert_fusion.4.v_ref = bf16[1024,512]{1,0:T(8,128)(2,1)} fusion(bf16[1024,1024]{1,0:T(8,128)(2,1)S(1)} %copy-done, bf16[1024,512]{1,0:T(8,128)(2,1)S(1)} %copy-done.5), kind=kOutput, calls=%fused_computation.4 | convolution fusion | flops 1074266112 | bytes 4194304 | tf_op jit(solution)/shard_map/dot_general | solution.py:232
  20.8 23.1 %all-to-all-done = bf16[64,32,512]{2,1,0:T(8,128)(2,1)} async-done(((bf16[64,32,512]{2,1,0:T(8,128)(2,1)}), bf16[64,32,512]{2,1,0:T(8,128)(2,1)}, u32[]{:S(2)}, u32[]{:S(2)}) %all-to-all-start) | async-done | bytes 2097184 | tf_op jit(solution)/shard_map/all_to_all | solution.py:258
  44.0 21.6 %cross.1 = bf16[64,136,128]{2,1,0:T(8,128)(2,1)} custom-call(s32[1]{0:T(128)} %bitcast.1.count_ref, bf16[2048,512]{1,0:T(8,128)(2,1)} %bitcast.2.q_ref, bf16[1024,512]{1,0:T(8,128)(2,1)} %convolution_convert_fusion.5.k_ref, bf16[1024,512]{1,0:T(8,128)(2,1)} %convolution_convert_fusion.4.v_ref), custom_call_target="tpu_custom_call" | custom-call | tf_op jit(solution)/shard_map/cross/pallas_call | solution.py:144
  65.6 0.0 copy-start.3
  65.6 7.7 %all-to-all-start.1 = ((bf16[64,136,128]{2,1,0:T(8,128)(2,1)}), bf16[64,136,128]{2,1,0:T(8,128)(2,1)}, u32[]{:S(2)}, u32[]{:S(2)}) async-start(bf16[64,136,128]{2,1,0:T(8,128)(2,1)} %cross.1), calls=%async_computation.1 | async-start | bytes 4456448 | tf_op jit(solution)/shard_map/all_to_all | solution.py:265
  73.3 29.8 %all-to-all-done.1.r_ref = bf16[64,136,128]{2,1,0:T(8,128)(2,1)} async-done(((bf16[64,136,128]{2,1,0:T(8,128)(2,1)}), bf16[64,136,128]{2,1,0:T(8,128)(2,1)}, u32[]{:S(2)}, u32[]{:S(2)}) %all-to-all-start.1) | async-done | bytes 2228256 | tf_op jit(solution)/shard_map/all_to_all | solution.py:265
  103.1 0.0 copy-start.2
  103.1 0.0 copy-done.3
  103.1 3.6 %combine.1 = (f32[16,1024]{1,0:T(8,128)S(1)}, bf16[16,1024]{1,0:T(8,128)(2,1)S(1)}) custom-call(s32[1]{0:T(128)} %bitcast.core_ref.base_ref, bf16[64,136,128]{2,1,0:T(8,128)(2,1)} %all-to-all-done.1.r_ref, bf16[512,1024]{1,0:T(8,128)(2,1)S(1)} %copy-done.3), custom_call_target="tpu_custom_call" | custom-call | tf_op jit(solution)/shard_map/combine/pallas_call | solution.py:166
  106.7 2.6 %collective-permute-start = (bf16[16,1024]{1,0:T(8,128)(2,1)S(1)}, bf16[16,1024]{1,0:T(8,128)(2,1)S(1)}, u32[]{:S(2)}, u32[]{:S(2)}) collective-permute-start(bf16[16,1024]{1,0:T(8,128)(2,1)S(1)} %get-tuple-element.8), channel_id=1, source_target_pairs={{0,1},{1,0},{2,3},{3,2},{4,5},{5,4},{6,7},{7,6},{8,9},{9,8},{10,11... | collective-permute-start | bytes 98312 | tf_op jit(solution)/shard_map/ppermute | solution.py:267
  109.3 0.9 collective-permute-done.recv_ref
  110.1 0.0 copy-done.2
  110.1 0.6 latent.1
  110.7 0.0 copy-start.6
  110.7 34.7 %all_to_all.15 = bf16[64,16,1024]{2,1,0:T(8,128)(2,1)S(1)} all-to-all(bf16[64,16,1024]{2,1,0:T(8,128)(2,1)S(1)} %latent.1), channel_id=1, replica_groups=mesh['pos'=64,'head'=2] {'pos'}, dimensions={0} | all-to-all | bytes 4194304 | tf_op jit(solution)/shard_map/all_to_all | solution.py:269
  145.4 2.0 %collective-permute-start.1 = (bf16[1024,1024]{1,0:T(8,128)(2,1)S(1)}, bf16[1024,1024]{1,0:T(8,128)(2,1)S(1)}, u32[]{:S(2)}, u32[]{:S(2)}) collective-permute-start(bf16[1024,1024]{1,0:T(8,128)(2,1)S(1)} %bitcast.20), channel_id=1, source_target_pairs={{0,1},{1,0},{2,3},{3,2},{4,5},{5,4},{6,7},{7,6},{8,9},{9,8},{10,11... | collective-permute-start | bytes 6291464 | tf_op jit(solution)/shard_map/ppermute | solution.py:270
  147.4 0.0 copy-done.6
  147.4 0.0 copy-start.7
  147.4 2.2 %convolution_convert_fusion.6.q_ref = bf16[1024,512]{1,0:T(8,128)(2,1)} fusion(bf16[1024,1024]{1,0:T(8,128)(2,1)S(1)} %copy-done, bf16[1024,512]{1,0:T(8,128)(2,1)S(1)} %copy-done.6), kind=kOutput, calls=%fused_computation.6 | convolution fusion | flops 1074266112 | bytes 4194304 | tf_op jit(solution)/shard_map/dot_general | solution.py:232
  149.7 0.0 copy-done.7
  149.7 0.0 copy-start.8
  149.7 2.2 %convolution_convert_fusion.2.va_ref = bf16[1024,512]{1,0:T(8,128)(2,1)} fusion(bf16[1024,1024]{1,0:T(8,128)(2,1)S(1)} %bitcast.21, bf16[1024,512]{1,0:T(8,128)(2,1)S(1)} %copy-done.7), kind=kOutput, calls=%fused_computation.2 | convolution fusion | flops 1074266112 | bytes 4194304 | tf_op jit(solution)/shard_map/dot_general | solution.py:232
  151.9 0.0 copy-done.8
  151.9 2.2 %convolution_convert_fusion.3.ka_ref = bf16[1024,512]{1,0:T(8,128)(2,1)} fusion(bf16[1024,1024]{1,0:T(8,128)(2,1)S(1)} %bitcast.22, bf16[1024,512]{1,0:T(8,128)(2,1)S(1)} %copy-done.8), kind=kOutput, calls=%fused_computation.3 | convolution fusion | flops 1074266112 | bytes 4194304 | tf_op jit(solution)/shard_map/dot_general | solution.py:232
  154.1 0.0 collective-permute-done.1
  154.1 2.3 %convolution_convert_fusion.vb_ref = bf16[1024,512]{1,0:T(8,128)(2,1)} fusion(bf16[1024,1024]{1,0:T(8,128)(2,1)S(1)} %collective-permute-done.1, bf16[1024,512]{1,0:T(8,128)(2,1)S(1)} %copy-done.7), kind=kOutput, calls=%fused_computation | convolution fusion | flops 1074266112 | bytes 4194304 | tf_op jit(solution)/shard_map/dot_general | solution.py:232
  156.4 2.2 %convolution_convert_fusion.1.kb_ref = bf16[1024,512]{1,0:T(8,128)(2,1)} fusion(bf16[1024,1024]{1,0:T(8,128)(2,1)S(1)} %collective-permute-done.1, bf16[1024,512]{1,0:T(8,128)(2,1)S(1)} %copy-done.8), kind=kOutput, calls=%fused_computation.1 | convolution fusion | flops 1074266112 | bytes 4194304 | tf_op jit(solution)/shard_map/dot_general | solution.py:232
  158.6 10.8 %decode.3 = bf16[512,1024]{1,0:T(8,128)(2,1)} custom-call(s32[1]{0:T(128)S(6)} %sub.3.base_ref, bf16[1024,512]{1,0:T(8,128)(2,1)} %convolution_convert_fusion.6.q_ref, bf16[1024,512]{1,0:T(8,128)(2,1)} %convolution_convert_fusion.3.ka_ref, bf16[1024,512]{1,0:T(8,128)(2,1)} %convolution_convert_fusion.2.va_ref, ...), custom_call_target="tpu_custom_call" | custom-call | flops 2147483648 | bytes 8388608 | tf_op jit(solution)/shard_map/decode/pallas_call | solution.py:196
  169.4 0.0 collective-permute-start.2
  169.4 11.0 %decode.2.own_ref = f32[512,1024]{1,0:T(8,128)} custom-call(s32[1]{0:T(128)} %bitcast.core_ref.base_ref, bf16[1024,512]{1,0:T(8,128)(2,1)} %convolution_convert_fusion.6.q_ref, bf16[1024,512]{1,0:T(8,128)(2,1)} %convolution_convert_fusion.3.ka_ref, bf16[1024,512]{1,0:T(8,128)(2,1)} %convolution_convert_fusion.2.va_ref, ...), custom_call_target="tpu_custom_call" | custom-call | flops 2147483648 | bytes 8388608 | tf_op jit(solution)/shard_map/decode/pallas_call | solution.py:196
  180.4 0.0 collective-permute-done.2.recv_ref
  180.4 0.0 copy-start.1
  180.4 1.6 copy-done.1
  182.0 1.3 finish.1
Async XLA Ops:
  0.0 16.4 %copy-start = (bf16[1024,1024]{1,0:T(8,128)(2,1)S(1)}, bf16[1024,1024]{1,0:T(8,128)(2,1)}, u32[]{:S(2)}) copy-start(bf16[1024,1024]{1,0:T(8,128)(2,1)} %param.12) | copy-start | bytes 6291460
  3.3 12.4 %copy-start.9 = (s32[8]{0:T(128)S(1)}, s32[8]{0:T(128)}, u32[]{:S(2)}) copy-start(s32[8]{0:T(128)} %param.13) | copy-start | bytes 100
  3.3 13.1 %copy-start.4 = (bf16[1024,512]{1,0:T(8,128)(2,1)S(1)}, bf16[1024,512]{1,0:T(8,128)(2,1)}, u32[]{:S(2)}) copy-start(bf16[1024,512]{1,0:T(8,128)(2,1)} %param.16) | copy-start | bytes 3145732
  3.3 40.7 %all-to-all-start = ((bf16[64,32,512]{2,1,0:T(8,128)(2,1)}), bf16[64,32,512]{2,1,0:T(8,128)(2,1)}, u32[]{:S(2)}, u32[]{:S(2)}) async-start(bf16[64,32,512]{2,1,0:T(8,128)(2,1)} %broadcast_in_dim.2), calls=%async_computation | async-start | bytes 4194304 | tf_op jit(solution)/shard_map/all_to_all | solution.py:258
  16.4 2.2 %copy-start.5 = (bf16[1024,512]{1,0:T(8,128)(2,1)S(1)}, bf16[1024,512]{1,0:T(8,128)(2,1)}, u32[]{:S(2)}) copy-start(bf16[1024,512]{1,0:T(8,128)(2,1)} %param.17) | copy-start | bytes 3145732
  65.6 37.5 %copy-start.3 = (bf16[512,1024]{1,0:T(8,128)(2,1)S(1)}, bf16[512,1024]{1,0:T(8,128)(2,1)}, u32[]{:S(2)}) copy-start(bf16[512,1024]{1,0:T(8,128)(2,1)} %w_ref.4) | copy-start | bytes 3145732
  65.6 37.5 %all-to-all-start.1 = ((bf16[64,136,128]{2,1,0:T(8,128)(2,1)}), bf16[64,136,128]{2,1,0:T(8,128)(2,1)}, u32[]{:S(2)}, u32[]{:S(2)}) async-start(bf16[64,136,128]{2,1,0:T(8,128)(2,1)} %cross.1), calls=%async_computation.1 | async-start | bytes 4456448 | tf_op jit(solution)/shard_map/all_to_all | solution.py:265
  103.1 7.0 %copy-start.2 = (bf16[1024,1024]{1,0:T(8,128)(2,1)S(1)}, bf16[1024,1024]{1,0:T(8,128)(2,1)}, u32[]{:S(2)}) copy-start(bf16[1024,1024]{1,0:T(8,128)(2,1)} %w_ref.5) | copy-start | bytes 6291460
  106.7 3.4 %collective-permute-start = (bf16[16,1024]{1,0:T(8,128)(2,1)S(1)}, bf16[16,1024]{1,0:T(8,128)(2,1)S(1)}, u32[]{:S(2)}, u32[]{:S(2)}) collective-permute-start(bf16[16,1024]{1,0:T(8,128)(2,1)S(1)} %get-tuple-element.8), channel_id=1, source_target_pairs={{0,1},{1,0},{2,3},{3,2},{4,5},{5,4},{6,7},{7,6},{8,9},{9,8},{10,11... | collective-permute-start | bytes 98312 | tf_op jit(solution)/shard_map/ppermute | solution.py:267
  110.7 36.7 %copy-start.6 = (bf16[1024,512]{1,0:T(8,128)(2,1)S(1)}, bf16[1024,512]{1,0:T(8,128)(2,1)}, u32[]{:S(2)}) copy-start(bf16[1024,512]{1,0:T(8,128)(2,1)} %param.22) | copy-start | bytes 3145732
  145.4 8.7 %collective-permute-start.1 = (bf16[1024,1024]{1,0:T(8,128)(2,1)S(1)}, bf16[1024,1024]{1,0:T(8,128)(2,1)S(1)}, u32[]{:S(2)}, u32[]{:S(2)}) collective-permute-start(bf16[1024,1024]{1,0:T(8,128)(2,1)S(1)} %bitcast.20), channel_id=1, source_target_pairs={{0,1},{1,0},{2,3},{3,2},{4,5},{5,4},{6,7},{7,6},{8,9},{9,8},{10,11... | collective-permute-start | bytes 6291464 | tf_op jit(solution)/shard_map/ppermute | solution.py:270
  147.4 2.2 %copy-start.7 = (bf16[1024,512]{1,0:T(8,128)(2,1)S(1)}, bf16[1024,512]{1,0:T(8,128)(2,1)}, u32[]{:S(2)}) copy-start(bf16[1024,512]{1,0:T(8,128)(2,1)} %param.21) | copy-start | bytes 3145732
  149.7 2.2 %copy-start.8 = (bf16[1024,512]{1,0:T(8,128)(2,1)S(1)}, bf16[1024,512]{1,0:T(8,128)(2,1)}, u32[]{:S(2)}) copy-start(bf16[1024,512]{1,0:T(8,128)(2,1)} %param.20) | copy-start | bytes 3145732
  169.4 11.0 %collective-permute-start.2 = (bf16[512,1024]{1,0:T(8,128)(2,1)}, bf16[512,1024]{1,0:T(8,128)(2,1)S(1)}, u32[]{:S(2)}, u32[]{:S(2)}) collective-permute-start(bf16[512,1024]{1,0:T(8,128)(2,1)} %decode.3), channel_id=1, source_target_pairs={{0,1},{1,0},{2,3},{3,2},{4,5},{5,4},{6,7},{7,6},{8,9},{9,8},{10,11... | collective-permute-start | bytes 3145736 | tf_op jit(solution)/shard_map/ppermute | solution.py:274
  180.4 1.6 copy-start.1

commit v2 on v1

v2 whole, which is shorter than its diff:
```python
import functools

import jax
import jax.numpy as jnp
from jax import lax
from jax.experimental import pallas as pl
from jax.experimental.pallas import tpu as pltpu
from jax.sharding import PartitionSpec as P


HEAD_DIM = 128
BLK = 128
SCALE = HEAD_DIM ** (-0.5)
LOG2E = 1.4426950408889634
MASKED = -1e30
EPS = 1e-05
F32 = jnp.float32
BF16 = jnp.bfloat16
ROW_BLOCK = 256
LSE_ROWS = 8


AXES = ("pos", "head")
SIDE = 4
ORDER = (1, 3, 2)


def plane_groups():
    def device(z, y, x, core):
        return ((z * SIDE + y) * SIDE + x) * 2 + core

    r = range(SIDE)
    plane = [[device(z, y, x, 0) for y in r for x in r] for z in r]
    plane += [[device(z, y, x, 1) for z in r for x in r] for y in r]
    long = {}
    for s in range(1, SIDE):
        long[s] = [
            pair
            for z in r
            for y in r
            for x in r
            for pair in (
                (device(z, y, x, 0), device((z + s) % SIDE, y, x, 0)),
                (device(z, y, x, 1), device(z, (y + s) % SIDE, x, 1)),
            )
        ]
    return plane, long


def rms_norm(values):
    return values * lax.rsqrt(jnp.mean(values * values, axis=-1, keepdims=True) + EPS)


def nt_dot(a, b):
    return lax.dot_general(a, b, (((1,), (1,)), ((), ())), preferred_element_type=F32)


def pieces(row):
    hi = row.astype(BF16).astype(F32)
    mid = (row - hi).astype(BF16).astype(F32)
    low = (row - hi - mid).astype(BF16).astype(F32)
    place = lax.broadcasted_iota(jnp.int32, row.shape, 0)
    packed = jnp.where(place == 0, hi, jnp.where(place == 1, mid, jnp.where(place == 2, low, 0.0)))
    return packed.astype(BF16)


def cross_kernel(count_ref, q_ref, k_ref, v_ref, out_ref, *, lat_local):
    heads = q_ref.shape[1] // HEAD_DIM
    rows = q_ref.shape[0]
    owners = rows // lat_local
    span = heads * lat_local
    keys = k_ref.shape[0]
    valid = count_ref[0] * BLK

    live = lax.broadcasted_iota(jnp.int32, (1, keys), 1) < valid
    bias = jnp.where(live, 0.0, MASKED)
    columns = []
    for h in range(heads):
        cols = slice(h * HEAD_DIM, (h + 1) * HEAD_DIM)
        s = nt_dot(q_ref[:, cols], k_ref[:, cols]) + bias
        m = jnp.max(s, axis=1, keepdims=True)
        p = jnp.exp2((s - m) * (SCALE * LOG2E))
        total = jnp.sum(p, axis=1, keepdims=True)
        o = jnp.dot(p.astype(BF16), v_ref[:, cols], preferred_element_type=F32)
        o = (o / total).astype(BF16)
        out_ref[:, h * lat_local : (h + 1) * lat_local, :] = o.reshape(owners, lat_local, HEAD_DIM)
        columns.append(m * SCALE + jnp.log(total))
    for d in range(owners):
        part = jnp.concatenate([c[d * lat_local : (d + 1) * lat_local] for c in columns], axis=0)
        row = jnp.transpose(jnp.broadcast_to(part, (span, HEAD_DIM)))[:LSE_ROWS]
        out_ref[d, span : span + LSE_ROWS, :] = pieces(row)


def join_kernel(*refs):
    *parts, out_ref = refs
    owners, tall, _ = out_ref.shape
    span = tall - LSE_ROWS
    lses = [jnp.sum(r[:, span : span + LSE_ROWS, :].astype(F32), axis=1) for r in parts]
    top = functools.reduce(jnp.maximum, lses)
    ws = [jnp.exp(x - top) for x in lses]
    total = functools.reduce(jnp.add, ws)
    lse = top + jnp.log(total)
    wts = [jnp.transpose(w / total) for w in ws]
    for d in range(owners):
        acc = jnp.zeros((span, HEAD_DIM), F32)
        for wt, r in zip(wts, parts):
            acc = acc + wt[:, d : d + 1] * r[d, :span, :].astype(F32)
        out_ref[d, :span, :] = acc.astype(BF16)
        row = jnp.broadcast_to(lse[d : d + 1, :], (LSE_ROWS, HEAD_DIM))
        out_ref[d, span : span + LSE_ROWS, :] = pieces(row)


def combine_kernel(core_ref, *refs, lat_local):
    *parts, w_ref, own_ref, other_ref, terms_ref = refs
    terms = jnp.zeros((lat_local, w_ref.shape[1]), F32)
    first = 0
    for r_ref in parts:
        devices, tall, _ = r_ref.shape
        span = tall - LSE_ROWS
        lse = jnp.sum(r_ref[:, span : span + LSE_ROWS, :].astype(F32), axis=1)
        w = jnp.exp(lse - jnp.max(lse, axis=0, keepdims=True))
        w = w / jnp.sum(w, axis=0, keepdims=True)
        wt = jnp.transpose(w)
        acc = jnp.zeros((span, HEAD_DIM), F32)
        for d in range(devices):
            acc = acc + wt[:span, d : d + 1] * r_ref[d, :span, :].astype(F32)
        attended = acc.astype(BF16)
        for h in range(span // lat_local):
            terms = terms + jnp.dot(
                attended[h * lat_local : (h + 1) * lat_local],
                w_ref[(first + h) * HEAD_DIM : (first + h + 1) * HEAD_DIM, :],
                preferred_element_type=F32,
            )
        first += span // lat_local
    half = lat_local // 2
    terms_ref[...] = terms.reshape(2, half, w_ref.shape[1])
    own_ref[...] = terms_ref[core_ref[0]]
    other_ref[...] = terms_ref[1 - core_ref[0]].astype(BF16)


def spread_kernel(l_ref, w_ref, out_ref):
    q = jnp.dot(l_ref[...], w_ref[...], preferred_element_type=F32).astype(BF16)
    out_ref[...] = jnp.broadcast_to(q[None], out_ref.shape)


def latent_kernel(own_ref, recv_ref, w_ref, out_ref):
    normed = rms_norm(own_ref[...] + recv_ref[...].astype(F32))
    hidden = jax.nn.gelu(jnp.dot(normed.astype(BF16), w_ref[...], preferred_element_type=F32))
    rows = (normed + hidden).astype(BF16)
    out_ref[...] = jnp.broadcast_to(rows[None], out_ref.shape)


def kv_kernel(*refs):
    *row_refs, k_ref, v_ref, out_ref = refs
    at = 0
    half = k_ref.shape[1]
    for r in row_refs:
        n = r.shape[0]
        rows = r[...]
        out_ref[at : at + n, :half] = jnp.dot(rows, k_ref[...], preferred_element_type=F32).astype(BF16)
        out_ref[at : at + n, half:] = jnp.dot(rows, v_ref[...], preferred_element_type=F32).astype(BF16)
        at += n


def attend(q_ref, kv_refs, w_ref):
    columns = q_ref.shape[1]
    outs = []
    for h in range(columns // HEAD_DIM):
        kc = slice(h * HEAD_DIM, (h + 1) * HEAD_DIM)
        vc = slice(columns + h * HEAD_DIM, columns + (h + 1) * HEAD_DIM)
        q = q_ref[:, kc]
        scores = [nt_dot(q, kv[:, kc]) for kv in kv_refs]
        m = functools.reduce(jnp.maximum, [jnp.max(s, axis=1, keepdims=True) for s in scores])
        total, o = 0.0, 0.0
        for s, kv in zip(scores, kv_refs):
            p = jnp.exp2((s - m) * (SCALE * LOG2E))
            total = total + jnp.sum(p, axis=1, keepdims=True)
            o = o + jnp.dot(p.astype(BF16), kv[:, vc], preferred_element_type=F32)
        outs.append((o / total).astype(BF16))
    attended = jnp.concatenate(outs, axis=1)
    return jnp.dot(attended, w_ref[...], preferred_element_type=F32)


def decode_kernel(base_ref, q_ref, *refs):
    *kv_refs, w_ref, out_ref = refs
    out_ref[...] = attend(q_ref, kv_refs, w_ref).astype(out_ref.dtype)


def last_kernel(base_ref, q_ref, *refs):
    *kv_refs, w_ref, first_ref, recv_ref, out_ref = refs
    n = first_ref.shape[0]
    out_ref[:n] = rms_norm(first_ref[...] + recv_ref[:n].astype(F32)).astype(out_ref.dtype)
    terms = attend(q_ref, kv_refs, w_ref)
    out_ref[n:] = rms_norm(terms + recv_ref[n:].astype(F32)).astype(out_ref.dtype)


def full_spec(array):
    return pl.BlockSpec(array.shape, lambda *_: (0,) * array.ndim)


def params(limit=56 << 20):
    return pltpu.CompilerParams(vmem_limit_bytes=limit)


def cross(count, q, k, v, lat_local):
    lat, columns = q.shape
    heads = columns // HEAD_DIM
    tall = heads * lat_local + LSE_ROWS
    block = min(ROW_BLOCK, lat)
    return pl.pallas_call(
        functools.partial(cross_kernel, lat_local=lat_local),
        out_shape=jax.ShapeDtypeStruct((lat // lat_local, tall, HEAD_DIM), BF16),
        grid_spec=pltpu.PrefetchScalarGridSpec(
            num_scalar_prefetch=1,
            grid=(lat // block,),
            in_specs=[pl.BlockSpec((block, columns), lambda i, c: (i, 0)), full_spec(k), full_spec(v)],
            out_specs=pl.BlockSpec((block // lat_local, tall, HEAD_DIM), lambda i, c: (i, 0, 0)),
        ),
        compiler_params=params(32 << 20),
        cost_estimate=pl.CostEstimate(
            flops=4 * lat * k.shape[0] * columns,
            bytes_accessed=4 << 20,
            transcendentals=lat * k.shape[0] * heads,
        ),
        name="cross",
    )(count, q, k, v)


def join(parts):
    vmem = pl.BlockSpec(memory_space=pltpu.VMEM)
    return pl.pallas_call(
        join_kernel,
        out_shape=jax.ShapeDtypeStruct(parts[0].shape, BF16),
        in_specs=[vmem] * len(parts),
        out_specs=vmem,
        compiler_params=params(24 << 20),
        name="join",
    )(*parts)


def combine(core, parts, w_out, lat_local):
    width = w_out.shape[1]
    half = lat_local // 2
    vmem = pl.BlockSpec(memory_space=pltpu.VMEM)
    return pl.pallas_call(
        functools.partial(combine_kernel, lat_local=lat_local),
        out_shape=(
            jax.ShapeDtypeStruct((half, width), F32),
            jax.ShapeDtypeStruct((half, width), BF16),
        ),
        in_specs=[pl.BlockSpec(memory_space=pltpu.SMEM)] + [vmem] * (len(parts) + 1),
        out_specs=(vmem, vmem),
        scratch_shapes=[pltpu.VMEM((2, half, width), F32)],
        compiler_params=params(24 << 20),
        name="combine",
    )(core, *parts, w_out)


def spread(latents, w_query, devices):
    vmem = pl.BlockSpec(memory_space=pltpu.VMEM)
    return pl.pallas_call(
        spread_kernel,
        out_shape=jax.ShapeDtypeStruct((devices, latents.shape[0], w_query.shape[1]), BF16),
        in_specs=[vmem, vmem],
        out_specs=vmem,
        compiler_params=params(24 << 20),
        name="spread",
    )(latents, w_query)


def latent_rows(own, recv, w_mlp, devices):
    vmem = pl.BlockSpec(memory_space=pltpu.VMEM)
    return pl.pallas_call(
        latent_kernel,
        out_shape=jax.ShapeDtypeStruct((devices,) + own.shape, BF16),
        in_specs=[vmem] * 3,
        out_specs=vmem,
        compiler_params=params(24 << 20),
        name="latent",
    )(own, recv, w_mlp)


def latent_kv(rows, w_lkey, w_lvalue):
    vmem = pl.BlockSpec(memory_space=pltpu.VMEM)
    total = sum(r.shape[0] for r in rows)
    wide = w_lkey.shape[1] * 2
    return pl.pallas_call(
        kv_kernel,
        out_shape=jax.ShapeDtypeStruct((total, wide), BF16),
        in_specs=[vmem] * (len(rows) + 2),
        out_specs=vmem,
        compiler_params=params(24 << 20),
        cost_estimate=pl.CostEstimate(
            flops=2 * total * wide * w_lkey.shape[0], bytes_accessed=4 << 20, transcendentals=0
        ),
        name="latent_kv",
    )(*rows, w_lkey, w_lvalue)


def decode(base, blocks, q, kvs, w_pout, dtype, finish=()):
    columns = q.shape[1]
    width = w_pout.shape[1]
    block = ROW_BLOCK
    rows = blocks * block
    out_rows = finish[1].shape[0] if finish else rows
    out_block = out_rows if finish else block
    keys = sum(kv.shape[0] for kv in kvs)
    return pl.pallas_call(
        last_kernel if finish else decode_kernel,
        out_shape=jax.ShapeDtypeStruct((out_rows, width), dtype),
        grid_spec=pltpu.PrefetchScalarGridSpec(
            num_scalar_prefetch=1,
            grid=(blocks,),
            in_specs=[
                pl.BlockSpec((block, columns), lambda i, b: (b[0] + i, 0)),
                *[full_spec(x) for x in (*kvs, w_pout, *finish)],
            ],
            out_specs=pl.BlockSpec((out_block, width), lambda i, b: (i, 0)),
        ),
        compiler_params=params(36 << 20),
        cost_estimate=pl.CostEstimate(
            flops=4 * rows * columns * keys, bytes_accessed=8 << 20, transcendentals=4 * rows * keys
        ),
        name="decode",
    )(base, q, *kvs, w_pout, *finish)


def project(a, w):
    return jnp.dot(a, w, preferred_element_type=F32).astype(BF16)


def per_device(
    inputs,
    valid_blocks,
    latents,
    w_query,
    w_key,
    w_value,
    w_out,
    w_mlp,
    w_lkey,
    w_lvalue,
    w_pquery,
    w_pout,
):
    lat_local = latents.shape[0]
    columns = w_key.shape[1]
    width = inputs.shape[1]
    core = lax.axis_index("head").astype(jnp.int32).reshape(1)
    swap = [(0, 1), (1, 0)]

    plane, long = plane_groups()

    def within_plane(x):
        return lax.all_to_all(x, AXES, 0, 0, axis_index_groups=plane)

    def along(x, shift):
        return lax.ppermute(x, AXES, long[shift % SIDE])

    queries = within_plane(spread(latents, w_query, SIDE * SIDE)).reshape(-1, columns)
    keys = project(inputs, w_key)
    values = project(inputs, w_value)
    count = jnp.sum(valid_blocks).astype(jnp.int32).reshape(1)
    queries, keys, values = lax.optimization_barrier((queries, keys, values))
    away = [along(queries, s) for s in ORDER]
    part = cross(count, queries, keys, values, lat_local)
    partials = [part]
    for s, there in zip(ORDER, away):
        part, there = lax.optimization_barrier((part, there))
        part = cross(count, there, keys, values, lat_local)
        partials.append(along(part, -s))
    gathered = within_plane(join(partials))
    own, other = combine(core, [gathered], w_out, lat_local)
    recv = lax.ppermute(other, "head", swap)
    rows = latent_rows(own, recv, w_mlp, SIDE * SIDE)
    rows, inputs = lax.optimization_barrier((rows, inputs))
    pos_queries = project(inputs, w_pquery)
    near, pos_queries = lax.optimization_barrier((within_plane(rows), pos_queries))
    near = near.reshape(-1, width)
    far = [along(near, s) for s in ORDER]
    near_kv = latent_kv([near, lax.ppermute(near, "head", swap)], w_lkey, w_lvalue)
    near_kv, *far = lax.optimization_barrier((near_kv, *far))
    far_swapped = [lax.ppermute(x, "head", swap) for x in far]
    kvs = [near_kv, latent_kv(far, w_lkey, w_lvalue), latent_kv(far_swapped, w_lkey, w_lvalue)]
    blocks = pos_queries.shape[0] // 2 // ROW_BLOCK
    terms = decode((1 - core) * blocks, blocks, pos_queries, kvs, w_pout, BF16)
    arrived = lax.ppermute(terms, "head", swap)
    first = decode(core * blocks, blocks - 1, pos_queries, kvs, w_pout, F32)
    return decode(core * blocks + blocks - 1, 1, pos_queries, kvs, w_pout, BF16, (first, arrived))


def solution(mesh):
    placed = (
        P("pos", None),
        P("pos"),
        P("pos", None),
        P(None, "head"),
        P(None, "head"),
        P(None, "head"),
        P("head", None),
        P(),
        P(None, "head"),
        P(None, "head"),
        P(None, "head"),
        P("head", None),
    )

    return jax.shard_map(
        per_device,
        mesh=mesh,
        in_specs=placed,
        out_specs=P(("pos", "head"), None),
        check_vma=False,
    )
```

time: 183 us -> 150 us (0.82)
  blocking collectives: 34.7 us -> 0 us
  starting transfers between devices: 24.7 us -> 36.9 us
  waiting for transfers between devices: 53.7 us -> 42.5 us
  matrix products: 17.3 us -> 8.24 us
  local copies, waits for them, and re-layouts: 3.23 us -> 9.96 us
  Pallas kernels: 48.9 us -> 51 us
    all_to_all x1 -> x0, blocking collectives: 34.7 us -> none  [per_device(): lax.all_to_all(rows, 'pos', 0, 0).reshape(devices * lat_local // 2, width)]
    all_to_all x2 -> x3, waiting for transfers between devices: 52.9 us -> 22.9 us  [within_plane(): return lax.all_to_all(x, AXES, 0, 0, axis_index_groups=plane)]
    ppermute x2 -> x14, waiting for transfers between devices: 0.01 us -> 18.7 us  [the longest x9 18 us: along(): return lax.ppermute(x, AXES, long[shift % SIDE])]
    ppermute x2 -> x14, starting transfers between devices: 2.03 us -> 17 us  [the longest x9 14.4 us: along(): return lax.ppermute(x, AXES, long[shift % SIDE])]
    dot_general x8 -> x3, matrix products: 17.3 us -> 8.24 us  [project(): return jnp.dot(a, w, preferred_element_type=F32).astype(BF16)]
    unnamed x20 -> x30, local copies, waits for them, and re-layouts: 1.63 us -> 9.96 us
    all_to_all x2 -> x3, starting transfers between devices: 20.1 us -> 16.2 us  [within_plane(): return lax.all_to_all(x, AXES, 0, 0, axis_index_groups=plane)]
    pallas_call x1, Pallas kernels: 3.58 us -> 0.75 us  [combine(): pl.pallas_call(functools.partial(combine_kernel, lat_local=lat_local), ou...]
  transfers between devices with their start and end apart: 5 -> 18, of which waited for: 3 -> 9; matrix products, arithmetic and copies ran while one was open for 6% -> 6% of each run, Pallas kernels for 6% -> 17%
where the time goes in v2:
time: 150 us; the launch traced here: 149 us
  Pallas kernels  51 us (34%)
  waiting for transfers between devices  42.5 us (28%)
  starting transfers between devices  36.9 us (25%)
  local copies, waits for them, and re-layouts  9.96 us (7%)
  matrix products  8.24 us (5%)
    pallas_call x4, Pallas kernels, cross(): pl.pallas_call(functools.partial(cross_kernel, lat_local=lat_local), out_...  23.3 us
    all_to_all x3, waiting for transfers between devices, within_plane(): return lax.all_to_all(x, AXES, 0, 0, axis_index_groups=plane)  22.9 us
    ppermute x9, waiting for transfers between devices, along(): return lax.ppermute(x, AXES, long[shift % SIDE])  18 us
    pallas_call x3, Pallas kernels, decode(): pl.pallas_call(last_kernel if finish else decode_kernel, out_shape=jax.Sh...  16.3 us
    all_to_all x3, starting transfers between devices, within_plane(): return lax.all_to_all(x, AXES, 0, 0, axis_index_groups=plane)  16.2 us
    ppermute x9, starting transfers between devices, along(): return lax.ppermute(x, AXES, long[shift % SIDE])  14.4 us
    unnamed x30, local copies, waits for them, and re-layouts  9.96 us
    dot_general x3, matrix products, project(): return jnp.dot(a, w, preferred_element_type=F32).astype(BF16)  8.24 us
  transfers between devices with their start and end apart: 18, of which 9 were waited for; matrix products, arithmetic and copies ran while one was open for 6% of the time, Pallas kernels for 17%

profile of v2, /device:TPU:1, one launch (start us, length us, event | category | flops | bytes accessed | tf_op | source)
XLA Modules:
  0.0 149.5 jit_solution(1434123003004503674)
XLA Ops:
  0.0 1.4 copy-done.3
  1.4 0.8 copy-done.8
  2.2 1.1 spread.1
  3.4 8.4 %all-to-all-start = ((bf16[16,32,512]{2,1,0:T(8,128)(2,1)}), bf16[16,32,512]{2,1,0:T(8,128)(2,1)S(1)}, u32[]{:S(2)}, u32[]{:S(2)}) async-start(bf16[16,32,512]{2,1,0:T(8,128)(2,1)} %spread.1), calls=%async_computation | async-start | bytes 1048576 | tf_op jit(solution)/shard_map/all_to_all | solution.py:355
  11.8 0.0 copy-start.13
  11.8 3.5 %convolution_convert_fusion.1.v_ref = bf16[1024,512]{1,0:T(8,128)(2,1)} fusion(bf16[1024,1024]{1,0:T(8,128)(2,1)S(1)} %copy-done, bf16[1024,512]{1,0:T(8,128)(2,1)} %param.17), kind=kOutput, calls=%fused_computation.1 | convolution fusion | flops 1074266112 | bytes 4194304 | tf_op jit(solution)/shard_map/dot_general | solution.py:329
  15.3 2.2 %convolution_convert_fusion.2.k_ref = bf16[1024,512]{1,0:T(8,128)(2,1)} fusion(bf16[1024,1024]{1,0:T(8,128)(2,1)S(1)} %copy-done, bf16[1024,512]{1,0:T(8,128)(2,1)S(1)} %copy-done.13), kind=kOutput, calls=%fused_computation.2 | convolution fusion | flops 1074266112 | bytes 4194304 | tf_op jit(solution)/shard_map/dot_general | solution.py:329
  17.6 4.4 %all-to-all-done = bf16[16,32,512]{2,1,0:T(8,128)(2,1)S(1)} async-done(((bf16[16,32,512]{2,1,0:T(8,128)(2,1)}), bf16[16,32,512]{2,1,0:T(8,128)(2,1)S(1)}, u32[]{:S(2)}, u32[]{:S(2)}) %all-to-all-start) | async-done | bytes 524320 | tf_op jit(solution)/shard_map/all_to_all | solution.py:355
  22.0 1.1 collective-permute-start
  23.1 1.7 %collective-permute-start.2 = (bf16[512,512]{1,0:T(8,128)(2,1)S(1)}, bf16[512,512]{1,0:T(8,128)(2,1)}, u32[]{:S(2)}, u32[]{:S(2)}) collective-permute-start(bf16[512,512]{1,0:T(8,128)(2,1)S(1)} %bitcast.11), channel_id=1, source_target_pairs={{0,96},{1,25},{2,98},{3,27},{4,100},{5,29},{6,102},{7,31},{8,104},... | collective-permute-start | bytes 1572872 | tf_op jit(solution)/shard_map/ppermute | solution.py:358
  24.8 1.5 %collective-permute-start.4 = (bf16[512,512]{1,0:T(8,128)(2,1)S(1)}, bf16[512,512]{1,0:T(8,128)(2,1)S(1)}, u32[]{:S(2)}, u32[]{:S(2)}) collective-permute-start(bf16[512,512]{1,0:T(8,128)(2,1)S(1)} %bitcast.12), channel_id=1, source_target_pairs={{0,64},{1,17},{2,66},{3,19},{4,68},{5,21},{6,70},{7,23},{8,72},{9,... | collective-permute-start | bytes 1572872 | tf_op jit(solution)/shard_map/ppermute | solution.py:358
  26.3 0.7 reduce_sum.9
  27.0 1.2 copy-done.9
  28.2 1.2 copy-done.11
  29.4 5.5 %cross.4.refs_0_ = bf16[16,136,128]{2,1,0:T(8,128)(2,1)S(1)} custom-call(s32[1]{0:T(128)} %bitcast.1.count_ref, bf16[512,512]{1,0:T(8,128)(2,1)S(1)} %bitcast.13, bf16[1024,512]{1,0:T(8,128)(2,1)S(1)} %copy-done.11, bf16[1024,512]{1,0:T(8,128)(2,1)S(1)} %copy-done.9), custom_call_target="tpu_custom_call" | custom-call | flops 1073741824 | bytes 4194304 | tf_op jit(solution)/shard_map/cross/pallas_call | solution.py:210
  34.9 0.0 collective-permute-done.q_ref
  34.9 6.3 %cross.5 = bf16[16,136,128]{2,1,0:T(8,128)(2,1)S(1)} custom-call(s32[1]{0:T(128)} %bitcast.1.count_ref, bf16[512,512]{1,0:T(8,128)(2,1)} %collective-permute-done.q_ref, bf16[1024,512]{1,0:T(8,128)(2,1)S(1)} %copy-done.12, bf16[1024,512]{1,0:T(8,128)(2,1)S(1)} %copy-done.10), custom_call_target="tpu_custom_call" | custom-call | flops 1073741824 | bytes 4194304 | tf_op jit(solution)/shard_map/cross/pallas_call | solution.py:210
  41.2 0.0 collective-permute-done.2.q_ref
  41.2 6.3 %cross.6 = bf16[16,136,128]{2,1,0:T(8,128)(2,1)S(1)} custom-call(s32[1]{0:T(128)} %bitcast.1.count_ref, bf16[512,512]{1,0:T(8,128)(2,1)} %collective-permute-done.2.q_ref, bf16[1024,512]{1,0:T(8,128)(2,1)S(1)} %copy-done.12, bf16[1024,512]{1,0:T(8,128)(2,1)S(1)} %copy-done.10), custom_call_target="tpu_custom_call" | custom-call | flops 1073741824 | bytes 4194304 | tf_op jit(solution)/shard_map/cross/pallas_call | solution.py:210
  47.5 0.0 collective-permute-done.4.q_ref
  47.5 5.3 %cross.7 = bf16[16,136,128]{2,1,0:T(8,128)(2,1)S(1)} custom-call(s32[1]{0:T(128)} %bitcast.1.count_ref, bf16[512,512]{1,0:T(8,128)(2,1)S(1)} %collective-permute-done.4.q_ref, bf16[1024,512]{1,0:T(8,128)(2,1)S(1)} %copy-done.12, bf16[1024,512]{1,0:T(8,128)(2,1)S(1)} %copy-done.10), custom_call_target="tpu_custom_call" | custom-call | flops 1073741824 | bytes 4194304 | tf_op jit(solution)/shard_map/cross/pallas_call | solution.py:210
  52.8 4.1 %collective-permute-start.5 = (bf16[16,136,128]{2,1,0:T(8,128)(2,1)S(1)}, bf16[16,136,128]{2,1,0:T(8,128)(2,1)S(1)}, u32[]{:S(2)}, u32[]{:S(2)}) collective-permute-start(bf16[16,136,128]{2,1,0:T(8,128)(2,1)S(1)} %cross.7), channel_id=1, source_target_pairs={{0,64},{1,17},{2,66},{3,19},{4,68},{5,21},{6,70},{7,23},{8,72},{9,... | collective-permute-start | bytes 1671176 | tf_op jit(solution)/shard_map/ppermute | solution.py:358
  56.9 0.0 collective-permute-start.3
  56.9 2.7 %collective-permute-start.1 = (bf16[16,136,128]{2,1,0:T(8,128)(2,1)S(1)}, bf16[16,136,128]{2,1,0:T(8,128)(2,1)S(1)}, u32[]{:S(2)}, u32[]{:S(2)}) collective-permute-start(bf16[16,136,128]{2,1,0:T(8,128)(2,1)S(1)} %cross.5), channel_id=1, source_target_pairs={{0,96},{1,25},{2,98},{3,27},{4,100},{5,29},{6,102},{7,31},{8,104},... | collective-permute-start | bytes 1671176 | tf_op jit(solution)/shard_map/ppermute | solution.py:358
  59.6 4.6 %collective-permute-done.5.refs_3_ = bf16[16,136,128]{2,1,0:T(8,128)(2,1)S(1)} collective-permute-done((bf16[16,136,128]{2,1,0:T(8,128)(2,1)S(1)}, bf16[16,136,128]{2,1,0:T(8,128)(2,1)S(1)}, u32[]{:S(2)}, u32[]{:S(2)}) %collective-permute-start.5) | collective-permute-done | bytes 557088 | tf_op jit(solution)/shard_map/ppermute | solution.py:358
  64.2 5.9 %collective-permute-done.3.refs_2_ = bf16[16,136,128]{2,1,0:T(8,128)(2,1)S(1)} collective-permute-done((bf16[16,136,128]{2,1,0:T(8,128)(2,1)S(1)}, bf16[16,136,128]{2,1,0:T(8,128)(2,1)S(1)}, u32[]{:S(2)}, u32[]{:S(2)}) %collective-permute-start.3) | collective-permute-done | bytes 557088 | tf_op jit(solution)/shard_map/ppermute | solution.py:358
  70.1 0.0 collective-permute-done.1.refs_1_
  70.1 2.2 %join.1 = bf16[16,136,128]{2,1,0:T(8,128)(2,1)} custom-call(bf16[16,136,128]{2,1,0:T(8,128)(2,1)S(1)} %cross.4.refs_0_, bf16[16,136,128]{2,1,0:T(8,128)(2,1)S(1)} %collective-permute-done.1.refs_1_, bf16[16,136,128]{2,1,0:T(8,128)(2,1)S(1)} %collective-permute-done.3.refs_2_, bf16[16,136,128]{2,1,0:T(8,128)(2,1)S(1)} %collective-permute-done.5.refs_3_), custom_call_target="tpu_custom_call" | custom-call | tf_op jit(solution)/shard_map/join/pallas_call | solution.py:231
  72.4 3.6 %all-to-all-start.1 = ((bf16[16,136,128]{2,1,0:T(8,128)(2,1)}), bf16[16,136,128]{2,1,0:T(8,128)(2,1)S(1)}, u32[]{:S(2)}, u32[]{:S(2)}) async-start(bf16[16,136,128]{2,1,0:T(8,128)(2,1)} %join.1), calls=%async_computation.1 | async-start | bytes 1114112 | tf_op jit(solution)/shard_map/all_to_all | solution.py:355
  76.0 10.0 %all-to-all-done.1.refs_0_ = bf16[16,136,128]{2,1,0:T(8,128)(2,1)S(1)} async-done(((bf16[16,136,128]{2,1,0:T(8,128)(2,1)}), bf16[16,136,128]{2,1,0:T(8,128)(2,1)S(1)}, u32[]{:S(2)}, u32[]{:S(2)}) %all-to-all-start.1) | async-done | bytes 557088 | tf_op jit(solution)/shard_map/all_to_all | solution.py:355
  86.0 1.2 copy-done.4
  87.2 0.8 combine.1
  87.9 3.7 %collective-permute-start.6 = (bf16[16,1024]{1,0:T(8,128)(2,1)S(1)}, bf16[16,1024]{1,0:T(8,128)(2,1)S(1)}, u32[]{:S(2)}, u32[]{:S(2)}) collective-permute-start(bf16[16,1024]{1,0:T(8,128)(2,1)S(1)} %get-tuple-element.28), channel_id=1, source_target_pairs={{0,1},{1,0},{2,3},{3,2},{4,5},{5,4},{6,7},{7,6},{8,9},{9,8},{10,11... | collective-permute-start | bytes 98312 | tf_op jit(solution)/shard_map/ppermute | solution.py:374
  91.6 0.9 collective-permute-done.6.recv_ref
  92.5 1.6 %copy-done.2 = bf16[1024,1024]{1,0:T(8,128)(2,1)S(1)} copy-done((bf16[1024,1024]{1,0:T(8,128)(2,1)S(1)}, bf16[1024,1024]{1,0:T(8,128)(2,1)}, u32[]{:S(2)}) %copy-start.2) | copy-done | bytes 2097176
  94.1 1.3 latent.1
  95.4 4.3 %all-to-all-start.2 = ((bf16[16,16,1024]{2,1,0:T(8,128)(2,1)}), bf16[16,16,1024]{2,1,0:T(8,128)(2,1)}, u32[]{:S(2)}, u32[]{:S(2)}) async-start(bf16[16,16,1024]{2,1,0:T(8,128)(2,1)} %latent.1), calls=%async_computation.2 | async-start | bytes 1048576 | tf_op jit(solution)/shard_map/all_to_all | solution.py:355
  99.6 2.5 %convolution_convert_fusion.q_ref = bf16[1024,512]{1,0:T(8,128)(2,1)S(1)} fusion(bf16[1024,1024]{1,0:T(8,128)(2,1)S(1)} %copy-done, bf16[1024,512]{1,0:T(8,128)(2,1)} %param.22), kind=kOutput, calls=%fused_computation | convolution fusion | flops 1074266112 | bytes 4194304 | tf_op jit(solution)/shard_map/dot_general | solution.py:329
  102.1 8.5 %all-to-all-done.2 = bf16[16,16,1024]{2,1,0:T(8,128)(2,1)} async-done(((bf16[16,16,1024]{2,1,0:T(8,128)(2,1)}), bf16[16,16,1024]{2,1,0:T(8,128)(2,1)}, u32[]{:S(2)}, u32[]{:S(2)}) %all-to-all-start.2) | async-done | bytes 524320 | tf_op jit(solution)/shard_map/all_to_all | solution.py:355
  110.6 0.0 collective-permute-start.7
  110.6 0.6 collective-permute-start.10
  111.3 0.4 collective-permute-start.8
  111.6 2.3 %collective-permute-start.9 = (bf16[256,1024]{1,0:T(8,128)(2,1)}, bf16[256,1024]{1,0:T(8,128)(2,1)S(1)}, u32[]{:S(2)}, u32[]{:S(2)}) collective-permute-start(bf16[256,1024]{1,0:T(8,128)(2,1)} %bitcast.3.refs_0_), channel_id=1, source_target_pairs={{0,96},{1,25},{2,98},{3,27},{4,100},{5,29},{6,102},{7,31},{8,104},... | collective-permute-start | bytes 1572872 | tf_op jit(solution)/shard_map/ppermute | solution.py:358
  113.9 0.0 collective-permute-done.7.refs_1_
  113.9 1.2 copy-done.5
  115.2 1.2 copy-done.7
  116.4 2.4 %latent_kv.3.refs_0_ = bf16[512,1024]{1,0:T(8,128)(2,1)S(1)} custom-call(bf16[256,1024]{1,0:T(8,128)(2,1)} %bitcast.3.refs_0_, bf16[256,1024]{1,0:T(8,128)(2,1)S(1)} %collective-permute-done.7.refs_1_, bf16[1024,512]{1,0:T(8,128)(2,1)S(1)} %copy-done.5, bf16[1024,512]{1,0:T(8,128)(2,1)S(1)} %copy-done.7), custom_call_target="tpu_custom_call" | custom-call | flops 1073741824 | bytes 4194304 | tf_op jit(solution)/shard_map/latent_kv/pallas_call | solution.py:287
  118.8 1.9 %collective-permute-done.10.refs_2_ = bf16[256,1024]{1,0:T(8,128)(2,1)S(1)} collective-permute-done((bf16[256,1024]{1,0:T(8,128)(2,1)}, bf16[256,1024]{1,0:T(8,128)(2,1)S(1)}, u32[]{:S(2)}, u32[]{:S(2)}) %collective-permute-start.10) | collective-permute-done | bytes 524320 | tf_op jit(solution)/shard_map/ppermute | solution.py:358
  120.7 5.6 %collective-permute-done.8.refs_0_ = bf16[256,1024]{1,0:T(8,128)(2,1)S(1)} collective-permute-done((bf16[256,1024]{1,0:T(8,128)(2,1)}, bf16[256,1024]{1,0:T(8,128)(2,1)S(1)}, u32[]{:S(2)}, u32[]{:S(2)}) %collective-permute-start.8) | collective-permute-done | bytes 524320 | tf_op jit(solution)/shard_map/ppermute | solution.py:358
  126.3 0.0 collective-permute-done.9.refs_1_
  126.3 1.4 collective-permute-start.11
  127.6 0.0 collective-permute-start.12
  127.7 0.5 collective-permute-start.13
  128.2 1.8 %latent_kv.4.refs_1_ = bf16[768,1024]{1,0:T(8,128)(2,1)S(1)} custom-call(bf16[256,1024]{1,0:T(8,128)(2,1)S(1)} %collective-permute-done.8.refs_0_, bf16[256,1024]{1,0:T(8,128)(2,1)S(1)} %collective-permute-done.9.refs_1_, bf16[256,1024]{1,0:T(8,128)(2,1)S(1)} %collective-permute-done.10.refs_2_, bf16[1024,512]{1,0:T(8,128)(2,1)S(1)} %copy-done.6, ...), custom_call_target="tpu_custom_call" | custom-call | flops 1610612736 | bytes 4194304 | tf_op jit(solution)/shard_map/latent_kv/pallas_call | solution.py:287
  130.0 0.0 copy-start.1
  130.0 0.0 collective-permute-done.11.refs_0_
  130.0 0.0 collective-permute-done.12.refs_1_
  130.0 0.7 collective-permute-done.13.refs_2_
  130.7 1.8 %latent_kv.5.refs_2_ = bf16[768,1024]{1,0:T(8,128)(2,1)S(1)} custom-call(bf16[256,1024]{1,0:T(8,128)(2,1)S(1)} %collective-permute-done.11.refs_0_, bf16[256,1024]{1,0:T(8,128)(2,1)S(1)} %collective-permute-done.12.refs_1_, bf16[256,1024]{1,0:T(8,128)(2,1)S(1)} %collective-permute-done.13.refs_2_, bf16[1024,512]{1,0:T(8,128)(2,1)S(1)} %copy-done.6, ...), custom_call_target="tpu_custom_call" | custom-call | flops 1610612736 | bytes 4194304 | tf_op jit(solution)/shard_map/latent_kv/pallas_call | solution.py:287
  132.5 7.6 %decode.4 = bf16[512,1024]{1,0:T(8,128)(2,1)S(1)} custom-call(s32[1]{0:T(128)S(6)} %mul.8.base_ref, bf16[1024,512]{1,0:T(8,128)(2,1)S(1)} %convolution_convert_fusion.q_ref, bf16[512,1024]{1,0:T(8,128)(2,1)S(1)} %latent_kv.3.refs_0_, bf16[768,1024]{1,0:T(8,128)(2,1)S(1)} %latent_kv.4.refs_1_, bf16[768,1024]{1,0:T(8,128)(2,1)S(1)} %latent_kv.5.refs_2_, ...), custom_call_target="tpu_custom_call" | custom-call | flops 2147483648 | bytes 8388608 | tf_op jit(solution)/shard_map/decode/pallas_call | solution.py:308
  140.0 0.7 collective-permute-start.14
  140.8 3.8 %decode.3.refs_4_ = f32[256,1024]{1,0:T(8,128)S(1)} custom-call(s32[1]{0:T(128)S(6)} %mul.7.base_ref, bf16[1024,512]{1,0:T(8,128)(2,1)S(1)} %convolution_convert_fusion.q_ref, bf16[512,1024]{1,0:T(8,128)(2,1)S(1)} %latent_kv.3.refs_0_, bf16[768,1024]{1,0:T(8,128)(2,1)S(1)} %latent_kv.4.refs_1_, bf16[768,1024]{1,0:T(8,128)(2,1)S(1)} %latent_kv.5.refs_2_, ...), custom_call_target="tpu_custom_call" | custom-call | flops 1073741824 | bytes 8388608 | tf_op jit(solution)/shard_map/decode/pallas_call | solution.py:308
  144.5 0.0 collective-permute-done.14.refs_5_
  144.5 5.0 %decode.5 = bf16[512,1024]{1,0:T(8,128)(2,1)} custom-call(s32[1]{0:T(128)S(6)} %sub.6.base_ref, bf16[1024,512]{1,0:T(8,128)(2,1)S(1)} %convolution_convert_fusion.q_ref, bf16[512,1024]{1,0:T(8,128)(2,1)S(1)} %latent_kv.3.refs_0_, bf16[768,1024]{1,0:T(8,128)(2,1)S(1)} %latent_kv.4.refs_1_, bf16[768,1024]{1,0:T(8,128)(2,1)S(1)} %latent_kv.5.refs_2_, ...), custom_call_target="tpu_custom_call" | custom-call | flops 1073741824 | bytes 8388608 | tf_op jit(solution)/shard_map/decode/pallas_call | solution.py:308
  (20 shorter events, 0.0 us)
Async XLA Ops:
  0.0 11.8 %copy-start = (bf16[1024,1024]{1,0:T(8,128)(2,1)S(1)}, bf16[1024,1024]{1,0:T(8,128)(2,1)}, u32[]{:S(2)}) copy-start(bf16[1024,1024]{1,0:T(8,128)(2,1)} %param.12) | copy-start | bytes 6291460
  0.0 1.4 copy-start.3
  1.4 0.8 copy-start.8
  3.4 18.6 %all-to-all-start = ((bf16[16,32,512]{2,1,0:T(8,128)(2,1)}), bf16[16,32,512]{2,1,0:T(8,128)(2,1)S(1)}, u32[]{:S(2)}, u32[]{:S(2)}) async-start(bf16[16,32,512]{2,1,0:T(8,128)(2,1)} %spread.1), calls=%async_computation | async-start | bytes 1048576 | tf_op jit(solution)/shard_map/all_to_all | solution.py:355
  11.8 3.6 %copy-start.13 = (bf16[1024,512]{1,0:T(8,128)(2,1)S(1)}, bf16[1024,512]{1,0:T(8,128)(2,1)}, u32[]{:S(2)}) copy-start(bf16[1024,512]{1,0:T(8,128)(2,1)} %param.16) | copy-start | bytes 3145732
  15.3 10.9 %copy-start.14 = (s32[8]{0:T(128)S(1)}, s32[8]{0:T(128)}, u32[]{:S(2)}) copy-start(s32[8]{0:T(128)} %param.13) | copy-start | bytes 100
  22.0 12.9 %collective-permute-start = (bf16[512,512]{1,0:T(8,128)(2,1)S(1)}, bf16[512,512]{1,0:T(8,128)(2,1)}, u32[]{:S(2)}, u32[]{:S(2)}) collective-permute-start(bf16[512,512]{1,0:T(8,128)(2,1)S(1)} %bitcast.10), channel_id=1, source_target_pairs={{0,32},{1,9},{2,34},{3,11},{4,36},{5,13},{6,38},{7,15},{8,40},{9,1... | collective-permute-start | bytes 1572872 | tf_op jit(solution)/shard_map/ppermute | solution.py:358
  23.1 18.1 %collective-permute-start.2 = (bf16[512,512]{1,0:T(8,128)(2,1)S(1)}, bf16[512,512]{1,0:T(8,128)(2,1)}, u32[]{:S(2)}, u32[]{:S(2)}) collective-permute-start(bf16[512,512]{1,0:T(8,128)(2,1)S(1)} %bitcast.11), channel_id=1, source_target_pairs={{0,96},{1,25},{2,98},{3,27},{4,100},{5,29},{6,102},{7,31},{8,104},... | collective-permute-start | bytes 1572872 | tf_op jit(solution)/shard_map/ppermute | solution.py:358
  24.8 22.8 %collective-permute-start.4 = (bf16[512,512]{1,0:T(8,128)(2,1)S(1)}, bf16[512,512]{1,0:T(8,128)(2,1)S(1)}, u32[]{:S(2)}, u32[]{:S(2)}) collective-permute-start(bf16[512,512]{1,0:T(8,128)(2,1)S(1)} %bitcast.12), channel_id=1, source_target_pairs={{0,64},{1,17},{2,66},{3,19},{4,68},{5,21},{6,70},{7,23},{8,72},{9,... | collective-permute-start | bytes 1572872 | tf_op jit(solution)/shard_map/ppermute | solution.py:358
  27.0 1.2 copy-start.9
  28.2 1.2 copy-start.11
  29.4 5.5 %copy-start.10 = (bf16[1024,512]{1,0:T(8,128)(2,1)S(1)}, bf16[1024,512]{1,0:T(8,128)(2,1)}, u32[]{:S(2)}) copy-start(bf16[1024,512]{1,0:T(8,128)(2,1)} %convolution_convert_fusion.1.v_ref) | copy-start | bytes 3145732
  29.4 5.5 %copy-start.12 = (bf16[1024,512]{1,0:T(8,128)(2,1)S(1)}, bf16[1024,512]{1,0:T(8,128)(2,1)}, u32[]{:S(2)}) copy-start(bf16[1024,512]{1,0:T(8,128)(2,1)} %convolution_convert_fusion.2.k_ref) | copy-start | bytes 3145732
  52.8 11.3 %collective-permute-start.5 = (bf16[16,136,128]{2,1,0:T(8,128)(2,1)S(1)}, bf16[16,136,128]{2,1,0:T(8,128)(2,1)S(1)}, u32[]{:S(2)}, u32[]{:S(2)}) collective-permute-start(bf16[16,136,128]{2,1,0:T(8,128)(2,1)S(1)} %cross.7), channel_id=1, source_target_pairs={{0,64},{1,17},{2,66},{3,19},{4,68},{5,21},{6,70},{7,23},{8,72},{9,... | collective-permute-start | bytes 1671176 | tf_op jit(solution)/shard_map/ppermute | solution.py:358
  56.9 13.2 %collective-permute-start.3 = (bf16[16,136,128]{2,1,0:T(8,128)(2,1)S(1)}, bf16[16,136,128]{2,1,0:T(8,128)(2,1)S(1)}, u32[]{:S(2)}, u32[]{:S(2)}) collective-permute-start(bf16[16,136,128]{2,1,0:T(8,128)(2,1)S(1)} %cross.6), channel_id=1, source_target_pairs={{0,32},{1,9},{2,34},{3,11},{4,36},{5,13},{6,38},{7,15},{8,40},{9,1... | collective-permute-start | bytes 1671176 | tf_op jit(solution)/shard_map/ppermute | solution.py:358
  56.9 13.2 %collective-permute-start.1 = (bf16[16,136,128]{2,1,0:T(8,128)(2,1)S(1)}, bf16[16,136,128]{2,1,0:T(8,128)(2,1)S(1)}, u32[]{:S(2)}, u32[]{:S(2)}) collective-permute-start(bf16[16,136,128]{2,1,0:T(8,128)(2,1)S(1)} %cross.5), channel_id=1, source_target_pairs={{0,96},{1,25},{2,98},{3,27},{4,100},{5,29},{6,102},{7,31},{8,104},... | collective-permute-start | bytes 1671176 | tf_op jit(solution)/shard_map/ppermute | solution.py:358
  72.4 13.6 %all-to-all-start.1 = ((bf16[16,136,128]{2,1,0:T(8,128)(2,1)}), bf16[16,136,128]{2,1,0:T(8,128)(2,1)S(1)}, u32[]{:S(2)}, u32[]{:S(2)}) async-start(bf16[16,136,128]{2,1,0:T(8,128)(2,1)} %join.1), calls=%async_computation.1 | async-start | bytes 1114112 | tf_op jit(solution)/shard_map/all_to_all | solution.py:355
  86.0 1.2 copy-start.4
  87.9 4.5 %collective-permute-start.6 = (bf16[16,1024]{1,0:T(8,128)(2,1)S(1)}, bf16[16,1024]{1,0:T(8,128)(2,1)S(1)}, u32[]{:S(2)}, u32[]{:S(2)}) collective-permute-start(bf16[16,1024]{1,0:T(8,128)(2,1)S(1)} %get-tuple-element.28), channel_id=1, source_target_pairs={{0,1},{1,0},{2,3},{3,2},{4,5},{5,4},{6,7},{7,6},{8,9},{9,8},{10,11... | collective-permute-start | bytes 98312 | tf_op jit(solution)/shard_map/ppermute | solution.py:374
  92.5 1.6 %copy-start.2 = (bf16[1024,1024]{1,0:T(8,128)(2,1)S(1)}, bf16[1024,1024]{1,0:T(8,128)(2,1)}, u32[]{:S(2)}) copy-start(bf16[1024,1024]{1,0:T(8,128)(2,1)} %w_ref.3) | copy-start | bytes 6291460
  95.4 15.3 %all-to-all-start.2 = ((bf16[16,16,1024]{2,1,0:T(8,128)(2,1)}), bf16[16,16,1024]{2,1,0:T(8,128)(2,1)}, u32[]{:S(2)}, u32[]{:S(2)}) async-start(bf16[16,16,1024]{2,1,0:T(8,128)(2,1)} %latent.1), calls=%async_computation.2 | async-start | bytes 1048576 | tf_op jit(solution)/shard_map/all_to_all | solution.py:355
  110.6 3.3 %collective-permute-start.7 = (bf16[256,1024]{1,0:T(8,128)(2,1)}, bf16[256,1024]{1,0:T(8,128)(2,1)S(1)}, u32[]{:S(2)}, u32[]{:S(2)}) collective-permute-start(bf16[256,1024]{1,0:T(8,128)(2,1)} %bitcast.3.refs_0_), channel_id=1, source_target_pairs={{0,1},{1,0},{2,3},{3,2},{4,5},{5,4},{6,7},{7,6},{8,9},{9,8},{10,11... | collective-permute-start | bytes 1572872 | tf_op jit(solution)/shard_map/ppermute | solution.py:381
  110.6 10.1 %collective-permute-start.10 = (bf16[256,1024]{1,0:T(8,128)(2,1)}, bf16[256,1024]{1,0:T(8,128)(2,1)S(1)}, u32[]{:S(2)}, u32[]{:S(2)}) collective-permute-start(bf16[256,1024]{1,0:T(8,128)(2,1)} %bitcast.3.refs_0_), channel_id=1, source_target_pairs={{0,64},{1,17},{2,66},{3,19},{4,68},{5,21},{6,70},{7,23},{8,72},{9,... | collective-permute-start | bytes 1572872 | tf_op jit(solution)/shard_map/ppermute | solution.py:358
  111.3 15.0 %collective-permute-start.8 = (bf16[256,1024]{1,0:T(8,128)(2,1)}, bf16[256,1024]{1,0:T(8,128)(2,1)S(1)}, u32[]{:S(2)}, u32[]{:S(2)}) collective-permute-start(bf16[256,1024]{1,0:T(8,128)(2,1)} %bitcast.3.refs_0_), channel_id=1, source_target_pairs={{0,32},{1,9},{2,34},{3,11},{4,36},{5,13},{6,38},{7,15},{8,40},{9,1... | collective-permute-start | bytes 1572872 | tf_op jit(solution)/shard_map/ppermute | solution.py:358
  111.6 14.7 %collective-permute-start.9 = (bf16[256,1024]{1,0:T(8,128)(2,1)}, bf16[256,1024]{1,0:T(8,128)(2,1)S(1)}, u32[]{:S(2)}, u32[]{:S(2)}) collective-permute-start(bf16[256,1024]{1,0:T(8,128)(2,1)} %bitcast.3.refs_0_), channel_id=1, source_target_pairs={{0,96},{1,25},{2,98},{3,27},{4,100},{5,29},{6,102},{7,31},{8,104},... | collective-permute-start | bytes 1572872 | tf_op jit(solution)/shard_map/ppermute | solution.py:358
  113.9 1.2 copy-start.5
  115.2 1.2 copy-start.7
  116.4 11.8 %copy-start.6 = (bf16[1024,512]{1,0:T(8,128)(2,1)S(1)}, bf16[1024,512]{1,0:T(8,128)(2,1)}, u32[]{:S(2)}) copy-start(bf16[1024,512]{1,0:T(8,128)(2,1)} %refs_3_.8) | copy-start | bytes 3145732
  126.3 3.7 %collective-permute-start.11 = (bf16[256,1024]{1,0:T(8,128)(2,1)S(1)}, bf16[256,1024]{1,0:T(8,128)(2,1)S(1)}, u32[]{:S(2)}, u32[]{:S(2)}) collective-permute-start(bf16[256,1024]{1,0:T(8,128)(2,1)S(1)} %collective-permute-done.8.refs_0_), channel_id=1, source_target_pairs={{0,1},{1,0},{2,3},{3,2},{4,5},{5,4},{6,7},{7,6},{8,9},{9,8},{10,11... | collective-permute-start | bytes 1572872 | tf_op jit(solution)/shard_map/ppermute | solution.py:383
  127.6 2.3 %collective-permute-start.12 = (bf16[256,1024]{1,0:T(8,128)(2,1)S(1)}, bf16[256,1024]{1,0:T(8,128)(2,1)S(1)}, u32[]{:S(2)}, u32[]{:S(2)}) collective-permute-start(bf16[256,1024]{1,0:T(8,128)(2,1)S(1)} %collective-permute-done.9.refs_1_), channel_id=1, source_target_pairs={{0,1},{1,0},{2,3},{3,2},{4,5},{5,4},{6,7},{7,6},{8,9},{9,8},{10,11... | collective-permute-start | bytes 1572872 | tf_op jit(solution)/shard_map/ppermute | solution.py:383
  127.7 3.0 %collective-permute-start.13 = (bf16[256,1024]{1,0:T(8,128)(2,1)S(1)}, bf16[256,1024]{1,0:T(8,128)(2,1)S(1)}, u32[]{:S(2)}, u32[]{:S(2)}) collective-permute-start(bf16[256,1024]{1,0:T(8,128)(2,1)S(1)} %collective-permute-done.10.refs_2_), channel_id=1, source_target_pairs={{0,1},{1,0},{2,3},{3,2},{4,5},{5,4},{6,7},{7,6},{8,9},{9,8},{10,11... | collective-permute-start | bytes 1572872 | tf_op jit(solution)/shard_map/ppermute | solution.py:383
  130.0 2.5 %copy-start.1 = (bf16[512,1024]{1,0:T(8,128)(2,1)S(1)}, bf16[512,1024]{1,0:T(8,128)(2,1)}, u32[]{:S(2)}) copy-start(bf16[512,1024]{1,0:T(8,128)(2,1)} %refs_3_.11) | copy-start | bytes 3145732
  140.0 4.5 %collective-permute-start.14 = (bf16[512,1024]{1,0:T(8,128)(2,1)S(1)}, bf16[512,1024]{1,0:T(8,128)(2,1)S(1)}, u32[]{:S(2)}, u32[]{:S(2)}) collective-permute-start(bf16[512,1024]{1,0:T(8,128)(2,1)S(1)} %decode.4), channel_id=1, source_target_pairs={{0,1},{1,0},{2,3},{3,2},{4,5},{5,4},{6,7},{7,6},{8,9},{9,8},{10,11... | collective-permute-start | bytes 3145736 | tf_op jit(solution)/shard_map/ppermute | solution.py:387

commit v3 on v2

--- a/solution.py
+++ b/solution.py
@@ -22,7 +22,7 @@
 
 AXES = ("pos", "head")
 SIDE = 4
-ORDER = (1, 3, 2)
+ORDER = (1, 2, 3)
 
 
 def plane_groups():
@@ -64,18 +64,21 @@
     return packed.astype(BF16)
 
 
-def cross_kernel(count_ref, q_ref, k_ref, v_ref, out_ref, *, lat_local):
-    heads = q_ref.shape[1] // HEAD_DIM
+def cross_kernel(valid_ref, q_ref, k_ref, v_ref, *refs, lat_local, first, heads):
+    before_ref, out_ref = refs if len(refs) == 2 else (None, refs[0])
     rows = q_ref.shape[0]
     owners = rows // lat_local
-    span = heads * lat_local
+    done = first * lat_local
+    span = done + heads * lat_local
     keys = k_ref.shape[0]
-    valid = count_ref[0] * BLK
-
+    valid = sum(valid_ref[i] for i in range(keys // BLK)) * BLK
     live = lax.broadcasted_iota(jnp.int32, (1, keys), 1) < valid
     bias = jnp.where(live, 0.0, MASKED)
-    columns = []
-    for h in range(heads):
+    if before_ref is not None:
+        out_ref[:, :done, :] = before_ref[:, :done, :]
+    zeros = jnp.zeros((rows, 1), F32)
+    columns = [zeros] * first
+    for h in range(first, first + heads):
         cols = slice(h * HEAD_DIM, (h + 1) * HEAD_DIM)
         s = nt_dot(q_ref[:, cols], k_ref[:, cols]) + bias
         m = jnp.max(s, axis=1, keepdims=True)
@@ -85,10 +88,24 @@
         o = (o / total).astype(BF16)
         out_ref[:, h * lat_local : (h + 1) * lat_local, :] = o.reshape(owners, lat_local, HEAD_DIM)
         columns.append(m * SCALE + jnp.log(total))
+    columns += [zeros] * (HEAD_DIM // lat_local - len(columns))
     for d in range(owners):
         part = jnp.concatenate([c[d * lat_local : (d + 1) * lat_local] for c in columns], axis=0)
-        row = jnp.transpose(jnp.broadcast_to(part, (span, HEAD_DIM)))[:LSE_ROWS]
-        out_ref[d, span : span + LSE_ROWS, :] = pieces(row)
+        row = jnp.transpose(jnp.broadcast_to(part, (HEAD_DIM, HEAD_DIM)))[:LSE_ROWS]
+        packed = pieces(row)
+        if before_ref is not None:
+            packed = packed + before_ref[d, done : done + LSE_ROWS, :]
+        out_ref[d, span : span + LSE_ROWS, :] = packed
+
+
+def load_kernel(*refs):
+    n = len(refs) // 2
+    *pairs, sems = refs
+    copies = [pltpu.make_async_copy(pairs[i], pairs[n + i], sems.at[i]) for i in range(n)]
+    for copy in copies:
+        copy.start()
+    for copy in copies:
+        copy.wait()
 
 
 def join_kernel(*refs):
@@ -110,36 +127,48 @@
         out_ref[d, span : span + LSE_ROWS, :] = pieces(row)
 
 
-def combine_kernel(core_ref, *refs, lat_local):
-    *parts, w_ref, own_ref, other_ref, terms_ref = refs
-    terms = jnp.zeros((lat_local, w_ref.shape[1]), F32)
-    first = 0
-    for r_ref in parts:
-        devices, tall, _ = r_ref.shape
-        span = tall - LSE_ROWS
-        lse = jnp.sum(r_ref[:, span : span + LSE_ROWS, :].astype(F32), axis=1)
-        w = jnp.exp(lse - jnp.max(lse, axis=0, keepdims=True))
-        w = w / jnp.sum(w, axis=0, keepdims=True)
-        wt = jnp.transpose(w)
-        acc = jnp.zeros((span, HEAD_DIM), F32)
-        for d in range(devices):
-            acc = acc + wt[:span, d : d + 1] * r_ref[d, :span, :].astype(F32)
-        attended = acc.astype(BF16)
-        for h in range(span // lat_local):
-            terms = terms + jnp.dot(
-                attended[h * lat_local : (h + 1) * lat_local],
-                w_ref[(first + h) * HEAD_DIM : (first + h + 1) * HEAD_DIM, :],
-                preferred_element_type=F32,
-            )
-        first += span // lat_local
+def combine_kernel(core_ref, r_ref, w_ref, mlp_ref, own_ref, other_ref, mlp_out, terms_ref, w_vmem, sems, *, lat_local):
+    copies = [
+        pltpu.make_async_copy(w_ref, w_vmem, sems.at[0]),
+        pltpu.make_async_copy(mlp_ref, mlp_out, sems.at[1]),
+    ]
+    for copy in copies:
+        copy.start()
+    devices, tall, _ = r_ref.shape
+    span = tall - LSE_ROWS
+    lse = jnp.sum(r_ref[:, span : span + LSE_ROWS, :].astype(F32), axis=1)
+    w = jnp.exp(lse - jnp.max(lse, axis=0, keepdims=True))
+    w = w / jnp.sum(w, axis=0, keepdims=True)
+    wt = jnp.transpose(w)
+    acc = jnp.zeros((span, HEAD_DIM), F32)
+    for d in range(devices):
+        acc = acc + wt[:span, d : d + 1] * r_ref[d, :span, :].astype(F32)
+    attended = acc.astype(BF16)
+    copies[0].wait()
+    terms = jnp.zeros((lat_local, w_vmem.shape[1]), F32)
+    for h in range(span // lat_local):
+        terms = terms + jnp.dot(
+            attended[h * lat_local : (h + 1) * lat_local],
+            w_vmem[h * HEAD_DIM : (h + 1) * HEAD_DIM, :],
+            preferred_element_type=F32,
+        )
     half = lat_local // 2
-    terms_ref[...] = terms.reshape(2, half, w_ref.shape[1])
+    terms_ref[...] = terms.reshape(2, half, w_vmem.shape[1])
     own_ref[...] = terms_ref[core_ref[0]]
     other_ref[...] = terms_ref[1 - core_ref[0]].astype(BF16)
-
-
-def spread_kernel(l_ref, w_ref, out_ref):
-    q = jnp.dot(l_ref[...], w_ref[...], preferred_element_type=F32).astype(BF16)
+    copies[1].wait()
+
+
+def spread_kernel(l_ref, w_ref, out_ref, l_vmem, w_vmem, sems):
+    copies = [
+        pltpu.make_async_copy(w_ref, w_vmem, sems.at[0]),
+        pltpu.make_async_copy(l_ref, l_vmem, sems.at[1]),
+    ]
+    for copy in copies:
+        copy.start()
+    for copy in copies:
+        copy.wait()
+    q = jnp.dot(l_vmem[...], w_vmem[...], preferred_element_type=F32).astype(BF16)
     out_ref[...] = jnp.broadcast_to(q[None], out_ref.shape)
 
 
@@ -150,28 +179,69 @@
     out_ref[...] = jnp.broadcast_to(rows[None], out_ref.shape)
 
 
+def write_kv(row_refs, w_ref, out_ref, first):
+    at = 0
+    wide = w_ref.shape[1]
+    for r in row_refs:
+        n = r.shape[0]
+        out_ref[at : at + n, first : first + wide] = jnp.dot(
+            r[...], w_ref[...], preferred_element_type=F32
+        ).astype(BF16)
+        at += n
+
+
 def kv_kernel(*refs):
     *row_refs, k_ref, v_ref, out_ref = refs
-    at = 0
-    half = k_ref.shape[1]
-    for r in row_refs:
-        n = r.shape[0]
-        rows = r[...]
-        out_ref[at : at + n, :half] = jnp.dot(rows, k_ref[...], preferred_element_type=F32).astype(BF16)
-        out_ref[at : at + n, half:] = jnp.dot(rows, v_ref[...], preferred_element_type=F32).astype(BF16)
-        at += n
-
-
-def attend(q_ref, kv_refs, w_ref):
+    write_kv(row_refs, k_ref, out_ref, 0)
+    write_kv(row_refs, v_ref, out_ref, k_ref.shape[1])
+
+
+def near_kv_kernel(near_ref, swapped_ref, k_ref, v_ref, p_ref, out_ref, k_out, v_out, p_out, sems):
+    pairs = ((k_ref, k_out), (v_ref, v_out), (p_ref, p_out))
+    copies = [pltpu.make_async_copy(a, b, sems.at[i]) for i, (a, b) in enumerate(pairs)]
+    for copy in copies:
+        copy.start()
+    rows = (near_ref, swapped_ref)
+    copies[0].wait()
+    write_kv(rows, k_out, out_ref, 0)
+    copies[1].wait()
+    write_kv(rows, v_out, out_ref, k_out.shape[1])
+    copies[2].wait()
+
+
+def head_columns(columns, h):
+    return (
+        slice(h * HEAD_DIM, (h + 1) * HEAD_DIM),
+        slice(columns + h * HEAD_DIM, columns + (h + 1) * HEAD_DIM),
+    )
+
+
+def near_kernel(q_ref, kv_ref, sums_ref, stats_ref):
     columns = q_ref.shape[1]
+    heads = columns // HEAD_DIM
+    for h in range(heads):
+        kc, vc = head_columns(columns, h)
+        s = nt_dot(q_ref[:, kc], kv_ref[:, kc])
+        m = jnp.max(s, axis=1, keepdims=True)
+        p = jnp.exp2((s - m) * (SCALE * LOG2E))
+        sums_ref[:, kc] = jnp.dot(p.astype(BF16), kv_ref[:, vc], preferred_element_type=F32)
+        stats_ref[:, h : h + 1] = m
+        stats_ref[:, heads + h : heads + h + 1] = jnp.sum(p, axis=1, keepdims=True)
+
+
+def attend(q_ref, sums_ref, stats_ref, kv_refs, w_ref):
+    columns = q_ref.shape[1]
+    heads = columns // HEAD_DIM
     outs = []
-    for h in range(columns // HEAD_DIM):
-        kc = slice(h * HEAD_DIM, (h + 1) * HEAD_DIM)
-        vc = slice(columns + h * HEAD_DIM, columns + (h + 1) * HEAD_DIM)
+    for h in range(heads):
+        kc, vc = head_columns(columns, h)
         q = q_ref[:, kc]
         scores = [nt_dot(q, kv[:, kc]) for kv in kv_refs]
-        m = functools.reduce(jnp.maximum, [jnp.max(s, axis=1, keepdims=True) for s in scores])
-        total, o = 0.0, 0.0
+        before = stats_ref[:, h : h + 1]
+        m = functools.reduce(jnp.maximum, [before, *[jnp.max(s, axis=1, keepdims=True) for s in scores]])
+        keep = jnp.exp2((before - m) * (SCALE * LOG2E))
+        total = stats_ref[:, heads + h : heads + h + 1] * keep
+        o = sums_ref[:, kc] * keep
         for s, kv in zip(scores, kv_refs):
             p = jnp.exp2((s - m) * (SCALE * LOG2E))
             total = total + jnp.sum(p, axis=1, keepdims=True)
@@ -181,16 +251,16 @@
     return jnp.dot(attended, w_ref[...], preferred_element_type=F32)
 
 
-def decode_kernel(base_ref, q_ref, *refs):
+def decode_kernel(base_ref, q_ref, sums_ref, stats_ref, *refs):
     *kv_refs, w_ref, out_ref = refs
-    out_ref[...] = attend(q_ref, kv_refs, w_ref).astype(out_ref.dtype)
-
-
-def last_kernel(base_ref, q_ref, *refs):
+    out_ref[...] = attend(q_ref, sums_ref, stats_ref, kv_refs, w_ref).astype(out_ref.dtype)
+
+
+def last_kernel(base_ref, q_ref, sums_ref, stats_ref, *refs):
     *kv_refs, w_ref, first_ref, recv_ref, out_ref = refs
     n = first_ref.shape[0]
     out_ref[:n] = rms_norm(first_ref[...] + recv_ref[:n].astype(F32)).astype(out_ref.dtype)
-    terms = attend(q_ref, kv_refs, w_ref)
+    terms = attend(q_ref, sums_ref, stats_ref, kv_refs, w_ref)
     out_ref[n:] = rms_norm(terms + recv_ref[n:].astype(F32)).astype(out_ref.dtype)
 
 
@@ -202,28 +272,49 @@
     return pltpu.CompilerParams(vmem_limit_bytes=limit)
 
 
-def cross(count, q, k, v, lat_local):
+def cross(valid, q, k, v, lat_local, first, heads, before=None):
     lat, columns = q.shape
-    heads = columns // HEAD_DIM
-    tall = heads * lat_local + LSE_ROWS
+    tall = (first + heads) * lat_local + LSE_ROWS
     block = min(ROW_BLOCK, lat)
-    return pl.pallas_call(
-        functools.partial(cross_kernel, lat_local=lat_local),
+    extra = () if before is None else (before,)
+    return pl.pallas_call(
+        functools.partial(cross_kernel, lat_local=lat_local, first=first, heads=heads),
         out_shape=jax.ShapeDtypeStruct((lat // lat_local, tall, HEAD_DIM), BF16),
         grid_spec=pltpu.PrefetchScalarGridSpec(
             num_scalar_prefetch=1,
             grid=(lat // block,),
-            in_specs=[pl.BlockSpec((block, columns), lambda i, c: (i, 0)), full_spec(k), full_spec(v)],
+            in_specs=[
+                pl.BlockSpec((block, columns), lambda i, c: (i, 0)),
+                full_spec(k),
+                full_spec(v),
+                *[pl.BlockSpec((block // lat_local,) + x.shape[1:], lambda i, c: (i, 0, 0)) for x in extra],
+            ],
             out_specs=pl.BlockSpec((block // lat_local, tall, HEAD_DIM), lambda i, c: (i, 0, 0)),
         ),
         compiler_params=params(32 << 20),
         cost_estimate=pl.CostEstimate(
-            flops=4 * lat * k.shape[0] * columns,
+            flops=4 * lat * k.shape[0] * heads * HEAD_DIM,
             bytes_accessed=4 << 20,
             transcendentals=lat * k.shape[0] * heads,
         ),
         name="cross",
-    )(count, q, k, v)
+    )(valid, q, k, v, *extra)
+
+
+def in_hbm(*arrays):
+    return [pltpu.with_memory_space_constraint(x, pltpu.HBM) for x in arrays]
+
+
+def load(arrays):
+    return pl.pallas_call(
+        load_kernel,
+        out_shape=[jax.ShapeDtypeStruct(x.shape, x.dtype) for x in arrays],
+        in_specs=[pl.BlockSpec(memory_space=pltpu.HBM)] * len(arrays),
+        out_specs=[pl.BlockSpec(memory_space=pltpu.VMEM)] * len(arrays),
+        scratch_shapes=[pltpu.SemaphoreType.DMA((len(arrays),))],
+        compiler_params=params(8 << 20),
+        name="load",
+    )(*in_hbm(*arrays))
 
 
 def join(parts):
@@ -238,34 +329,45 @@
     )(*parts)
 
 
-def combine(core, parts, w_out, lat_local):
+def combine(core, gathered, w_out, w_mlp, lat_local):
     width = w_out.shape[1]
     half = lat_local // 2
     vmem = pl.BlockSpec(memory_space=pltpu.VMEM)
+    hbm = pl.BlockSpec(memory_space=pltpu.HBM)
     return pl.pallas_call(
         functools.partial(combine_kernel, lat_local=lat_local),
         out_shape=(
             jax.ShapeDtypeStruct((half, width), F32),
             jax.ShapeDtypeStruct((half, width), BF16),
-        ),
-        in_specs=[pl.BlockSpec(memory_space=pltpu.SMEM)] + [vmem] * (len(parts) + 1),
-        out_specs=(vmem, vmem),
-        scratch_shapes=[pltpu.VMEM((2, half, width), F32)],
+            jax.ShapeDtypeStruct(w_mlp.shape, BF16),
+        ),
+        in_specs=[pl.BlockSpec(memory_space=pltpu.SMEM), vmem, hbm, hbm],
+        out_specs=(vmem, vmem, vmem),
+        scratch_shapes=[
+            pltpu.VMEM((2, half, width), F32),
+            pltpu.VMEM(w_out.shape, BF16),
+            pltpu.SemaphoreType.DMA((2,)),
+        ],
         compiler_params=params(24 << 20),
         name="combine",
-    )(core, *parts, w_out)
+    )(core, gathered, *in_hbm(w_out, w_mlp))
 
 
 def spread(latents, w_query, devices):
-    vmem = pl.BlockSpec(memory_space=pltpu.VMEM)
+    hbm = pl.BlockSpec(memory_space=pltpu.HBM)
     return pl.pallas_call(
         spread_kernel,
         out_shape=jax.ShapeDtypeStruct((devices, latents.shape[0], w_query.shape[1]), BF16),
-        in_specs=[vmem, vmem],
-        out_specs=vmem,
-        compiler_params=params(24 << 20),
+        in_specs=[hbm, hbm],
+        out_specs=pl.BlockSpec(memory_space=pltpu.VMEM),
+        scratch_shapes=[
+            pltpu.VMEM(latents.shape, BF16),
+            pltpu.VMEM(w_query.shape, BF16),
+            pltpu.SemaphoreType.DMA((2,)),
+        ],
+        compiler_params=params(60 << 20),
         name="spread",
-    )(latents, w_query)
+    )(*in_hbm(latents, w_query))
 
 
 def latent_rows(own, recv, w_mlp, devices):
@@ -297,7 +399,51 @@
     )(*rows, w_lkey, w_lvalue)
 
 
-def decode(base, blocks, q, kvs, w_pout, dtype, finish=()):
+def near_kv(near, swapped, w_lkey, w_lvalue, w_pout):
+    vmem = pl.BlockSpec(memory_space=pltpu.VMEM)
+    hbm = pl.BlockSpec(memory_space=pltpu.HBM)
+    rows = near.shape[0] + swapped.shape[0]
+    return pl.pallas_call(
+        near_kv_kernel,
+        out_shape=[
+            jax.ShapeDtypeStruct((rows, 2 * w_lkey.shape[1]), BF16),
+            *[jax.ShapeDtypeStruct(w.shape, BF16) for w in (w_lkey, w_lvalue, w_pout)],
+        ],
+        in_specs=[vmem, vmem, hbm, hbm, hbm],
+        out_specs=[vmem] * 4,
+        scratch_shapes=[pltpu.SemaphoreType.DMA((3,))],
+        compiler_params=params(24 << 20),
+        cost_estimate=pl.CostEstimate(
+            flops=4 * rows * w_lkey.size // 2, bytes_accessed=4 << 20, transcendentals=0
+        ),
+        name="near_kv",
+    )(near, swapped, *in_hbm(w_lkey, w_lvalue, w_pout))
+
+
+def near_decode(q, kv):
+    rows, columns = q.shape
+    block = ROW_BLOCK
+    return pl.pallas_call(
+        near_kernel,
+        out_shape=(
+            jax.ShapeDtypeStruct((rows, columns), F32),
+            jax.ShapeDtypeStruct((rows, HEAD_DIM), F32),
+        ),
+        grid=(rows // block,),
+        in_specs=[pl.BlockSpec((block, columns), lambda i: (i, 0)), full_spec(kv)],
+        out_specs=(
+            pl.BlockSpec((block, columns), lambda i: (i, 0)),
+            pl.BlockSpec((block, HEAD_DIM), lambda i: (i, 0)),
+        ),
+        compiler_params=params(24 << 20),
+        cost_estimate=pl.CostEstimate(
+            flops=4 * rows * columns * kv.shape[0], bytes_accessed=4 << 20, transcendentals=4 * rows * kv.shape[0]
+        ),
+        name="near_decode",
+    )(q, kv)
+
+
+def decode(base, blocks, q, carried, kvs, w_pout, dtype, finish=()):
     columns = q.shape[1]
     width = w_pout.shape[1]
     block = ROW_BLOCK
@@ -312,7 +458,7 @@
             num_scalar_prefetch=1,
             grid=(blocks,),
             in_specs=[
-                pl.BlockSpec((block, columns), lambda i, b: (b[0] + i, 0)),
+                *[pl.BlockSpec((block, x.shape[1]), lambda i, b: (b[0] + i, 0)) for x in (q, *carried)],
                 *[full_spec(x) for x in (*kvs, w_pout, *finish)],
             ],
             out_specs=pl.BlockSpec((out_block, width), lambda i, b: (i, 0)),
@@ -322,7 +468,7 @@
             flops=4 * rows * columns * keys, bytes_accessed=8 << 20, transcendentals=4 * rows * keys
         ),
         name="decode",
-    )(base, q, *kvs, w_pout, *finish)
+    )(base, q, *carried, *kvs, w_pout, *finish)
 
 
 def project(a, w):
@@ -360,17 +506,20 @@
     queries = within_plane(spread(latents, w_query, SIDE * SIDE)).reshape(-1, columns)
     keys = project(inputs, w_key)
     values = project(inputs, w_value)
-    count = jnp.sum(valid_blocks).astype(jnp.int32).reshape(1)
     queries, keys, values = lax.optimization_barrier((queries, keys, values))
     away = [along(queries, s) for s in ORDER]
-    part = cross(count, queries, keys, values, lat_local)
-    partials = [part]
+    keys, values = load((keys, values))
+    heads = columns // HEAD_DIM
+    half = cross(valid_blocks, queries, keys, values, lat_local, 0, heads // 2)
+    part, partials = half, []
     for s, there in zip(ORDER, away):
         part, there = lax.optimization_barrier((part, there))
-        part = cross(count, there, keys, values, lat_local)
+        part = cross(valid_blocks, there, keys, values, lat_local, 0, heads)
         partials.append(along(part, -s))
+    part, half = lax.optimization_barrier((part, half))
+    partials.append(cross(valid_blocks, queries, keys, values, lat_local, heads // 2, heads // 2, half))
     gathered = within_plane(join(partials))
-    own, other = combine(core, [gathered], w_out, lat_local)
+    own, other, w_mlp = combine(core, gathered, w_out, w_mlp, lat_local)
     recv = lax.ppermute(other, "head", swap)
     rows = latent_rows(own, recv, w_mlp, SIDE * SIDE)
     rows, inputs = lax.optimization_barrier((rows, inputs))
@@ -378,15 +527,16 @@
     near, pos_queries = lax.optimization_barrier((within_plane(rows), pos_queries))
     near = near.reshape(-1, width)
     far = [along(near, s) for s in ORDER]
-    near_kv = latent_kv([near, lax.ppermute(near, "head", swap)], w_lkey, w_lvalue)
-    near_kv, *far = lax.optimization_barrier((near_kv, *far))
+    kv, w_lkey, w_lvalue, w_pout = near_kv(near, lax.ppermute(near, "head", swap), w_lkey, w_lvalue, w_pout)
+    carried = near_decode(pos_queries, kv)
+    carried, far = lax.optimization_barrier((carried, far))
     far_swapped = [lax.ppermute(x, "head", swap) for x in far]
-    kvs = [near_kv, latent_kv(far, w_lkey, w_lvalue), latent_kv(far_swapped, w_lkey, w_lvalue)]
+    kvs = [latent_kv(far, w_lkey, w_lvalue), latent_kv(far_swapped, w_lkey, w_lvalue)]
     blocks = pos_queries.shape[0] // 2 // ROW_BLOCK
-    terms = decode((1 - core) * blocks, blocks, pos_queries, kvs, w_pout, BF16)
+    terms = decode((1 - core) * blocks, blocks, pos_queries, carried, kvs, w_pout, BF16)
     arrived = lax.ppermute(terms, "head", swap)
-    first = decode(core * blocks, blocks - 1, pos_queries, kvs, w_pout, F32)
-    return decode(core * blocks + blocks - 1, 1, pos_queries, kvs, w_pout, BF16, (first, arrived))
+    first = decode(core * blocks, blocks - 1, pos_queries, carried, kvs, w_pout, F32)
+    return decode(core * blocks + blocks - 1, 1, pos_queries, carried, kvs, w_pout, BF16, (first, arrived))
 
 
 def solution(mesh):

time: 150 us -> 150 us (level)
  Pallas kernels: 51 us -> 62.2 us
  local copies, waits for them, and re-layouts: 9.96 us -> 0.01 us
  waiting for transfers between devices: 42.5 us -> 36.8 us
  starting transfers between devices: 36.9 us -> 41.6 us
    unnamed x30 -> x6, local copies, waits for them, and re-layouts: 9.96 us -> 0.01 us
    pallas_call x4 -> x8, Pallas kernels: 23.3 us -> 32.8 us  [the longest x5 21.9 us: cross(): pl.pallas_call(functools.partial(cross_kernel, lat_local=lat_local, first...]
    ppermute x9, waiting for transfers between devices: 18 us -> 13 us  [along(): return lax.ppermute(x, AXES, long[shift % SIDE])]
    pallas_call x3 -> x2, Pallas kernels: 5.94 us -> 3.57 us  [latent_kv(): pl.pallas_call(kv_kernel, out_shape=jax.ShapeDtypeStruct((total, wide), B...]
    pallas_call x3, Pallas kernels: 16.3 us -> 17.9 us  [decode(): pl.pallas_call(last_kernel if finish else decode_kernel, out_shape=jax.Sh...]
  transfers between devices with their start and end apart: 18 -> 18, of which waited for: 9 -> 8; matrix products, arithmetic and copies ran while one was open for 6% -> 6% of each run, Pallas kernels for 17% -> 22%
where the time goes in v3:
time: 150 us; the launch traced here: 149 us
  Pallas kernels  62.2 us (41%)
  starting transfers between devices  41.6 us (28%)
  waiting for transfers between devices  36.8 us (25%)
  matrix products  8.27 us (6%)
    all_to_all x3, waiting for transfers between devices, within_plane(): return lax.all_to_all(x, AXES, 0, 0, axis_index_groups=plane)  22.2 us
    pallas_call x5, Pallas kernels, cross(): pl.pallas_call(functools.partial(cross_kernel, lat_local=lat_local, first...  21.9 us
    pallas_call x3, Pallas kernels, decode(): pl.pallas_call(last_kernel if finish else decode_kernel, out_shape=jax.Sh...  17.9 us
    all_to_all x3, starting transfers between devices, within_plane(): return lax.all_to_all(x, AXES, 0, 0, axis_index_groups=plane)  17.5 us
    ppermute x9, starting transfers between devices, along(): return lax.ppermute(x, AXES, long[shift % SIDE])  15.4 us
    ppermute x9, waiting for transfers between devices, along(): return lax.ppermute(x, AXES, long[shift % SIDE])  13 us
    dot_general x3, matrix products, project(): return jnp.dot(a, w, preferred_element_type=F32).astype(BF16)  8.27 us
    pallas_call x1, Pallas kernels, near_decode(): pl.pallas_call(near_kernel, out_shape=(jax.ShapeDtypeStruct((rows, column...  5.55 us
  transfers between devices with their start and end apart: 18, of which 8 were waited for; matrix products, arithmetic and copies ran while one was open for 6% of the time, Pallas kernels for 22%

profile of v3, /device:TPU:1, one launch (start us, length us, event | category | flops | bytes accessed | tf_op | source)
XLA Modules:
  0.0 149.2 jit_solution(14649546279566221165)
XLA Ops:
  0.0 0.0 copy-start
  0.0 2.5 %spread.1 = bf16[16,32,512]{2,1,0:T(8,128)(2,1)} custom-call(bf16[32,1024]{1,0:T(8,128)(2,1)} %l_ref.1, bf16[1024,512]{1,0:T(8,128)(2,1)} %w_ref.2), custom_call_target="tpu_custom_call" | custom-call | tf_op jit(solution)/shard_map/spread/pallas_call | solution.py:358
  2.5 8.4 %all-to-all-start = ((bf16[16,32,512]{2,1,0:T(8,128)(2,1)}), bf16[16,32,512]{2,1,0:T(8,128)(2,1)S(1)}, u32[]{:S(2)}, u32[]{:S(2)}) async-start(bf16[16,32,512]{2,1,0:T(8,128)(2,1)} %spread.1), calls=%async_computation | async-start | bytes 1048576 | tf_op jit(solution)/shard_map/all_to_all | solution.py:501
  11.0 0.0 copy-done
  11.0 0.0 copy-start.2
  11.0 3.6 %convolution_convert_fusion.1.refs_1_ = bf16[1024,512]{1,0:T(8,128)(2,1)} fusion(bf16[1024,1024]{1,0:T(8,128)(2,1)S(1)} %copy-done, bf16[1024,512]{1,0:T(8,128)(2,1)} %param.17), kind=kOutput, calls=%fused_computation.1 | convolution fusion | flops 1074266112 | bytes 4194304 | tf_op jit(solution)/shard_map/dot_general | solution.py:475
  14.6 0.0 copy-done.2
  14.6 2.2 %convolution_convert_fusion.2.refs_0_ = bf16[1024,512]{1,0:T(8,128)(2,1)} fusion(bf16[1024,1024]{1,0:T(8,128)(2,1)S(1)} %copy-done, bf16[1024,512]{1,0:T(8,128)(2,1)S(1)} %copy-done.2), kind=kOutput, calls=%fused_computation.2 | convolution fusion | flops 1074266112 | bytes 4194304 | tf_op jit(solution)/shard_map/dot_general | solution.py:475
  16.8 0.0 copy-start.1
  16.8 4.4 %all-to-all-done = bf16[16,32,512]{2,1,0:T(8,128)(2,1)S(1)} async-done(((bf16[16,32,512]{2,1,0:T(8,128)(2,1)}), bf16[16,32,512]{2,1,0:T(8,128)(2,1)S(1)}, u32[]{:S(2)}, u32[]{:S(2)}) %all-to-all-start) | async-done | bytes 524320 | tf_op jit(solution)/shard_map/all_to_all | solution.py:501
  21.2 1.1 collective-permute-start
  22.3 2.8 %collective-permute-start.2 = (bf16[512,512]{1,0:T(8,128)(2,1)S(1)}, bf16[512,512]{1,0:T(8,128)(2,1)S(1)}, u32[]{:S(2)}, u32[]{:S(2)}) collective-permute-start(bf16[512,512]{1,0:T(8,128)(2,1)S(1)} %bitcast.10), channel_id=1, source_target_pairs={{0,64},{1,17},{2,66},{3,19},{4,68},{5,21},{6,70},{7,23},{8,72},{9,... | collective-permute-start | bytes 1572872 | tf_op jit(solution)/shard_map/ppermute | solution.py:504
  25.1 1.0 collective-permute-start.4
  26.1 1.6 %load.1 = (bf16[1024,512]{1,0:T(8,128)(2,1)S(1)}, bf16[1024,512]{1,0:T(8,128)(2,1)S(1)}) custom-call(bf16[1024,512]{1,0:T(8,128)(2,1)} %convolution_convert_fusion.2.refs_0_, bf16[1024,512]{1,0:T(8,128)(2,1)} %convolution_convert_fusion.1.refs_1_), custom_call_target="tpu_custom_call" | custom-call | tf_op jit(solution)/shard_map/load/pallas_call | solution.py:309
  27.7 0.0 copy-done.1
  27.7 3.2 %cross.5.refs_0_ = bf16[16,72,128]{2,1,0:T(8,128)(2,1)S(1)} custom-call(s32[8]{0:T(128)S(1)} %copy-done.1, bf16[512,512]{1,0:T(8,128)(2,1)S(1)} %bitcast.12, bf16[1024,512]{1,0:T(8,128)(2,1)S(1)} %get-tuple-element.35.k_ref, bf16[1024,512]{1,0:T(8,128)(2,1)S(1)} %get-tuple-element.36.v_ref), custom_call_target="tpu_custom_call" | custom-call | flops 536870912 | bytes 4194304 | tf_op jit(solution)/shard_map/cross/pallas_call | solution.py:280
  30.8 0.0 collective-permute-done.q_ref
  30.8 5.2 %cross.6 = bf16[16,136,128]{2,1,0:T(8,128)(2,1)S(1)} custom-call(s32[8]{0:T(128)S(1)} %copy-done.1, bf16[512,512]{1,0:T(8,128)(2,1)S(1)} %collective-permute-done.q_ref, bf16[1024,512]{1,0:T(8,128)(2,1)S(1)} %get-tuple-element.35.k_ref, bf16[1024,512]{1,0:T(8,128)(2,1)S(1)} %get-tuple-element.36.v_ref), custom_call_target="tpu_custom_call" | custom-call | flops 1073741824 | bytes 4194304 | tf_op jit(solution)/shard_map/cross/pallas_call | solution.py:280
  36.0 1.6 %collective-permute-done.2.q_ref = bf16[512,512]{1,0:T(8,128)(2,1)S(1)} collective-permute-done((bf16[512,512]{1,0:T(8,128)(2,1)S(1)}, bf16[512,512]{1,0:T(8,128)(2,1)S(1)}, u32[]{:S(2)}, u32[]{:S(2)}) %collective-permute-start.2) | collective-permute-done | bytes 524320 | tf_op jit(solution)/shard_map/ppermute | solution.py:504
  37.6 5.2 %cross.7 = bf16[16,136,128]{2,1,0:T(8,128)(2,1)S(1)} custom-call(s32[8]{0:T(128)S(1)} %copy-done.1, bf16[512,512]{1,0:T(8,128)(2,1)S(1)} %collective-permute-done.2.q_ref, bf16[1024,512]{1,0:T(8,128)(2,1)S(1)} %get-tuple-element.35.k_ref, bf16[1024,512]{1,0:T(8,128)(2,1)S(1)} %get-tuple-element.36.v_ref), custom_call_target="tpu_custom_call" | custom-call | flops 1073741824 | bytes 4194304 | tf_op jit(solution)/shard_map/cross/pallas_call | solution.py:280
  42.8 0.0 collective-permute-done.4.q_ref
  42.8 5.2 %cross.8 = bf16[16,136,128]{2,1,0:T(8,128)(2,1)S(1)} custom-call(s32[8]{0:T(128)S(1)} %copy-done.1, bf16[512,512]{1,0:T(8,128)(2,1)S(1)} %collective-permute-done.4.q_ref, bf16[1024,512]{1,0:T(8,128)(2,1)S(1)} %get-tuple-element.35.k_ref, bf16[1024,512]{1,0:T(8,128)(2,1)S(1)} %get-tuple-element.36.v_ref), custom_call_target="tpu_custom_call" | custom-call | flops 1073741824 | bytes 4194304 | tf_op jit(solution)/shard_map/cross/pallas_call | solution.py:280
  48.0 0.1 collective-permute-start.5
  48.1 5.6 %collective-permute-start.3 = (bf16[16,136,128]{2,1,0:T(8,128)(2,1)S(1)}, bf16[16,136,128]{2,1,0:T(8,128)(2,1)S(1)}, u32[]{:S(2)}, u32[]{:S(2)}) collective-permute-start(bf16[16,136,128]{2,1,0:T(8,128)(2,1)S(1)} %cross.7), channel_id=1, source_target_pairs={{0,64},{1,17},{2,66},{3,19},{4,68},{5,21},{6,70},{7,23},{8,72},{9,... | collective-permute-start | bytes 1671176 | tf_op jit(solution)/shard_map/ppermute | solution.py:504
  53.7 2.0 %collective-permute-start.1 = (bf16[16,136,128]{2,1,0:T(8,128)(2,1)S(1)}, bf16[16,136,128]{2,1,0:T(8,128)(2,1)S(1)}, u32[]{:S(2)}, u32[]{:S(2)}) collective-permute-start(bf16[16,136,128]{2,1,0:T(8,128)(2,1)S(1)} %cross.6), channel_id=1, source_target_pairs={{0,96},{1,25},{2,98},{3,27},{4,100},{5,29},{6,102},{7,31},{8,104},... | collective-permute-start | bytes 1671176 | tf_op jit(solution)/shard_map/ppermute | solution.py:504
  55.7 3.2 %cross.9.refs_3_ = bf16[16,136,128]{2,1,0:T(8,128)(2,1)S(1)} custom-call(s32[8]{0:T(128)S(1)} %copy-done.1, bf16[512,512]{1,0:T(8,128)(2,1)S(1)} %bitcast.13, bf16[1024,512]{1,0:T(8,128)(2,1)S(1)} %get-tuple-element.35.k_ref, bf16[1024,512]{1,0:T(8,128)(2,1)S(1)} %get-tuple-element.36.v_ref, bf16[16,72,128]{2,1,0:T(8,128)(2,1)S(1)} %cross.5.refs_0_), custom_call_target="tpu_custom_call" | custom-call | flops 536870912 | bytes 4194304 | tf_op jit(solution)/shard_map/cross/pallas_call | solution.py:280
  58.9 0.0 collective-permute-done.5.refs_2_
  58.9 7.6 %collective-permute-done.3.refs_1_ = bf16[16,136,128]{2,1,0:T(8,128)(2,1)S(1)} collective-permute-done((bf16[16,136,128]{2,1,0:T(8,128)(2,1)S(1)}, bf16[16,136,128]{2,1,0:T(8,128)(2,1)S(1)}, u32[]{:S(2)}, u32[]{:S(2)}) %collective-permute-start.3) | collective-permute-done | bytes 557088 | tf_op jit(solution)/shard_map/ppermute | solution.py:504
  66.5 0.0 collective-permute-done.1.refs_0_
  66.6 2.2 %join.1 = bf16[16,136,128]{2,1,0:T(8,128)(2,1)} custom-call(bf16[16,136,128]{2,1,0:T(8,128)(2,1)S(1)} %collective-permute-done.1.refs_0_, bf16[16,136,128]{2,1,0:T(8,128)(2,1)S(1)} %collective-permute-done.3.refs_1_, bf16[16,136,128]{2,1,0:T(8,128)(2,1)S(1)} %collective-permute-done.5.refs_2_, bf16[16,136,128]{2,1,0:T(8,128)(2,1)S(1)} %cross.9.refs_3_), custom_call_target="tpu_custom_call" | custom-call | tf_op jit(solution)/shard_map/join/pallas_call | solution.py:322
  68.8 3.6 %all-to-all-start.1 = ((bf16[16,136,128]{2,1,0:T(8,128)(2,1)}), bf16[16,136,128]{2,1,0:T(8,128)(2,1)S(1)}, u32[]{:S(2)}, u32[]{:S(2)}) async-start(bf16[16,136,128]{2,1,0:T(8,128)(2,1)} %join.1), calls=%async_computation.1 | async-start | bytes 1114112 | tf_op jit(solution)/shard_map/all_to_all | solution.py:501
  72.4 9.1 %all-to-all-done.1.r_ref = bf16[16,136,128]{2,1,0:T(8,128)(2,1)S(1)} async-done(((bf16[16,136,128]{2,1,0:T(8,128)(2,1)}), bf16[16,136,128]{2,1,0:T(8,128)(2,1)S(1)}, u32[]{:S(2)}, u32[]{:S(2)}) %all-to-all-start.1) | async-done | bytes 557088 | tf_op jit(solution)/shard_map/all_to_all | solution.py:501
  81.5 1.9 %combine.1 = (f32[16,1024]{1,0:T(8,128)S(1)}, bf16[16,1024]{1,0:T(8,128)(2,1)S(1)}, bf16[1024,1024]{1,0:T(8,128)(2,1)S(1)}) custom-call(s32[1]{0:T(128)} %bitcast.core_ref, bf16[16,136,128]{2,1,0:T(8,128)(2,1)S(1)} %all-to-all-done.1.r_ref, bf16[512,1024]{1,0:T(8,128)(2,1)} %w_ref.3, bf16[1024,1024]{1,0:T(8,128)(2,1)} %mlp_ref.1), custom_call_target="tpu_custom_call" | custom-call | tf_op jit(solution)/shard_map/combine/pallas_call | solution.py:337
  83.5 4.7 %collective-permute-start.6 = (bf16[16,1024]{1,0:T(8,128)(2,1)S(1)}, bf16[16,1024]{1,0:T(8,128)(2,1)S(1)}, u32[]{:S(2)}, u32[]{:S(2)}) collective-permute-start(bf16[16,1024]{1,0:T(8,128)(2,1)S(1)} %get-tuple-element.42), channel_id=1, source_target_pairs={{0,1},{1,0},{2,3},{3,2},{4,5},{5,4},{6,7},{7,6},{8,9},{9,8},{10,11... | collective-permute-start | bytes 98312 | tf_op jit(solution)/shard_map/ppermute | solution.py:523
  88.2 0.9 collective-permute-done.6.recv_ref
  89.0 1.3 latent.1
  90.3 5.5 %all-to-all-start.2 = ((bf16[16,16,1024]{2,1,0:T(8,128)(2,1)}), bf16[16,16,1024]{2,1,0:T(8,128)(2,1)}, u32[]{:S(2)}, u32[]{:S(2)}) async-start(bf16[16,16,1024]{2,1,0:T(8,128)(2,1)} %latent.1), calls=%async_computation.2 | async-start | bytes 1048576 | tf_op jit(solution)/shard_map/all_to_all | solution.py:501
  95.9 2.5 %convolution_convert_fusion.q_ref = bf16[1024,512]{1,0:T(8,128)(2,1)S(1)} fusion(bf16[1024,1024]{1,0:T(8,128)(2,1)S(1)} %copy-done, bf16[1024,512]{1,0:T(8,128)(2,1)} %param.22), kind=kOutput, calls=%fused_computation | convolution fusion | flops 1074266112 | bytes 4194304 | tf_op jit(solution)/shard_map/dot_general | solution.py:475
  98.3 8.7 %all-to-all-done.2 = bf16[16,16,1024]{2,1,0:T(8,128)(2,1)} async-done(((bf16[16,16,1024]{2,1,0:T(8,128)(2,1)}), bf16[16,16,1024]{2,1,0:T(8,128)(2,1)}, u32[]{:S(2)}, u32[]{:S(2)}) %all-to-all-start.2) | async-done | bytes 524320 | tf_op jit(solution)/shard_map/all_to_all | solution.py:501
  107.1 0.0 collective-permute-start.7
  107.1 0.5 collective-permute-start.10
  107.6 1.0 collective-permute-start.8
  108.5 1.3 collective-permute-start.9
  109.8 0.0 collective-permute-done.7.swapped_ref
  109.8 3.7 %near_kv.1 = (bf16[512,1024]{1,0:T(8,128)(2,1)S(1)}, bf16[1024,512]{1,0:T(8,128)(2,1)S(1)}, bf16[1024,512]{1,0:T(8,128)(2,1)S(1)}, bf16[512,1024]{1,0:T(8,128)(2,1)S(1)}) custom-call(bf16[256,1024]{1,0:T(8,128)(2,1)} %bitcast.2.near_ref, bf16[256,1024]{1,0:T(8,128)(2,1)S(1)} %collective-permute-done.7.swapped_ref, bf16[1024,512]{1,0:T(8,128)(2,1)} %k_ref.1, ...), custom_call_target="tpu_custom_call" | custom-call | flops 536870912 | bytes 4194304 | tf_op jit(solution)/shard_map/near_kv/pallas_call | solution.py:406
  113.6 5.5 %near_decode.1 = (f32[1024,512]{1,0:T(8,128)S(1)}, f32[1024,128]{1,0:T(8,128)S(1)}) custom-call(bf16[1024,512]{1,0:T(8,128)(2,1)S(1)} %convolution_convert_fusion.q_ref, bf16[512,1024]{1,0:T(8,128)(2,1)S(1)} %get-tuple-element.48.kv_ref), custom_call_target="tpu_custom_call" | custom-call | flops 1073741824 | bytes 4194304 | tf_op jit(solution)/shard_map/near_decode/pallas_call | solution.py:426
  119.1 0.0 collective-permute-done.10.refs_2_
  119.1 3.8 %collective-permute-done.8.refs_0_ = bf16[256,1024]{1,0:T(8,128)(2,1)S(1)} collective-permute-done((bf16[256,1024]{1,0:T(8,128)(2,1)}, bf16[256,1024]{1,0:T(8,128)(2,1)S(1)}, u32[]{:S(2)}, u32[]{:S(2)}) %collective-permute-start.8) | collective-permute-done | bytes 524320 | tf_op jit(solution)/shard_map/ppermute | solution.py:504
  122.9 0.0 collective-permute-done.9.refs_1_
  122.9 2.8 %collective-permute-start.11 = (bf16[256,1024]{1,0:T(8,128)(2,1)S(1)}, bf16[256,1024]{1,0:T(8,128)(2,1)S(1)}, u32[]{:S(2)}, u32[]{:S(2)}) collective-permute-start(bf16[256,1024]{1,0:T(8,128)(2,1)S(1)} %collective-permute-done.8.refs_0_), channel_id=1, source_target_pairs={{0,1},{1,0},{2,3},{3,2},{4,5},{5,4},{6,7},{7,6},{8,9},{9,8},{10,11... | collective-permute-start | bytes 1572872 | tf_op jit(solution)/shard_map/ppermute | solution.py:533
  125.7 0.0 collective-permute-start.12
  125.7 0.5 collective-permute-start.13
  126.2 1.8 %latent_kv.2.refs_0_ = bf16[768,1024]{1,0:T(8,128)(2,1)S(1)} custom-call(bf16[256,1024]{1,0:T(8,128)(2,1)S(1)} %collective-permute-done.8.refs_0_, bf16[256,1024]{1,0:T(8,128)(2,1)S(1)} %collective-permute-done.9.refs_1_, bf16[256,1024]{1,0:T(8,128)(2,1)S(1)} %collective-permute-done.10.refs_2_, bf16[1024,512]{1,0:T(8,128)(2,1)S(1)} %get-tuple-element.56.refs_3_, ...), custom_call_target="tpu_custom_call" | custom-call | flops 1610612736 | bytes 4194304 | tf_op jit(solution)/shard_map/latent_kv/pallas_call | solution.py:389
  128.0 0.0 collective-permute-done.11.refs_0_
  128.0 0.0 collective-permute-done.12.refs_1_
  128.0 0.7 collective-permute-done.13.refs_2_
  128.7 1.8 %latent_kv.3.refs_1_ = bf16[768,1024]{1,0:T(8,128)(2,1)S(1)} custom-call(bf16[256,1024]{1,0:T(8,128)(2,1)S(1)} %collective-permute-done.11.refs_0_, bf16[256,1024]{1,0:T(8,128)(2,1)S(1)} %collective-permute-done.12.refs_1_, bf16[256,1024]{1,0:T(8,128)(2,1)S(1)} %collective-permute-done.13.refs_2_, bf16[1024,512]{1,0:T(8,128)(2,1)S(1)} %get-tuple-element.56.refs_3_, ...), custom_call_target="tpu_custom_call" | custom-call | flops 1610612736 | bytes 4194304 | tf_op jit(solution)/shard_map/latent_kv/pallas_call | solution.py:389
  130.5 8.3 %decode.4 = bf16[512,1024]{1,0:T(8,128)(2,1)S(1)} custom-call(s32[1]{0:T(128)S(6)} %mul.8.base_ref, bf16[1024,512]{1,0:T(8,128)(2,1)S(1)} %convolution_convert_fusion.q_ref, f32[1024,512]{1,0:T(8,128)S(1)} %get-tuple-element.51.sums_ref, f32[1024,128]{1,0:T(8,128)S(1)} %get-tuple-element.52.stats_ref, bf16[768,1024]{1,0:T(8,128)(2,1)S(1)} %latent_kv.2.refs_0_, ...), custom_call_target="tpu_custom_call" | custom-call | flops 1610612736 | bytes 8388608 | tf_op jit(solution)/shard_map/decode/pallas_call | solution.py:454
  138.8 0.7 collective-permute-start.14
  139.5 4.2 %decode.3.refs_3_ = f32[256,1024]{1,0:T(8,128)S(1)} custom-call(s32[1]{0:T(128)S(6)} %mul.7.base_ref, bf16[1024,512]{1,0:T(8,128)(2,1)S(1)} %convolution_convert_fusion.q_ref, f32[1024,512]{1,0:T(8,128)S(1)} %get-tuple-element.51.sums_ref, f32[1024,128]{1,0:T(8,128)S(1)} %get-tuple-element.52.stats_ref, bf16[768,1024]{1,0:T(8,128)(2,1)S(1)} %latent_kv.2.refs_0_, ...), custom_call_target="tpu_custom_call" | custom-call | flops 805306368 | bytes 8388608 | tf_op jit(solution)/shard_map/decode/pallas_call | solution.py:454
  143.7 0.0 collective-permute-done.14.refs_4_
  143.7 5.5 %decode.5 = bf16[512,1024]{1,0:T(8,128)(2,1)} custom-call(s32[1]{0:T(128)S(6)} %sub.6.base_ref, bf16[1024,512]{1,0:T(8,128)(2,1)S(1)} %convolution_convert_fusion.q_ref, f32[1024,512]{1,0:T(8,128)S(1)} %get-tuple-element.51.sums_ref, f32[1024,128]{1,0:T(8,128)S(1)} %get-tuple-element.52.stats_ref, bf16[768,1024]{1,0:T(8,128)(2,1)S(1)} %latent_kv.2.refs_0_, ...), custom_call_target="tpu_custom_call" | custom-call | flops 805306368 | bytes 8388608 | tf_op jit(solution)/shard_map/decode/pallas_call | solution.py:454
Async XLA Ops:
  0.0 11.0 %copy-start = (bf16[1024,1024]{1,0:T(8,128)(2,1)S(1)}, bf16[1024,1024]{1,0:T(8,128)(2,1)}, u32[]{:S(2)}) copy-start(bf16[1024,1024]{1,0:T(8,128)(2,1)} %param.12) | copy-start | bytes 6291460
  2.5 18.6 %all-to-all-start = ((bf16[16,32,512]{2,1,0:T(8,128)(2,1)}), bf16[16,32,512]{2,1,0:T(8,128)(2,1)S(1)}, u32[]{:S(2)}, u32[]{:S(2)}) async-start(bf16[16,32,512]{2,1,0:T(8,128)(2,1)} %spread.1), calls=%async_computation | async-start | bytes 1048576 | tf_op jit(solution)/shard_map/all_to_all | solution.py:501
  11.0 3.6 %copy-start.2 = (bf16[1024,512]{1,0:T(8,128)(2,1)S(1)}, bf16[1024,512]{1,0:T(8,128)(2,1)}, u32[]{:S(2)}) copy-start(bf16[1024,512]{1,0:T(8,128)(2,1)} %param.16) | copy-start | bytes 3145732
  16.8 10.9 %copy-start.1 = (s32[8]{0:T(128)S(1)}, s32[8]{0:T(128)}, u32[]{:S(2)}) copy-start(s32[8]{0:T(128)} %valid_ref.9) | copy-start | bytes 100
  21.2 9.6 %collective-permute-start = (bf16[512,512]{1,0:T(8,128)(2,1)S(1)}, bf16[512,512]{1,0:T(8,128)(2,1)S(1)}, u32[]{:S(2)}, u32[]{:S(2)}) collective-permute-start(bf16[512,512]{1,0:T(8,128)(2,1)S(1)} %bitcast.9), channel_id=1, source_target_pairs={{0,32},{1,9},{2,34},{3,11},{4,36},{5,13},{6,38},{7,15},{8,40},{9,1... | collective-permute-start | bytes 1572872 | tf_op jit(solution)/shard_map/ppermute | solution.py:504
  22.3 15.3 %collective-permute-start.2 = (bf16[512,512]{1,0:T(8,128)(2,1)S(1)}, bf16[512,512]{1,0:T(8,128)(2,1)S(1)}, u32[]{:S(2)}, u32[]{:S(2)}) collective-permute-start(bf16[512,512]{1,0:T(8,128)(2,1)S(1)} %bitcast.10), channel_id=1, source_target_pairs={{0,64},{1,17},{2,66},{3,19},{4,68},{5,21},{6,70},{7,23},{8,72},{9,... | collective-permute-start | bytes 1572872 | tf_op jit(solution)/shard_map/ppermute | solution.py:504
  25.1 17.7 %collective-permute-start.4 = (bf16[512,512]{1,0:T(8,128)(2,1)S(1)}, bf16[512,512]{1,0:T(8,128)(2,1)S(1)}, u32[]{:S(2)}, u32[]{:S(2)}) collective-permute-start(bf16[512,512]{1,0:T(8,128)(2,1)S(1)} %bitcast.11), channel_id=1, source_target_pairs={{0,96},{1,25},{2,98},{3,27},{4,100},{5,29},{6,102},{7,31},{8,104},... | collective-permute-start | bytes 1572872 | tf_op jit(solution)/shard_map/ppermute | solution.py:504
  48.0 10.9 %collective-permute-start.5 = (bf16[16,136,128]{2,1,0:T(8,128)(2,1)S(1)}, bf16[16,136,128]{2,1,0:T(8,128)(2,1)S(1)}, u32[]{:S(2)}, u32[]{:S(2)}) collective-permute-start(bf16[16,136,128]{2,1,0:T(8,128)(2,1)S(1)} %cross.8), channel_id=1, source_target_pairs={{0,32},{1,9},{2,34},{3,11},{4,36},{5,13},{6,38},{7,15},{8,40},{9,1... | collective-permute-start | bytes 1671176 | tf_op jit(solution)/shard_map/ppermute | solution.py:504
  48.1 18.4 %collective-permute-start.3 = (bf16[16,136,128]{2,1,0:T(8,128)(2,1)S(1)}, bf16[16,136,128]{2,1,0:T(8,128)(2,1)S(1)}, u32[]{:S(2)}, u32[]{:S(2)}) collective-permute-start(bf16[16,136,128]{2,1,0:T(8,128)(2,1)S(1)} %cross.7), channel_id=1, source_target_pairs={{0,64},{1,17},{2,66},{3,19},{4,68},{5,21},{6,70},{7,23},{8,72},{9,... | collective-permute-start | bytes 1671176 | tf_op jit(solution)/shard_map/ppermute | solution.py:504
  53.7 12.8 %collective-permute-start.1 = (bf16[16,136,128]{2,1,0:T(8,128)(2,1)S(1)}, bf16[16,136,128]{2,1,0:T(8,128)(2,1)S(1)}, u32[]{:S(2)}, u32[]{:S(2)}) collective-permute-start(bf16[16,136,128]{2,1,0:T(8,128)(2,1)S(1)} %cross.6), channel_id=1, source_target_pairs={{0,96},{1,25},{2,98},{3,27},{4,100},{5,29},{6,102},{7,31},{8,104},... | collective-permute-start | bytes 1671176 | tf_op jit(solution)/shard_map/ppermute | solution.py:504
  68.8 12.7 %all-to-all-start.1 = ((bf16[16,136,128]{2,1,0:T(8,128)(2,1)}), bf16[16,136,128]{2,1,0:T(8,128)(2,1)S(1)}, u32[]{:S(2)}, u32[]{:S(2)}) async-start(bf16[16,136,128]{2,1,0:T(8,128)(2,1)} %join.1), calls=%async_computation.1 | async-start | bytes 1114112 | tf_op jit(solution)/shard_map/all_to_all | solution.py:501
  83.5 5.6 %collective-permute-start.6 = (bf16[16,1024]{1,0:T(8,128)(2,1)S(1)}, bf16[16,1024]{1,0:T(8,128)(2,1)S(1)}, u32[]{:S(2)}, u32[]{:S(2)}) collective-permute-start(bf16[16,1024]{1,0:T(8,128)(2,1)S(1)} %get-tuple-element.42), channel_id=1, source_target_pairs={{0,1},{1,0},{2,3},{3,2},{4,5},{5,4},{6,7},{7,6},{8,9},{9,8},{10,11... | collective-permute-start | bytes 98312 | tf_op jit(solution)/shard_map/ppermute | solution.py:523
  90.3 16.7 %all-to-all-start.2 = ((bf16[16,16,1024]{2,1,0:T(8,128)(2,1)}), bf16[16,16,1024]{2,1,0:T(8,128)(2,1)}, u32[]{:S(2)}, u32[]{:S(2)}) async-start(bf16[16,16,1024]{2,1,0:T(8,128)(2,1)} %latent.1), calls=%async_computation.2 | async-start | bytes 1048576 | tf_op jit(solution)/shard_map/all_to_all | solution.py:501
  107.1 2.8 %collective-permute-start.7 = (bf16[256,1024]{1,0:T(8,128)(2,1)}, bf16[256,1024]{1,0:T(8,128)(2,1)S(1)}, u32[]{:S(2)}, u32[]{:S(2)}) collective-permute-start(bf16[256,1024]{1,0:T(8,128)(2,1)} %bitcast.2.near_ref), channel_id=1, source_target_pairs={{0,1},{1,0},{2,3},{3,2},{4,5},{5,4},{6,7},{7,6},{8,9},{9,8},{10,11... | collective-permute-start | bytes 1572872 | tf_op jit(solution)/shard_map/ppermute | solution.py:530
  107.1 12.1 %collective-permute-start.10 = (bf16[256,1024]{1,0:T(8,128)(2,1)}, bf16[256,1024]{1,0:T(8,128)(2,1)S(1)}, u32[]{:S(2)}, u32[]{:S(2)}) collective-permute-start(bf16[256,1024]{1,0:T(8,128)(2,1)} %bitcast.2.near_ref), channel_id=1, source_target_pairs={{0,96},{1,25},{2,98},{3,27},{4,100},{5,29},{6,102},{7,31},{8,104},... | collective-permute-start | bytes 1572872 | tf_op jit(solution)/shard_map/ppermute | solution.py:504
  107.6 15.4 %collective-permute-start.8 = (bf16[256,1024]{1,0:T(8,128)(2,1)}, bf16[256,1024]{1,0:T(8,128)(2,1)S(1)}, u32[]{:S(2)}, u32[]{:S(2)}) collective-permute-start(bf16[256,1024]{1,0:T(8,128)(2,1)} %bitcast.2.near_ref), channel_id=1, source_target_pairs={{0,32},{1,9},{2,34},{3,11},{4,36},{5,13},{6,38},{7,15},{8,40},{9,1... | collective-permute-start | bytes 1572872 | tf_op jit(solution)/shard_map/ppermute | solution.py:504
  108.5 14.4 %collective-permute-start.9 = (bf16[256,1024]{1,0:T(8,128)(2,1)}, bf16[256,1024]{1,0:T(8,128)(2,1)S(1)}, u32[]{:S(2)}, u32[]{:S(2)}) collective-permute-start(bf16[256,1024]{1,0:T(8,128)(2,1)} %bitcast.2.near_ref), channel_id=1, source_target_pairs={{0,64},{1,17},{2,66},{3,19},{4,68},{5,21},{6,70},{7,23},{8,72},{9,... | collective-permute-start | bytes 1572872 | tf_op jit(solution)/shard_map/ppermute | solution.py:504
  122.9 5.1 %collective-permute-start.11 = (bf16[256,1024]{1,0:T(8,128)(2,1)S(1)}, bf16[256,1024]{1,0:T(8,128)(2,1)S(1)}, u32[]{:S(2)}, u32[]{:S(2)}) collective-permute-start(bf16[256,1024]{1,0:T(8,128)(2,1)S(1)} %collective-permute-done.8.refs_0_), channel_id=1, source_target_pairs={{0,1},{1,0},{2,3},{3,2},{4,5},{5,4},{6,7},{7,6},{8,9},{9,8},{10,11... | collective-permute-start | bytes 1572872 | tf_op jit(solution)/shard_map/ppermute | solution.py:533
  125.7 2.3 %collective-permute-start.12 = (bf16[256,1024]{1,0:T(8,128)(2,1)S(1)}, bf16[256,1024]{1,0:T(8,128)(2,1)S(1)}, u32[]{:S(2)}, u32[]{:S(2)}) collective-permute-start(bf16[256,1024]{1,0:T(8,128)(2,1)S(1)} %collective-permute-done.9.refs_1_), channel_id=1, source_target_pairs={{0,1},{1,0},{2,3},{3,2},{4,5},{5,4},{6,7},{7,6},{8,9},{9,8},{10,11... | collective-permute-start | bytes 1572872 | tf_op jit(solution)/shard_map/ppermute | solution.py:533
  125.7 3.0 %collective-permute-start.13 = (bf16[256,1024]{1,0:T(8,128)(2,1)S(1)}, bf16[256,1024]{1,0:T(8,128)(2,1)S(1)}, u32[]{:S(2)}, u32[]{:S(2)}) collective-permute-start(bf16[256,1024]{1,0:T(8,128)(2,1)S(1)} %collective-permute-done.10.refs_2_), channel_id=1, source_target_pairs={{0,1},{1,0},{2,3},{3,2},{4,5},{5,4},{6,7},{7,6},{8,9},{9,8},{10,11... | collective-permute-start | bytes 1572872 | tf_op jit(solution)/shard_map/ppermute | solution.py:533
  138.8 4.9 %collective-permute-start.14 = (bf16[512,1024]{1,0:T(8,128)(2,1)S(1)}, bf16[512,1024]{1,0:T(8,128)(2,1)S(1)}, u32[]{:S(2)}, u32[]{:S(2)}) collective-permute-start(bf16[512,1024]{1,0:T(8,128)(2,1)S(1)} %decode.4), channel_id=1, source_target_pairs={{0,1},{1,0},{2,3},{3,2},{4,5},{5,4},{6,7},{7,6},{8,9},{9,8},{10,11... | collective-permute-start | bytes 3145736 | tf_op jit(solution)/shard_map/ppermute | solution.py:537

commit v4 on v3

--- a/solution.py
+++ b/solution.py
@@ -17,7 +17,7 @@
 F32 = jnp.float32
 BF16 = jnp.bfloat16
 ROW_BLOCK = 256
-LSE_ROWS = 8
+LSE_ROWS = 16
 
 
 AXES = ("pos", "head")
@@ -47,6 +47,11 @@
     return plane, long
 
 
+def lane_offset(lat_local):
+    x = lax.axis_index("pos") % SIDE
+    return (x % (HEAD_DIM // lat_local) * lat_local).astype(jnp.int32).reshape(1)
+
+
 def rms_norm(values):
     return values * lax.rsqrt(jnp.mean(values * values, axis=-1, keepdims=True) + EPS)
 
@@ -55,47 +60,82 @@
     return lax.dot_general(a, b, (((1,), (1,)), ((), ())), preferred_element_type=F32)
 
 
-def pieces(row):
-    hi = row.astype(BF16).astype(F32)
-    mid = (row - hi).astype(BF16).astype(F32)
-    low = (row - hi - mid).astype(BF16).astype(F32)
-    place = lax.broadcasted_iota(jnp.int32, row.shape, 0)
-    packed = jnp.where(place == 0, hi, jnp.where(place == 1, mid, jnp.where(place == 2, low, 0.0)))
-    return packed.astype(BF16)
+def bf16_pieces(x):
+    hi = x.astype(BF16).astype(F32)
+    mid = (x - hi).astype(BF16).astype(F32)
+    low = (x - hi - mid).astype(BF16).astype(F32)
+    return hi, mid, low
+
+
+def pack_rows(lse, heads):
+    rows = jnp.concatenate([p[:heads] for p in bf16_pieces(lse)], axis=0)
+    pad = jnp.zeros((LSE_ROWS - rows.shape[0], rows.shape[1]), F32)
+    return jnp.concatenate([rows, pad], axis=0).astype(BF16)
+
+
+def unpack_rows(packed, heads):
+    x = packed.astype(F32)
+    return x[:heads] + x[heads : 2 * heads] + x[2 * heads : 3 * heads]
+
+
+def pipelined(count, score, use):
+    score(0)
+    for i in range(count):
+        if i + 1 < count:
+            score(i + 1)
+        use(i)
 
 
 def cross_kernel(valid_ref, q_ref, k_ref, v_ref, *refs, lat_local, first, heads):
-    before_ref, out_ref = refs if len(refs) == 2 else (None, refs[0])
+    *before, out_ref, s_ref = refs
     rows = q_ref.shape[0]
     owners = rows // lat_local
+    all_heads = q_ref.shape[1] // HEAD_DIM
     done = first * lat_local
     span = done + heads * lat_local
     keys = k_ref.shape[0]
     valid = sum(valid_ref[i] for i in range(keys // BLK)) * BLK
     live = lax.broadcasted_iota(jnp.int32, (1, keys), 1) < valid
     bias = jnp.where(live, 0.0, MASKED)
-    if before_ref is not None:
-        out_ref[:, :done, :] = before_ref[:, :done, :]
-    zeros = jnp.zeros((rows, 1), F32)
-    columns = [zeros] * first
-    for h in range(first, first + heads):
-        cols = slice(h * HEAD_DIM, (h + 1) * HEAD_DIM)
-        s = nt_dot(q_ref[:, cols], k_ref[:, cols]) + bias
+    lane = lax.broadcasted_iota(jnp.int32, (rows, HEAD_DIM), 1)
+    if before:
+        out_ref[:, :done, :] = before[0][:, :done, :]
+    tops = jnp.zeros((rows, HEAD_DIM), F32)
+    totals = jnp.ones((rows, HEAD_DIM), F32)
+
+    def columns(i):
+        return slice((first + i) * HEAD_DIM, (first + i + 1) * HEAD_DIM)
+
+    def score(i):
+        s_ref[i % 2] = nt_dot(q_ref[:, columns(i)], k_ref[:, columns(i)]) + bias
+
+    def use(i):
+        nonlocal tops, totals
+        s = s_ref[i % 2]
         m = jnp.max(s, axis=1, keepdims=True)
         p = jnp.exp2((s - m) * (SCALE * LOG2E))
         total = jnp.sum(p, axis=1, keepdims=True)
-        o = jnp.dot(p.astype(BF16), v_ref[:, cols], preferred_element_type=F32)
+        o = jnp.dot(p.astype(BF16), v_ref[:, columns(i)], preferred_element_type=F32)
         o = (o / total).astype(BF16)
-        out_ref[:, h * lat_local : (h + 1) * lat_local, :] = o.reshape(owners, lat_local, HEAD_DIM)
-        columns.append(m * SCALE + jnp.log(total))
-    columns += [zeros] * (HEAD_DIM // lat_local - len(columns))
+        top = (first + i) * lat_local
+        out_ref[:, top : top + lat_local, :] = o.reshape(owners, lat_local, HEAD_DIM)
+        mine = lane % all_heads == first + i
+        tops = jnp.where(mine, m, tops)
+        totals = jnp.where(mine, total, totals)
+
+    pipelined(heads, score, use)
+    hi, mid, low = bf16_pieces(tops * SCALE + jnp.log(totals))
+    place = lane // all_heads
+    packed = jnp.where(place == 0, hi, jnp.where(place == 1, mid, jnp.where(place == 2, low, 0.0)))
+    eye = lax.broadcasted_iota(jnp.int32, (LSE_ROWS, HEAD_DIM), 0)
+    eye = (eye == lax.broadcasted_iota(jnp.int32, (LSE_ROWS, HEAD_DIM), 1)).astype(BF16)
+    turned = nt_dot(eye, packed.astype(BF16)).astype(BF16)
     for d in range(owners):
-        part = jnp.concatenate([c[d * lat_local : (d + 1) * lat_local] for c in columns], axis=0)
-        row = jnp.transpose(jnp.broadcast_to(part, (HEAD_DIM, HEAD_DIM)))[:LSE_ROWS]
-        packed = pieces(row)
-        if before_ref is not None:
-            packed = packed + before_ref[d, done : done + LSE_ROWS, :]
-        out_ref[d, span : span + LSE_ROWS, :] = packed
+        at = d * lat_local // HEAD_DIM * HEAD_DIM
+        rows_d = turned[:, at : at + HEAD_DIM]
+        if before:
+            rows_d = rows_d + before[0][d, done : done + LSE_ROWS, :]
+        out_ref[d, span : span + LSE_ROWS, :] = rows_d
 
 
 def load_kernel(*refs):
@@ -108,26 +148,32 @@
         copy.wait()
 
 
-def join_kernel(*refs):
+def join_kernel(*refs, lat_local):
     *parts, out_ref = refs
     owners, tall, _ = out_ref.shape
     span = tall - LSE_ROWS
-    lses = [jnp.sum(r[:, span : span + LSE_ROWS, :].astype(F32), axis=1) for r in parts]
-    top = functools.reduce(jnp.maximum, lses)
-    ws = [jnp.exp(x - top) for x in lses]
-    total = functools.reduce(jnp.add, ws)
-    lse = top + jnp.log(total)
-    wts = [jnp.transpose(w / total) for w in ws]
-    for d in range(owners):
-        acc = jnp.zeros((span, HEAD_DIM), F32)
-        for wt, r in zip(wts, parts):
-            acc = acc + wt[:, d : d + 1] * r[d, :span, :].astype(F32)
-        out_ref[d, :span, :] = acc.astype(BF16)
-        row = jnp.broadcast_to(lse[d : d + 1, :], (LSE_ROWS, HEAD_DIM))
-        out_ref[d, span : span + LSE_ROWS, :] = pieces(row)
-
-
-def combine_kernel(core_ref, r_ref, w_ref, mlp_ref, own_ref, other_ref, mlp_out, terms_ref, w_vmem, sems, *, lat_local):
+    heads = span // lat_local
+    group = HEAD_DIM // lat_local
+    for g in range(0, owners, group):
+        lses = [unpack_rows(r[g, span : span + LSE_ROWS, :], heads) for r in parts]
+        top = functools.reduce(jnp.maximum, lses)
+        ws = [jnp.exp(x - top) for x in lses]
+        total = functools.reduce(jnp.add, ws)
+        packed = pack_rows(top + jnp.log(total), heads)
+        stacked = jnp.concatenate([w / total for w in ws], axis=0)
+        wt = jnp.transpose(stacked)
+        for d in range(group):
+            out_ref[g + d, span : span + LSE_ROWS, :] = packed
+            for h in range(heads):
+                rows = slice(h * lat_local, (h + 1) * lat_local)
+                acc = jnp.zeros((lat_local, HEAD_DIM), F32)
+                for i, r in enumerate(parts):
+                    w = wt[d * lat_local : (d + 1) * lat_local, i * heads + h : i * heads + h + 1]
+                    acc = acc + w * r[g + d, rows, :].astype(F32)
+                out_ref[g + d, rows, :] = acc.astype(BF16)
+
+
+def combine_kernel(core_ref, r_ref, w_ref, mlp_ref, own_ref, other_ref, mlp_out, terms_ref, spot_ref, w_vmem, sems, *, lat_local):
     copies = [
         pltpu.make_async_copy(w_ref, w_vmem, sems.at[0]),
         pltpu.make_async_copy(mlp_ref, mlp_out, sems.at[1]),
@@ -136,19 +182,26 @@
         copy.start()
     devices, tall, _ = r_ref.shape
     span = tall - LSE_ROWS
-    lse = jnp.sum(r_ref[:, span : span + LSE_ROWS, :].astype(F32), axis=1)
-    w = jnp.exp(lse - jnp.max(lse, axis=0, keepdims=True))
-    w = w / jnp.sum(w, axis=0, keepdims=True)
-    wt = jnp.transpose(w)
-    acc = jnp.zeros((span, HEAD_DIM), F32)
-    for d in range(devices):
-        acc = acc + wt[:span, d : d + 1] * r_ref[d, :span, :].astype(F32)
-    attended = acc.astype(BF16)
+    heads = span // lat_local
+    lses = [unpack_rows(r_ref[d, span : span + LSE_ROWS, :], heads) for d in range(devices)]
+    top = functools.reduce(jnp.maximum, lses)
+    ws = [jnp.exp(x - top) for x in lses]
+    total = functools.reduce(jnp.add, ws)
+    stacked = jnp.concatenate([w / total for w in ws], axis=0)
+    spot_ref[...] = jnp.transpose(stacked)
+    wt = spot_ref[pl.ds(pl.multiple_of(core_ref[1], lat_local), lat_local), :]
+    parts = []
+    for h in range(heads):
+        acc = jnp.zeros((lat_local, HEAD_DIM), F32)
+        for d in range(devices):
+            w = wt[:, d * heads + h : d * heads + h + 1]
+            acc = acc + w * r_ref[d, h * lat_local : (h + 1) * lat_local, :].astype(F32)
+        parts.append(acc.astype(BF16))
     copies[0].wait()
     terms = jnp.zeros((lat_local, w_vmem.shape[1]), F32)
     for h in range(span // lat_local):
         terms = terms + jnp.dot(
-            attended[h * lat_local : (h + 1) * lat_local],
+            parts[h],
             w_vmem[h * HEAD_DIM : (h + 1) * HEAD_DIM, :],
             preferred_element_type=F32,
         )
@@ -216,51 +269,68 @@
     )
 
 
-def near_kernel(q_ref, kv_ref, sums_ref, stats_ref):
+def near_kernel(q_ref, kv_ref, sums_ref, tops_ref, totals_ref, s_ref):
     columns = q_ref.shape[1]
-    heads = columns // HEAD_DIM
-    for h in range(heads):
+    shape = (q_ref.shape[0], HEAD_DIM)
+
+    def score(h):
+        kc, _ = head_columns(columns, h)
+        s_ref[h % 2] = nt_dot(q_ref[:, kc], kv_ref[:, kc])
+
+    def use(h):
         kc, vc = head_columns(columns, h)
-        s = nt_dot(q_ref[:, kc], kv_ref[:, kc])
+        s = s_ref[h % 2]
         m = jnp.max(s, axis=1, keepdims=True)
         p = jnp.exp2((s - m) * (SCALE * LOG2E))
         sums_ref[:, kc] = jnp.dot(p.astype(BF16), kv_ref[:, vc], preferred_element_type=F32)
-        stats_ref[:, h : h + 1] = m
-        stats_ref[:, heads + h : heads + h + 1] = jnp.sum(p, axis=1, keepdims=True)
-
-
-def attend(q_ref, sums_ref, stats_ref, kv_refs, w_ref):
+        tops_ref[:, kc] = jnp.broadcast_to(m, shape)
+        totals_ref[:, kc] = jnp.broadcast_to(jnp.sum(p, axis=1, keepdims=True), shape)
+
+    pipelined(columns // HEAD_DIM, score, use)
+
+
+def attend(q_ref, carried_refs, kv_refs, w_ref, s_ref, o_ref):
+    sums_ref, tops_ref, totals_ref = carried_refs
     columns = q_ref.shape[1]
-    heads = columns // HEAD_DIM
-    outs = []
-    for h in range(heads):
+    spots = []
+    at = 0
+    for kv in kv_refs:
+        spots.append(slice(at, at + kv.shape[0]))
+        at += kv.shape[0]
+
+    def score(h):
+        kc, _ = head_columns(columns, h)
+        for spot, kv in zip(spots, kv_refs):
+            s_ref[h % 2, :, spot] = nt_dot(q_ref[:, kc], kv[:, kc])
+
+    def use(h):
         kc, vc = head_columns(columns, h)
-        q = q_ref[:, kc]
-        scores = [nt_dot(q, kv[:, kc]) for kv in kv_refs]
-        before = stats_ref[:, h : h + 1]
-        m = functools.reduce(jnp.maximum, [before, *[jnp.max(s, axis=1, keepdims=True) for s in scores]])
+        s = s_ref[h % 2]
+        before = tops_ref[:, kc]
+        m = jnp.maximum(before, jnp.max(s, axis=1, keepdims=True))
         keep = jnp.exp2((before - m) * (SCALE * LOG2E))
-        total = stats_ref[:, heads + h : heads + h + 1] * keep
+        p = jnp.exp2((s - m[:, :1]) * (SCALE * LOG2E))
+        total = totals_ref[:, kc] * keep + jnp.sum(p, axis=1, keepdims=True)
         o = sums_ref[:, kc] * keep
-        for s, kv in zip(scores, kv_refs):
-            p = jnp.exp2((s - m) * (SCALE * LOG2E))
-            total = total + jnp.sum(p, axis=1, keepdims=True)
-            o = o + jnp.dot(p.astype(BF16), kv[:, vc], preferred_element_type=F32)
-        outs.append((o / total).astype(BF16))
-    attended = jnp.concatenate(outs, axis=1)
-    return jnp.dot(attended, w_ref[...], preferred_element_type=F32)
-
-
-def decode_kernel(base_ref, q_ref, sums_ref, stats_ref, *refs):
-    *kv_refs, w_ref, out_ref = refs
-    out_ref[...] = attend(q_ref, sums_ref, stats_ref, kv_refs, w_ref).astype(out_ref.dtype)
-
-
-def last_kernel(base_ref, q_ref, sums_ref, stats_ref, *refs):
-    *kv_refs, w_ref, first_ref, recv_ref, out_ref = refs
+        pb = p.astype(BF16)
+        for spot, kv in zip(spots, kv_refs):
+            o = o + jnp.dot(pb[:, spot], kv[:, vc], preferred_element_type=F32)
+        o_ref[:, kc] = (o / total).astype(BF16)
+
+    pipelined(columns // HEAD_DIM, score, use)
+    return jnp.dot(o_ref[...], w_ref[...], preferred_element_type=F32)
+
+
+def decode_kernel(base_ref, q_ref, *refs):
+    *carried, kv_a, kv_b, w_ref, out_ref, s_ref, o_ref = refs
+    out_ref[...] = attend(q_ref, carried, (kv_a, kv_b), w_ref, s_ref, o_ref).astype(out_ref.dtype)
+
+
+def last_kernel(base_ref, q_ref, *refs):
+    *carried, kv_a, kv_b, w_ref, first_ref, recv_ref, out_ref, s_ref, o_ref = refs
     n = first_ref.shape[0]
     out_ref[:n] = rms_norm(first_ref[...] + recv_ref[:n].astype(F32)).astype(out_ref.dtype)
-    terms = attend(q_ref, sums_ref, stats_ref, kv_refs, w_ref)
+    terms = attend(q_ref, carried, (kv_a, kv_b), w_ref, s_ref, o_ref)
     out_ref[n:] = rms_norm(terms + recv_ref[n:].astype(F32)).astype(out_ref.dtype)
 
 
@@ -290,6 +360,7 @@
                 *[pl.BlockSpec((block // lat_local,) + x.shape[1:], lambda i, c: (i, 0, 0)) for x in extra],
             ],
             out_specs=pl.BlockSpec((block // lat_local, tall, HEAD_DIM), lambda i, c: (i, 0, 0)),
+            scratch_shapes=[pltpu.VMEM((2, block, k.shape[0]), F32)],
         ),
         compiler_params=params(32 << 20),
         cost_estimate=pl.CostEstimate(
@@ -317,10 +388,10 @@
     )(*in_hbm(*arrays))
 
 
-def join(parts):
+def join(parts, lat_local):
     vmem = pl.BlockSpec(memory_space=pltpu.VMEM)
     return pl.pallas_call(
-        join_kernel,
+        functools.partial(join_kernel, lat_local=lat_local),
         out_shape=jax.ShapeDtypeStruct(parts[0].shape, BF16),
         in_specs=[vmem] * len(parts),
         out_specs=vmem,
@@ -345,6 +416,7 @@
         out_specs=(vmem, vmem, vmem),
         scratch_shapes=[
             pltpu.VMEM((2, half, width), F32),
+            pltpu.VMEM((HEAD_DIM, gathered.shape[0] * (w_out.shape[0] // HEAD_DIM)), F32),
             pltpu.VMEM(w_out.shape, BF16),
             pltpu.SemaphoreType.DMA((2,)),
         ],
@@ -427,14 +499,12 @@
         near_kernel,
         out_shape=(
             jax.ShapeDtypeStruct((rows, columns), F32),
-            jax.ShapeDtypeStruct((rows, HEAD_DIM), F32),
-        ),
+        )
+        * 3,
         grid=(rows // block,),
         in_specs=[pl.BlockSpec((block, columns), lambda i: (i, 0)), full_spec(kv)],
-        out_specs=(
-            pl.BlockSpec((block, columns), lambda i: (i, 0)),
-            pl.BlockSpec((block, HEAD_DIM), lambda i: (i, 0)),
-        ),
+        out_specs=(pl.BlockSpec((block, columns), lambda i: (i, 0)),) * 3,
+        scratch_shapes=[pltpu.VMEM((2, block, kv.shape[0]), F32)],
         compiler_params=params(24 << 20),
         cost_estimate=pl.CostEstimate(
             flops=4 * rows * columns * kv.shape[0], bytes_accessed=4 << 20, transcendentals=4 * rows * kv.shape[0]
@@ -462,6 +532,7 @@
                 *[full_spec(x) for x in (*kvs, w_pout, *finish)],
             ],
             out_specs=pl.BlockSpec((out_block, width), lambda i, b: (i, 0)),
+            scratch_shapes=[pltpu.VMEM((2, block, keys), F32), pltpu.VMEM((block, columns), BF16)],
         ),
         compiler_params=params(36 << 20),
         cost_estimate=pl.CostEstimate(
@@ -518,8 +589,8 @@
         partials.append(along(part, -s))
     part, half = lax.optimization_barrier((part, half))
     partials.append(cross(valid_blocks, queries, keys, values, lat_local, heads // 2, heads // 2, half))
-    gathered = within_plane(join(partials))
-    own, other, w_mlp = combine(core, gathered, w_out, w_mlp, lat_local)
+    gathered = within_plane(join(partials, lat_local))
+    own, other, w_mlp = combine(jnp.concatenate([core, lane_offset(lat_local)]), gathered, w_out, w_mlp, lat_local)
     recv = lax.ppermute(other, "head", swap)
     rows = latent_rows(own, recv, w_mlp, SIDE * SIDE)
     rows, inputs = lax.optimization_barrier((rows, inputs))

time: 150 us -> 142 us (0.947)
  Pallas kernels: 62.2 us -> 51.6 us
  waiting for transfers between devices: 36.8 us -> 41.7 us
  starting transfers between devices: 41.6 us -> 40.1 us
    pallas_call x3, Pallas kernels: 17.9 us -> 12.9 us  [decode(): pl.pallas_call(last_kernel if finish else decode_kernel, out_shape=jax.Sh...]
    pallas_call x5, Pallas kernels: 21.9 us -> 17 us  [cross(): pl.pallas_call(functools.partial(cross_kernel, lat_local=lat_local, first...]
    ppermute x9, waiting for transfers between devices: 13 us -> 17.8 us  [along(): return lax.ppermute(x, AXES, long[shift % SIDE])]
    pallas_call x1, Pallas kernels: 5.55 us -> 3.86 us  [near_decode(): pl.pallas_call(near_kernel, out_shape=(jax.ShapeDtypeStruct((rows, column...]
  transfers between devices with their start and end apart: 18 -> 18, of which waited for: 8 -> 10; matrix products, arithmetic and copies ran while one was open for 6% -> 6% of each run, Pallas kernels for 22% -> 19%
where the time goes in v4:
time: 142 us
  Pallas kernels  51.6 us (36%)
  waiting for transfers between devices  41.7 us (29%)
  starting transfers between devices  40.1 us (28%)
  matrix products  8.27 us (6%)
    all_to_all x3, waiting for transfers between devices, within_plane(): return lax.all_to_all(x, AXES, 0, 0, axis_index_groups=plane)  22.3 us
    ppermute x9, waiting for transfers between devices, along(): return lax.ppermute(x, AXES, long[shift % SIDE])  17.8 us
    all_to_all x3, starting transfers between devices, within_plane(): return lax.all_to_all(x, AXES, 0, 0, axis_index_groups=plane)  17.5 us
    pallas_call x5, Pallas kernels, cross(): pl.pallas_call(functools.partial(cross_kernel, lat_local=lat_local, first...  17 us
    ppermute x9, starting transfers between devices, along(): return lax.ppermute(x, AXES, long[shift % SIDE])  14.1 us
    pallas_call x3, Pallas kernels, decode(): pl.pallas_call(last_kernel if finish else decode_kernel, out_shape=jax.Sh...  12.9 us
    dot_general x3, matrix products, project(): return jnp.dot(a, w, preferred_element_type=F32).astype(BF16)  8.27 us
    ppermute x1, starting transfers between devices, per_device(): recv = lax.ppermute(other, 'head', swap)  4.74 us
  transfers between devices with their start and end apart: 18, of which 10 were waited for; matrix products, arithmetic and copies ran while one was open for 6% of the time, Pallas kernels for 19%

profile of v4, /device:TPU:1, one launch (start us, length us, event | category | flops | bytes accessed | tf_op | source)
XLA Modules:
  0.0 141.9 jit_solution(7183592088227468579)
XLA Ops:
  0.0 0.0 copy-start
  0.0 2.5 %spread.1 = bf16[16,32,512]{2,1,0:T(8,128)(2,1)} custom-call(bf16[32,1024]{1,0:T(8,128)(2,1)} %l_ref.1, bf16[1024,512]{1,0:T(8,128)(2,1)} %w_ref.2), custom_call_target="tpu_custom_call" | custom-call | tf_op jit(solution)/shard_map/spread/pallas_call | solution.py:430
  2.5 8.4 %all-to-all-start = ((bf16[16,32,512]{2,1,0:T(8,128)(2,1)}), bf16[16,32,512]{2,1,0:T(8,128)(2,1)S(1)}, u32[]{:S(2)}, u32[]{:S(2)}) async-start(bf16[16,32,512]{2,1,0:T(8,128)(2,1)} %spread.1), calls=%async_computation | async-start | bytes 1048576 | tf_op jit(solution)/shard_map/all_to_all | solution.py:572
  11.0 0.0 copy-done
  11.0 0.0 copy-start.2
  11.0 3.6 %convolution_convert_fusion.1.refs_1_ = bf16[1024,512]{1,0:T(8,128)(2,1)} fusion(bf16[1024,1024]{1,0:T(8,128)(2,1)S(1)} %copy-done, bf16[1024,512]{1,0:T(8,128)(2,1)} %param.17), kind=kOutput, calls=%fused_computation.1 | convolution fusion | flops 1074266112 | bytes 4194304 | tf_op jit(solution)/shard_map/dot_general | solution.py:546
  14.6 0.0 copy-done.2
  14.6 2.2 %convolution_convert_fusion.2.refs_0_ = bf16[1024,512]{1,0:T(8,128)(2,1)} fusion(bf16[1024,1024]{1,0:T(8,128)(2,1)S(1)} %copy-done, bf16[1024,512]{1,0:T(8,128)(2,1)S(1)} %copy-done.2), kind=kOutput, calls=%fused_computation.2 | convolution fusion | flops 1074266112 | bytes 4194304 | tf_op jit(solution)/shard_map/dot_general | solution.py:546
  16.8 0.0 copy-start.1
  16.8 4.4 %all-to-all-done = bf16[16,32,512]{2,1,0:T(8,128)(2,1)S(1)} async-done(((bf16[16,32,512]{2,1,0:T(8,128)(2,1)}), bf16[16,32,512]{2,1,0:T(8,128)(2,1)S(1)}, u32[]{:S(2)}, u32[]{:S(2)}) %all-to-all-start) | async-done | bytes 524320 | tf_op jit(solution)/shard_map/all_to_all | solution.py:572
  21.2 1.1 collective-permute-start
  22.3 2.8 %collective-permute-start.2 = (bf16[512,512]{1,0:T(8,128)(2,1)S(1)}, bf16[512,512]{1,0:T(8,128)(2,1)S(1)}, u32[]{:S(2)}, u32[]{:S(2)}) collective-permute-start(bf16[512,512]{1,0:T(8,128)(2,1)S(1)} %bitcast.11), channel_id=1, source_target_pairs={{0,64},{1,17},{2,66},{3,19},{4,68},{5,21},{6,70},{7,23},{8,72},{9,... | collective-permute-start | bytes 1572872 | tf_op jit(solution)/shard_map/ppermute | solution.py:575
  25.1 1.0 collective-permute-start.4
  26.1 1.6 %load.1 = (bf16[1024,512]{1,0:T(8,128)(2,1)S(1)}, bf16[1024,512]{1,0:T(8,128)(2,1)S(1)}) custom-call(bf16[1024,512]{1,0:T(8,128)(2,1)} %convolution_convert_fusion.2.refs_0_, bf16[1024,512]{1,0:T(8,128)(2,1)} %convolution_convert_fusion.1.refs_1_), custom_call_target="tpu_custom_call" | custom-call | tf_op jit(solution)/shard_map/load/pallas_call | solution.py:380
  27.7 0.0 copy-done.1
  27.7 2.6 %cross.5.refs_0_ = bf16[16,80,128]{2,1,0:T(8,128)(2,1)S(1)} custom-call(s32[8]{0:T(128)S(1)} %copy-done.1, bf16[512,512]{1,0:T(8,128)(2,1)S(1)} %bitcast.13, bf16[1024,512]{1,0:T(8,128)(2,1)S(1)} %get-tuple-element.37.k_ref, bf16[1024,512]{1,0:T(8,128)(2,1)S(1)} %get-tuple-element.38.v_ref), custom_call_target="tpu_custom_call" | custom-call | flops 536870912 | bytes 4194304 | tf_op jit(solution)/shard_map/cross/pallas_call | solution.py:350
  30.2 0.6 collective-permute-done.q_ref
  30.8 3.9 %cross.6 = bf16[16,144,128]{2,1,0:T(8,128)(2,1)S(1)} custom-call(s32[8]{0:T(128)S(1)} %copy-done.1, bf16[512,512]{1,0:T(8,128)(2,1)S(1)} %collective-permute-done.q_ref, bf16[1024,512]{1,0:T(8,128)(2,1)S(1)} %get-tuple-element.37.k_ref, bf16[1024,512]{1,0:T(8,128)(2,1)S(1)} %get-tuple-element.38.v_ref), custom_call_target="tpu_custom_call" | custom-call | flops 1073741824 | bytes 4194304 | tf_op jit(solution)/shard_map/cross/pallas_call | solution.py:350
  34.7 2.9 %collective-permute-done.2.q_ref = bf16[512,512]{1,0:T(8,128)(2,1)S(1)} collective-permute-done((bf16[512,512]{1,0:T(8,128)(2,1)S(1)}, bf16[512,512]{1,0:T(8,128)(2,1)S(1)}, u32[]{:S(2)}, u32[]{:S(2)}) %collective-permute-start.2) | collective-permute-done | bytes 524320 | tf_op jit(solution)/shard_map/ppermute | solution.py:575
  37.6 3.9 %cross.7 = bf16[16,144,128]{2,1,0:T(8,128)(2,1)S(1)} custom-call(s32[8]{0:T(128)S(1)} %copy-done.1, bf16[512,512]{1,0:T(8,128)(2,1)S(1)} %collective-permute-done.2.q_ref, bf16[1024,512]{1,0:T(8,128)(2,1)S(1)} %get-tuple-element.37.k_ref, bf16[1024,512]{1,0:T(8,128)(2,1)S(1)} %get-tuple-element.38.v_ref), custom_call_target="tpu_custom_call" | custom-call | flops 1073741824 | bytes 4194304 | tf_op jit(solution)/shard_map/cross/pallas_call | solution.py:350
  41.5 0.0 collective-permute-done.4.q_ref
  41.5 3.9 %cross.8 = bf16[16,144,128]{2,1,0:T(8,128)(2,1)S(1)} custom-call(s32[8]{0:T(128)S(1)} %copy-done.1, bf16[512,512]{1,0:T(8,128)(2,1)S(1)} %collective-permute-done.4.q_ref, bf16[1024,512]{1,0:T(8,128)(2,1)S(1)} %get-tuple-element.37.k_ref, bf16[1024,512]{1,0:T(8,128)(2,1)S(1)} %get-tuple-element.38.v_ref), custom_call_target="tpu_custom_call" | custom-call | flops 1073741824 | bytes 4194304 | tf_op jit(solution)/shard_map/cross/pallas_call | solution.py:350
  45.5 0.0 collective-permute-start.5
  45.5 4.4 %collective-permute-start.3 = (bf16[16,144,128]{2,1,0:T(8,128)(2,1)S(1)}, bf16[16,144,128]{2,1,0:T(8,128)(2,1)S(1)}, u32[]{:S(2)}, u32[]{:S(2)}) collective-permute-start(bf16[16,144,128]{2,1,0:T(8,128)(2,1)S(1)} %cross.7), channel_id=1, source_target_pairs={{0,64},{1,17},{2,66},{3,19},{4,68},{5,21},{6,70},{7,23},{8,72},{9,... | collective-permute-start | bytes 1769480 | tf_op jit(solution)/shard_map/ppermute | solution.py:575
  49.9 2.0 %collective-permute-start.1 = (bf16[16,144,128]{2,1,0:T(8,128)(2,1)S(1)}, bf16[16,144,128]{2,1,0:T(8,128)(2,1)S(1)}, u32[]{:S(2)}, u32[]{:S(2)}) collective-permute-start(bf16[16,144,128]{2,1,0:T(8,128)(2,1)S(1)} %cross.6), channel_id=1, source_target_pairs={{0,96},{1,25},{2,98},{3,27},{4,100},{5,29},{6,102},{7,31},{8,104},... | collective-permute-start | bytes 1769480 | tf_op jit(solution)/shard_map/ppermute | solution.py:575
  51.9 2.6 %cross.9.refs_3_ = bf16[16,144,128]{2,1,0:T(8,128)(2,1)S(1)} custom-call(s32[8]{0:T(128)S(1)} %copy-done.1, bf16[512,512]{1,0:T(8,128)(2,1)S(1)} %bitcast.14, bf16[1024,512]{1,0:T(8,128)(2,1)S(1)} %get-tuple-element.37.k_ref, bf16[1024,512]{1,0:T(8,128)(2,1)S(1)} %get-tuple-element.38.v_ref, bf16[16,80,128]{2,1,0:T(8,128)(2,1)S(1)} %cross.5.refs_0_), custom_call_target="tpu_custom_call" | custom-call | flops 536870912 | bytes 4194304 | tf_op jit(solution)/shard_map/cross/pallas_call | solution.py:350
  54.5 1.3 collective-permute-done.5.refs_2_
  55.8 7.6 %collective-permute-done.3.refs_1_ = bf16[16,144,128]{2,1,0:T(8,128)(2,1)S(1)} collective-permute-done((bf16[16,144,128]{2,1,0:T(8,128)(2,1)S(1)}, bf16[16,144,128]{2,1,0:T(8,128)(2,1)S(1)}, u32[]{:S(2)}, u32[]{:S(2)}) %collective-permute-start.3) | collective-permute-done | bytes 589856 | tf_op jit(solution)/shard_map/ppermute | solution.py:575
  63.4 0.0 collective-permute-done.1.refs_0_
  63.4 2.5 %join.1 = bf16[16,144,128]{2,1,0:T(8,128)(2,1)} custom-call(bf16[16,144,128]{2,1,0:T(8,128)(2,1)S(1)} %collective-permute-done.1.refs_0_, bf16[16,144,128]{2,1,0:T(8,128)(2,1)S(1)} %collective-permute-done.3.refs_1_, bf16[16,144,128]{2,1,0:T(8,128)(2,1)S(1)} %collective-permute-done.5.refs_2_, bf16[16,144,128]{2,1,0:T(8,128)(2,1)S(1)} %cross.9.refs_3_), custom_call_target="tpu_custom_call" | custom-call | tf_op jit(solution)/shard_map/join/pallas_call | solution.py:393
  65.9 3.6 %all-to-all-start.1 = ((bf16[16,144,128]{2,1,0:T(8,128)(2,1)}), bf16[16,144,128]{2,1,0:T(8,128)(2,1)S(1)}, u32[]{:S(2)}, u32[]{:S(2)}) async-start(bf16[16,144,128]{2,1,0:T(8,128)(2,1)} %join.1), calls=%async_computation.1 | async-start | bytes 1179648 | tf_op jit(solution)/shard_map/all_to_all | solution.py:572
  69.5 0.1 pad_add_fusion.core_ref
  69.6 9.2 %all-to-all-done.1.r_ref = bf16[16,144,128]{2,1,0:T(8,128)(2,1)S(1)} async-done(((bf16[16,144,128]{2,1,0:T(8,128)(2,1)}), bf16[16,144,128]{2,1,0:T(8,128)(2,1)S(1)}, u32[]{:S(2)}, u32[]{:S(2)}) %all-to-all-start.1) | async-done | bytes 589856 | tf_op jit(solution)/shard_map/all_to_all | solution.py:572
  78.8 2.7 %combine.1 = (f32[16,1024]{1,0:T(8,128)S(1)}, bf16[16,1024]{1,0:T(8,128)(2,1)S(1)}, bf16[1024,1024]{1,0:T(8,128)(2,1)S(1)}) custom-call(s32[2]{0:T(128)S(1)} %pad_add_fusion.core_ref, bf16[16,144,128]{2,1,0:T(8,128)(2,1)S(1)} %all-to-all-done.1.r_ref, bf16[512,1024]{1,0:T(8,128)(2,1)} %w_ref.3, bf16[1024,1024]{1,0:T(8,128)(2,1)} %mlp_ref.1), custom_call_target="tpu_custom_call" | custom-call | tf_op jit(solution)/shard_map/combine/pallas_call | solution.py:408
  81.5 4.7 %collective-permute-start.6 = (bf16[16,1024]{1,0:T(8,128)(2,1)S(1)}, bf16[16,1024]{1,0:T(8,128)(2,1)S(1)}, u32[]{:S(2)}, u32[]{:S(2)}) collective-permute-start(bf16[16,1024]{1,0:T(8,128)(2,1)S(1)} %get-tuple-element.44), channel_id=1, source_target_pairs={{0,1},{1,0},{2,3},{3,2},{4,5},{5,4},{6,7},{7,6},{8,9},{9,8},{10,11... | collective-permute-start | bytes 98312 | tf_op jit(solution)/shard_map/ppermute | solution.py:594
  86.2 0.9 collective-permute-done.6.recv_ref
  87.1 1.3 latent.1
  88.4 5.5 %all-to-all-start.2 = ((bf16[16,16,1024]{2,1,0:T(8,128)(2,1)}), bf16[16,16,1024]{2,1,0:T(8,128)(2,1)}, u32[]{:S(2)}, u32[]{:S(2)}) async-start(bf16[16,16,1024]{2,1,0:T(8,128)(2,1)} %latent.1), calls=%async_computation.2 | async-start | bytes 1048576 | tf_op jit(solution)/shard_map/all_to_all | solution.py:572
  93.9 2.5 %convolution_convert_fusion.q_ref = bf16[1024,512]{1,0:T(8,128)(2,1)S(1)} fusion(bf16[1024,1024]{1,0:T(8,128)(2,1)S(1)} %copy-done, bf16[1024,512]{1,0:T(8,128)(2,1)} %param.22), kind=kOutput, calls=%fused_computation | convolution fusion | flops 1074266112 | bytes 4194304 | tf_op jit(solution)/shard_map/dot_general | solution.py:546
  96.4 8.7 %all-to-all-done.2 = bf16[16,16,1024]{2,1,0:T(8,128)(2,1)} async-done(((bf16[16,16,1024]{2,1,0:T(8,128)(2,1)}), bf16[16,16,1024]{2,1,0:T(8,128)(2,1)}, u32[]{:S(2)}, u32[]{:S(2)}) %all-to-all-start.2) | async-done | bytes 524320 | tf_op jit(solution)/shard_map/all_to_all | solution.py:572
  105.1 0.0 collective-permute-start.7
  105.1 0.5 collective-permute-start.10
  105.6 0.9 collective-permute-start.8
  106.6 1.4 collective-permute-start.9
  107.9 0.0 collective-permute-done.7.swapped_ref
  107.9 3.7 %near_kv.1 = (bf16[512,1024]{1,0:T(8,128)(2,1)S(1)}, bf16[1024,512]{1,0:T(8,128)(2,1)S(1)}, bf16[1024,512]{1,0:T(8,128)(2,1)S(1)}, bf16[512,1024]{1,0:T(8,128)(2,1)S(1)}) custom-call(bf16[256,1024]{1,0:T(8,128)(2,1)} %bitcast.3.near_ref, bf16[256,1024]{1,0:T(8,128)(2,1)S(1)} %collective-permute-done.7.swapped_ref, bf16[1024,512]{1,0:T(8,128)(2,1)} %k_ref.1, ...), custom_call_target="tpu_custom_call" | custom-call | flops 536870912 | bytes 4194304 | tf_op jit(solution)/shard_map/near_kv/pallas_call | solution.py:478
  111.7 3.9 %near_decode.1 = (f32[1024,512]{1,0:T(8,128)S(1)}, f32[1024,512]{1,0:T(8,128)S(1)}, f32[1024,512]{1,0:T(8,128)S(1)}) custom-call(bf16[1024,512]{1,0:T(8,128)(2,1)S(1)} %convolution_convert_fusion.q_ref, bf16[512,1024]{1,0:T(8,128)(2,1)S(1)} %get-tuple-element.50.kv_ref), custom_call_target="tpu_custom_call" | custom-call | flops 1073741824 | bytes 4194304 | tf_op jit(solution)/shard_map/near_decode/pallas_call | solution.py:498
  115.6 0.0 collective-permute-done.10.refs_2_
  115.6 5.4 %collective-permute-done.8.refs_0_ = bf16[256,1024]{1,0:T(8,128)(2,1)S(1)} collective-permute-done((bf16[256,1024]{1,0:T(8,128)(2,1)}, bf16[256,1024]{1,0:T(8,128)(2,1)S(1)}, u32[]{:S(2)}, u32[]{:S(2)}) %collective-permute-start.8) | collective-permute-done | bytes 524320 | tf_op jit(solution)/shard_map/ppermute | solution.py:575
  121.0 0.0 collective-permute-done.9.refs_1_
  121.0 2.7 %collective-permute-start.11 = (bf16[256,1024]{1,0:T(8,128)(2,1)S(1)}, bf16[256,1024]{1,0:T(8,128)(2,1)S(1)}, u32[]{:S(2)}, u32[]{:S(2)}) collective-permute-start(bf16[256,1024]{1,0:T(8,128)(2,1)S(1)} %collective-permute-done.8.refs_0_), channel_id=1, source_target_pairs={{0,1},{1,0},{2,3},{3,2},{4,5},{5,4},{6,7},{7,6},{8,9},{9,8},{10,11... | collective-permute-start | bytes 1572872 | tf_op jit(solution)/shard_map/ppermute | solution.py:604
  123.7 0.0 collective-permute-start.12
  123.7 0.5 collective-permute-start.13
  124.2 1.8 %latent_kv.2.refs_3_ = bf16[768,1024]{1,0:T(8,128)(2,1)S(1)} custom-call(bf16[256,1024]{1,0:T(8,128)(2,1)S(1)} %collective-permute-done.8.refs_0_, bf16[256,1024]{1,0:T(8,128)(2,1)S(1)} %collective-permute-done.9.refs_1_, bf16[256,1024]{1,0:T(8,128)(2,1)S(1)} %collective-permute-done.10.refs_2_, bf16[1024,512]{1,0:T(8,128)(2,1)S(1)} %get-tuple-element.60.refs_3_, ...), custom_call_target="tpu_custom_call" | custom-call | flops 1610612736 | bytes 4194304 | tf_op jit(solution)/shard_map/latent_kv/pallas_call | solution.py:461
  126.0 0.0 collective-permute-done.11.refs_0_
  126.0 0.0 collective-permute-done.12.refs_1_
  126.0 0.7 collective-permute-done.13.refs_2_
  126.7 1.8 %latent_kv.3.refs_4_ = bf16[768,1024]{1,0:T(8,128)(2,1)S(1)} custom-call(bf16[256,1024]{1,0:T(8,128)(2,1)S(1)} %collective-permute-done.11.refs_0_, bf16[256,1024]{1,0:T(8,128)(2,1)S(1)} %collective-permute-done.12.refs_1_, bf16[256,1024]{1,0:T(8,128)(2,1)S(1)} %collective-permute-done.13.refs_2_, bf16[1024,512]{1,0:T(8,128)(2,1)S(1)} %get-tuple-element.60.refs_3_, ...), custom_call_target="tpu_custom_call" | custom-call | flops 1610612736 | bytes 4194304 | tf_op jit(solution)/shard_map/latent_kv/pallas_call | solution.py:461
  128.5 5.9 %decode.4 = bf16[512,1024]{1,0:T(8,128)(2,1)S(1)} custom-call(s32[1]{0:T(128)S(6)} %mul.12.base_ref, bf16[1024,512]{1,0:T(8,128)(2,1)S(1)} %convolution_convert_fusion.q_ref, f32[1024,512]{1,0:T(8,128)S(1)} %get-tuple-element.54.refs_0_, f32[1024,512]{1,0:T(8,128)S(1)} %get-tuple-element.55.refs_1_, f32[1024,512]{1,0:T(8,128)S(1)} %get-tuple-element.56.refs_2_, ...), custom_call_target="tpu_custom_call" | custom-call | flops 1610612736 | bytes 8388608 | tf_op jit(solution)/shard_map/decode/pallas_call | solution.py:524
  134.4 0.4 collective-permute-start.14
  134.9 2.9 %decode.3.refs_6_ = f32[256,1024]{1,0:T(8,128)S(1)} custom-call(s32[1]{0:T(128)S(6)} %mul.10.base_ref, bf16[1024,512]{1,0:T(8,128)(2,1)S(1)} %convolution_convert_fusion.q_ref, f32[1024,512]{1,0:T(8,128)S(1)} %get-tuple-element.54.refs_0_, f32[1024,512]{1,0:T(8,128)S(1)} %get-tuple-element.55.refs_1_, f32[1024,512]{1,0:T(8,128)S(1)} %get-tuple-element.56.refs_2_, ...), custom_call_target="tpu_custom_call" | custom-call | flops 805306368 | bytes 8388608 | tf_op jit(solution)/shard_map/decode/pallas_call | solution.py:524
  137.8 0.0 collective-permute-done.14.refs_7_
  137.8 4.1 %decode.5 = bf16[512,1024]{1,0:T(8,128)(2,1)} custom-call(s32[1]{0:T(128)S(6)} %sub.6.base_ref, bf16[1024,512]{1,0:T(8,128)(2,1)S(1)} %convolution_convert_fusion.q_ref, f32[1024,512]{1,0:T(8,128)S(1)} %get-tuple-element.54.refs_0_, f32[1024,512]{1,0:T(8,128)S(1)} %get-tuple-element.55.refs_1_, f32[1024,512]{1,0:T(8,128)S(1)} %get-tuple-element.56.refs_2_, ...), custom_call_target="tpu_custom_call" | custom-call | flops 805306368 | bytes 8388608 | tf_op jit(solution)/shard_map/decode/pallas_call | solution.py:524
Async XLA Ops:
  0.0 11.0 %copy-start = (bf16[1024,1024]{1,0:T(8,128)(2,1)S(1)}, bf16[1024,1024]{1,0:T(8,128)(2,1)}, u32[]{:S(2)}) copy-start(bf16[1024,1024]{1,0:T(8,128)(2,1)} %param.12) | copy-start | bytes 6291460
  2.5 18.6 %all-to-all-start = ((bf16[16,32,512]{2,1,0:T(8,128)(2,1)}), bf16[16,32,512]{2,1,0:T(8,128)(2,1)S(1)}, u32[]{:S(2)}, u32[]{:S(2)}) async-start(bf16[16,32,512]{2,1,0:T(8,128)(2,1)} %spread.1), calls=%async_computation | async-start | bytes 1048576 | tf_op jit(solution)/shard_map/all_to_all | solution.py:572
  11.0 3.6 %copy-start.2 = (bf16[1024,512]{1,0:T(8,128)(2,1)S(1)}, bf16[1024,512]{1,0:T(8,128)(2,1)}, u32[]{:S(2)}) copy-start(bf16[1024,512]{1,0:T(8,128)(2,1)} %param.16) | copy-start | bytes 3145732
  16.8 10.9 %copy-start.1 = (s32[8]{0:T(128)S(1)}, s32[8]{0:T(128)}, u32[]{:S(2)}) copy-start(s32[8]{0:T(128)} %valid_ref.9) | copy-start | bytes 100
  21.2 9.6 %collective-permute-start = (bf16[512,512]{1,0:T(8,128)(2,1)S(1)}, bf16[512,512]{1,0:T(8,128)(2,1)S(1)}, u32[]{:S(2)}, u32[]{:S(2)}) collective-permute-start(bf16[512,512]{1,0:T(8,128)(2,1)S(1)} %bitcast.10), channel_id=1, source_target_pairs={{0,32},{1,9},{2,34},{3,11},{4,36},{5,13},{6,38},{7,15},{8,40},{9,1... | collective-permute-start | bytes 1572872 | tf_op jit(solution)/shard_map/ppermute | solution.py:575
  22.3 15.3 %collective-permute-start.2 = (bf16[512,512]{1,0:T(8,128)(2,1)S(1)}, bf16[512,512]{1,0:T(8,128)(2,1)S(1)}, u32[]{:S(2)}, u32[]{:S(2)}) collective-permute-start(bf16[512,512]{1,0:T(8,128)(2,1)S(1)} %bitcast.11), channel_id=1, source_target_pairs={{0,64},{1,17},{2,66},{3,19},{4,68},{5,21},{6,70},{7,23},{8,72},{9,... | collective-permute-start | bytes 1572872 | tf_op jit(solution)/shard_map/ppermute | solution.py:575
  25.1 16.4 %collective-permute-start.4 = (bf16[512,512]{1,0:T(8,128)(2,1)S(1)}, bf16[512,512]{1,0:T(8,128)(2,1)S(1)}, u32[]{:S(2)}, u32[]{:S(2)}) collective-permute-start(bf16[512,512]{1,0:T(8,128)(2,1)S(1)} %bitcast.12), channel_id=1, source_target_pairs={{0,96},{1,25},{2,98},{3,27},{4,100},{5,29},{6,102},{7,31},{8,104},... | collective-permute-start | bytes 1572872 | tf_op jit(solution)/shard_map/ppermute | solution.py:575
  45.5 10.3 %collective-permute-start.5 = (bf16[16,144,128]{2,1,0:T(8,128)(2,1)S(1)}, bf16[16,144,128]{2,1,0:T(8,128)(2,1)S(1)}, u32[]{:S(2)}, u32[]{:S(2)}) collective-permute-start(bf16[16,144,128]{2,1,0:T(8,128)(2,1)S(1)} %cross.8), channel_id=1, source_target_pairs={{0,32},{1,9},{2,34},{3,11},{4,36},{5,13},{6,38},{7,15},{8,40},{9,1... | collective-permute-start | bytes 1769480 | tf_op jit(solution)/shard_map/ppermute | solution.py:575
  45.5 17.9 %collective-permute-start.3 = (bf16[16,144,128]{2,1,0:T(8,128)(2,1)S(1)}, bf16[16,144,128]{2,1,0:T(8,128)(2,1)S(1)}, u32[]{:S(2)}, u32[]{:S(2)}) collective-permute-start(bf16[16,144,128]{2,1,0:T(8,128)(2,1)S(1)} %cross.7), channel_id=1, source_target_pairs={{0,64},{1,17},{2,66},{3,19},{4,68},{5,21},{6,70},{7,23},{8,72},{9,... | collective-permute-start | bytes 1769480 | tf_op jit(solution)/shard_map/ppermute | solution.py:575
  49.9 13.5 %collective-permute-start.1 = (bf16[16,144,128]{2,1,0:T(8,128)(2,1)S(1)}, bf16[16,144,128]{2,1,0:T(8,128)(2,1)S(1)}, u32[]{:S(2)}, u32[]{:S(2)}) collective-permute-start(bf16[16,144,128]{2,1,0:T(8,128)(2,1)S(1)} %cross.6), channel_id=1, source_target_pairs={{0,96},{1,25},{2,98},{3,27},{4,100},{5,29},{6,102},{7,31},{8,104},... | collective-permute-start | bytes 1769480 | tf_op jit(solution)/shard_map/ppermute | solution.py:575
  65.9 12.9 %all-to-all-start.1 = ((bf16[16,144,128]{2,1,0:T(8,128)(2,1)}), bf16[16,144,128]{2,1,0:T(8,128)(2,1)S(1)}, u32[]{:S(2)}, u32[]{:S(2)}) async-start(bf16[16,144,128]{2,1,0:T(8,128)(2,1)} %join.1), calls=%async_computation.1 | async-start | bytes 1179648 | tf_op jit(solution)/shard_map/all_to_all | solution.py:572
  81.5 5.6 %collective-permute-start.6 = (bf16[16,1024]{1,0:T(8,128)(2,1)S(1)}, bf16[16,1024]{1,0:T(8,128)(2,1)S(1)}, u32[]{:S(2)}, u32[]{:S(2)}) collective-permute-start(bf16[16,1024]{1,0:T(8,128)(2,1)S(1)} %get-tuple-element.44), channel_id=1, source_target_pairs={{0,1},{1,0},{2,3},{3,2},{4,5},{5,4},{6,7},{7,6},{8,9},{9,8},{10,11... | collective-permute-start | bytes 98312 | tf_op jit(solution)/shard_map/ppermute | solution.py:594
  88.4 16.7 %all-to-all-start.2 = ((bf16[16,16,1024]{2,1,0:T(8,128)(2,1)}), bf16[16,16,1024]{2,1,0:T(8,128)(2,1)}, u32[]{:S(2)}, u32[]{:S(2)}) async-start(bf16[16,16,1024]{2,1,0:T(8,128)(2,1)} %latent.1), calls=%async_computation.2 | async-start | bytes 1048576 | tf_op jit(solution)/shard_map/all_to_all | solution.py:572
  105.1 2.8 %collective-permute-start.7 = (bf16[256,1024]{1,0:T(8,128)(2,1)}, bf16[256,1024]{1,0:T(8,128)(2,1)S(1)}, u32[]{:S(2)}, u32[]{:S(2)}) collective-permute-start(bf16[256,1024]{1,0:T(8,128)(2,1)} %bitcast.3.near_ref), channel_id=1, source_target_pairs={{0,1},{1,0},{2,3},{3,2},{4,5},{5,4},{6,7},{7,6},{8,9},{9,8},{10,11... | collective-permute-start | bytes 1572872 | tf_op jit(solution)/shard_map/ppermute | solution.py:601
  105.1 10.5 %collective-permute-start.10 = (bf16[256,1024]{1,0:T(8,128)(2,1)}, bf16[256,1024]{1,0:T(8,128)(2,1)S(1)}, u32[]{:S(2)}, u32[]{:S(2)}) collective-permute-start(bf16[256,1024]{1,0:T(8,128)(2,1)} %bitcast.3.near_ref), channel_id=1, source_target_pairs={{0,96},{1,25},{2,98},{3,27},{4,100},{5,29},{6,102},{7,31},{8,104},... | collective-permute-start | bytes 1572872 | tf_op jit(solution)/shard_map/ppermute | solution.py:575
  105.6 15.4 %collective-permute-start.8 = (bf16[256,1024]{1,0:T(8,128)(2,1)}, bf16[256,1024]{1,0:T(8,128)(2,1)S(1)}, u32[]{:S(2)}, u32[]{:S(2)}) collective-permute-start(bf16[256,1024]{1,0:T(8,128)(2,1)} %bitcast.3.near_ref), channel_id=1, source_target_pairs={{0,32},{1,9},{2,34},{3,11},{4,36},{5,13},{6,38},{7,15},{8,40},{9,1... | collective-permute-start | bytes 1572872 | tf_op jit(solution)/shard_map/ppermute | solution.py:575
  106.6 14.4 %collective-permute-start.9 = (bf16[256,1024]{1,0:T(8,128)(2,1)}, bf16[256,1024]{1,0:T(8,128)(2,1)S(1)}, u32[]{:S(2)}, u32[]{:S(2)}) collective-permute-start(bf16[256,1024]{1,0:T(8,128)(2,1)} %bitcast.3.near_ref), channel_id=1, source_target_pairs={{0,64},{1,17},{2,66},{3,19},{4,68},{5,21},{6,70},{7,23},{8,72},{9,... | collective-permute-start | bytes 1572872 | tf_op jit(solution)/shard_map/ppermute | solution.py:575
  121.0 5.0 %collective-permute-start.11 = (bf16[256,1024]{1,0:T(8,128)(2,1)S(1)}, bf16[256,1024]{1,0:T(8,128)(2,1)S(1)}, u32[]{:S(2)}, u32[]{:S(2)}) collective-permute-start(bf16[256,1024]{1,0:T(8,128)(2,1)S(1)} %collective-permute-done.8.refs_0_), channel_id=1, source_target_pairs={{0,1},{1,0},{2,3},{3,2},{4,5},{5,4},{6,7},{7,6},{8,9},{9,8},{10,11... | collective-permute-start | bytes 1572872 | tf_op jit(solution)/shard_map/ppermute | solution.py:604
  123.7 2.3 %collective-permute-start.12 = (bf16[256,1024]{1,0:T(8,128)(2,1)S(1)}, bf16[256,1024]{1,0:T(8,128)(2,1)S(1)}, u32[]{:S(2)}, u32[]{:S(2)}) collective-permute-start(bf16[256,1024]{1,0:T(8,128)(2,1)S(1)} %collective-permute-done.9.refs_1_), channel_id=1, source_target_pairs={{0,1},{1,0},{2,3},{3,2},{4,5},{5,4},{6,7},{7,6},{8,9},{9,8},{10,11... | collective-permute-start | bytes 1572872 | tf_op jit(solution)/shard_map/ppermute | solution.py:604
  123.7 3.0 %collective-permute-start.13 = (bf16[256,1024]{1,0:T(8,128)(2,1)S(1)}, bf16[256,1024]{1,0:T(8,128)(2,1)S(1)}, u32[]{:S(2)}, u32[]{:S(2)}) collective-permute-start(bf16[256,1024]{1,0:T(8,128)(2,1)S(1)} %collective-permute-done.10.refs_2_), channel_id=1, source_target_pairs={{0,1},{1,0},{2,3},{3,2},{4,5},{5,4},{6,7},{7,6},{8,9},{9,8},{10,11... | collective-permute-start | bytes 1572872 | tf_op jit(solution)/shard_map/ppermute | solution.py:604
  134.4 3.4 %collective-permute-start.14 = (bf16[512,1024]{1,0:T(8,128)(2,1)S(1)}, bf16[512,1024]{1,0:T(8,128)(2,1)S(1)}, u32[]{:S(2)}, u32[]{:S(2)}) collective-permute-start(bf16[512,1024]{1,0:T(8,128)(2,1)S(1)} %decode.4), channel_id=1, source_target_pairs={{0,1},{1,0},{2,3},{3,2},{4,5},{5,4},{6,7},{7,6},{8,9},{9,8},{10,11... | collective-permute-start | bytes 3145736 | tf_op jit(solution)/shard_map/ppermute | solution.py:608

commit v5 on v4

--- a/solution.py
+++ b/solution.py
@@ -23,6 +23,7 @@
 AXES = ("pos", "head")
 SIDE = 4
 ORDER = (1, 2, 3)
+FAR_ORDER = (2, 1, 3)
 
 
 def plane_groups():
@@ -322,15 +323,15 @@
 
 
 def decode_kernel(base_ref, q_ref, *refs):
-    *carried, kv_a, kv_b, w_ref, out_ref, s_ref, o_ref = refs
-    out_ref[...] = attend(q_ref, carried, (kv_a, kv_b), w_ref, s_ref, o_ref).astype(out_ref.dtype)
+    carried, (*kv_refs, w_ref, out_ref, s_ref, o_ref) = refs[:3], refs[3:]
+    out_ref[...] = attend(q_ref, carried, kv_refs, w_ref, s_ref, o_ref).astype(out_ref.dtype)
 
 
 def last_kernel(base_ref, q_ref, *refs):
-    *carried, kv_a, kv_b, w_ref, first_ref, recv_ref, out_ref, s_ref, o_ref = refs
+    carried, (*kv_refs, w_ref, first_ref, recv_ref, out_ref, s_ref, o_ref) = refs[:3], refs[3:]
     n = first_ref.shape[0]
     out_ref[:n] = rms_norm(first_ref[...] + recv_ref[:n].astype(F32)).astype(out_ref.dtype)
-    terms = attend(q_ref, carried, (kv_a, kv_b), w_ref, s_ref, o_ref)
+    terms = attend(q_ref, carried, kv_refs, w_ref, s_ref, o_ref)
     out_ref[n:] = rms_norm(terms + recv_ref[n:].astype(F32)).astype(out_ref.dtype)
 
 
@@ -588,7 +589,10 @@
         part = cross(valid_blocks, there, keys, values, lat_local, 0, heads)
         partials.append(along(part, -s))
     part, half = lax.optimization_barrier((part, half))
-    partials.append(cross(valid_blocks, queries, keys, values, lat_local, heads // 2, heads // 2, half))
+    stay = cross(valid_blocks, queries, keys, values, lat_local, heads // 2, heads // 2, half)
+    *early, late = partials
+    stay, late = lax.optimization_barrier((join([stay, *early], lat_local), late))
+    partials = [stay, late]
     gathered = within_plane(join(partials, lat_local))
     own, other, w_mlp = combine(jnp.concatenate([core, lane_offset(lat_local)]), gathered, w_out, w_mlp, lat_local)
     recv = lax.ppermute(other, "head", swap)
@@ -597,12 +601,21 @@
     pos_queries = project(inputs, w_pquery)
     near, pos_queries = lax.optimization_barrier((within_plane(rows), pos_queries))
     near = near.reshape(-1, width)
-    far = [along(near, s) for s in ORDER]
-    kv, w_lkey, w_lvalue, w_pout = near_kv(near, lax.ppermute(near, "head", swap), w_lkey, w_lvalue, w_pout)
+    far = []
+    for s in FAR_ORDER:
+        far.append(along(near, s))
+    near_swapped = lax.ppermute(near, "head", swap)
+    kv, w_lkey, w_lvalue, w_pout = near_kv(near, near_swapped, w_lkey, w_lvalue, w_pout)
     carried = near_decode(pos_queries, kv)
-    carried, far = lax.optimization_barrier((carried, far))
-    far_swapped = [lax.ppermute(x, "head", swap) for x in far]
-    kvs = [latent_kv(far, w_lkey, w_lvalue), latent_kv(far_swapped, w_lkey, w_lvalue)]
+    slow, *quick = far
+    carried, quick = lax.optimization_barrier((carried, quick))
+    quick_swapped = [lax.ppermute(x, "head", swap) for x in quick]
+    quick_kv = latent_kv(quick, w_lkey, w_lvalue)
+    slow, quick_kv = lax.optimization_barrier((slow, quick_kv))
+    slow_swapped = lax.ppermute(slow, "head", swap)
+    swapped_kv = latent_kv(quick_swapped, w_lkey, w_lvalue)
+    slow_kv = latent_kv([slow, slow_swapped], w_lkey, w_lvalue)
+    kvs = [quick_kv, swapped_kv, slow_kv]
     blocks = pos_queries.shape[0] // 2 // ROW_BLOCK
     terms = decode((1 - core) * blocks, blocks, pos_queries, carried, kvs, w_pout, BF16)
     arrived = lax.ppermute(terms, "head", swap)

time: 142 us -> 135 us (0.951)
  waiting for transfers between devices: 41.7 us -> 36.7 us
  starting transfers between devices: 40.1 us -> 37 us
    ppermute x9, waiting for transfers between devices: 17.8 us -> 11.3 us  [along(): return lax.ppermute(x, AXES, long[shift % SIDE])]
    ppermute x1, starting transfers between devices: 4.74 us -> 2.87 us  [per_device(): recv = lax.ppermute(other, 'head', swap)]
    pallas_call x1 -> x2, Pallas kernels: 2.49 us -> 3.01 us  [join(): pl.pallas_call(functools.partial(join_kernel, lat_local=lat_local), out_s...]
    pallas_call x2 -> x3, Pallas kernels: 3.57 us -> 3.73 us  [latent_kv(): pl.pallas_call(kv_kernel, out_shape=jax.ShapeDtypeStruct((total, wide), B...]
  transfers between devices with their start and end apart: 18 -> 18, of which waited for: 10 -> 10; matrix products, arithmetic and copies ran while one was open for 6% -> 6% of each run, Pallas kernels for 19% -> 24%
where the time goes in v5:
time: 135 us
  Pallas kernels  52.3 us (39%)
  starting transfers between devices  37 us (27%)
  waiting for transfers between devices  36.7 us (27%)
  matrix products  8.27 us (6%)
    all_to_all x3, waiting for transfers between devices, within_plane(): return lax.all_to_all(x, AXES, 0, 0, axis_index_groups=plane)  23.3 us
    pallas_call x5, Pallas kernels, cross(): pl.pallas_call(functools.partial(cross_kernel, lat_local=lat_local, first...  16.9 us
    all_to_all x3, starting transfers between devices, within_plane(): return lax.all_to_all(x, AXES, 0, 0, axis_index_groups=plane)  16.2 us
    ppermute x9, starting transfers between devices, along(): return lax.ppermute(x, AXES, long[shift % SIDE])  15.1 us
    pallas_call x3, Pallas kernels, decode(): pl.pallas_call(last_kernel if finish else decode_kernel, out_shape=jax.Sh...  12.9 us
    ppermute x9, waiting for transfers between devices, along(): return lax.ppermute(x, AXES, long[shift % SIDE])  11.3 us
    dot_general x3, matrix products, project(): return jnp.dot(a, w, preferred_element_type=F32).astype(BF16)  8.27 us
    pallas_call x1, Pallas kernels, near_decode(): pl.pallas_call(near_kernel, out_shape=(jax.ShapeDtypeStruct((rows, column...  3.87 us
  transfers between devices with their start and end apart: 18, of which 10 were waited for; matrix products, arithmetic and copies ran while one was open for 6% of the time, Pallas kernels for 24%

profile of v5, /device:TPU:1, one launch (start us, length us, event | category | flops | bytes accessed | tf_op | source)
XLA Modules:
  0.0 134.6 jit_solution(17486789777152525691)
XLA Ops:
  0.0 0.0 copy-start
  0.0 2.5 %spread.1 = bf16[16,32,512]{2,1,0:T(8,128)(2,1)} custom-call(bf16[32,1024]{1,0:T(8,128)(2,1)} %l_ref.1, bf16[1024,512]{1,0:T(8,128)(2,1)} %w_ref.2), custom_call_target="tpu_custom_call" | custom-call | tf_op jit(solution)/shard_map/spread/pallas_call | solution.py:431
  2.5 8.4 %all-to-all-start = ((bf16[16,32,512]{2,1,0:T(8,128)(2,1)}), bf16[16,32,512]{2,1,0:T(8,128)(2,1)S(1)}, u32[]{:S(2)}, u32[]{:S(2)}) async-start(bf16[16,32,512]{2,1,0:T(8,128)(2,1)} %spread.1), calls=%async_computation | async-start | bytes 1048576 | tf_op jit(solution)/shard_map/all_to_all | solution.py:573
  11.0 0.0 copy-done
  11.0 0.0 copy-start.2
  11.0 3.6 %convolution_convert_fusion.1.refs_1_ = bf16[1024,512]{1,0:T(8,128)(2,1)} fusion(bf16[1024,1024]{1,0:T(8,128)(2,1)S(1)} %copy-done, bf16[1024,512]{1,0:T(8,128)(2,1)} %param.17), kind=kOutput, calls=%fused_computation.1 | convolution fusion | flops 1074266112 | bytes 4194304 | tf_op jit(solution)/shard_map/dot_general | solution.py:547
  14.6 0.0 copy-done.2
  14.6 2.2 %convolution_convert_fusion.2.refs_0_ = bf16[1024,512]{1,0:T(8,128)(2,1)} fusion(bf16[1024,1024]{1,0:T(8,128)(2,1)S(1)} %copy-done, bf16[1024,512]{1,0:T(8,128)(2,1)S(1)} %copy-done.2), kind=kOutput, calls=%fused_computation.2 | convolution fusion | flops 1074266112 | bytes 4194304 | tf_op jit(solution)/shard_map/dot_general | solution.py:547
  16.8 4.4 %all-to-all-done = bf16[16,32,512]{2,1,0:T(8,128)(2,1)S(1)} async-done(((bf16[16,32,512]{2,1,0:T(8,128)(2,1)}), bf16[16,32,512]{2,1,0:T(8,128)(2,1)S(1)}, u32[]{:S(2)}, u32[]{:S(2)}) %all-to-all-start) | async-done | bytes 524320 | tf_op jit(solution)/shard_map/all_to_all | solution.py:573
  21.2 1.1 collective-permute-start
  22.3 2.8 %collective-permute-start.1 = (bf16[512,512]{1,0:T(8,128)(2,1)S(1)}, bf16[512,512]{1,0:T(8,128)(2,1)S(1)}, u32[]{:S(2)}, u32[]{:S(2)}) collective-permute-start(bf16[512,512]{1,0:T(8,128)(2,1)S(1)} %bitcast.11), channel_id=1, source_target_pairs={{0,64},{1,17},{2,66},{3,19},{4,68},{5,21},{6,70},{7,23},{8,72},{9,... | collective-permute-start | bytes 1572872 | tf_op jit(solution)/shard_map/ppermute | solution.py:576
  25.1 1.0 collective-permute-start.2
  26.1 1.6 %load.1 = (bf16[1024,512]{1,0:T(8,128)(2,1)S(1)}, bf16[1024,512]{1,0:T(8,128)(2,1)S(1)}) custom-call(bf16[1024,512]{1,0:T(8,128)(2,1)} %convolution_convert_fusion.2.refs_0_, bf16[1024,512]{1,0:T(8,128)(2,1)} %convolution_convert_fusion.1.refs_1_), custom_call_target="tpu_custom_call" | custom-call | tf_op jit(solution)/shard_map/load/pallas_call | solution.py:381
  27.7 0.0 copy-done.1
  27.7 2.6 %cross.5.refs_0_ = bf16[16,80,128]{2,1,0:T(8,128)(2,1)S(1)} custom-call(s32[8]{0:T(128)S(1)} %copy-done.1, bf16[512,512]{1,0:T(8,128)(2,1)S(1)} %bitcast.13, bf16[1024,512]{1,0:T(8,128)(2,1)S(1)} %get-tuple-element.40.k_ref, bf16[1024,512]{1,0:T(8,128)(2,1)S(1)} %get-tuple-element.41.v_ref), custom_call_target="tpu_custom_call" | custom-call | flops 536870912 | bytes 4194304 | tf_op jit(solution)/shard_map/cross/pallas_call | solution.py:351
  30.2 0.6 collective-permute-done.q_ref
  30.8 3.9 %cross.6 = bf16[16,144,128]{2,1,0:T(8,128)(2,1)S(1)} custom-call(s32[8]{0:T(128)S(1)} %copy-done.1, bf16[512,512]{1,0:T(8,128)(2,1)S(1)} %collective-permute-done.q_ref, bf16[1024,512]{1,0:T(8,128)(2,1)S(1)} %get-tuple-element.40.k_ref, bf16[1024,512]{1,0:T(8,128)(2,1)S(1)} %get-tuple-element.41.v_ref), custom_call_target="tpu_custom_call" | custom-call | flops 1073741824 | bytes 4194304 | tf_op jit(solution)/shard_map/cross/pallas_call | solution.py:351
  34.7 1.5 %collective-permute-start.3 = (bf16[16,144,128]{2,1,0:T(8,128)(2,1)S(1)}, bf16[16,144,128]{2,1,0:T(8,128)(2,1)S(1)}, u32[]{:S(2)}, u32[]{:S(2)}) collective-permute-start(bf16[16,144,128]{2,1,0:T(8,128)(2,1)S(1)} %cross.6), channel_id=1, source_target_pairs={{0,96},{1,25},{2,98},{3,27},{4,100},{5,29},{6,102},{7,31},{8,104},... | collective-permute-start | bytes 1769480 | tf_op jit(solution)/shard_map/ppermute | solution.py:576
  36.3 1.4 %collective-permute-done.1.q_ref = bf16[512,512]{1,0:T(8,128)(2,1)S(1)} collective-permute-done((bf16[512,512]{1,0:T(8,128)(2,1)S(1)}, bf16[512,512]{1,0:T(8,128)(2,1)S(1)}, u32[]{:S(2)}, u32[]{:S(2)}) %collective-permute-start.1) | collective-permute-done | bytes 524320 | tf_op jit(solution)/shard_map/ppermute | solution.py:576
  37.6 3.9 %cross.7 = bf16[16,144,128]{2,1,0:T(8,128)(2,1)S(1)} custom-call(s32[8]{0:T(128)S(1)} %copy-done.1, bf16[512,512]{1,0:T(8,128)(2,1)S(1)} %collective-permute-done.1.q_ref, bf16[1024,512]{1,0:T(8,128)(2,1)S(1)} %get-tuple-element.40.k_ref, bf16[1024,512]{1,0:T(8,128)(2,1)S(1)} %get-tuple-element.41.v_ref), custom_call_target="tpu_custom_call" | custom-call | flops 1073741824 | bytes 4194304 | tf_op jit(solution)/shard_map/cross/pallas_call | solution.py:351
  41.5 4.4 %collective-permute-start.4 = (bf16[16,144,128]{2,1,0:T(8,128)(2,1)S(1)}, bf16[16,144,128]{2,1,0:T(8,128)(2,1)S(1)}, u32[]{:S(2)}, u32[]{:S(2)}) collective-permute-start(bf16[16,144,128]{2,1,0:T(8,128)(2,1)S(1)} %cross.7), channel_id=1, source_target_pairs={{0,64},{1,17},{2,66},{3,19},{4,68},{5,21},{6,70},{7,23},{8,72},{9,... | collective-permute-start | bytes 1769480 | tf_op jit(solution)/shard_map/ppermute | solution.py:576
  45.9 0.0 collective-permute-done.2.q_ref
  45.9 3.9 %cross.8 = bf16[16,144,128]{2,1,0:T(8,128)(2,1)S(1)} custom-call(s32[8]{0:T(128)S(1)} %copy-done.1, bf16[512,512]{1,0:T(8,128)(2,1)S(1)} %collective-permute-done.2.q_ref, bf16[1024,512]{1,0:T(8,128)(2,1)S(1)} %get-tuple-element.40.k_ref, bf16[1024,512]{1,0:T(8,128)(2,1)S(1)} %get-tuple-element.41.v_ref), custom_call_target="tpu_custom_call" | custom-call | flops 1073741824 | bytes 4194304 | tf_op jit(solution)/shard_map/cross/pallas_call | solution.py:351
  49.9 1.1 collective-permute-start.5
  50.9 2.6 %cross.9.refs_0_ = bf16[16,144,128]{2,1,0:T(8,128)(2,1)S(1)} custom-call(s32[8]{0:T(128)S(1)} %copy-done.1, bf16[512,512]{1,0:T(8,128)(2,1)S(1)} %bitcast.14, bf16[1024,512]{1,0:T(8,128)(2,1)S(1)} %get-tuple-element.40.k_ref, bf16[1024,512]{1,0:T(8,128)(2,1)S(1)} %get-tuple-element.41.v_ref, bf16[16,80,128]{2,1,0:T(8,128)(2,1)S(1)} %cross.5.refs_0_), custom_call_target="tpu_custom_call" | custom-call | flops 536870912 | bytes 4194304 | tf_op jit(solution)/shard_map/cross/pallas_call | solution.py:351
  53.5 0.0 collective-permute-done.4.refs_2_
  53.5 0.0 collective-permute-done.3.refs_1_
  53.5 1.3 join.2.refs_0_
  54.8 5.5 %collective-permute-done.5.refs_1_ = bf16[16,144,128]{2,1,0:T(8,128)(2,1)S(1)} collective-permute-done((bf16[16,144,128]{2,1,0:T(8,128)(2,1)S(1)}, bf16[16,144,128]{2,1,0:T(8,128)(2,1)S(1)}, u32[]{:S(2)}, u32[]{:S(2)}) %collective-permute-start.5) | collective-permute-done | bytes 589856 | tf_op jit(solution)/shard_map/ppermute | solution.py:576
  60.3 1.7 %join.3 = bf16[16,144,128]{2,1,0:T(8,128)(2,1)} custom-call(bf16[16,144,128]{2,1,0:T(8,128)(2,1)S(1)} %join.2.refs_0_, bf16[16,144,128]{2,1,0:T(8,128)(2,1)S(1)} %collective-permute-done.5.refs_1_), custom_call_target="tpu_custom_call" | custom-call | tf_op jit(solution)/shard_map/join/pallas_call | solution.py:394
  62.1 3.6 %all-to-all-start.1 = ((bf16[16,144,128]{2,1,0:T(8,128)(2,1)}), bf16[16,144,128]{2,1,0:T(8,128)(2,1)S(1)}, u32[]{:S(2)}, u32[]{:S(2)}) async-start(bf16[16,144,128]{2,1,0:T(8,128)(2,1)} %join.3), calls=%async_computation.1 | async-start | bytes 1179648 | tf_op jit(solution)/shard_map/all_to_all | solution.py:573
  65.7 0.1 pad_add_fusion.core_ref
  65.8 11.3 %all-to-all-done.1.r_ref = bf16[16,144,128]{2,1,0:T(8,128)(2,1)S(1)} async-done(((bf16[16,144,128]{2,1,0:T(8,128)(2,1)}), bf16[16,144,128]{2,1,0:T(8,128)(2,1)S(1)}, u32[]{:S(2)}, u32[]{:S(2)}) %all-to-all-start.1) | async-done | bytes 589856 | tf_op jit(solution)/shard_map/all_to_all | solution.py:573
  77.1 2.7 %combine.1 = (f32[16,1024]{1,0:T(8,128)S(1)}, bf16[16,1024]{1,0:T(8,128)(2,1)S(1)}, bf16[1024,1024]{1,0:T(8,128)(2,1)S(1)}) custom-call(s32[2]{0:T(128)S(1)} %pad_add_fusion.core_ref, bf16[16,144,128]{2,1,0:T(8,128)(2,1)S(1)} %all-to-all-done.1.r_ref, bf16[512,1024]{1,0:T(8,128)(2,1)} %w_ref.3, bf16[1024,1024]{1,0:T(8,128)(2,1)} %mlp_ref.1), custom_call_target="tpu_custom_call" | custom-call | tf_op jit(solution)/shard_map/combine/pallas_call | solution.py:409
  79.8 2.9 %collective-permute-start.6 = (bf16[16,1024]{1,0:T(8,128)(2,1)S(1)}, bf16[16,1024]{1,0:T(8,128)(2,1)S(1)}, u32[]{:S(2)}, u32[]{:S(2)}) collective-permute-start(bf16[16,1024]{1,0:T(8,128)(2,1)S(1)} %get-tuple-element.49), channel_id=1, source_target_pairs={{0,1},{1,0},{2,3},{3,2},{4,5},{5,4},{6,7},{7,6},{8,9},{9,8},{10,11... | collective-permute-start | bytes 98312 | tf_op jit(solution)/shard_map/ppermute | solution.py:598
  82.6 0.9 collective-permute-done.6.recv_ref
  83.5 1.3 latent.1
  84.8 4.2 %all-to-all-start.2 = ((bf16[16,16,1024]{2,1,0:T(8,128)(2,1)}), bf16[16,16,1024]{2,1,0:T(8,128)(2,1)}, u32[]{:S(2)}, u32[]{:S(2)}) async-start(bf16[16,16,1024]{2,1,0:T(8,128)(2,1)} %latent.1), calls=%async_computation.2 | async-start | bytes 1048576 | tf_op jit(solution)/shard_map/all_to_all | solution.py:573
  89.0 2.5 %convolution_convert_fusion.q_ref = bf16[1024,512]{1,0:T(8,128)(2,1)S(1)} fusion(bf16[1024,1024]{1,0:T(8,128)(2,1)S(1)} %copy-done, bf16[1024,512]{1,0:T(8,128)(2,1)} %param.22), kind=kOutput, calls=%fused_computation | convolution fusion | flops 1074266112 | bytes 4194304 | tf_op jit(solution)/shard_map/dot_general | solution.py:547
  91.5 7.6 %all-to-all-done.2 = bf16[16,16,1024]{2,1,0:T(8,128)(2,1)} async-done(((bf16[16,16,1024]{2,1,0:T(8,128)(2,1)}), bf16[16,16,1024]{2,1,0:T(8,128)(2,1)}, u32[]{:S(2)}, u32[]{:S(2)}) %all-to-all-start.2) | async-done | bytes 524320 | tf_op jit(solution)/shard_map/all_to_all | solution.py:573
  99.1 0.6 collective-permute-start.7
  99.7 0.8 collective-permute-start.8
  100.5 1.8 %collective-permute-start.9 = (bf16[256,1024]{1,0:T(8,128)(2,1)}, bf16[256,1024]{1,0:T(8,128)(2,1)S(1)}, u32[]{:S(2)}, u32[]{:S(2)}) collective-permute-start(bf16[256,1024]{1,0:T(8,128)(2,1)} %bitcast.3.near_ref), channel_id=1, source_target_pairs={{0,96},{1,25},{2,98},{3,27},{4,100},{5,29},{6,102},{7,31},{8,104},... | collective-permute-start | bytes 1572872 | tf_op jit(solution)/shard_map/ppermute | solution.py:576
  102.4 0.6 collective-permute-start.10
  102.9 0.0 collective-permute-done.7.swapped_ref
  102.9 3.7 %near_kv.1 = (bf16[512,1024]{1,0:T(8,128)(2,1)S(1)}, bf16[1024,512]{1,0:T(8,128)(2,1)S(1)}, bf16[1024,512]{1,0:T(8,128)(2,1)S(1)}, bf16[512,1024]{1,0:T(8,128)(2,1)S(1)}) custom-call(bf16[256,1024]{1,0:T(8,128)(2,1)} %bitcast.3.near_ref, bf16[256,1024]{1,0:T(8,128)(2,1)S(1)} %collective-permute-done.7.swapped_ref, bf16[1024,512]{1,0:T(8,128)(2,1)} %k_ref.1, ...), custom_call_target="tpu_custom_call" | custom-call | flops 536870912 | bytes 4194304 | tf_op jit(solution)/shard_map/near_kv/pallas_call | solution.py:479
  106.7 3.9 %near_decode.1 = (f32[1024,512]{1,0:T(8,128)S(1)}, f32[1024,512]{1,0:T(8,128)S(1)}, f32[1024,512]{1,0:T(8,128)S(1)}) custom-call(bf16[1024,512]{1,0:T(8,128)(2,1)S(1)} %convolution_convert_fusion.q_ref, bf16[512,1024]{1,0:T(8,128)(2,1)S(1)} %get-tuple-element.55.kv_ref), custom_call_target="tpu_custom_call" | custom-call | flops 1073741824 | bytes 4194304 | tf_op jit(solution)/shard_map/near_decode/pallas_call | solution.py:499
  110.6 0.0 collective-permute-done.8.refs_0_
  110.6 3.9 %collective-permute-done.9.refs_1_ = bf16[256,1024]{1,0:T(8,128)(2,1)S(1)} collective-permute-done((bf16[256,1024]{1,0:T(8,128)(2,1)}, bf16[256,1024]{1,0:T(8,128)(2,1)S(1)}, u32[]{:S(2)}, u32[]{:S(2)}) %collective-permute-start.9) | collective-permute-done | bytes 524320 | tf_op jit(solution)/shard_map/ppermute | solution.py:576
  114.4 1.2 latent_kv.3.refs_3_
  115.7 0.0 collective-permute-done.10.refs_0_
  115.7 1.2 collective-permute-start.13
  116.9 0.1 collective-permute-start.11
  117.0 0.4 collective-permute-start.12
  117.4 1.0 collective-permute-done.13.refs_1_
  118.5 1.2 latent_kv.5.refs_5_
  119.7 0.0 collective-permute-done.11.refs_0_
  119.7 0.2 collective-permute-done.12.refs_1_
  120.0 1.2 latent_kv.4.refs_4_
  121.2 5.9 %decode.4 = bf16[512,1024]{1,0:T(8,128)(2,1)S(1)} custom-call(s32[1]{0:T(128)S(6)} %mul.12.base_ref, bf16[1024,512]{1,0:T(8,128)(2,1)S(1)} %convolution_convert_fusion.q_ref, f32[1024,512]{1,0:T(8,128)S(1)} %get-tuple-element.59.refs_0_, f32[1024,512]{1,0:T(8,128)S(1)} %get-tuple-element.60.refs_1_, f32[1024,512]{1,0:T(8,128)S(1)} %get-tuple-element.61.refs_2_, ...), custom_call_target="tpu_custom_call" | custom-call | flops 1610612736 | bytes 8388608 | tf_op jit(solution)/shard_map/decode/pallas_call | solution.py:525
  127.1 0.5 collective-permute-start.14
  127.6 2.9 %decode.3.refs_7_ = f32[256,1024]{1,0:T(8,128)S(1)} custom-call(s32[1]{0:T(128)S(6)} %mul.10.base_ref, bf16[1024,512]{1,0:T(8,128)(2,1)S(1)} %convolution_convert_fusion.q_ref, f32[1024,512]{1,0:T(8,128)S(1)} %get-tuple-element.59.refs_0_, f32[1024,512]{1,0:T(8,128)S(1)} %get-tuple-element.60.refs_1_, f32[1024,512]{1,0:T(8,128)S(1)} %get-tuple-element.61.refs_2_, ...), custom_call_target="tpu_custom_call" | custom-call | flops 805306368 | bytes 8388608 | tf_op jit(solution)/shard_map/decode/pallas_call | solution.py:525
  130.5 0.0 collective-permute-done.14.refs_8_
  130.5 4.1 %decode.5 = bf16[512,1024]{1,0:T(8,128)(2,1)} custom-call(s32[1]{0:T(128)S(6)} %sub.6.base_ref, bf16[1024,512]{1,0:T(8,128)(2,1)S(1)} %convolution_convert_fusion.q_ref, f32[1024,512]{1,0:T(8,128)S(1)} %get-tuple-element.59.refs_0_, f32[1024,512]{1,0:T(8,128)S(1)} %get-tuple-element.60.refs_1_, f32[1024,512]{1,0:T(8,128)S(1)} %get-tuple-element.61.refs_2_, ...), custom_call_target="tpu_custom_call" | custom-call | flops 805306368 | bytes 8388608 | tf_op jit(solution)/shard_map/decode/pallas_call | solution.py:525
  (1 shorter events, 0.0 us)
Async XLA Ops:
  0.0 11.0 %copy-start = (bf16[1024,1024]{1,0:T(8,128)(2,1)S(1)}, bf16[1024,1024]{1,0:T(8,128)(2,1)}, u32[]{:S(2)}) copy-start(bf16[1024,1024]{1,0:T(8,128)(2,1)} %param.12) | copy-start | bytes 6291460
  2.5 18.6 %all-to-all-start = ((bf16[16,32,512]{2,1,0:T(8,128)(2,1)}), bf16[16,32,512]{2,1,0:T(8,128)(2,1)S(1)}, u32[]{:S(2)}, u32[]{:S(2)}) async-start(bf16[16,32,512]{2,1,0:T(8,128)(2,1)} %spread.1), calls=%async_computation | async-start | bytes 1048576 | tf_op jit(solution)/shard_map/all_to_all | solution.py:573
  11.0 3.6 %copy-start.2 = (bf16[1024,512]{1,0:T(8,128)(2,1)S(1)}, bf16[1024,512]{1,0:T(8,128)(2,1)}, u32[]{:S(2)}) copy-start(bf16[1024,512]{1,0:T(8,128)(2,1)} %param.16) | copy-start | bytes 3145732
  16.8 10.9 %copy-start.1 = (s32[8]{0:T(128)S(1)}, s32[8]{0:T(128)}, u32[]{:S(2)}) copy-start(s32[8]{0:T(128)} %valid_ref.9) | copy-start | bytes 100
  21.2 9.6 %collective-permute-start = (bf16[512,512]{1,0:T(8,128)(2,1)S(1)}, bf16[512,512]{1,0:T(8,128)(2,1)S(1)}, u32[]{:S(2)}, u32[]{:S(2)}) collective-permute-start(bf16[512,512]{1,0:T(8,128)(2,1)S(1)} %bitcast.10), channel_id=1, source_target_pairs={{0,32},{1,9},{2,34},{3,11},{4,36},{5,13},{6,38},{7,15},{8,40},{9,1... | collective-permute-start | bytes 1572872 | tf_op jit(solution)/shard_map/ppermute | solution.py:576
  22.3 15.3 %collective-permute-start.1 = (bf16[512,512]{1,0:T(8,128)(2,1)S(1)}, bf16[512,512]{1,0:T(8,128)(2,1)S(1)}, u32[]{:S(2)}, u32[]{:S(2)}) collective-permute-start(bf16[512,512]{1,0:T(8,128)(2,1)S(1)} %bitcast.11), channel_id=1, source_target_pairs={{0,64},{1,17},{2,66},{3,19},{4,68},{5,21},{6,70},{7,23},{8,72},{9,... | collective-permute-start | bytes 1572872 | tf_op jit(solution)/shard_map/ppermute | solution.py:576
  25.1 20.8 %collective-permute-start.2 = (bf16[512,512]{1,0:T(8,128)(2,1)S(1)}, bf16[512,512]{1,0:T(8,128)(2,1)S(1)}, u32[]{:S(2)}, u32[]{:S(2)}) collective-permute-start(bf16[512,512]{1,0:T(8,128)(2,1)S(1)} %bitcast.12), channel_id=1, source_target_pairs={{0,96},{1,25},{2,98},{3,27},{4,100},{5,29},{6,102},{7,31},{8,104},... | collective-permute-start | bytes 1572872 | tf_op jit(solution)/shard_map/ppermute | solution.py:576
  34.7 18.8 %collective-permute-start.3 = (bf16[16,144,128]{2,1,0:T(8,128)(2,1)S(1)}, bf16[16,144,128]{2,1,0:T(8,128)(2,1)S(1)}, u32[]{:S(2)}, u32[]{:S(2)}) collective-permute-start(bf16[16,144,128]{2,1,0:T(8,128)(2,1)S(1)} %cross.6), channel_id=1, source_target_pairs={{0,96},{1,25},{2,98},{3,27},{4,100},{5,29},{6,102},{7,31},{8,104},... | collective-permute-start | bytes 1769480 | tf_op jit(solution)/shard_map/ppermute | solution.py:576
  41.5 12.0 %collective-permute-start.4 = (bf16[16,144,128]{2,1,0:T(8,128)(2,1)S(1)}, bf16[16,144,128]{2,1,0:T(8,128)(2,1)S(1)}, u32[]{:S(2)}, u32[]{:S(2)}) collective-permute-start(bf16[16,144,128]{2,1,0:T(8,128)(2,1)S(1)} %cross.7), channel_id=1, source_target_pairs={{0,64},{1,17},{2,66},{3,19},{4,68},{5,21},{6,70},{7,23},{8,72},{9,... | collective-permute-start | bytes 1769480 | tf_op jit(solution)/shard_map/ppermute | solution.py:576
  49.9 10.5 %collective-permute-start.5 = (bf16[16,144,128]{2,1,0:T(8,128)(2,1)S(1)}, bf16[16,144,128]{2,1,0:T(8,128)(2,1)S(1)}, u32[]{:S(2)}, u32[]{:S(2)}) collective-permute-start(bf16[16,144,128]{2,1,0:T(8,128)(2,1)S(1)} %cross.8), channel_id=1, source_target_pairs={{0,32},{1,9},{2,34},{3,11},{4,36},{5,13},{6,38},{7,15},{8,40},{9,1... | collective-permute-start | bytes 1769480 | tf_op jit(solution)/shard_map/ppermute | solution.py:576
  62.1 15.0 %all-to-all-start.1 = ((bf16[16,144,128]{2,1,0:T(8,128)(2,1)}), bf16[16,144,128]{2,1,0:T(8,128)(2,1)S(1)}, u32[]{:S(2)}, u32[]{:S(2)}) async-start(bf16[16,144,128]{2,1,0:T(8,128)(2,1)} %join.3), calls=%async_computation.1 | async-start | bytes 1179648 | tf_op jit(solution)/shard_map/all_to_all | solution.py:573
  79.8 3.7 %collective-permute-start.6 = (bf16[16,1024]{1,0:T(8,128)(2,1)S(1)}, bf16[16,1024]{1,0:T(8,128)(2,1)S(1)}, u32[]{:S(2)}, u32[]{:S(2)}) collective-permute-start(bf16[16,1024]{1,0:T(8,128)(2,1)S(1)} %get-tuple-element.49), channel_id=1, source_target_pairs={{0,1},{1,0},{2,3},{3,2},{4,5},{5,4},{6,7},{7,6},{8,9},{9,8},{10,11... | collective-permute-start | bytes 98312 | tf_op jit(solution)/shard_map/ppermute | solution.py:598
  84.8 14.3 %all-to-all-start.2 = ((bf16[16,16,1024]{2,1,0:T(8,128)(2,1)}), bf16[16,16,1024]{2,1,0:T(8,128)(2,1)}, u32[]{:S(2)}, u32[]{:S(2)}) async-start(bf16[16,16,1024]{2,1,0:T(8,128)(2,1)} %latent.1), calls=%async_computation.2 | async-start | bytes 1048576 | tf_op jit(solution)/shard_map/all_to_all | solution.py:573
  99.1 3.9 %collective-permute-start.7 = (bf16[256,1024]{1,0:T(8,128)(2,1)}, bf16[256,1024]{1,0:T(8,128)(2,1)S(1)}, u32[]{:S(2)}, u32[]{:S(2)}) collective-permute-start(bf16[256,1024]{1,0:T(8,128)(2,1)} %bitcast.3.near_ref), channel_id=1, source_target_pairs={{0,1},{1,0},{2,3},{3,2},{4,5},{5,4},{6,7},{7,6},{8,9},{9,8},{10,11... | collective-permute-start | bytes 1572872 | tf_op jit(solution)/shard_map/ppermute | solution.py:607
  99.7 10.9 %collective-permute-start.8 = (bf16[256,1024]{1,0:T(8,128)(2,1)}, bf16[256,1024]{1,0:T(8,128)(2,1)S(1)}, u32[]{:S(2)}, u32[]{:S(2)}) collective-permute-start(bf16[256,1024]{1,0:T(8,128)(2,1)} %bitcast.3.near_ref), channel_id=1, source_target_pairs={{0,32},{1,9},{2,34},{3,11},{4,36},{5,13},{6,38},{7,15},{8,40},{9,1... | collective-permute-start | bytes 1572872 | tf_op jit(solution)/shard_map/ppermute | solution.py:576
  100.5 13.9 %collective-permute-start.9 = (bf16[256,1024]{1,0:T(8,128)(2,1)}, bf16[256,1024]{1,0:T(8,128)(2,1)S(1)}, u32[]{:S(2)}, u32[]{:S(2)}) collective-permute-start(bf16[256,1024]{1,0:T(8,128)(2,1)} %bitcast.3.near_ref), channel_id=1, source_target_pairs={{0,96},{1,25},{2,98},{3,27},{4,100},{5,29},{6,102},{7,31},{8,104},... | collective-permute-start | bytes 1572872 | tf_op jit(solution)/shard_map/ppermute | solution.py:576
  102.4 13.3 %collective-permute-start.10 = (bf16[256,1024]{1,0:T(8,128)(2,1)}, bf16[256,1024]{1,0:T(8,128)(2,1)S(1)}, u32[]{:S(2)}, u32[]{:S(2)}) collective-permute-start(bf16[256,1024]{1,0:T(8,128)(2,1)} %bitcast.3.near_ref), channel_id=1, source_target_pairs={{0,64},{1,17},{2,66},{3,19},{4,68},{5,21},{6,70},{7,23},{8,72},{9,... | collective-permute-start | bytes 1572872 | tf_op jit(solution)/shard_map/ppermute | solution.py:576
  115.7 2.8 %collective-permute-start.13 = (bf16[256,1024]{1,0:T(8,128)(2,1)S(1)}, bf16[256,1024]{1,0:T(8,128)(2,1)S(1)}, u32[]{:S(2)}, u32[]{:S(2)}) collective-permute-start(bf16[256,1024]{1,0:T(8,128)(2,1)S(1)} %collective-permute-done.10.refs_0_), channel_id=1, source_target_pairs={{0,1},{1,0},{2,3},{3,2},{4,5},{5,4},{6,7},{7,6},{8,9},{9,8},{10,11... | collective-permute-start | bytes 1572872 | tf_op jit(solution)/shard_map/ppermute | solution.py:615
  116.9 2.8 %collective-permute-start.11 = (bf16[256,1024]{1,0:T(8,128)(2,1)S(1)}, bf16[256,1024]{1,0:T(8,128)(2,1)S(1)}, u32[]{:S(2)}, u32[]{:S(2)}) collective-permute-start(bf16[256,1024]{1,0:T(8,128)(2,1)S(1)} %collective-permute-done.8.refs_0_), channel_id=1, source_target_pairs={{0,1},{1,0},{2,3},{3,2},{4,5},{5,4},{6,7},{7,6},{8,9},{9,8},{10,11... | collective-permute-start | bytes 1572872 | tf_op jit(solution)/shard_map/ppermute | solution.py:612
  117.0 2.9 %collective-permute-start.12 = (bf16[256,1024]{1,0:T(8,128)(2,1)S(1)}, bf16[256,1024]{1,0:T(8,128)(2,1)S(1)}, u32[]{:S(2)}, u32[]{:S(2)}) collective-permute-start(bf16[256,1024]{1,0:T(8,128)(2,1)S(1)} %collective-permute-done.9.refs_1_), channel_id=1, source_target_pairs={{0,1},{1,0},{2,3},{3,2},{4,5},{5,4},{6,7},{7,6},{8,9},{9,8},{10,11... | collective-permute-start | bytes 1572872 | tf_op jit(solution)/shard_map/ppermute | solution.py:612
  127.1 3.4 %collective-permute-start.14 = (bf16[512,1024]{1,0:T(8,128)(2,1)S(1)}, bf16[512,1024]{1,0:T(8,128)(2,1)S(1)}, u32[]{:S(2)}, u32[]{:S(2)}) collective-permute-start(bf16[512,1024]{1,0:T(8,128)(2,1)S(1)} %decode.4), channel_id=1, source_target_pairs={{0,1},{1,0},{2,3},{3,2},{4,5},{5,4},{6,7},{7,6},{8,9},{9,8},{10,11... | collective-permute-start | bytes 3145736 | tf_op jit(solution)/shard_map/ppermute | solution.py:621

commit v6 on v5

--- a/solution.py
+++ b/solution.py
@@ -23,7 +23,6 @@
 AXES = ("pos", "head")
 SIDE = 4
 ORDER = (1, 2, 3)
-FAR_ORDER = (2, 1, 3)
 
 
 def plane_groups():
@@ -250,19 +249,6 @@
     write_kv(row_refs, v_ref, out_ref, k_ref.shape[1])
 
 
-def near_kv_kernel(near_ref, swapped_ref, k_ref, v_ref, p_ref, out_ref, k_out, v_out, p_out, sems):
-    pairs = ((k_ref, k_out), (v_ref, v_out), (p_ref, p_out))
-    copies = [pltpu.make_async_copy(a, b, sems.at[i]) for i, (a, b) in enumerate(pairs)]
-    for copy in copies:
-        copy.start()
-    rows = (near_ref, swapped_ref)
-    copies[0].wait()
-    write_kv(rows, k_out, out_ref, 0)
-    copies[1].wait()
-    write_kv(rows, v_out, out_ref, k_out.shape[1])
-    copies[2].wait()
-
-
 def head_columns(columns, h):
     return (
         slice(h * HEAD_DIM, (h + 1) * HEAD_DIM),
@@ -290,7 +276,7 @@
     pipelined(columns // HEAD_DIM, score, use)
 
 
-def attend(q_ref, carried_refs, kv_refs, w_ref, s_ref, o_ref):
+def attend(q_ref, carried_refs, kv_refs, s_ref, put):
     sums_ref, tops_ref, totals_ref = carried_refs
     columns = q_ref.shape[1]
     spots = []
@@ -316,23 +302,39 @@
         pb = p.astype(BF16)
         for spot, kv in zip(spots, kv_refs):
             o = o + jnp.dot(pb[:, spot], kv[:, vc], preferred_element_type=F32)
+        put(kc, o, m, total)
+
+    pipelined(columns // HEAD_DIM, score, use)
+
+
+def middle_kernel(base_ref, q_ref, *refs):
+    carried, (*kv_refs, sums_out, tops_out, totals_out, s_ref) = refs[:3], refs[3:]
+
+    def put(kc, o, m, total):
+        sums_out[:, kc] = o
+        tops_out[:, kc] = m
+        totals_out[:, kc] = total
+
+    attend(q_ref, carried, kv_refs, s_ref, put)
+
+
+def projected(q_ref, carried, kv_refs, w_ref, s_ref, o_ref):
+    def put(kc, o, m, total):
         o_ref[:, kc] = (o / total).astype(BF16)
 
-    pipelined(columns // HEAD_DIM, score, use)
+    attend(q_ref, carried, kv_refs, s_ref, put)
     return jnp.dot(o_ref[...], w_ref[...], preferred_element_type=F32)
 
 
-def decode_kernel(base_ref, q_ref, *refs):
+def away_kernel(base_ref, q_ref, *refs):
     carried, (*kv_refs, w_ref, out_ref, s_ref, o_ref) = refs[:3], refs[3:]
-    out_ref[...] = attend(q_ref, carried, kv_refs, w_ref, s_ref, o_ref).astype(out_ref.dtype)
-
-
-def last_kernel(base_ref, q_ref, *refs):
-    carried, (*kv_refs, w_ref, first_ref, recv_ref, out_ref, s_ref, o_ref) = refs[:3], refs[3:]
-    n = first_ref.shape[0]
-    out_ref[:n] = rms_norm(first_ref[...] + recv_ref[:n].astype(F32)).astype(out_ref.dtype)
-    terms = attend(q_ref, carried, kv_refs, w_ref, s_ref, o_ref)
-    out_ref[n:] = rms_norm(terms + recv_ref[n:].astype(F32)).astype(out_ref.dtype)
+    out_ref[...] = projected(q_ref, carried, kv_refs, w_ref, s_ref, o_ref).astype(BF16)
+
+
+def home_kernel(base_ref, q_ref, *refs):
+    carried, (*kv_refs, w_ref, recv_ref, out_ref, s_ref, o_ref) = refs[:3], refs[3:]
+    terms = projected(q_ref, carried, kv_refs, w_ref, s_ref, o_ref)
+    out_ref[...] = rms_norm(terms + recv_ref[...].astype(F32)).astype(BF16)
 
 
 def full_spec(array):
@@ -472,27 +474,6 @@
     )(*rows, w_lkey, w_lvalue)
 
 
-def near_kv(near, swapped, w_lkey, w_lvalue, w_pout):
-    vmem = pl.BlockSpec(memory_space=pltpu.VMEM)
-    hbm = pl.BlockSpec(memory_space=pltpu.HBM)
-    rows = near.shape[0] + swapped.shape[0]
-    return pl.pallas_call(
-        near_kv_kernel,
-        out_shape=[
-            jax.ShapeDtypeStruct((rows, 2 * w_lkey.shape[1]), BF16),
-            *[jax.ShapeDtypeStruct(w.shape, BF16) for w in (w_lkey, w_lvalue, w_pout)],
-        ],
-        in_specs=[vmem, vmem, hbm, hbm, hbm],
-        out_specs=[vmem] * 4,
-        scratch_shapes=[pltpu.SemaphoreType.DMA((3,))],
-        compiler_params=params(24 << 20),
-        cost_estimate=pl.CostEstimate(
-            flops=4 * rows * w_lkey.size // 2, bytes_accessed=4 << 20, transcendentals=0
-        ),
-        name="near_kv",
-    )(near, swapped, *in_hbm(w_lkey, w_lvalue, w_pout))
-
-
 def near_decode(q, kv):
     rows, columns = q.shape
     block = ROW_BLOCK
@@ -514,33 +495,45 @@
     )(q, kv)
 
 
-def decode(base, blocks, q, carried, kvs, w_pout, dtype, finish=()):
-    columns = q.shape[1]
-    width = w_pout.shape[1]
-    block = ROW_BLOCK
-    rows = blocks * block
-    out_rows = finish[1].shape[0] if finish else rows
-    out_block = out_rows if finish else block
+def decode(kernel, base, q, carried, kvs, w_pout=None, recv=None):
+    rows, columns = q.shape[0] // 2, q.shape[1]
+    block = min(ROW_BLOCK, rows)
     keys = sum(kv.shape[0] for kv in kvs)
-    return pl.pallas_call(
-        last_kernel if finish else decode_kernel,
-        out_shape=jax.ShapeDtypeStruct((out_rows, width), dtype),
+    blocks = rows // block
+
+    def at_base(x):
+        if x.shape[0] == rows:
+            return pl.BlockSpec((block, x.shape[1]), lambda i, b: (i, 0))
+        return pl.BlockSpec((block, x.shape[1]), lambda i, b: (b[0] * blocks + i, 0))
+
+    scratch = [pltpu.VMEM((2, block, keys), F32)]
+    if w_pout is None:
+        out_shape = (jax.ShapeDtypeStruct((rows, columns), F32),) * 3
+        out_specs = (pl.BlockSpec((block, columns), lambda i, b: (i, 0)),) * 3
+        extra, extra_specs = (), []
+    else:
+        width = w_pout.shape[1]
+        out_shape = jax.ShapeDtypeStruct((rows, width), BF16)
+        out_specs = pl.BlockSpec((block, width), lambda i, b: (i, 0))
+        scratch.append(pltpu.VMEM((block, columns), BF16))
+        extra = (w_pout,) if recv is None else (w_pout, recv)
+        extra_specs = [full_spec(w_pout)] + ([] if recv is None else [at_base(recv)])
+    return pl.pallas_call(
+        kernel,
+        out_shape=out_shape,
         grid_spec=pltpu.PrefetchScalarGridSpec(
             num_scalar_prefetch=1,
             grid=(blocks,),
-            in_specs=[
-                *[pl.BlockSpec((block, x.shape[1]), lambda i, b: (b[0] + i, 0)) for x in (q, *carried)],
-                *[full_spec(x) for x in (*kvs, w_pout, *finish)],
-            ],
-            out_specs=pl.BlockSpec((out_block, width), lambda i, b: (i, 0)),
-            scratch_shapes=[pltpu.VMEM((2, block, keys), F32), pltpu.VMEM((block, columns), BF16)],
+            in_specs=[*[at_base(x) for x in (q, *carried)], *[full_spec(x) for x in kvs], *extra_specs],
+            out_specs=out_specs,
+            scratch_shapes=scratch,
         ),
-        compiler_params=params(36 << 20),
+        compiler_params=params(30 << 20),
         cost_estimate=pl.CostEstimate(
             flops=4 * rows * columns * keys, bytes_accessed=8 << 20, transcendentals=4 * rows * keys
         ),
         name="decode",
-    )(base, q, *carried, *kvs, w_pout, *finish)
+    )(base, q, *carried, *kvs, *extra)
 
 
 def project(a, w):
@@ -601,26 +594,29 @@
     pos_queries = project(inputs, w_pquery)
     near, pos_queries = lax.optimization_barrier((within_plane(rows), pos_queries))
     near = near.reshape(-1, width)
-    far = []
-    for s in FAR_ORDER:
-        far.append(along(near, s))
+    quick = []
+    for s in (1, 3):
+        quick.append(along(near, s))
     near_swapped = lax.ppermute(near, "head", swap)
-    kv, w_lkey, w_lvalue, w_pout = near_kv(near, near_swapped, w_lkey, w_lvalue, w_pout)
+    near, w_lkey, w_lvalue, w_pout = lax.optimization_barrier((near, w_lkey, w_lvalue, w_pout))
+    w_lkey, w_lvalue, w_pout = load((w_lkey, w_lvalue, w_pout))
+    kv = latent_kv([near, near_swapped], w_lkey, w_lvalue)
+    near, kv = lax.optimization_barrier((near, kv))
+    slow = along(near, 2)
     carried = near_decode(pos_queries, kv)
-    slow, *quick = far
     carried, quick = lax.optimization_barrier((carried, quick))
     quick_swapped = [lax.ppermute(x, "head", swap) for x in quick]
     quick_kv = latent_kv(quick, w_lkey, w_lvalue)
-    slow, quick_kv = lax.optimization_barrier((slow, quick_kv))
+    swapped_kv = latent_kv(quick_swapped, w_lkey, w_lvalue)
+    further = decode(middle_kernel, 1 - core, pos_queries, carried, [quick_kv, swapped_kv])
+    slow, further = lax.optimization_barrier((slow, further))
     slow_swapped = lax.ppermute(slow, "head", swap)
-    swapped_kv = latent_kv(quick_swapped, w_lkey, w_lvalue)
-    slow_kv = latent_kv([slow, slow_swapped], w_lkey, w_lvalue)
-    kvs = [quick_kv, swapped_kv, slow_kv]
-    blocks = pos_queries.shape[0] // 2 // ROW_BLOCK
-    terms = decode((1 - core) * blocks, blocks, pos_queries, carried, kvs, w_pout, BF16)
+    slow_kv = latent_kv([slow], w_lkey, w_lvalue)
+    slow_swapped_kv = latent_kv([slow_swapped], w_lkey, w_lvalue)
+    slow_kvs = [slow_kv, slow_swapped_kv]
+    terms = decode(away_kernel, 1 - core, pos_queries, further, slow_kvs, w_pout)
     arrived = lax.ppermute(terms, "head", swap)
-    first = decode(core * blocks, blocks - 1, pos_queries, carried, kvs, w_pout, F32)
-    return decode(core * blocks + blocks - 1, 1, pos_queries, carried, kvs, w_pout, BF16, (first, arrived))
+    return decode(home_kernel, core, pos_queries, carried, [quick_kv, swapped_kv, *slow_kvs], w_pout, arrived)
 
 
 def solution(mesh):

time: 135 us -> 139 us (1.030)
  Pallas kernels: 52.3 us -> 54.3 us
  starting transfers between devices: 37 us -> 39 us
    ppermute x9, waiting for transfers between devices: 11.3 us -> 8.74 us  [along(): return lax.ppermute(x, AXES, long[shift % SIDE])]
    pallas_call x3 -> x5, Pallas kernels: 3.73 us -> 6.18 us  [latent_kv(): pl.pallas_call(kv_kernel, out_shape=jax.ShapeDtypeStruct((total, wide), B...]
    ppermute x1, waiting for transfers between devices: 0.01 us -> 2.3 us  [per_device(): arrived = lax.ppermute(terms, 'head', swap)]
    pallas_call x4 -> x3, Pallas kernels: 16.7 us -> 14.4 us  [decode(): pl.pallas_call(kernel, out_shape=out_shape, grid_spec=pltpu.PrefetchScala...]
    pallas_call x1 -> x2, Pallas kernels: 1.56 us -> 3.44 us  [load(): pl.pallas_call(load_kernel, out_shape=[jax.ShapeDtypeStruct(x.shape, x.dt...]
    ppermute x9, starting transfers between devices: 15.1 us -> 16.8 us  [along(): return lax.ppermute(x, AXES, long[shift % SIDE])]
  transfers between devices with their start and end apart: 18 -> 18, of which waited for: 10 -> 10; matrix products, arithmetic and copies ran while one was open for 6% -> 6% of each run, Pallas kernels for 24% -> 25%
where the time goes in v6:
time: 139 us; the launch traced here: 138 us
  Pallas kernels  54.3 us (39%)
  starting transfers between devices  39 us (28%)
  waiting for transfers between devices  36 us (26%)
  matrix products  8.28 us (6%)
    all_to_all x3, waiting for transfers between devices, within_plane(): return lax.all_to_all(x, AXES, 0, 0, axis_index_groups=plane)  23.2 us
    pallas_call x5, Pallas kernels, cross(): pl.pallas_call(functools.partial(cross_kernel, lat_local=lat_local, first...  16.9 us
    ppermute x9, starting transfers between devices, along(): return lax.ppermute(x, AXES, long[shift % SIDE])  16.8 us
    all_to_all x3, starting transfers between devices, within_plane(): return lax.all_to_all(x, AXES, 0, 0, axis_index_groups=plane)  16.3 us
    pallas_call x3, Pallas kernels, decode(): pl.pallas_call(kernel, out_shape=out_shape, grid_spec=pltpu.PrefetchScala...  14.4 us
    ppermute x9, waiting for transfers between devices, along(): return lax.ppermute(x, AXES, long[shift % SIDE])  8.74 us
    dot_general x3, matrix products, project(): return jnp.dot(a, w, preferred_element_type=F32).astype(BF16)  8.28 us
    pallas_call x5, Pallas kernels, latent_kv(): pl.pallas_call(kv_kernel, out_shape=jax.ShapeDtypeStruct((total, wide), B...  6.18 us
  transfers between devices with their start and end apart: 18, of which 10 were waited for; matrix products, arithmetic and copies ran while one was open for 6% of the time, Pallas kernels for 25%

profile of v6, /device:TPU:1, one launch (start us, length us, event | category | flops | bytes accessed | tf_op | source)
XLA Modules:
  0.0 137.9 jit_solution(4026150650095608152)
XLA Ops:
  0.0 0.0 copy-start
  0.0 2.5 %spread.1 = bf16[16,32,512]{2,1,0:T(8,128)(2,1)} custom-call(bf16[32,1024]{1,0:T(8,128)(2,1)} %l_ref.1, bf16[1024,512]{1,0:T(8,128)(2,1)} %w_ref.2), custom_call_target="tpu_custom_call" | custom-call | tf_op jit(solution)/shard_map/spread/pallas_call | solution.py:433
  2.5 8.4 %all-to-all-start = ((bf16[16,32,512]{2,1,0:T(8,128)(2,1)}), bf16[16,32,512]{2,1,0:T(8,128)(2,1)S(1)}, u32[]{:S(2)}, u32[]{:S(2)}) async-start(bf16[16,32,512]{2,1,0:T(8,128)(2,1)} %spread.1), calls=%async_computation | async-start | bytes 1048576 | tf_op jit(solution)/shard_map/all_to_all | solution.py:566
  11.0 0.0 copy-done
  11.0 0.0 copy-start.2
  11.0 3.6 %convolution_convert_fusion.1.refs_1_ = bf16[1024,512]{1,0:T(8,128)(2,1)} fusion(bf16[1024,1024]{1,0:T(8,128)(2,1)S(1)} %copy-done, bf16[1024,512]{1,0:T(8,128)(2,1)} %param.17), kind=kOutput, calls=%fused_computation.1 | convolution fusion | flops 1074266112 | bytes 4194304 | tf_op jit(solution)/shard_map/dot_general | solution.py:540
  14.6 2.2 %convolution_convert_fusion.2.refs_0_ = bf16[1024,512]{1,0:T(8,128)(2,1)} fusion(bf16[1024,1024]{1,0:T(8,128)(2,1)S(1)} %copy-done, bf16[1024,512]{1,0:T(8,128)(2,1)S(1)} %copy-done.2), kind=kOutput, calls=%fused_computation.2 | convolution fusion | flops 1074266112 | bytes 4194304 | tf_op jit(solution)/shard_map/dot_general | solution.py:540
  16.8 4.4 %all-to-all-done = bf16[16,32,512]{2,1,0:T(8,128)(2,1)S(1)} async-done(((bf16[16,32,512]{2,1,0:T(8,128)(2,1)}), bf16[16,32,512]{2,1,0:T(8,128)(2,1)S(1)}, u32[]{:S(2)}, u32[]{:S(2)}) %all-to-all-start) | async-done | bytes 524320 | tf_op jit(solution)/shard_map/all_to_all | solution.py:566
  21.2 1.1 collective-permute-start
  22.3 2.8 %collective-permute-start.1 = (bf16[512,512]{1,0:T(8,128)(2,1)S(1)}, bf16[512,512]{1,0:T(8,128)(2,1)S(1)}, u32[]{:S(2)}, u32[]{:S(2)}) collective-permute-start(bf16[512,512]{1,0:T(8,128)(2,1)S(1)} %bitcast.11), channel_id=1, source_target_pairs={{0,64},{1,17},{2,66},{3,19},{4,68},{5,21},{6,70},{7,23},{8,72},{9,... | collective-permute-start | bytes 1572872 | tf_op jit(solution)/shard_map/ppermute | solution.py:569
  25.1 1.0 collective-permute-start.2
  26.1 1.6 %load.2 = (bf16[1024,512]{1,0:T(8,128)(2,1)S(1)}, bf16[1024,512]{1,0:T(8,128)(2,1)S(1)}) custom-call(bf16[1024,512]{1,0:T(8,128)(2,1)} %convolution_convert_fusion.2.refs_0_, bf16[1024,512]{1,0:T(8,128)(2,1)} %convolution_convert_fusion.1.refs_1_), custom_call_target="tpu_custom_call" | custom-call | tf_op jit(solution)/shard_map/load/pallas_call | solution.py:383
  27.7 2.6 %cross.5.refs_0_ = bf16[16,80,128]{2,1,0:T(8,128)(2,1)S(1)} custom-call(s32[8]{0:T(128)S(1)} %copy-done.1, bf16[512,512]{1,0:T(8,128)(2,1)S(1)} %bitcast.13, bf16[1024,512]{1,0:T(8,128)(2,1)S(1)} %get-tuple-element.50.k_ref, bf16[1024,512]{1,0:T(8,128)(2,1)S(1)} %get-tuple-element.51.v_ref), custom_call_target="tpu_custom_call" | custom-call | flops 536870912 | bytes 4194304 | tf_op jit(solution)/shard_map/cross/pallas_call | solution.py:353
  30.2 0.6 collective-permute-done.q_ref
  30.8 3.9 %cross.6 = bf16[16,144,128]{2,1,0:T(8,128)(2,1)S(1)} custom-call(s32[8]{0:T(128)S(1)} %copy-done.1, bf16[512,512]{1,0:T(8,128)(2,1)S(1)} %collective-permute-done.q_ref, bf16[1024,512]{1,0:T(8,128)(2,1)S(1)} %get-tuple-element.50.k_ref, bf16[1024,512]{1,0:T(8,128)(2,1)S(1)} %get-tuple-element.51.v_ref), custom_call_target="tpu_custom_call" | custom-call | flops 1073741824 | bytes 4194304 | tf_op jit(solution)/shard_map/cross/pallas_call | solution.py:353
  34.7 1.5 %collective-permute-start.3 = (bf16[16,144,128]{2,1,0:T(8,128)(2,1)S(1)}, bf16[16,144,128]{2,1,0:T(8,128)(2,1)S(1)}, u32[]{:S(2)}, u32[]{:S(2)}) collective-permute-start(bf16[16,144,128]{2,1,0:T(8,128)(2,1)S(1)} %cross.6), channel_id=1, source_target_pairs={{0,96},{1,25},{2,98},{3,27},{4,100},{5,29},{6,102},{7,31},{8,104},... | collective-permute-start | bytes 1769480 | tf_op jit(solution)/shard_map/ppermute | solution.py:569
  36.2 1.4 collective-permute-done.1.q_ref
  37.6 3.9 %cross.7 = bf16[16,144,128]{2,1,0:T(8,128)(2,1)S(1)} custom-call(s32[8]{0:T(128)S(1)} %copy-done.1, bf16[512,512]{1,0:T(8,128)(2,1)S(1)} %collective-permute-done.1.q_ref, bf16[1024,512]{1,0:T(8,128)(2,1)S(1)} %get-tuple-element.50.k_ref, bf16[1024,512]{1,0:T(8,128)(2,1)S(1)} %get-tuple-element.51.v_ref), custom_call_target="tpu_custom_call" | custom-call | flops 1073741824 | bytes 4194304 | tf_op jit(solution)/shard_map/cross/pallas_call | solution.py:353
  41.5 4.4 %collective-permute-start.4 = (bf16[16,144,128]{2,1,0:T(8,128)(2,1)S(1)}, bf16[16,144,128]{2,1,0:T(8,128)(2,1)S(1)}, u32[]{:S(2)}, u32[]{:S(2)}) collective-permute-start(bf16[16,144,128]{2,1,0:T(8,128)(2,1)S(1)} %cross.7), channel_id=1, source_target_pairs={{0,64},{1,17},{2,66},{3,19},{4,68},{5,21},{6,70},{7,23},{8,72},{9,... | collective-permute-start | bytes 1769480 | tf_op jit(solution)/shard_map/ppermute | solution.py:569
  45.9 0.0 collective-permute-done.2.q_ref
  45.9 3.9 %cross.8 = bf16[16,144,128]{2,1,0:T(8,128)(2,1)S(1)} custom-call(s32[8]{0:T(128)S(1)} %copy-done.1, bf16[512,512]{1,0:T(8,128)(2,1)S(1)} %collective-permute-done.2.q_ref, bf16[1024,512]{1,0:T(8,128)(2,1)S(1)} %get-tuple-element.50.k_ref, bf16[1024,512]{1,0:T(8,128)(2,1)S(1)} %get-tuple-element.51.v_ref), custom_call_target="tpu_custom_call" | custom-call | flops 1073741824 | bytes 4194304 | tf_op jit(solution)/shard_map/cross/pallas_call | solution.py:353
  49.9 1.1 collective-permute-start.5
  50.9 2.6 %cross.9.refs_0_ = bf16[16,144,128]{2,1,0:T(8,128)(2,1)S(1)} custom-call(s32[8]{0:T(128)S(1)} %copy-done.1, bf16[512,512]{1,0:T(8,128)(2,1)S(1)} %bitcast.14, bf16[1024,512]{1,0:T(8,128)(2,1)S(1)} %get-tuple-element.50.k_ref, bf16[1024,512]{1,0:T(8,128)(2,1)S(1)} %get-tuple-element.51.v_ref, bf16[16,80,128]{2,1,0:T(8,128)(2,1)S(1)} %cross.5.refs_0_), custom_call_target="tpu_custom_call" | custom-call | flops 536870912 | bytes 4194304 | tf_op jit(solution)/shard_map/cross/pallas_call | solution.py:353
  53.5 0.0 collective-permute-done.4.refs_2_
  53.5 0.0 collective-permute-done.3.refs_1_
  53.5 1.3 join.2.refs_0_
  54.8 5.5 %collective-permute-done.5.refs_1_ = bf16[16,144,128]{2,1,0:T(8,128)(2,1)S(1)} collective-permute-done((bf16[16,144,128]{2,1,0:T(8,128)(2,1)S(1)}, bf16[16,144,128]{2,1,0:T(8,128)(2,1)S(1)}, u32[]{:S(2)}, u32[]{:S(2)}) %collective-permute-start.5) | collective-permute-done | bytes 589856 | tf_op jit(solution)/shard_map/ppermute | solution.py:569
  60.3 1.7 %join.3 = bf16[16,144,128]{2,1,0:T(8,128)(2,1)} custom-call(bf16[16,144,128]{2,1,0:T(8,128)(2,1)S(1)} %join.2.refs_0_, bf16[16,144,128]{2,1,0:T(8,128)(2,1)S(1)} %collective-permute-done.5.refs_1_), custom_call_target="tpu_custom_call" | custom-call | tf_op jit(solution)/shard_map/join/pallas_call | solution.py:396
  62.0 3.6 %all-to-all-start.1 = ((bf16[16,144,128]{2,1,0:T(8,128)(2,1)}), bf16[16,144,128]{2,1,0:T(8,128)(2,1)S(1)}, u32[]{:S(2)}, u32[]{:S(2)}) async-start(bf16[16,144,128]{2,1,0:T(8,128)(2,1)} %join.3), calls=%async_computation.1 | async-start | bytes 1179648 | tf_op jit(solution)/shard_map/all_to_all | solution.py:566
  65.7 0.1 pad_add_fusion.core_ref
  65.7 11.3 %all-to-all-done.1.r_ref = bf16[16,144,128]{2,1,0:T(8,128)(2,1)S(1)} async-done(((bf16[16,144,128]{2,1,0:T(8,128)(2,1)}), bf16[16,144,128]{2,1,0:T(8,128)(2,1)S(1)}, u32[]{:S(2)}, u32[]{:S(2)}) %all-to-all-start.1) | async-done | bytes 589856 | tf_op jit(solution)/shard_map/all_to_all | solution.py:566
  77.1 2.7 %combine.1 = (f32[16,1024]{1,0:T(8,128)S(1)}, bf16[16,1024]{1,0:T(8,128)(2,1)S(1)}, bf16[1024,1024]{1,0:T(8,128)(2,1)S(1)}) custom-call(s32[2]{0:T(128)S(1)} %pad_add_fusion.core_ref, bf16[16,144,128]{2,1,0:T(8,128)(2,1)S(1)} %all-to-all-done.1.r_ref, bf16[512,1024]{1,0:T(8,128)(2,1)} %w_ref.3, bf16[1024,1024]{1,0:T(8,128)(2,1)} %mlp_ref.1), custom_call_target="tpu_custom_call" | custom-call | tf_op jit(solution)/shard_map/combine/pallas_call | solution.py:411
  79.7 2.9 %collective-permute-start.6 = (bf16[16,1024]{1,0:T(8,128)(2,1)S(1)}, bf16[16,1024]{1,0:T(8,128)(2,1)S(1)}, u32[]{:S(2)}, u32[]{:S(2)}) collective-permute-start(bf16[16,1024]{1,0:T(8,128)(2,1)S(1)} %get-tuple-element.59), channel_id=1, source_target_pairs={{0,1},{1,0},{2,3},{3,2},{4,5},{5,4},{6,7},{7,6},{8,9},{9,8},{10,11... | collective-permute-start | bytes 98312 | tf_op jit(solution)/shard_map/ppermute | solution.py:591
  82.6 0.9 collective-permute-done.6.recv_ref
  83.5 1.3 latent.1
  84.8 4.2 %all-to-all-start.2 = ((bf16[16,16,1024]{2,1,0:T(8,128)(2,1)}), bf16[16,16,1024]{2,1,0:T(8,128)(2,1)}, u32[]{:S(2)}, u32[]{:S(2)}) async-start(bf16[16,16,1024]{2,1,0:T(8,128)(2,1)} %latent.1), calls=%async_computation.2 | async-start | bytes 1048576 | tf_op jit(solution)/shard_map/all_to_all | solution.py:566
  89.0 2.5 %convolution_convert_fusion.q_ref = bf16[1024,512]{1,0:T(8,128)(2,1)S(1)} fusion(bf16[1024,1024]{1,0:T(8,128)(2,1)S(1)} %copy-done, bf16[1024,512]{1,0:T(8,128)(2,1)} %param.22), kind=kOutput, calls=%fused_computation | convolution fusion | flops 1074266112 | bytes 4194304 | tf_op jit(solution)/shard_map/dot_general | solution.py:540
  91.5 7.5 %all-to-all-done.2 = bf16[16,16,1024]{2,1,0:T(8,128)(2,1)} async-done(((bf16[16,16,1024]{2,1,0:T(8,128)(2,1)}), bf16[16,16,1024]{2,1,0:T(8,128)(2,1)}, u32[]{:S(2)}, u32[]{:S(2)}) %all-to-all-start.2) | async-done | bytes 524320 | tf_op jit(solution)/shard_map/all_to_all | solution.py:566
  99.0 0.6 collective-permute-start.7
  99.7 0.8 collective-permute-start.8
  100.5 1.8 %collective-permute-start.9 = (bf16[256,1024]{1,0:T(8,128)(2,1)}, bf16[256,1024]{1,0:T(8,128)(2,1)S(1)}, u32[]{:S(2)}, u32[]{:S(2)}) collective-permute-start(bf16[256,1024]{1,0:T(8,128)(2,1)} %bitcast.3.refs_0_), channel_id=1, source_target_pairs={{0,96},{1,25},{2,98},{3,27},{4,100},{5,29},{6,102},{7,31},{8,104},... | collective-permute-start | bytes 1572872 | tf_op jit(solution)/shard_map/ppermute | solution.py:569
  102.3 1.9 %load.3 = (bf16[1024,512]{1,0:T(8,128)(2,1)S(1)}, bf16[1024,512]{1,0:T(8,128)(2,1)S(1)}, bf16[512,1024]{1,0:T(8,128)(2,1)S(1)}) custom-call(bf16[1024,512]{1,0:T(8,128)(2,1)} %refs_0_, bf16[1024,512]{1,0:T(8,128)(2,1)} %refs_1_, bf16[512,1024]{1,0:T(8,128)(2,1)} %refs_2_), custom_call_target="tpu_custom_call" | custom-call | tf_op jit(solution)/shard_map/load/pallas_call | solution.py:383
  104.2 0.0 collective-permute-done.7.refs_1_
  104.2 2.3 %latent_kv.5.kv_ref = bf16[512,1024]{1,0:T(8,128)(2,1)S(1)} custom-call(bf16[256,1024]{1,0:T(8,128)(2,1)} %bitcast.3.refs_0_, bf16[256,1024]{1,0:T(8,128)(2,1)S(1)} %collective-permute-done.7.refs_1_, bf16[1024,512]{1,0:T(8,128)(2,1)S(1)} %get-tuple-element.69.refs_2_.refs_1_, bf16[1024,512]{1,0:T(8,128)(2,1)S(1)} %get-tuple-element.70.refs_3_.refs_2_), custom_call_target="tpu_custom_call" | custom-call | flops 1073741824 | bytes 4194304 | tf_op jit(solution)/shard_map/latent_kv/pallas_call | solution.py:464
  106.5 3.9 %near_decode.1 = (f32[1024,512]{1,0:T(8,128)S(1)}, f32[1024,512]{1,0:T(8,128)S(1)}, f32[1024,512]{1,0:T(8,128)S(1)}) custom-call(bf16[1024,512]{1,0:T(8,128)(2,1)S(1)} %convolution_convert_fusion.q_ref, bf16[512,1024]{1,0:T(8,128)(2,1)S(1)} %latent_kv.5.kv_ref), custom_call_target="tpu_custom_call" | custom-call | flops 1073741824 | bytes 4194304 | tf_op jit(solution)/shard_map/near_decode/pallas_call | solution.py:480
  110.4 0.0 collective-permute-done.8.refs_0_
  110.4 0.0 collective-permute-done.9.refs_1_
  110.4 0.6 collective-permute-start.10
  111.1 0.1 collective-permute-start.11
  111.2 2.3 %collective-permute-start.12 = (bf16[256,1024]{1,0:T(8,128)(2,1)}, bf16[256,1024]{1,0:T(8,128)(2,1)S(1)}, u32[]{:S(2)}, u32[]{:S(2)}) collective-permute-start(bf16[256,1024]{1,0:T(8,128)(2,1)} %bitcast.3.refs_0_), channel_id=1, source_target_pairs={{0,64},{1,17},{2,66},{3,19},{4,68},{5,21},{6,70},{7,23},{8,72},{9,... | collective-permute-start | bytes 1572872 | tf_op jit(solution)/shard_map/ppermute | solution.py:569
  113.5 1.2 latent_kv.6.refs_3_
  114.7 0.0 collective-permute-done.10.refs_0_
  114.7 0.0 collective-permute-done.11.refs_1_
  114.7 1.2 latent_kv.7.refs_4_
  116.0 4.0 %decode.3 = (f32[512,512]{1,0:T(8,128)S(1)}, f32[512,512]{1,0:T(8,128)S(1)}, f32[512,512]{1,0:T(8,128)S(1)}) custom-call(s32[1]{0:T(128)S(6)} %sub.4.base_ref, bf16[1024,512]{1,0:T(8,128)(2,1)S(1)} %convolution_convert_fusion.q_ref, f32[1024,512]{1,0:T(8,128)S(1)} %get-tuple-element.75.refs_0_, f32[1024,512]{1,0:T(8,128)S(1)} %get-tuple-element.76.refs_1_, ...), custom_call_target="tpu_custom_call" | custom-call | flops 1073741824 | bytes 8388608 | tf_op jit(solution)/shard_map/decode/pallas_call | solution.py:521
  119.9 1.3 collective-permute-done.12.refs_0_
  121.2 1.3 collective-permute-start.13
  122.5 0.7 latent_kv.8.refs_3_.refs_5_
  123.2 0.8 collective-permute-done.13.refs_0_
  124.0 0.7 latent_kv.9.refs_4_.refs_6_
  124.7 3.6 %decode.4 = bf16[512,1024]{1,0:T(8,128)(2,1)S(1)} custom-call(s32[1]{0:T(128)S(6)} %sub.4.base_ref, bf16[1024,512]{1,0:T(8,128)(2,1)S(1)} %convolution_convert_fusion.q_ref, f32[512,512]{1,0:T(8,128)S(1)} %get-tuple-element.86.refs_0_, f32[512,512]{1,0:T(8,128)S(1)} %get-tuple-element.87.refs_1_, f32[512,512]{1,0:T(8,128)S(1)} %get-tuple-element.88.refs_2_, ...), custom_call_target="tpu_custom_call" | custom-call | flops 536870912 | bytes 8388608 | tf_op jit(solution)/shard_map/decode/pallas_call | solution.py:521
  128.3 0.4 collective-permute-start.14
  128.7 2.3 %collective-permute-done.14.refs_8_ = bf16[512,1024]{1,0:T(8,128)(2,1)S(1)} collective-permute-done((bf16[512,1024]{1,0:T(8,128)(2,1)S(1)}, bf16[512,1024]{1,0:T(8,128)(2,1)S(1)}, u32[]{:S(2)}, u32[]{:S(2)}) %collective-permute-start.14) | collective-permute-done | bytes 1048608 | tf_op jit(solution)/shard_map/ppermute | solution.py:618
  131.0 6.9 %decode.5 = bf16[512,1024]{1,0:T(8,128)(2,1)} custom-call(s32[1]{0:T(128)} %bitcast.base_ref, bf16[1024,512]{1,0:T(8,128)(2,1)S(1)} %convolution_convert_fusion.q_ref, f32[1024,512]{1,0:T(8,128)S(1)} %get-tuple-element.75.refs_0_, f32[1024,512]{1,0:T(8,128)S(1)} %get-tuple-element.76.refs_1_, f32[1024,512]{1,0:T(8,128)S(1)} %get-tuple-element.77.refs_2_, ...), custom_call_target="tpu_custom_call" | custom-call | flops 1610612736 | bytes 8388608 | tf_op jit(solution)/shard_map/decode/pallas_call | solution.py:521
  (3 shorter events, 0.0 us)
Async XLA Ops:
  0.0 11.0 %copy-start = (bf16[1024,1024]{1,0:T(8,128)(2,1)S(1)}, bf16[1024,1024]{1,0:T(8,128)(2,1)}, u32[]{:S(2)}) copy-start(bf16[1024,1024]{1,0:T(8,128)(2,1)} %param.12) | copy-start | bytes 6291460
  2.5 18.6 %all-to-all-start = ((bf16[16,32,512]{2,1,0:T(8,128)(2,1)}), bf16[16,32,512]{2,1,0:T(8,128)(2,1)S(1)}, u32[]{:S(2)}, u32[]{:S(2)}) async-start(bf16[16,32,512]{2,1,0:T(8,128)(2,1)} %spread.1), calls=%async_computation | async-start | bytes 1048576 | tf_op jit(solution)/shard_map/all_to_all | solution.py:566
  11.0 3.6 %copy-start.2 = (bf16[1024,512]{1,0:T(8,128)(2,1)S(1)}, bf16[1024,512]{1,0:T(8,128)(2,1)}, u32[]{:S(2)}) copy-start(bf16[1024,512]{1,0:T(8,128)(2,1)} %param.16) | copy-start | bytes 3145732
  16.8 10.9 %copy-start.1 = (s32[8]{0:T(128)S(1)}, s32[8]{0:T(128)}, u32[]{:S(2)}) copy-start(s32[8]{0:T(128)} %valid_ref.9) | copy-start | bytes 100
  21.2 9.6 %collective-permute-start = (bf16[512,512]{1,0:T(8,128)(2,1)S(1)}, bf16[512,512]{1,0:T(8,128)(2,1)S(1)}, u32[]{:S(2)}, u32[]{:S(2)}) collective-permute-start(bf16[512,512]{1,0:T(8,128)(2,1)S(1)} %bitcast.10), channel_id=1, source_target_pairs={{0,32},{1,9},{2,34},{3,11},{4,36},{5,13},{6,38},{7,15},{8,40},{9,1... | collective-permute-start | bytes 1572872 | tf_op jit(solution)/shard_map/ppermute | solution.py:569
  22.3 15.3 %collective-permute-start.1 = (bf16[512,512]{1,0:T(8,128)(2,1)S(1)}, bf16[512,512]{1,0:T(8,128)(2,1)S(1)}, u32[]{:S(2)}, u32[]{:S(2)}) collective-permute-start(bf16[512,512]{1,0:T(8,128)(2,1)S(1)} %bitcast.11), channel_id=1, source_target_pairs={{0,64},{1,17},{2,66},{3,19},{4,68},{5,21},{6,70},{7,23},{8,72},{9,... | collective-permute-start | bytes 1572872 | tf_op jit(solution)/shard_map/ppermute | solution.py:569
  25.1 20.8 %collective-permute-start.2 = (bf16[512,512]{1,0:T(8,128)(2,1)S(1)}, bf16[512,512]{1,0:T(8,128)(2,1)S(1)}, u32[]{:S(2)}, u32[]{:S(2)}) collective-permute-start(bf16[512,512]{1,0:T(8,128)(2,1)S(1)} %bitcast.12), channel_id=1, source_target_pairs={{0,96},{1,25},{2,98},{3,27},{4,100},{5,29},{6,102},{7,31},{8,104},... | collective-permute-start | bytes 1572872 | tf_op jit(solution)/shard_map/ppermute | solution.py:569
  34.7 18.8 %collective-permute-start.3 = (bf16[16,144,128]{2,1,0:T(8,128)(2,1)S(1)}, bf16[16,144,128]{2,1,0:T(8,128)(2,1)S(1)}, u32[]{:S(2)}, u32[]{:S(2)}) collective-permute-start(bf16[16,144,128]{2,1,0:T(8,128)(2,1)S(1)} %cross.6), channel_id=1, source_target_pairs={{0,96},{1,25},{2,98},{3,27},{4,100},{5,29},{6,102},{7,31},{8,104},... | collective-permute-start | bytes 1769480 | tf_op jit(solution)/shard_map/ppermute | solution.py:569
  41.5 12.0 %collective-permute-start.4 = (bf16[16,144,128]{2,1,0:T(8,128)(2,1)S(1)}, bf16[16,144,128]{2,1,0:T(8,128)(2,1)S(1)}, u32[]{:S(2)}, u32[]{:S(2)}) collective-permute-start(bf16[16,144,128]{2,1,0:T(8,128)(2,1)S(1)} %cross.7), channel_id=1, source_target_pairs={{0,64},{1,17},{2,66},{3,19},{4,68},{5,21},{6,70},{7,23},{8,72},{9,... | collective-permute-start | bytes 1769480 | tf_op jit(solution)/shard_map/ppermute | solution.py:569
  49.9 10.5 %collective-permute-start.5 = (bf16[16,144,128]{2,1,0:T(8,128)(2,1)S(1)}, bf16[16,144,128]{2,1,0:T(8,128)(2,1)S(1)}, u32[]{:S(2)}, u32[]{:S(2)}) collective-permute-start(bf16[16,144,128]{2,1,0:T(8,128)(2,1)S(1)} %cross.8), channel_id=1, source_target_pairs={{0,32},{1,9},{2,34},{3,11},{4,36},{5,13},{6,38},{7,15},{8,40},{9,1... | collective-permute-start | bytes 1769480 | tf_op jit(solution)/shard_map/ppermute | solution.py:569
  62.0 15.0 %all-to-all-start.1 = ((bf16[16,144,128]{2,1,0:T(8,128)(2,1)}), bf16[16,144,128]{2,1,0:T(8,128)(2,1)S(1)}, u32[]{:S(2)}, u32[]{:S(2)}) async-start(bf16[16,144,128]{2,1,0:T(8,128)(2,1)} %join.3), calls=%async_computation.1 | async-start | bytes 1179648 | tf_op jit(solution)/shard_map/all_to_all | solution.py:566
  79.7 3.7 %collective-permute-start.6 = (bf16[16,1024]{1,0:T(8,128)(2,1)S(1)}, bf16[16,1024]{1,0:T(8,128)(2,1)S(1)}, u32[]{:S(2)}, u32[]{:S(2)}) collective-permute-start(bf16[16,1024]{1,0:T(8,128)(2,1)S(1)} %get-tuple-element.59), channel_id=1, source_target_pairs={{0,1},{1,0},{2,3},{3,2},{4,5},{5,4},{6,7},{7,6},{8,9},{9,8},{10,11... | collective-permute-start | bytes 98312 | tf_op jit(solution)/shard_map/ppermute | solution.py:591
  84.8 14.3 %all-to-all-start.2 = ((bf16[16,16,1024]{2,1,0:T(8,128)(2,1)}), bf16[16,16,1024]{2,1,0:T(8,128)(2,1)}, u32[]{:S(2)}, u32[]{:S(2)}) async-start(bf16[16,16,1024]{2,1,0:T(8,128)(2,1)} %latent.1), calls=%async_computation.2 | async-start | bytes 1048576 | tf_op jit(solution)/shard_map/all_to_all | solution.py:566
  99.0 5.2 %collective-permute-start.7 = (bf16[256,1024]{1,0:T(8,128)(2,1)}, bf16[256,1024]{1,0:T(8,128)(2,1)S(1)}, u32[]{:S(2)}, u32[]{:S(2)}) collective-permute-start(bf16[256,1024]{1,0:T(8,128)(2,1)} %bitcast.3.refs_0_), channel_id=1, source_target_pairs={{0,1},{1,0},{2,3},{3,2},{4,5},{5,4},{6,7},{7,6},{8,9},{9,8},{10,11... | collective-permute-start | bytes 1572872 | tf_op jit(solution)/shard_map/ppermute | solution.py:600
  99.7 10.7 %collective-permute-start.8 = (bf16[256,1024]{1,0:T(8,128)(2,1)}, bf16[256,1024]{1,0:T(8,128)(2,1)S(1)}, u32[]{:S(2)}, u32[]{:S(2)}) collective-permute-start(bf16[256,1024]{1,0:T(8,128)(2,1)} %bitcast.3.refs_0_), channel_id=1, source_target_pairs={{0,32},{1,9},{2,34},{3,11},{4,36},{5,13},{6,38},{7,15},{8,40},{9,1... | collective-permute-start | bytes 1572872 | tf_op jit(solution)/shard_map/ppermute | solution.py:569
  100.5 9.9 %collective-permute-start.9 = (bf16[256,1024]{1,0:T(8,128)(2,1)}, bf16[256,1024]{1,0:T(8,128)(2,1)S(1)}, u32[]{:S(2)}, u32[]{:S(2)}) collective-permute-start(bf16[256,1024]{1,0:T(8,128)(2,1)} %bitcast.3.refs_0_), channel_id=1, source_target_pairs={{0,96},{1,25},{2,98},{3,27},{4,100},{5,29},{6,102},{7,31},{8,104},... | collective-permute-start | bytes 1572872 | tf_op jit(solution)/shard_map/ppermute | solution.py:569
  110.4 4.3 %collective-permute-start.10 = (bf16[256,1024]{1,0:T(8,128)(2,1)S(1)}, bf16[256,1024]{1,0:T(8,128)(2,1)S(1)}, u32[]{:S(2)}, u32[]{:S(2)}) collective-permute-start(bf16[256,1024]{1,0:T(8,128)(2,1)S(1)} %collective-permute-done.8.refs_0_), channel_id=1, source_target_pairs={{0,1},{1,0},{2,3},{3,2},{4,5},{5,4},{6,7},{7,6},{8,9},{9,8},{10,11... | collective-permute-start | bytes 1572872 | tf_op jit(solution)/shard_map/ppermute | solution.py:608
  111.1 3.6 %collective-permute-start.11 = (bf16[256,1024]{1,0:T(8,128)(2,1)S(1)}, bf16[256,1024]{1,0:T(8,128)(2,1)S(1)}, u32[]{:S(2)}, u32[]{:S(2)}) collective-permute-start(bf16[256,1024]{1,0:T(8,128)(2,1)S(1)} %collective-permute-done.9.refs_1_), channel_id=1, source_target_pairs={{0,1},{1,0},{2,3},{3,2},{4,5},{5,4},{6,7},{7,6},{8,9},{9,8},{10,11... | collective-permute-start | bytes 1572872 | tf_op jit(solution)/shard_map/ppermute | solution.py:608
  111.2 10.0 %collective-permute-start.12 = (bf16[256,1024]{1,0:T(8,128)(2,1)}, bf16[256,1024]{1,0:T(8,128)(2,1)S(1)}, u32[]{:S(2)}, u32[]{:S(2)}) collective-permute-start(bf16[256,1024]{1,0:T(8,128)(2,1)} %bitcast.3.refs_0_), channel_id=1, source_target_pairs={{0,64},{1,17},{2,66},{3,19},{4,68},{5,21},{6,70},{7,23},{8,72},{9,... | collective-permute-start | bytes 1572872 | tf_op jit(solution)/shard_map/ppermute | solution.py:569
  121.2 2.8 %collective-permute-start.13 = (bf16[256,1024]{1,0:T(8,128)(2,1)S(1)}, bf16[256,1024]{1,0:T(8,128)(2,1)S(1)}, u32[]{:S(2)}, u32[]{:S(2)}) collective-permute-start(bf16[256,1024]{1,0:T(8,128)(2,1)S(1)} %collective-permute-done.12.refs_0_), channel_id=1, source_target_pairs={{0,1},{1,0},{2,3},{3,2},{4,5},{5,4},{6,7},{7,6},{8,9},{9,8},{10,11... | collective-permute-start | bytes 1572872 | tf_op jit(solution)/shard_map/ppermute | solution.py:613
  128.3 2.7 %collective-permute-start.14 = (bf16[512,1024]{1,0:T(8,128)(2,1)S(1)}, bf16[512,1024]{1,0:T(8,128)(2,1)S(1)}, u32[]{:S(2)}, u32[]{:S(2)}) collective-permute-start(bf16[512,1024]{1,0:T(8,128)(2,1)S(1)} %decode.4), channel_id=1, source_target_pairs={{0,1},{1,0},{2,3},{3,2},{4,5},{5,4},{6,7},{7,6},{8,9},{9,8},{10,11... | collective-permute-start | bytes 3145736 | tf_op jit(solution)/shard_map/ppermute | solution.py:618

commit v7 on v5

--- a/solution.py
+++ b/solution.py
@@ -155,8 +155,13 @@
     span = tall - LSE_ROWS
     heads = span // lat_local
     group = HEAD_DIM // lat_local
+    whole = [r for r in parts if r.shape[0] == owners]
+    split = [r for r in parts if r.shape[0] != owners]
     for g in range(0, owners, group):
-        lses = [unpack_rows(r[g, span : span + LSE_ROWS, :], heads) for r in parts]
+        parts = [(r, g) for r in whole]
+        if split:
+            parts.append((split[g // split[0].shape[0]], g % split[0].shape[0]))
+        lses = [unpack_rows(r[at, span : span + LSE_ROWS, :], heads) for r, at in parts]
         top = functools.reduce(jnp.maximum, lses)
         ws = [jnp.exp(x - top) for x in lses]
         total = functools.reduce(jnp.add, ws)
@@ -168,9 +173,9 @@
             for h in range(heads):
                 rows = slice(h * lat_local, (h + 1) * lat_local)
                 acc = jnp.zeros((lat_local, HEAD_DIM), F32)
-                for i, r in enumerate(parts):
+                for i, (r, at) in enumerate(parts):
                     w = wt[d * lat_local : (d + 1) * lat_local, i * heads + h : i * heads + h + 1]
-                    acc = acc + w * r[g + d, rows, :].astype(F32)
+                    acc = acc + w * r[at + d, rows, :].astype(F32)
                 out_ref[g + d, rows, :] = acc.astype(BF16)
 
 
@@ -343,10 +348,12 @@
     return pltpu.CompilerParams(vmem_limit_bytes=limit)
 
 
-def cross(valid, q, k, v, lat_local, first, heads, before=None):
-    lat, columns = q.shape
+def cross(valid, q, k, v, lat_local, first, heads, before=None, block_at=0, blocks=None):
+    columns = q.shape[1]
     tall = (first + heads) * lat_local + LSE_ROWS
-    block = min(ROW_BLOCK, lat)
+    block = min(ROW_BLOCK, q.shape[0])
+    blocks = q.shape[0] // block if blocks is None else blocks
+    lat = blocks * block
     extra = () if before is None else (before,)
     return pl.pallas_call(
         functools.partial(cross_kernel, lat_local=lat_local, first=first, heads=heads),
@@ -355,7 +362,7 @@
             num_scalar_prefetch=1,
             grid=(lat // block,),
             in_specs=[
-                pl.BlockSpec((block, columns), lambda i, c: (i, 0)),
+                pl.BlockSpec((block, columns), lambda i, c: (block_at + i, 0)),
                 full_spec(k),
                 full_spec(v),
                 *[pl.BlockSpec((block // lat_local,) + x.shape[1:], lambda i, c: (i, 0, 0)) for x in extra],
@@ -578,28 +585,33 @@
     queries = within_plane(spread(latents, w_query, SIDE * SIDE)).reshape(-1, columns)
     keys = project(inputs, w_key)
     values = project(inputs, w_value)
-    queries, keys, values = lax.optimization_barrier((queries, keys, values))
+    places = jnp.concatenate([core, lane_offset(lat_local)])
+    queries, keys, values, places = lax.optimization_barrier((queries, keys, values, places))
     away = [along(queries, s) for s in ORDER]
     keys, values = load((keys, values))
     heads = columns // HEAD_DIM
     half = cross(valid_blocks, queries, keys, values, lat_local, 0, heads // 2)
     part, partials = half, []
-    for s, there in zip(ORDER, away):
+    *soon, final = ORDER
+    for s, there in zip(soon, away):
         part, there = lax.optimization_barrier((part, there))
         part = cross(valid_blocks, there, keys, values, lat_local, 0, heads)
         partials.append(along(part, -s))
-    part, half = lax.optimization_barrier((part, half))
+    there, late = away[-1], []
+    for i in range(2):
+        part, there = lax.optimization_barrier((part, there))
+        part = cross(valid_blocks, there, keys, values, lat_local, 0, heads, None, i, 1)
+        late.append(along(part, -final))
+    part, half, inputs = lax.optimization_barrier((part, half, inputs))
     stay = cross(valid_blocks, queries, keys, values, lat_local, heads // 2, heads // 2, half)
-    *early, late = partials
-    stay, late = lax.optimization_barrier((join([stay, *early], lat_local), late))
-    partials = [stay, late]
+    pos_queries = project(inputs, w_pquery)
+    stay, pos_queries, late = lax.optimization_barrier((join([stay, *partials], lat_local), pos_queries, late))
+    partials = [stay, *late]
     gathered = within_plane(join(partials, lat_local))
-    own, other, w_mlp = combine(jnp.concatenate([core, lane_offset(lat_local)]), gathered, w_out, w_mlp, lat_local)
+    own, other, w_mlp = combine(places, gathered, w_out, w_mlp, lat_local)
     recv = lax.ppermute(other, "head", swap)
     rows = latent_rows(own, recv, w_mlp, SIDE * SIDE)
-    rows, inputs = lax.optimization_barrier((rows, inputs))
-    pos_queries = project(inputs, w_pquery)
-    near, pos_queries = lax.optimization_barrier((within_plane(rows), pos_queries))
+    near = within_plane(rows)
     near = near.reshape(-1, width)
     far = []
     for s in FAR_ORDER:

time: 135 us -> 136 us (level)
  blocking collectives: 0 us -> 28.8 us
  waiting for transfers between devices: 36.7 us -> 19.5 us
  starting transfers between devices: 37 us -> 28.9 us
  Pallas kernels: 52.3 us -> 50.1 us
    all_to_all x0 -> x2, blocking collectives: none -> 28.8 us  [within_plane(): return lax.all_to_all(x, AXES, 0, 0, axis_index_groups=plane)]
    all_to_all x3 -> x1, waiting for transfers between devices: 23.3 us -> 3.2 us  [within_plane(): return lax.all_to_all(x, AXES, 0, 0, axis_index_groups=plane)]
    all_to_all x3 -> x1, starting transfers between devices: 16.2 us -> 8.43 us  [within_plane(): return lax.all_to_all(x, AXES, 0, 0, axis_index_groups=plane)]
    ppermute x9 -> x10, waiting for transfers between devices: 11.3 us -> 14.1 us  [along(): return lax.ppermute(x, AXES, long[shift % SIDE])]
    ppermute x9 -> x10, starting transfers between devices: 15.1 us -> 14 us  [along(): return lax.ppermute(x, AXES, long[shift % SIDE])]
    pallas_call x5 -> x6, Pallas kernels: 16.9 us -> 17.5 us  [cross(): pl.pallas_call(functools.partial(cross_kernel, lat_local=lat_local, first...]
  transfers between devices with their start and end apart: 18 -> 17, of which waited for: 10 -> 10; matrix products, arithmetic and copies ran while one was open for 6% -> 6% of each run, Pallas kernels for 24% -> 24%
where the time goes in v7:
time: 136 us
  Pallas kernels  50.1 us (37%)
  starting transfers between devices  28.9 us (21%)
  blocking collectives  28.8 us (21%)
  waiting for transfers between devices  19.5 us (14%)
  matrix products  8.17 us (6%)
    all_to_all x2, blocking collectives, within_plane(): return lax.all_to_all(x, AXES, 0, 0, axis_index_groups=plane)  28.8 us
    pallas_call x6, Pallas kernels, cross(): pl.pallas_call(functools.partial(cross_kernel, lat_local=lat_local, first...  17.5 us
    ppermute x10, waiting for transfers between devices, along(): return lax.ppermute(x, AXES, long[shift % SIDE])  14.1 us
    ppermute x10, starting transfers between devices, along(): return lax.ppermute(x, AXES, long[shift % SIDE])  14 us
    pallas_call x3, Pallas kernels, decode(): pl.pallas_call(last_kernel if finish else decode_kernel, out_shape=jax.Sh...  12.9 us
    all_to_all x1, starting transfers between devices, within_plane(): return lax.all_to_all(x, AXES, 0, 0, axis_index_groups=plane)  8.43 us
    dot_general x3, matrix products, project(): return jnp.dot(a, w, preferred_element_type=F32).astype(BF16)  8.17 us
    pallas_call x1, Pallas kernels, near_decode(): pl.pallas_call(near_kernel, out_shape=(jax.ShapeDtypeStruct((rows, column...  3.87 us
  transfers between devices with their start and end apart: 17, of which 10 were waited for; matrix products, arithmetic and copies ran while one was open for 6% of the time, Pallas kernels for 24%

profile of v7, /device:TPU:1, one launch (start us, length us, event | category | flops | bytes accessed | tf_op | source)
XLA Modules:
  0.0 135.7 jit_solution(11456346607999054760)
XLA Ops:
  0.0 0.0 copy-start
  0.0 2.5 %spread.1 = bf16[16,32,512]{2,1,0:T(8,128)(2,1)} custom-call(bf16[32,1024]{1,0:T(8,128)(2,1)} %l_ref.1, bf16[1024,512]{1,0:T(8,128)(2,1)} %w_ref.2), custom_call_target="tpu_custom_call" | custom-call | tf_op jit(solution)/shard_map/spread/pallas_call | solution.py:438
  2.5 8.4 %all-to-all-start = ((bf16[16,32,512]{2,1,0:T(8,128)(2,1)}), bf16[16,32,512]{2,1,0:T(8,128)(2,1)S(1)}, u32[]{:S(2)}, u32[]{:S(2)}) async-start(bf16[16,32,512]{2,1,0:T(8,128)(2,1)} %spread.1), calls=%async_computation | async-start | bytes 1048576 | tf_op jit(solution)/shard_map/all_to_all | solution.py:580
  11.0 0.0 copy-done
  11.0 3.5 %convolution_convert_fusion.1.refs_1_ = bf16[1024,512]{1,0:T(8,128)(2,1)} fusion(bf16[1024,1024]{1,0:T(8,128)(2,1)S(1)} %copy-done, bf16[1024,512]{1,0:T(8,128)(2,1)} %param.17), kind=kOutput, calls=%fused_computation.1 | convolution fusion | flops 1074266112 | bytes 4194304 | tf_op jit(solution)/shard_map/dot_general | solution.py:554
  14.5 0.1 pad_add_fusion.core_ref
  14.5 3.4 %convolution_convert_fusion.2.refs_0_ = bf16[1024,512]{1,0:T(8,128)(2,1)} fusion(bf16[1024,1024]{1,0:T(8,128)(2,1)S(1)} %copy-done, bf16[1024,512]{1,0:T(8,128)(2,1)} %param.16), kind=kOutput, calls=%fused_computation.2 | convolution fusion | flops 1074266112 | bytes 4194304 | tf_op jit(solution)/shard_map/dot_general | solution.py:554
  18.0 3.2 %all-to-all-done = bf16[16,32,512]{2,1,0:T(8,128)(2,1)S(1)} async-done(((bf16[16,32,512]{2,1,0:T(8,128)(2,1)}), bf16[16,32,512]{2,1,0:T(8,128)(2,1)S(1)}, u32[]{:S(2)}, u32[]{:S(2)}) %all-to-all-start) | async-done | bytes 524320 | tf_op jit(solution)/shard_map/all_to_all | solution.py:580
  21.2 1.1 collective-permute-start
  22.3 2.8 %collective-permute-start.1 = (bf16[512,512]{1,0:T(8,128)(2,1)S(1)}, bf16[512,512]{1,0:T(8,128)(2,1)S(1)}, u32[]{:S(2)}, u32[]{:S(2)}) collective-permute-start(bf16[512,512]{1,0:T(8,128)(2,1)S(1)} %bitcast.11), channel_id=1, source_target_pairs={{0,64},{1,17},{2,66},{3,19},{4,68},{5,21},{6,70},{7,23},{8,72},{9,... | collective-permute-start | bytes 1572872 | tf_op jit(solution)/shard_map/ppermute | solution.py:583
  25.1 1.0 collective-permute-start.2
  26.1 1.6 %load.1 = (bf16[1024,512]{1,0:T(8,128)(2,1)S(1)}, bf16[1024,512]{1,0:T(8,128)(2,1)S(1)}) custom-call(bf16[1024,512]{1,0:T(8,128)(2,1)} %convolution_convert_fusion.2.refs_0_, bf16[1024,512]{1,0:T(8,128)(2,1)} %convolution_convert_fusion.1.refs_1_), custom_call_target="tpu_custom_call" | custom-call | tf_op jit(solution)/shard_map/load/pallas_call | solution.py:388
  27.6 0.0 copy-done.1
  27.7 2.6 %cross.6.refs_0_ = bf16[16,80,128]{2,1,0:T(8,128)(2,1)S(1)} custom-call(s32[8]{0:T(128)S(1)} %copy-done.1, bf16[512,512]{1,0:T(8,128)(2,1)S(1)} %bitcast.13, bf16[1024,512]{1,0:T(8,128)(2,1)S(1)} %get-tuple-element.41.k_ref, bf16[1024,512]{1,0:T(8,128)(2,1)S(1)} %get-tuple-element.42.v_ref), custom_call_target="tpu_custom_call" | custom-call | flops 536870912 | bytes 4194304 | tf_op jit(solution)/shard_map/cross/pallas_call | solution.py:358
  30.2 0.6 collective-permute-done.q_ref
  30.8 3.9 %cross.7 = bf16[16,144,128]{2,1,0:T(8,128)(2,1)S(1)} custom-call(s32[8]{0:T(128)S(1)} %copy-done.1, bf16[512,512]{1,0:T(8,128)(2,1)S(1)} %collective-permute-done.q_ref, bf16[1024,512]{1,0:T(8,128)(2,1)S(1)} %get-tuple-element.41.k_ref, bf16[1024,512]{1,0:T(8,128)(2,1)S(1)} %get-tuple-element.42.v_ref), custom_call_target="tpu_custom_call" | custom-call | flops 1073741824 | bytes 4194304 | tf_op jit(solution)/shard_map/cross/pallas_call | solution.py:358
  34.7 2.9 %collective-permute-done.1.q_ref = bf16[512,512]{1,0:T(8,128)(2,1)S(1)} collective-permute-done((bf16[512,512]{1,0:T(8,128)(2,1)S(1)}, bf16[512,512]{1,0:T(8,128)(2,1)S(1)}, u32[]{:S(2)}, u32[]{:S(2)}) %collective-permute-start.1) | collective-permute-done | bytes 524320 | tf_op jit(solution)/shard_map/ppermute | solution.py:583
  37.6 3.9 %cross.8 = bf16[16,144,128]{2,1,0:T(8,128)(2,1)S(1)} custom-call(s32[8]{0:T(128)S(1)} %copy-done.1, bf16[512,512]{1,0:T(8,128)(2,1)S(1)} %collective-permute-done.1.q_ref, bf16[1024,512]{1,0:T(8,128)(2,1)S(1)} %get-tuple-element.41.k_ref, bf16[1024,512]{1,0:T(8,128)(2,1)S(1)} %get-tuple-element.42.v_ref), custom_call_target="tpu_custom_call" | custom-call | flops 1073741824 | bytes 4194304 | tf_op jit(solution)/shard_map/cross/pallas_call | solution.py:358
  41.5 4.3 %collective-permute-start.4 = (bf16[16,144,128]{2,1,0:T(8,128)(2,1)S(1)}, bf16[16,144,128]{2,1,0:T(8,128)(2,1)S(1)}, u32[]{:S(2)}, u32[]{:S(2)}) collective-permute-start(bf16[16,144,128]{2,1,0:T(8,128)(2,1)S(1)} %cross.8), channel_id=1, source_target_pairs={{0,64},{1,17},{2,66},{3,19},{4,68},{5,21},{6,70},{7,23},{8,72},{9,... | collective-permute-start | bytes 1769480 | tf_op jit(solution)/shard_map/ppermute | solution.py:583
  45.9 0.0 collective-permute-start.3
  45.9 0.0 collective-permute-done.2.q_ref
  45.9 2.2 %cross.9 = bf16[8,144,128]{2,1,0:T(8,128)(2,1)S(1)} custom-call(s32[8]{0:T(128)S(1)} %copy-done.1, bf16[512,512]{1,0:T(8,128)(2,1)S(1)} %collective-permute-done.2.q_ref, bf16[1024,512]{1,0:T(8,128)(2,1)S(1)} %get-tuple-element.41.k_ref, bf16[1024,512]{1,0:T(8,128)(2,1)S(1)} %get-tuple-element.42.v_ref), custom_call_target="tpu_custom_call" | custom-call | flops 536870912 | bytes 4194304 | tf_op jit(solution)/shard_map/cross/pallas_call | solution.py:358
  48.1 2.2 %cross.10 = bf16[8,144,128]{2,1,0:T(8,128)(2,1)S(1)} custom-call(s32[8]{0:T(128)S(1)} %copy-done.1, bf16[512,512]{1,0:T(8,128)(2,1)S(1)} %collective-permute-done.2.q_ref, bf16[1024,512]{1,0:T(8,128)(2,1)S(1)} %get-tuple-element.41.k_ref, bf16[1024,512]{1,0:T(8,128)(2,1)S(1)} %get-tuple-element.42.v_ref), custom_call_target="tpu_custom_call" | custom-call | flops 536870912 | bytes 4194304 | tf_op jit(solution)/shard_map/cross/pallas_call | solution.py:358
  50.3 1.5 %collective-permute-start.6 = (bf16[8,144,128]{2,1,0:T(8,128)(2,1)S(1)}, bf16[8,144,128]{2,1,0:T(8,128)(2,1)S(1)}, u32[]{:S(2)}, u32[]{:S(2)}) collective-permute-start(bf16[8,144,128]{2,1,0:T(8,128)(2,1)S(1)} %cross.10), channel_id=1, source_target_pairs={{0,32},{1,9},{2,34},{3,11},{4,36},{5,13},{6,38},{7,15},{8,40},{9,1... | collective-permute-start | bytes 884744 | tf_op jit(solution)/shard_map/ppermute | solution.py:583
  51.8 0.3 collective-permute-start.5
  52.1 2.6 %cross.11.refs_0_ = bf16[16,144,128]{2,1,0:T(8,128)(2,1)S(1)} custom-call(s32[8]{0:T(128)S(1)} %copy-done.1, bf16[512,512]{1,0:T(8,128)(2,1)S(1)} %bitcast.14, bf16[1024,512]{1,0:T(8,128)(2,1)S(1)} %get-tuple-element.41.k_ref, bf16[1024,512]{1,0:T(8,128)(2,1)S(1)} %get-tuple-element.42.v_ref, bf16[16,80,128]{2,1,0:T(8,128)(2,1)S(1)} %cross.6.refs_0_), custom_call_target="tpu_custom_call" | custom-call | flops 536870912 | bytes 4194304 | tf_op jit(solution)/shard_map/cross/pallas_call | solution.py:358
  54.7 0.0 copy-done.2
  54.7 1.2 convolution_convert_fusion.q_ref
  55.9 0.0 collective-permute-done.4.refs_2_
  55.9 0.0 collective-permute-done.3.refs_1_
  56.0 1.3 join.2.refs_0_
  57.2 0.2 collective-permute-done.6.refs_2_
  57.4 3.2 %collective-permute-done.5.refs_1_ = bf16[8,144,128]{2,1,0:T(8,128)(2,1)S(1)} collective-permute-done((bf16[8,144,128]{2,1,0:T(8,128)(2,1)S(1)}, bf16[8,144,128]{2,1,0:T(8,128)(2,1)S(1)}, u32[]{:S(2)}, u32[]{:S(2)}) %collective-permute-start.5) | collective-permute-done | bytes 294944 | tf_op jit(solution)/shard_map/ppermute | solution.py:583
  60.6 0.9 join.3
  61.5 14.5 %all_to_all.15.r_ref = bf16[16,144,128]{2,1,0:T(8,128)(2,1)S(1)} all-to-all(bf16[16,144,128]{2,1,0:T(8,128)(2,1)S(1)} %join.3), channel_id=1, replica_groups={{0,2,4,6,8,10,12,14,16,18,20,22,24,26,28,30},{32,34,36,38,40,42,44,46,4..., dimensions={0} | all-to-all | bytes 1179648 | tf_op jit(solution)/shard_map/all_to_all | solution.py:580
  76.0 2.7 %combine.1 = (f32[16,1024]{1,0:T(8,128)S(1)}, bf16[16,1024]{1,0:T(8,128)(2,1)S(1)}, bf16[1024,1024]{1,0:T(8,128)(2,1)S(1)}) custom-call(s32[2]{0:T(128)S(1)} %pad_add_fusion.core_ref, bf16[16,144,128]{2,1,0:T(8,128)(2,1)S(1)} %all_to_all.15.r_ref, bf16[512,1024]{1,0:T(8,128)(2,1)} %w_ref.3, bf16[1024,1024]{1,0:T(8,128)(2,1)} %mlp_ref.1), custom_call_target="tpu_custom_call" | custom-call | tf_op jit(solution)/shard_map/combine/pallas_call | solution.py:416
  78.7 3.2 %collective-permute-start.7 = (bf16[16,1024]{1,0:T(8,128)(2,1)S(1)}, bf16[16,1024]{1,0:T(8,128)(2,1)S(1)}, u32[]{:S(2)}, u32[]{:S(2)}) collective-permute-start(bf16[16,1024]{1,0:T(8,128)(2,1)S(1)} %get-tuple-element.55), channel_id=1, source_target_pairs={{0,1},{1,0},{2,3},{3,2},{4,5},{5,4},{6,7},{7,6},{8,9},{9,8},{10,11... | collective-permute-start | bytes 98312 | tf_op jit(solution)/shard_map/ppermute | solution.py:612
  81.9 0.9 collective-permute-done.7.recv_ref
  82.8 0.5 latent.1
  83.3 14.3 %all_to_all.16 = bf16[16,16,1024]{2,1,0:T(8,128)(2,1)S(1)} all-to-all(bf16[16,16,1024]{2,1,0:T(8,128)(2,1)S(1)} %latent.1), channel_id=1, replica_groups={{0,2,4,6,8,10,12,14,16,18,20,22,24,26,28,30},{32,34,36,38,40,42,44,46,4..., dimensions={0} | all-to-all | bytes 1048576 | tf_op jit(solution)/shard_map/all_to_all | solution.py:580
  97.6 0.4 collective-permute-start.8
  98.0 1.7 %collective-permute-start.10 = (bf16[256,1024]{1,0:T(8,128)(2,1)S(1)}, bf16[256,1024]{1,0:T(8,128)(2,1)S(1)}, u32[]{:S(2)}, u32[]{:S(2)}) collective-permute-start(bf16[256,1024]{1,0:T(8,128)(2,1)S(1)} %bitcast.16), channel_id=1, source_target_pairs={{0,96},{1,25},{2,98},{3,27},{4,100},{5,29},{6,102},{7,31},{8,104},... | collective-permute-start | bytes 1572872 | tf_op jit(solution)/shard_map/ppermute | solution.py:583
  99.7 0.0 collective-permute-start.9
  99.7 1.3 collective-permute-start.11
  101.0 0.0 collective-permute-done.8.swapped_ref
  101.0 2.7 %near_kv.1 = (bf16[512,1024]{1,0:T(8,128)(2,1)S(1)}, bf16[1024,512]{1,0:T(8,128)(2,1)S(1)}, bf16[1024,512]{1,0:T(8,128)(2,1)S(1)}, bf16[512,1024]{1,0:T(8,128)(2,1)S(1)}) custom-call(bf16[256,1024]{1,0:T(8,128)(2,1)S(1)} %bitcast.19, bf16[256,1024]{1,0:T(8,128)(2,1)S(1)} %collective-permute-done.8.swapped_ref, bf16[1024,512]{1,0:T(8,128)(2,1)} %k_ref.1, ...), custom_call_target="tpu_custom_call" | custom-call | flops 536870912 | bytes 4194304 | tf_op jit(solution)/shard_map/near_kv/pallas_call | solution.py:486
  103.7 3.9 %near_decode.1 = (f32[1024,512]{1,0:T(8,128)S(1)}, f32[1024,512]{1,0:T(8,128)S(1)}, f32[1024,512]{1,0:T(8,128)S(1)}) custom-call(bf16[1024,512]{1,0:T(8,128)(2,1)S(1)} %convolution_convert_fusion.q_ref, bf16[512,1024]{1,0:T(8,128)(2,1)S(1)} %get-tuple-element.57.kv_ref), custom_call_target="tpu_custom_call" | custom-call | flops 1073741824 | bytes 4194304 | tf_op jit(solution)/shard_map/near_decode/pallas_call | solution.py:506
  107.5 3.9 %collective-permute-done.10.refs_1_ = bf16[256,1024]{1,0:T(8,128)(2,1)S(1)} collective-permute-done((bf16[256,1024]{1,0:T(8,128)(2,1)S(1)}, bf16[256,1024]{1,0:T(8,128)(2,1)S(1)}, u32[]{:S(2)}, u32[]{:S(2)}) %collective-permute-start.10) | collective-permute-done | bytes 524320 | tf_op jit(solution)/shard_map/ppermute | solution.py:583
  111.5 3.4 %collective-permute-done.9.refs_0_ = bf16[256,1024]{1,0:T(8,128)(2,1)S(1)} collective-permute-done((bf16[256,1024]{1,0:T(8,128)(2,1)S(1)}, bf16[256,1024]{1,0:T(8,128)(2,1)S(1)}, u32[]{:S(2)}, u32[]{:S(2)}) %collective-permute-start.9) | collective-permute-done | bytes 524320 | tf_op jit(solution)/shard_map/ppermute | solution.py:583
  114.9 1.2 latent_kv.3.refs_3_
  116.1 0.0 collective-permute-done.11.refs_0_
  116.1 1.9 %collective-permute-start.14 = (bf16[256,1024]{1,0:T(8,128)(2,1)S(1)}, bf16[256,1024]{1,0:T(8,128)(2,1)S(1)}, u32[]{:S(2)}, u32[]{:S(2)}) collective-permute-start(bf16[256,1024]{1,0:T(8,128)(2,1)S(1)} %collective-permute-done.11.refs_0_), channel_id=1, source_target_pairs={{0,1},{1,0},{2,3},{3,2},{4,5},{5,4},{6,7},{7,6},{8,9},{9,8},{10,11... | collective-permute-start | bytes 1572872 | tf_op jit(solution)/shard_map/ppermute | solution.py:627
  118.0 0.1 collective-permute-start.12
  118.1 0.4 collective-permute-start.13
  118.5 1.0 collective-permute-done.14.refs_1_
  119.6 1.2 latent_kv.5.refs_5_
  120.8 0.0 collective-permute-done.12.refs_0_
  120.8 0.2 collective-permute-done.13.refs_1_
  121.1 1.2 latent_kv.4.refs_4_
  122.3 5.9 %decode.4 = bf16[512,1024]{1,0:T(8,128)(2,1)S(1)} custom-call(s32[1]{0:T(128)S(6)} %mul.12.base_ref, bf16[1024,512]{1,0:T(8,128)(2,1)S(1)} %convolution_convert_fusion.q_ref, f32[1024,512]{1,0:T(8,128)S(1)} %get-tuple-element.61.refs_0_, f32[1024,512]{1,0:T(8,128)S(1)} %get-tuple-element.62.refs_1_, f32[1024,512]{1,0:T(8,128)S(1)} %get-tuple-element.63.refs_2_, ...), custom_call_target="tpu_custom_call" | custom-call | flops 1610612736 | bytes 8388608 | tf_op jit(solution)/shard_map/decode/pallas_call | solution.py:532
  128.2 0.5 collective-permute-start.15
  128.7 2.9 %decode.3.refs_7_ = f32[256,1024]{1,0:T(8,128)S(1)} custom-call(s32[1]{0:T(128)S(6)} %mul.10.base_ref, bf16[1024,512]{1,0:T(8,128)(2,1)S(1)} %convolution_convert_fusion.q_ref, f32[1024,512]{1,0:T(8,128)S(1)} %get-tuple-element.61.refs_0_, f32[1024,512]{1,0:T(8,128)S(1)} %get-tuple-element.62.refs_1_, f32[1024,512]{1,0:T(8,128)S(1)} %get-tuple-element.63.refs_2_, ...), custom_call_target="tpu_custom_call" | custom-call | flops 805306368 | bytes 8388608 | tf_op jit(solution)/shard_map/decode/pallas_call | solution.py:532
  131.6 0.0 collective-permute-done.15.refs_8_
  131.6 4.1 %decode.5 = bf16[512,1024]{1,0:T(8,128)(2,1)} custom-call(s32[1]{0:T(128)S(6)} %sub.6.base_ref, bf16[1024,512]{1,0:T(8,128)(2,1)S(1)} %convolution_convert_fusion.q_ref, f32[1024,512]{1,0:T(8,128)S(1)} %get-tuple-element.61.refs_0_, f32[1024,512]{1,0:T(8,128)S(1)} %get-tuple-element.62.refs_1_, f32[1024,512]{1,0:T(8,128)S(1)} %get-tuple-element.63.refs_2_, ...), custom_call_target="tpu_custom_call" | custom-call | flops 805306368 | bytes 8388608 | tf_op jit(solution)/shard_map/decode/pallas_call | solution.py:532
  (2 shorter events, 0.0 us)
Async XLA Ops:
  0.0 11.0 %copy-start = (bf16[1024,1024]{1,0:T(8,128)(2,1)S(1)}, bf16[1024,1024]{1,0:T(8,128)(2,1)}, u32[]{:S(2)}) copy-start(bf16[1024,1024]{1,0:T(8,128)(2,1)} %param.12) | copy-start | bytes 6291460
  2.5 18.6 %all-to-all-start = ((bf16[16,32,512]{2,1,0:T(8,128)(2,1)}), bf16[16,32,512]{2,1,0:T(8,128)(2,1)S(1)}, u32[]{:S(2)}, u32[]{:S(2)}) async-start(bf16[16,32,512]{2,1,0:T(8,128)(2,1)} %spread.1), calls=%async_computation | async-start | bytes 1048576 | tf_op jit(solution)/shard_map/all_to_all | solution.py:580
  18.0 9.7 %copy-start.1 = (s32[8]{0:T(128)S(1)}, s32[8]{0:T(128)}, u32[]{:S(2)}) copy-start(s32[8]{0:T(128)} %valid_ref.11) | copy-start | bytes 100
  21.2 9.6 %collective-permute-start = (bf16[512,512]{1,0:T(8,128)(2,1)S(1)}, bf16[512,512]{1,0:T(8,128)(2,1)S(1)}, u32[]{:S(2)}, u32[]{:S(2)}) collective-permute-start(bf16[512,512]{1,0:T(8,128)(2,1)S(1)} %bitcast.10), channel_id=1, source_target_pairs={{0,32},{1,9},{2,34},{3,11},{4,36},{5,13},{6,38},{7,15},{8,40},{9,1... | collective-permute-start | bytes 1572872 | tf_op jit(solution)/shard_map/ppermute | solution.py:583
  22.3 15.3 %collective-permute-start.1 = (bf16[512,512]{1,0:T(8,128)(2,1)S(1)}, bf16[512,512]{1,0:T(8,128)(2,1)S(1)}, u32[]{:S(2)}, u32[]{:S(2)}) collective-permute-start(bf16[512,512]{1,0:T(8,128)(2,1)S(1)} %bitcast.11), channel_id=1, source_target_pairs={{0,64},{1,17},{2,66},{3,19},{4,68},{5,21},{6,70},{7,23},{8,72},{9,... | collective-permute-start | bytes 1572872 | tf_op jit(solution)/shard_map/ppermute | solution.py:583
  25.1 20.8 %collective-permute-start.2 = (bf16[512,512]{1,0:T(8,128)(2,1)S(1)}, bf16[512,512]{1,0:T(8,128)(2,1)S(1)}, u32[]{:S(2)}, u32[]{:S(2)}) collective-permute-start(bf16[512,512]{1,0:T(8,128)(2,1)S(1)} %bitcast.12), channel_id=1, source_target_pairs={{0,96},{1,25},{2,98},{3,27},{4,100},{5,29},{6,102},{7,31},{8,104},... | collective-permute-start | bytes 1572872 | tf_op jit(solution)/shard_map/ppermute | solution.py:583
  41.5 14.4 %collective-permute-start.4 = (bf16[16,144,128]{2,1,0:T(8,128)(2,1)S(1)}, bf16[16,144,128]{2,1,0:T(8,128)(2,1)S(1)}, u32[]{:S(2)}, u32[]{:S(2)}) collective-permute-start(bf16[16,144,128]{2,1,0:T(8,128)(2,1)S(1)} %cross.8), channel_id=1, source_target_pairs={{0,64},{1,17},{2,66},{3,19},{4,68},{5,21},{6,70},{7,23},{8,72},{9,... | collective-permute-start | bytes 1769480 | tf_op jit(solution)/shard_map/ppermute | solution.py:583
  45.9 10.1 %collective-permute-start.3 = (bf16[16,144,128]{2,1,0:T(8,128)(2,1)S(1)}, bf16[16,144,128]{2,1,0:T(8,128)(2,1)S(1)}, u32[]{:S(2)}, u32[]{:S(2)}) collective-permute-start(bf16[16,144,128]{2,1,0:T(8,128)(2,1)S(1)} %cross.7), channel_id=1, source_target_pairs={{0,96},{1,25},{2,98},{3,27},{4,100},{5,29},{6,102},{7,31},{8,104},... | collective-permute-start | bytes 1769480 | tf_op jit(solution)/shard_map/ppermute | solution.py:583
  50.3 4.3 %copy-start.2 = (bf16[1024,512]{1,0:T(8,128)(2,1)S(1)}, bf16[1024,512]{1,0:T(8,128)(2,1)}, u32[]{:S(2)}) copy-start(bf16[1024,512]{1,0:T(8,128)(2,1)} %param.22) | copy-start | bytes 3145732
  50.3 7.1 %collective-permute-start.6 = (bf16[8,144,128]{2,1,0:T(8,128)(2,1)S(1)}, bf16[8,144,128]{2,1,0:T(8,128)(2,1)S(1)}, u32[]{:S(2)}, u32[]{:S(2)}) collective-permute-start(bf16[8,144,128]{2,1,0:T(8,128)(2,1)S(1)} %cross.10), channel_id=1, source_target_pairs={{0,32},{1,9},{2,34},{3,11},{4,36},{5,13},{6,38},{7,15},{8,40},{9,1... | collective-permute-start | bytes 884744 | tf_op jit(solution)/shard_map/ppermute | solution.py:583
  51.8 8.8 %collective-permute-start.5 = (bf16[8,144,128]{2,1,0:T(8,128)(2,1)S(1)}, bf16[8,144,128]{2,1,0:T(8,128)(2,1)S(1)}, u32[]{:S(2)}, u32[]{:S(2)}) collective-permute-start(bf16[8,144,128]{2,1,0:T(8,128)(2,1)S(1)} %cross.9), channel_id=1, source_target_pairs={{0,32},{1,9},{2,34},{3,11},{4,36},{5,13},{6,38},{7,15},{8,40},{9,1... | collective-permute-start | bytes 884744 | tf_op jit(solution)/shard_map/ppermute | solution.py:583
  78.7 4.1 %collective-permute-start.7 = (bf16[16,1024]{1,0:T(8,128)(2,1)S(1)}, bf16[16,1024]{1,0:T(8,128)(2,1)S(1)}, u32[]{:S(2)}, u32[]{:S(2)}) collective-permute-start(bf16[16,1024]{1,0:T(8,128)(2,1)S(1)} %get-tuple-element.55), channel_id=1, source_target_pairs={{0,1},{1,0},{2,3},{3,2},{4,5},{5,4},{6,7},{7,6},{8,9},{9,8},{10,11... | collective-permute-start | bytes 98312 | tf_op jit(solution)/shard_map/ppermute | solution.py:612
  97.6 3.4 %collective-permute-start.8 = (bf16[256,1024]{1,0:T(8,128)(2,1)S(1)}, bf16[256,1024]{1,0:T(8,128)(2,1)S(1)}, u32[]{:S(2)}, u32[]{:S(2)}) collective-permute-start(bf16[256,1024]{1,0:T(8,128)(2,1)S(1)} %bitcast.15), channel_id=1, source_target_pairs={{0,1},{1,0},{2,3},{3,2},{4,5},{5,4},{6,7},{7,6},{8,9},{9,8},{10,11... | collective-permute-start | bytes 1572872 | tf_op jit(solution)/shard_map/ppermute | solution.py:619
  98.0 13.5 %collective-permute-start.10 = (bf16[256,1024]{1,0:T(8,128)(2,1)S(1)}, bf16[256,1024]{1,0:T(8,128)(2,1)S(1)}, u32[]{:S(2)}, u32[]{:S(2)}) collective-permute-start(bf16[256,1024]{1,0:T(8,128)(2,1)S(1)} %bitcast.16), channel_id=1, source_target_pairs={{0,96},{1,25},{2,98},{3,27},{4,100},{5,29},{6,102},{7,31},{8,104},... | collective-permute-start | bytes 1572872 | tf_op jit(solution)/shard_map/ppermute | solution.py:583
  99.7 15.2 %collective-permute-start.9 = (bf16[256,1024]{1,0:T(8,128)(2,1)S(1)}, bf16[256,1024]{1,0:T(8,128)(2,1)S(1)}, u32[]{:S(2)}, u32[]{:S(2)}) collective-permute-start(bf16[256,1024]{1,0:T(8,128)(2,1)S(1)} %bitcast.17), channel_id=1, source_target_pairs={{0,32},{1,9},{2,34},{3,11},{4,36},{5,13},{6,38},{7,15},{8,40},{9,1... | collective-permute-start | bytes 1572872 | tf_op jit(solution)/shard_map/ppermute | solution.py:583
  99.7 16.4 %collective-permute-start.11 = (bf16[256,1024]{1,0:T(8,128)(2,1)S(1)}, bf16[256,1024]{1,0:T(8,128)(2,1)S(1)}, u32[]{:S(2)}, u32[]{:S(2)}) collective-permute-start(bf16[256,1024]{1,0:T(8,128)(2,1)S(1)} %bitcast.18), channel_id=1, source_target_pairs={{0,64},{1,17},{2,66},{3,19},{4,68},{5,21},{6,70},{7,23},{8,72},{9,... | collective-permute-start | bytes 1572872 | tf_op jit(solution)/shard_map/ppermute | solution.py:583
  116.1 3.4 %collective-permute-start.14 = (bf16[256,1024]{1,0:T(8,128)(2,1)S(1)}, bf16[256,1024]{1,0:T(8,128)(2,1)S(1)}, u32[]{:S(2)}, u32[]{:S(2)}) collective-permute-start(bf16[256,1024]{1,0:T(8,128)(2,1)S(1)} %collective-permute-done.11.refs_0_), channel_id=1, source_target_pairs={{0,1},{1,0},{2,3},{3,2},{4,5},{5,4},{6,7},{7,6},{8,9},{9,8},{10,11... | collective-permute-start | bytes 1572872 | tf_op jit(solution)/shard_map/ppermute | solution.py:627
  118.0 2.8 %collective-permute-start.12 = (bf16[256,1024]{1,0:T(8,128)(2,1)S(1)}, bf16[256,1024]{1,0:T(8,128)(2,1)S(1)}, u32[]{:S(2)}, u32[]{:S(2)}) collective-permute-start(bf16[256,1024]{1,0:T(8,128)(2,1)S(1)} %collective-permute-done.9.refs_0_), channel_id=1, source_target_pairs={{0,1},{1,0},{2,3},{3,2},{4,5},{5,4},{6,7},{7,6},{8,9},{9,8},{10,11... | collective-permute-start | bytes 1572872 | tf_op jit(solution)/shard_map/ppermute | solution.py:624
  118.1 2.9 %collective-permute-start.13 = (bf16[256,1024]{1,0:T(8,128)(2,1)S(1)}, bf16[256,1024]{1,0:T(8,128)(2,1)S(1)}, u32[]{:S(2)}, u32[]{:S(2)}) collective-permute-start(bf16[256,1024]{1,0:T(8,128)(2,1)S(1)} %collective-permute-done.10.refs_1_), channel_id=1, source_target_pairs={{0,1},{1,0},{2,3},{3,2},{4,5},{5,4},{6,7},{7,6},{8,9},{9,8},{10,11... | collective-permute-start | bytes 1572872 | tf_op jit(solution)/shard_map/ppermute | solution.py:624
  128.2 3.4 %collective-permute-start.15 = (bf16[512,1024]{1,0:T(8,128)(2,1)S(1)}, bf16[512,1024]{1,0:T(8,128)(2,1)S(1)}, u32[]{:S(2)}, u32[]{:S(2)}) collective-permute-start(bf16[512,1024]{1,0:T(8,128)(2,1)S(1)} %decode.4), channel_id=1, source_target_pairs={{0,1},{1,0},{2,3},{3,2},{4,5},{5,4},{6,7},{7,6},{8,9},{9,8},{10,11... | collective-permute-start | bytes 3145736 | tf_op jit(solution)/shard_map/ppermute | solution.py:633

commit v8 on v7

--- a/solution.py
+++ b/solution.py
@@ -87,9 +87,21 @@
         use(i)
 
 
-def cross_kernel(valid_ref, q_ref, k_ref, v_ref, *refs, lat_local, first, heads):
+def row_blocks(count, body):
+    if count == 1:
+        body(0)
+    else:
+        lax.fori_loop(0, count, lambda i, _: (body(i), 0)[1], 0)
+
+
+def block_rows(i):
+    start = i * ROW_BLOCK
+    return pl.ds(start if isinstance(start, int) else pl.multiple_of(start, ROW_BLOCK), ROW_BLOCK)
+
+
+def cross_kernel(valid_ref, q_ref, k_ref, v_ref, *refs, lat_local, first, heads, block_at, blocks):
     *before, out_ref, s_ref = refs
-    rows = q_ref.shape[0]
+    rows = ROW_BLOCK
     owners = rows // lat_local
     all_heads = q_ref.shape[1] // HEAD_DIM
     done = first * lat_local
@@ -98,45 +110,49 @@
     valid = sum(valid_ref[i] for i in range(keys // BLK)) * BLK
     live = lax.broadcasted_iota(jnp.int32, (1, keys), 1) < valid
     bias = jnp.where(live, 0.0, MASKED)
-    lane = lax.broadcasted_iota(jnp.int32, (rows, HEAD_DIM), 1)
-    if before:
-        out_ref[:, :done, :] = before[0][:, :done, :]
-    tops = jnp.zeros((rows, HEAD_DIM), F32)
-    totals = jnp.ones((rows, HEAD_DIM), F32)
-
-    def columns(i):
-        return slice((first + i) * HEAD_DIM, (first + i + 1) * HEAD_DIM)
-
-    def score(i):
-        s_ref[i % 2] = nt_dot(q_ref[:, columns(i)], k_ref[:, columns(i)]) + bias
-
-    def use(i):
-        nonlocal tops, totals
-        s = s_ref[i % 2]
-        m = jnp.max(s, axis=1, keepdims=True)
-        p = jnp.exp2((s - m) * (SCALE * LOG2E))
-        total = jnp.sum(p, axis=1, keepdims=True)
-        o = jnp.dot(p.astype(BF16), v_ref[:, columns(i)], preferred_element_type=F32)
-        o = (o / total).astype(BF16)
-        top = (first + i) * lat_local
-        out_ref[:, top : top + lat_local, :] = o.reshape(owners, lat_local, HEAD_DIM)
-        mine = lane % all_heads == first + i
-        tops = jnp.where(mine, m, tops)
-        totals = jnp.where(mine, total, totals)
-
-    pipelined(heads, score, use)
-    hi, mid, low = bf16_pieces(tops * SCALE + jnp.log(totals))
-    place = lane // all_heads
-    packed = jnp.where(place == 0, hi, jnp.where(place == 1, mid, jnp.where(place == 2, low, 0.0)))
-    eye = lax.broadcasted_iota(jnp.int32, (LSE_ROWS, HEAD_DIM), 0)
-    eye = (eye == lax.broadcasted_iota(jnp.int32, (LSE_ROWS, HEAD_DIM), 1)).astype(BF16)
-    turned = nt_dot(eye, packed.astype(BF16)).astype(BF16)
-    for d in range(owners):
-        at = d * lat_local // HEAD_DIM * HEAD_DIM
-        rows_d = turned[:, at : at + HEAD_DIM]
+
+    def block(step):
+        lane = lax.broadcasted_iota(jnp.int32, (rows, HEAD_DIM), 1)
+        mine_rows = block_rows(block_at + step)
+        to = pl.ds(step * owners, owners)
         if before:
-            rows_d = rows_d + before[0][d, done : done + LSE_ROWS, :]
-        out_ref[d, span : span + LSE_ROWS, :] = rows_d
+            out_ref[to, :done, :] = before[0][to, :done, :]
+        stats = [jnp.zeros((rows, HEAD_DIM), F32), jnp.ones((rows, HEAD_DIM), F32)]
+
+        def columns(i):
+            return slice((first + i) * HEAD_DIM, (first + i + 1) * HEAD_DIM)
+
+        def score(i):
+            s_ref[i % 2] = nt_dot(q_ref[mine_rows, columns(i)], k_ref[:, columns(i)]) + bias
+
+        def use(i):
+            s = s_ref[i % 2]
+            m = jnp.max(s, axis=1, keepdims=True)
+            p = jnp.exp2((s - m) * (SCALE * LOG2E))
+            total = jnp.sum(p, axis=1, keepdims=True)
+            o = jnp.dot(p.astype(BF16), v_ref[:, columns(i)], preferred_element_type=F32)
+            o = (o / total).astype(BF16)
+            top = (first + i) * lat_local
+            out_ref[to, top : top + lat_local, :] = o.reshape(owners, lat_local, HEAD_DIM)
+            mine = lane % all_heads == first + i
+            stats[0] = jnp.where(mine, m, stats[0])
+            stats[1] = jnp.where(mine, total, stats[1])
+
+        pipelined(heads, score, use)
+        hi, mid, low = bf16_pieces(stats[0] * SCALE + jnp.log(stats[1]))
+        place = lane // all_heads
+        packed = jnp.where(place == 0, hi, jnp.where(place == 1, mid, jnp.where(place == 2, low, 0.0)))
+        eye = lax.broadcasted_iota(jnp.int32, (LSE_ROWS, HEAD_DIM), 0)
+        eye = (eye == lax.broadcasted_iota(jnp.int32, (LSE_ROWS, HEAD_DIM), 1)).astype(BF16)
+        turned = nt_dot(eye, packed.astype(BF16)).astype(BF16)
+        for d in range(owners):
+            at = d * lat_local // HEAD_DIM * HEAD_DIM
+            rows_d = turned[:, at : at + HEAD_DIM]
+            if before:
+                rows_d = rows_d + before[0][step * owners + d, done : done + LSE_ROWS, :]
+            out_ref[step * owners + d, span : span + LSE_ROWS, :] = rows_d
+
+    row_blocks(blocks, block)
 
 
 def load_kernel(*refs):
@@ -255,8 +271,8 @@
     write_kv(row_refs, v_ref, out_ref, k_ref.shape[1])
 
 
-def near_kv_kernel(near_ref, swapped_ref, k_ref, v_ref, p_ref, out_ref, k_out, v_out, p_out, sems):
-    pairs = ((k_ref, k_out), (v_ref, v_out), (p_ref, p_out))
+def near_kv_kernel(near_ref, swapped_ref, k_ref, v_ref, p_ref, q_ref, out_ref, k_out, v_out, p_out, q_out, sems):
+    pairs = ((k_ref, k_out), (v_ref, v_out), (p_ref, p_out), (q_ref, q_out))
     copies = [pltpu.make_async_copy(a, b, sems.at[i]) for i, (a, b) in enumerate(pairs)]
     for copy in copies:
         copy.start()
@@ -266,6 +282,7 @@
     copies[1].wait()
     write_kv(rows, v_out, out_ref, k_out.shape[1])
     copies[2].wait()
+    copies[3].wait()
 
 
 def head_columns(columns, h):
@@ -277,25 +294,30 @@
 
 def near_kernel(q_ref, kv_ref, sums_ref, tops_ref, totals_ref, s_ref):
     columns = q_ref.shape[1]
-    shape = (q_ref.shape[0], HEAD_DIM)
-
-    def score(h):
-        kc, _ = head_columns(columns, h)
-        s_ref[h % 2] = nt_dot(q_ref[:, kc], kv_ref[:, kc])
-
-    def use(h):
-        kc, vc = head_columns(columns, h)
-        s = s_ref[h % 2]
-        m = jnp.max(s, axis=1, keepdims=True)
-        p = jnp.exp2((s - m) * (SCALE * LOG2E))
-        sums_ref[:, kc] = jnp.dot(p.astype(BF16), kv_ref[:, vc], preferred_element_type=F32)
-        tops_ref[:, kc] = jnp.broadcast_to(m, shape)
-        totals_ref[:, kc] = jnp.broadcast_to(jnp.sum(p, axis=1, keepdims=True), shape)
-
-    pipelined(columns // HEAD_DIM, score, use)
-
-
-def attend(q_ref, carried_refs, kv_refs, w_ref, s_ref, o_ref):
+    shape = (ROW_BLOCK, HEAD_DIM)
+
+    def block(step):
+        rows = block_rows(step)
+
+        def score(h):
+            kc, _ = head_columns(columns, h)
+            s_ref[h % 2] = nt_dot(q_ref[rows, kc], kv_ref[:, kc])
+
+        def use(h):
+            kc, vc = head_columns(columns, h)
+            s = s_ref[h % 2]
+            m = jnp.max(s, axis=1, keepdims=True)
+            p = jnp.exp2((s - m) * (SCALE * LOG2E))
+            sums_ref[rows, kc] = jnp.dot(p.astype(BF16), kv_ref[:, vc], preferred_element_type=F32)
+            tops_ref[rows, kc] = jnp.broadcast_to(m, shape)
+            totals_ref[rows, kc] = jnp.broadcast_to(jnp.sum(p, axis=1, keepdims=True), shape)
+
+        pipelined(columns // HEAD_DIM, score, use)
+
+    row_blocks(q_ref.shape[0] // ROW_BLOCK, block)
+
+
+def attend(rows, q_ref, carried_refs, kv_refs, w_ref, s_ref, o_ref):
     sums_ref, tops_ref, totals_ref = carried_refs
     columns = q_ref.shape[1]
     spots = []
@@ -307,17 +329,17 @@
     def score(h):
         kc, _ = head_columns(columns, h)
         for spot, kv in zip(spots, kv_refs):
-            s_ref[h % 2, :, spot] = nt_dot(q_ref[:, kc], kv[:, kc])
+            s_ref[h % 2, :, spot] = nt_dot(q_ref[rows, kc], kv[:, kc])
 
     def use(h):
         kc, vc = head_columns(columns, h)
         s = s_ref[h % 2]
-        before = tops_ref[:, kc]
+        before = tops_ref[rows, kc]
         m = jnp.maximum(before, jnp.max(s, axis=1, keepdims=True))
         keep = jnp.exp2((before - m) * (SCALE * LOG2E))
         p = jnp.exp2((s - m[:, :1]) * (SCALE * LOG2E))
-        total = totals_ref[:, kc] * keep + jnp.sum(p, axis=1, keepdims=True)
-        o = sums_ref[:, kc] * keep
+        total = totals_ref[rows, kc] * keep + jnp.sum(p, axis=1, keepdims=True)
+        o = sums_ref[rows, kc] * keep
         pb = p.astype(BF16)
         for spot, kv in zip(spots, kv_refs):
             o = o + jnp.dot(pb[:, spot], kv[:, vc], preferred_element_type=F32)
@@ -329,19 +351,30 @@
 
 def decode_kernel(base_ref, q_ref, *refs):
     carried, (*kv_refs, w_ref, out_ref, s_ref, o_ref) = refs[:3], refs[3:]
-    out_ref[...] = attend(q_ref, carried, kv_refs, w_ref, s_ref, o_ref).astype(out_ref.dtype)
+
+    def block(step):
+        rows = block_rows(base_ref[0] + step)
+        terms = attend(rows, q_ref, carried, kv_refs, w_ref, s_ref, o_ref)
+        out_ref[block_rows(step), :] = terms.astype(out_ref.dtype)
+
+    row_blocks(out_ref.shape[0] // ROW_BLOCK, block)
 
 
 def last_kernel(base_ref, q_ref, *refs):
-    carried, (*kv_refs, w_ref, first_ref, recv_ref, out_ref, s_ref, o_ref) = refs[:3], refs[3:]
+    carried, (*kv_refs, w_ref, first_ref, recv_ref, out_ref, s_ref, o_ref, out_vmem, sems) = refs[:3], refs[3:]
     n = first_ref.shape[0]
-    out_ref[:n] = rms_norm(first_ref[...] + recv_ref[:n].astype(F32)).astype(out_ref.dtype)
-    terms = attend(q_ref, carried, kv_refs, w_ref, s_ref, o_ref)
-    out_ref[n:] = rms_norm(terms + recv_ref[n:].astype(F32)).astype(out_ref.dtype)
-
-
-def full_spec(array):
-    return pl.BlockSpec(array.shape, lambda *_: (0,) * array.ndim)
+
+    def leave(i, rows, terms):
+        out_vmem[rows, :] = rms_norm(terms + recv_ref[rows, :].astype(F32)).astype(BF16)
+        copy = pltpu.make_async_copy(out_vmem.at[rows, :], out_ref.at[rows, :], sems.at[i])
+        copy.start()
+        return copy
+
+    early = leave(0, pl.ds(0, n), first_ref[...])
+    terms = attend(block_rows(base_ref[0]), q_ref, carried, kv_refs, w_ref, s_ref, o_ref)
+    late = leave(1, pl.ds(n, ROW_BLOCK), terms)
+    early.wait()
+    late.wait()
 
 
 def params(limit=56 << 20):
@@ -349,27 +382,19 @@
 
 
 def cross(valid, q, k, v, lat_local, first, heads, before=None, block_at=0, blocks=None):
-    columns = q.shape[1]
+    blocks = q.shape[0] // ROW_BLOCK if blocks is None else blocks
+    lat = blocks * ROW_BLOCK
     tall = (first + heads) * lat_local + LSE_ROWS
-    block = min(ROW_BLOCK, q.shape[0])
-    blocks = q.shape[0] // block if blocks is None else blocks
-    lat = blocks * block
     extra = () if before is None else (before,)
-    return pl.pallas_call(
-        functools.partial(cross_kernel, lat_local=lat_local, first=first, heads=heads),
+    vmem = pl.BlockSpec(memory_space=pltpu.VMEM)
+    return pl.pallas_call(
+        functools.partial(
+            cross_kernel, lat_local=lat_local, first=first, heads=heads, block_at=block_at, blocks=blocks
+        ),
         out_shape=jax.ShapeDtypeStruct((lat // lat_local, tall, HEAD_DIM), BF16),
-        grid_spec=pltpu.PrefetchScalarGridSpec(
-            num_scalar_prefetch=1,
-            grid=(lat // block,),
-            in_specs=[
-                pl.BlockSpec((block, columns), lambda i, c: (block_at + i, 0)),
-                full_spec(k),
-                full_spec(v),
-                *[pl.BlockSpec((block // lat_local,) + x.shape[1:], lambda i, c: (i, 0, 0)) for x in extra],
-            ],
-            out_specs=pl.BlockSpec((block // lat_local, tall, HEAD_DIM), lambda i, c: (i, 0, 0)),
-            scratch_shapes=[pltpu.VMEM((2, block, k.shape[0]), F32)],
-        ),
+        in_specs=[pl.BlockSpec(memory_space=pltpu.SMEM)] + [vmem] * (3 + len(extra)),
+        out_specs=vmem,
+        scratch_shapes=[pltpu.VMEM((2, ROW_BLOCK, k.shape[0]), F32)],
         compiler_params=params(32 << 20),
         cost_estimate=pl.CostEstimate(
             flops=4 * lat * k.shape[0] * heads * HEAD_DIM,
@@ -479,7 +504,7 @@
     )(*rows, w_lkey, w_lvalue)
 
 
-def near_kv(near, swapped, w_lkey, w_lvalue, w_pout):
+def near_kv(near, swapped, w_lkey, w_lvalue, w_pout, queries):
     vmem = pl.BlockSpec(memory_space=pltpu.VMEM)
     hbm = pl.BlockSpec(memory_space=pltpu.HBM)
     rows = near.shape[0] + swapped.shape[0]
@@ -487,32 +512,28 @@
         near_kv_kernel,
         out_shape=[
             jax.ShapeDtypeStruct((rows, 2 * w_lkey.shape[1]), BF16),
-            *[jax.ShapeDtypeStruct(w.shape, BF16) for w in (w_lkey, w_lvalue, w_pout)],
+            *[jax.ShapeDtypeStruct(w.shape, BF16) for w in (w_lkey, w_lvalue, w_pout, queries)],
         ],
-        in_specs=[vmem, vmem, hbm, hbm, hbm],
-        out_specs=[vmem] * 4,
-        scratch_shapes=[pltpu.SemaphoreType.DMA((3,))],
+        in_specs=[vmem, vmem, hbm, hbm, hbm, hbm],
+        out_specs=[vmem] * 5,
+        scratch_shapes=[pltpu.SemaphoreType.DMA((4,))],
         compiler_params=params(24 << 20),
         cost_estimate=pl.CostEstimate(
             flops=4 * rows * w_lkey.size // 2, bytes_accessed=4 << 20, transcendentals=0
         ),
         name="near_kv",
-    )(near, swapped, *in_hbm(w_lkey, w_lvalue, w_pout))
+    )(near, swapped, *in_hbm(w_lkey, w_lvalue, w_pout, queries))
 
 
 def near_decode(q, kv):
     rows, columns = q.shape
-    block = ROW_BLOCK
+    vmem = pl.BlockSpec(memory_space=pltpu.VMEM)
     return pl.pallas_call(
         near_kernel,
-        out_shape=(
-            jax.ShapeDtypeStruct((rows, columns), F32),
-        )
-        * 3,
-        grid=(rows // block,),
-        in_specs=[pl.BlockSpec((block, columns), lambda i: (i, 0)), full_spec(kv)],
-        out_specs=(pl.BlockSpec((block, columns), lambda i: (i, 0)),) * 3,
-        scratch_shapes=[pltpu.VMEM((2, block, kv.shape[0]), F32)],
+        out_shape=(jax.ShapeDtypeStruct((rows, columns), F32),) * 3,
+        in_specs=[vmem] * 2,
+        out_specs=(vmem,) * 3,
+        scratch_shapes=[pltpu.VMEM((2, ROW_BLOCK, kv.shape[0]), F32)],
         compiler_params=params(24 << 20),
         cost_estimate=pl.CostEstimate(
             flops=4 * rows * columns * kv.shape[0], bytes_accessed=4 << 20, transcendentals=4 * rows * kv.shape[0]
@@ -524,30 +545,26 @@
 def decode(base, blocks, q, carried, kvs, w_pout, dtype, finish=()):
     columns = q.shape[1]
     width = w_pout.shape[1]
-    block = ROW_BLOCK
-    rows = blocks * block
+    rows = blocks * ROW_BLOCK
     out_rows = finish[1].shape[0] if finish else rows
-    out_block = out_rows if finish else block
     keys = sum(kv.shape[0] for kv in kvs)
+    vmem = pl.BlockSpec(memory_space=pltpu.VMEM)
+    scratch = [pltpu.VMEM((2, ROW_BLOCK, keys), F32), pltpu.VMEM((ROW_BLOCK, columns), BF16)]
+    if finish:
+        scratch += [pltpu.VMEM((out_rows, width), BF16), pltpu.SemaphoreType.DMA((2,))]
+    operands = (q, *carried, *kvs, w_pout, *finish)
     return pl.pallas_call(
         last_kernel if finish else decode_kernel,
         out_shape=jax.ShapeDtypeStruct((out_rows, width), dtype),
-        grid_spec=pltpu.PrefetchScalarGridSpec(
-            num_scalar_prefetch=1,
-            grid=(blocks,),
-            in_specs=[
-                *[pl.BlockSpec((block, x.shape[1]), lambda i, b: (b[0] + i, 0)) for x in (q, *carried)],
-                *[full_spec(x) for x in (*kvs, w_pout, *finish)],
-            ],
-            out_specs=pl.BlockSpec((out_block, width), lambda i, b: (i, 0)),
-            scratch_shapes=[pltpu.VMEM((2, block, keys), F32), pltpu.VMEM((block, columns), BF16)],
-        ),
-        compiler_params=params(36 << 20),
+        in_specs=[pl.BlockSpec(memory_space=pltpu.SMEM)] + [vmem] * len(operands),
+        out_specs=pl.BlockSpec(memory_space=pltpu.HBM) if finish else vmem,
+        scratch_shapes=scratch,
+        compiler_params=params(30 << 20),
         cost_estimate=pl.CostEstimate(
             flops=4 * rows * columns * keys, bytes_accessed=8 << 20, transcendentals=4 * rows * keys
         ),
         name="decode",
-    )(base, q, *carried, *kvs, w_pout, *finish)
+    )(base, *operands)
 
 
 def project(a, w):
@@ -617,7 +634,9 @@
     for s in FAR_ORDER:
         far.append(along(near, s))
     near_swapped = lax.ppermute(near, "head", swap)
-    kv, w_lkey, w_lvalue, w_pout = near_kv(near, near_swapped, w_lkey, w_lvalue, w_pout)
+    kv, w_lkey, w_lvalue, w_pout, pos_queries = near_kv(
+        near, near_swapped, w_lkey, w_lvalue, w_pout, pos_queries
+    )
     carried = near_decode(pos_queries, kv)
     slow, *quick = far
     carried, quick = lax.optimization_barrier((carried, quick))

time: 136 us -> 136 us (level)
  transfers between devices with their start and end apart: 17 -> 17, of which waited for: 10 -> 9; matrix products, arithmetic and copies ran while one was open for 6% -> 7% of each run, Pallas kernels for 24% -> 24%
where the time goes in v8:
time: 136 us
  Pallas kernels  50 us (37%)
  starting transfers between devices  30 us (22%)
  blocking collectives  27.8 us (20%)
  waiting for transfers between devices  18.5 us (14%)
  matrix products  9.14 us (7%)
    all_to_all x2, blocking collectives, within_plane(): return lax.all_to_all(x, AXES, 0, 0, axis_index_groups=plane)  27.8 us
    pallas_call x6, Pallas kernels, cross(): pl.pallas_call(functools.partial(cross_kernel, lat_local=lat_local, first...  17.5 us
    ppermute x10, starting transfers between devices, along(): return lax.ppermute(x, AXES, long[shift % SIDE])  13.9 us
    ppermute x10, waiting for transfers between devices, along(): return lax.ppermute(x, AXES, long[shift % SIDE])  13.2 us
    pallas_call x3, Pallas kernels, decode(): pl.pallas_call(last_kernel if finish else decode_kernel, out_shape=jax.Sh...  12.8 us
    dot_general x3, matrix products, project(): return jnp.dot(a, w, preferred_element_type=F32).astype(BF16)  9.14 us
    all_to_all x1, starting transfers between devices, within_plane(): return lax.all_to_all(x, AXES, 0, 0, axis_index_groups=plane)  8.43 us
    ppermute x1, starting transfers between devices, per_device(): recv = lax.ppermute(other, 'head', swap)  4.28 us
  transfers between devices with their start and end apart: 17, of which 9 were waited for; matrix products, arithmetic and copies ran while one was open for 7% of the time, Pallas kernels for 24%

profile of v8, /device:TPU:1, one launch (start us, length us, event | category | flops | bytes accessed | tf_op | source)
XLA Modules:
  0.0 135.8 jit_solution(12832520112632532589)
XLA Ops:
  0.0 0.0 copy-start
  0.0 2.5 %spread.1 = bf16[16,32,512]{2,1,0:T(8,128)(2,1)} custom-call(bf16[32,1024]{1,0:T(8,128)(2,1)} %l_ref.1, bf16[1024,512]{1,0:T(8,128)(2,1)} %w_ref.2), custom_call_target="tpu_custom_call" | custom-call | tf_op jit(solution)/shard_map/spread/pallas_call | solution.py:463
  2.5 8.4 %all-to-all-start = ((bf16[16,32,512]{2,1,0:T(8,128)(2,1)}), bf16[16,32,512]{2,1,0:T(8,128)(2,1)S(1)}, u32[]{:S(2)}, u32[]{:S(2)}) async-start(bf16[16,32,512]{2,1,0:T(8,128)(2,1)} %spread.1), calls=%async_computation | async-start | bytes 1048576 | tf_op jit(solution)/shard_map/all_to_all | solution.py:597
  11.0 0.0 copy-done
  11.0 3.5 %convolution_convert_fusion.1.refs_1_ = bf16[1024,512]{1,0:T(8,128)(2,1)} fusion(bf16[1024,1024]{1,0:T(8,128)(2,1)S(1)} %copy-done, bf16[1024,512]{1,0:T(8,128)(2,1)} %param.17), kind=kOutput, calls=%fused_computation.1 | convolution fusion | flops 1074266112 | bytes 4194304 | tf_op jit(solution)/shard_map/dot_general | solution.py:571
  14.5 0.1 pad_add_fusion.core_ref
  14.5 3.4 %convolution_convert_fusion.2.refs_0_ = bf16[1024,512]{1,0:T(8,128)(2,1)} fusion(bf16[1024,1024]{1,0:T(8,128)(2,1)S(1)} %copy-done, bf16[1024,512]{1,0:T(8,128)(2,1)} %param.16), kind=kOutput, calls=%fused_computation.2 | convolution fusion | flops 1074266112 | bytes 4194304 | tf_op jit(solution)/shard_map/dot_general | solution.py:571
  18.0 3.2 %all-to-all-done = bf16[16,32,512]{2,1,0:T(8,128)(2,1)S(1)} async-done(((bf16[16,32,512]{2,1,0:T(8,128)(2,1)}), bf16[16,32,512]{2,1,0:T(8,128)(2,1)S(1)}, u32[]{:S(2)}, u32[]{:S(2)}) %all-to-all-start) | async-done | bytes 524320 | tf_op jit(solution)/shard_map/all_to_all | solution.py:597
  21.2 1.1 collective-permute-start
  22.3 2.8 %collective-permute-start.1 = (bf16[512,512]{1,0:T(8,128)(2,1)S(1)}, bf16[512,512]{1,0:T(8,128)(2,1)S(1)}, u32[]{:S(2)}, u32[]{:S(2)}) collective-permute-start(bf16[512,512]{1,0:T(8,128)(2,1)S(1)} %bitcast.11), channel_id=1, source_target_pairs={{0,64},{1,17},{2,66},{3,19},{4,68},{5,21},{6,70},{7,23},{8,72},{9,... | collective-permute-start | bytes 1572872 | tf_op jit(solution)/shard_map/ppermute | solution.py:600
  25.1 1.0 collective-permute-start.2
  26.1 1.6 %load.1 = (bf16[1024,512]{1,0:T(8,128)(2,1)S(1)}, bf16[1024,512]{1,0:T(8,128)(2,1)S(1)}) custom-call(bf16[1024,512]{1,0:T(8,128)(2,1)} %convolution_convert_fusion.2.refs_0_, bf16[1024,512]{1,0:T(8,128)(2,1)} %convolution_convert_fusion.1.refs_1_), custom_call_target="tpu_custom_call" | custom-call | tf_op jit(solution)/shard_map/load/pallas_call | solution.py:413
  27.6 0.0 copy-done.1
  27.7 2.6 %cross.6.refs_0_ = bf16[16,80,128]{2,1,0:T(8,128)(2,1)S(1)} custom-call(s32[8]{0:T(128)S(1)} %copy-done.1, bf16[512,512]{1,0:T(8,128)(2,1)S(1)} %bitcast.13, bf16[1024,512]{1,0:T(8,128)(2,1)S(1)} %get-tuple-element.43.k_ref, bf16[1024,512]{1,0:T(8,128)(2,1)S(1)} %get-tuple-element.44.v_ref), custom_call_target="tpu_custom_call" | custom-call | flops 536870912 | bytes 4194304 | tf_op jit(solution)/shard_map/cross/pallas_call | solution.py:390
  30.2 0.6 collective-permute-done.q_ref
  30.8 3.9 %cross.7 = bf16[16,144,128]{2,1,0:T(8,128)(2,1)S(1)} custom-call(s32[8]{0:T(128)S(1)} %copy-done.1, bf16[512,512]{1,0:T(8,128)(2,1)S(1)} %collective-permute-done.q_ref, bf16[1024,512]{1,0:T(8,128)(2,1)S(1)} %get-tuple-element.43.k_ref, bf16[1024,512]{1,0:T(8,128)(2,1)S(1)} %get-tuple-element.44.v_ref), custom_call_target="tpu_custom_call" | custom-call | flops 1073741824 | bytes 4194304 | tf_op jit(solution)/shard_map/cross/pallas_call | solution.py:390
  34.7 2.9 %collective-permute-done.1.q_ref = bf16[512,512]{1,0:T(8,128)(2,1)S(1)} collective-permute-done((bf16[512,512]{1,0:T(8,128)(2,1)S(1)}, bf16[512,512]{1,0:T(8,128)(2,1)S(1)}, u32[]{:S(2)}, u32[]{:S(2)}) %collective-permute-start.1) | collective-permute-done | bytes 524320 | tf_op jit(solution)/shard_map/ppermute | solution.py:600
  37.6 3.9 %cross.8 = bf16[16,144,128]{2,1,0:T(8,128)(2,1)S(1)} custom-call(s32[8]{0:T(128)S(1)} %copy-done.1, bf16[512,512]{1,0:T(8,128)(2,1)S(1)} %collective-permute-done.1.q_ref, bf16[1024,512]{1,0:T(8,128)(2,1)S(1)} %get-tuple-element.43.k_ref, bf16[1024,512]{1,0:T(8,128)(2,1)S(1)} %get-tuple-element.44.v_ref), custom_call_target="tpu_custom_call" | custom-call | flops 1073741824 | bytes 4194304 | tf_op jit(solution)/shard_map/cross/pallas_call | solution.py:390
  41.5 4.3 %collective-permute-start.4 = (bf16[16,144,128]{2,1,0:T(8,128)(2,1)S(1)}, bf16[16,144,128]{2,1,0:T(8,128)(2,1)S(1)}, u32[]{:S(2)}, u32[]{:S(2)}) collective-permute-start(bf16[16,144,128]{2,1,0:T(8,128)(2,1)S(1)} %cross.8), channel_id=1, source_target_pairs={{0,64},{1,17},{2,66},{3,19},{4,68},{5,21},{6,70},{7,23},{8,72},{9,... | collective-permute-start | bytes 1769480 | tf_op jit(solution)/shard_map/ppermute | solution.py:600
  45.9 0.0 collective-permute-start.3
  45.9 0.0 collective-permute-done.2.q_ref
  45.9 2.2 %cross.9 = bf16[8,144,128]{2,1,0:T(8,128)(2,1)S(1)} custom-call(s32[8]{0:T(128)S(1)} %copy-done.1, bf16[512,512]{1,0:T(8,128)(2,1)S(1)} %collective-permute-done.2.q_ref, bf16[1024,512]{1,0:T(8,128)(2,1)S(1)} %get-tuple-element.43.k_ref, bf16[1024,512]{1,0:T(8,128)(2,1)S(1)} %get-tuple-element.44.v_ref), custom_call_target="tpu_custom_call" | custom-call | flops 536870912 | bytes 4194304 | tf_op jit(solution)/shard_map/cross/pallas_call | solution.py:390
  48.1 2.2 %cross.10 = bf16[8,144,128]{2,1,0:T(8,128)(2,1)S(1)} custom-call(s32[8]{0:T(128)S(1)} %copy-done.1, bf16[512,512]{1,0:T(8,128)(2,1)S(1)} %collective-permute-done.2.q_ref, bf16[1024,512]{1,0:T(8,128)(2,1)S(1)} %get-tuple-element.43.k_ref, bf16[1024,512]{1,0:T(8,128)(2,1)S(1)} %get-tuple-element.44.v_ref), custom_call_target="tpu_custom_call" | custom-call | flops 536870912 | bytes 4194304 | tf_op jit(solution)/shard_map/cross/pallas_call | solution.py:390
  50.3 1.5 %collective-permute-start.6 = (bf16[8,144,128]{2,1,0:T(8,128)(2,1)S(1)}, bf16[8,144,128]{2,1,0:T(8,128)(2,1)S(1)}, u32[]{:S(2)}, u32[]{:S(2)}) collective-permute-start(bf16[8,144,128]{2,1,0:T(8,128)(2,1)S(1)} %cross.10), channel_id=1, source_target_pairs={{0,32},{1,9},{2,34},{3,11},{4,36},{5,13},{6,38},{7,15},{8,40},{9,1... | collective-permute-start | bytes 884744 | tf_op jit(solution)/shard_map/ppermute | solution.py:600
  51.8 0.3 collective-permute-start.5
  52.1 2.6 %cross.11.refs_0_ = bf16[16,144,128]{2,1,0:T(8,128)(2,1)S(1)} custom-call(s32[8]{0:T(128)S(1)} %copy-done.1, bf16[512,512]{1,0:T(8,128)(2,1)S(1)} %bitcast.14, bf16[1024,512]{1,0:T(8,128)(2,1)S(1)} %get-tuple-element.43.k_ref, bf16[1024,512]{1,0:T(8,128)(2,1)S(1)} %get-tuple-element.44.v_ref, bf16[16,80,128]{2,1,0:T(8,128)(2,1)S(1)} %cross.6.refs_0_), custom_call_target="tpu_custom_call" | custom-call | flops 536870912 | bytes 4194304 | tf_op jit(solution)/shard_map/cross/pallas_call | solution.py:390
  54.7 0.0 copy-done.2
  54.7 2.2 %convolution_convert_fusion.q_ref = bf16[1024,512]{1,0:T(8,128)(2,1)} fusion(bf16[1024,1024]{1,0:T(8,128)(2,1)S(1)} %copy-done, bf16[1024,512]{1,0:T(8,128)(2,1)S(1)} %copy-done.2), kind=kOutput, calls=%fused_computation | convolution fusion | flops 1074266112 | bytes 4194304 | tf_op jit(solution)/shard_map/dot_general | solution.py:571
  56.9 0.0 collective-permute-done.4.refs_2_
  56.9 0.0 collective-permute-done.3.refs_1_
  56.9 1.3 join.2.refs_0_
  58.2 0.0 collective-permute-done.6.refs_2_
  58.2 2.4 %collective-permute-done.5.refs_1_ = bf16[8,144,128]{2,1,0:T(8,128)(2,1)S(1)} collective-permute-done((bf16[8,144,128]{2,1,0:T(8,128)(2,1)S(1)}, bf16[8,144,128]{2,1,0:T(8,128)(2,1)S(1)}, u32[]{:S(2)}, u32[]{:S(2)}) %collective-permute-start.5) | collective-permute-done | bytes 294944 | tf_op jit(solution)/shard_map/ppermute | solution.py:600
  60.6 0.9 join.3
  61.5 13.4 %all_to_all.15.r_ref = bf16[16,144,128]{2,1,0:T(8,128)(2,1)S(1)} all-to-all(bf16[16,144,128]{2,1,0:T(8,128)(2,1)S(1)} %join.3), channel_id=1, replica_groups={{0,2,4,6,8,10,12,14,16,18,20,22,24,26,28,30},{32,34,36,38,40,42,44,46,4..., dimensions={0} | all-to-all | bytes 1179648 | tf_op jit(solution)/shard_map/all_to_all | solution.py:597
  74.9 2.7 %combine.1 = (f32[16,1024]{1,0:T(8,128)S(1)}, bf16[16,1024]{1,0:T(8,128)(2,1)S(1)}, bf16[1024,1024]{1,0:T(8,128)(2,1)S(1)}) custom-call(s32[2]{0:T(128)S(1)} %pad_add_fusion.core_ref, bf16[16,144,128]{2,1,0:T(8,128)(2,1)S(1)} %all_to_all.15.r_ref, bf16[512,1024]{1,0:T(8,128)(2,1)} %w_ref.3, bf16[1024,1024]{1,0:T(8,128)(2,1)} %mlp_ref.1), custom_call_target="tpu_custom_call" | custom-call | tf_op jit(solution)/shard_map/combine/pallas_call | solution.py:441
  77.6 4.3 %collective-permute-start.7 = (bf16[16,1024]{1,0:T(8,128)(2,1)S(1)}, bf16[16,1024]{1,0:T(8,128)(2,1)S(1)}, u32[]{:S(2)}, u32[]{:S(2)}) collective-permute-start(bf16[16,1024]{1,0:T(8,128)(2,1)S(1)} %get-tuple-element.55), channel_id=1, source_target_pairs={{0,1},{1,0},{2,3},{3,2},{4,5},{5,4},{6,7},{7,6},{8,9},{9,8},{10,11... | collective-permute-start | bytes 98312 | tf_op jit(solution)/shard_map/ppermute | solution.py:629
  81.9 0.9 collective-permute-done.7.recv_ref
  82.8 0.5 latent.1
  83.3 14.3 %all_to_all.16 = bf16[16,16,1024]{2,1,0:T(8,128)(2,1)S(1)} all-to-all(bf16[16,16,1024]{2,1,0:T(8,128)(2,1)S(1)} %latent.1), channel_id=1, replica_groups={{0,2,4,6,8,10,12,14,16,18,20,22,24,26,28,30},{32,34,36,38,40,42,44,46,4..., dimensions={0} | all-to-all | bytes 1048576 | tf_op jit(solution)/shard_map/all_to_all | solution.py:597
  97.6 0.4 collective-permute-start.8
  98.0 1.7 %collective-permute-start.10 = (bf16[256,1024]{1,0:T(8,128)(2,1)S(1)}, bf16[256,1024]{1,0:T(8,128)(2,1)S(1)}, u32[]{:S(2)}, u32[]{:S(2)}) collective-permute-start(bf16[256,1024]{1,0:T(8,128)(2,1)S(1)} %bitcast.16), channel_id=1, source_target_pairs={{0,96},{1,25},{2,98},{3,27},{4,100},{5,29},{6,102},{7,31},{8,104},... | collective-permute-start | bytes 1572872 | tf_op jit(solution)/shard_map/ppermute | solution.py:600
  99.6 0.0 collective-permute-start.9
  99.7 1.3 collective-permute-start.11
  100.9 0.0 collective-permute-done.8.swapped_ref
  100.9 2.7 %near_kv.1 = (bf16[512,1024]{1,0:T(8,128)(2,1)S(1)}, bf16[1024,512]{1,0:T(8,128)(2,1)S(1)}, bf16[1024,512]{1,0:T(8,128)(2,1)S(1)}, bf16[512,1024]{1,0:T(8,128)(2,1)S(1)}, bf16[1024,512]{1,0:T(8,128)(2,1)S(1)}) custom-call(bf16[256,1024]{1,0:T(8,128)(2,1)S(1)} %bitcast.19, bf16[256,1024]{1,0:T(8,128)(2,1)S(1)} %collective-permute-done.8.swapped_ref, ...), custom_call_target="tpu_custom_call" | custom-call | flops 536870912 | bytes 4194304 | tf_op jit(solution)/shard_map/near_kv/pallas_call | solution.py:511
  103.6 3.8 %near_decode.1 = (f32[1024,512]{1,0:T(8,128)S(1)}, f32[1024,512]{1,0:T(8,128)S(1)}, f32[1024,512]{1,0:T(8,128)S(1)}) custom-call(bf16[1024,512]{1,0:T(8,128)(2,1)S(1)} %get-tuple-element.58.q_ref, bf16[512,1024]{1,0:T(8,128)(2,1)S(1)} %get-tuple-element.59.kv_ref), custom_call_target="tpu_custom_call" | custom-call | flops 1073741824 | bytes 4194304 | tf_op jit(solution)/shard_map/near_decode/pallas_call | solution.py:531
  107.5 3.9 %collective-permute-done.10.refs_1_ = bf16[256,1024]{1,0:T(8,128)(2,1)S(1)} collective-permute-done((bf16[256,1024]{1,0:T(8,128)(2,1)S(1)}, bf16[256,1024]{1,0:T(8,128)(2,1)S(1)}, u32[]{:S(2)}, u32[]{:S(2)}) %collective-permute-start.10) | collective-permute-done | bytes 524320 | tf_op jit(solution)/shard_map/ppermute | solution.py:600
  111.4 3.4 %collective-permute-done.9.refs_0_ = bf16[256,1024]{1,0:T(8,128)(2,1)S(1)} collective-permute-done((bf16[256,1024]{1,0:T(8,128)(2,1)S(1)}, bf16[256,1024]{1,0:T(8,128)(2,1)S(1)}, u32[]{:S(2)}, u32[]{:S(2)}) %collective-permute-start.9) | collective-permute-done | bytes 524320 | tf_op jit(solution)/shard_map/ppermute | solution.py:600
  114.8 1.2 latent_kv.3.refs_3_
  116.1 0.0 collective-permute-done.11.refs_0_
  116.1 2.0 %collective-permute-start.14 = (bf16[256,1024]{1,0:T(8,128)(2,1)S(1)}, bf16[256,1024]{1,0:T(8,128)(2,1)S(1)}, u32[]{:S(2)}, u32[]{:S(2)}) collective-permute-start(bf16[256,1024]{1,0:T(8,128)(2,1)S(1)} %collective-permute-done.11.refs_0_), channel_id=1, source_target_pairs={{0,1},{1,0},{2,3},{3,2},{4,5},{5,4},{6,7},{7,6},{8,9},{9,8},{10,11... | collective-permute-start | bytes 1572872 | tf_op jit(solution)/shard_map/ppermute | solution.py:646
  118.0 0.1 collective-permute-start.12
  118.1 0.4 collective-permute-start.13
  118.5 1.0 collective-permute-done.14.refs_1_
  119.6 1.2 latent_kv.5.refs_5_
  120.8 0.0 collective-permute-done.12.refs_0_
  120.8 0.2 collective-permute-done.13.refs_1_
  121.1 1.2 latent_kv.4.refs_4_
  122.3 5.9 %decode.4 = bf16[512,1024]{1,0:T(8,128)(2,1)S(1)} custom-call(s32[1]{0:T(128)S(6)} %mul.12.base_ref, bf16[1024,512]{1,0:T(8,128)(2,1)S(1)} %get-tuple-element.58.q_ref, f32[1024,512]{1,0:T(8,128)S(1)} %get-tuple-element.63.refs_0_, f32[1024,512]{1,0:T(8,128)S(1)} %get-tuple-element.64.refs_1_, f32[1024,512]{1,0:T(8,128)S(1)} %get-tuple-element.65.refs_2_, ...), custom_call_target="tpu_custom_call" | custom-call | flops 1610612736 | bytes 8388608 | tf_op jit(solution)/shard_map/decode/pallas_call | solution.py:556
  128.2 0.5 collective-permute-start.15
  128.6 2.9 %decode.3.refs_7_ = f32[256,1024]{1,0:T(8,128)S(1)} custom-call(s32[1]{0:T(128)S(6)} %mul.10.base_ref, bf16[1024,512]{1,0:T(8,128)(2,1)S(1)} %get-tuple-element.58.q_ref, f32[1024,512]{1,0:T(8,128)S(1)} %get-tuple-element.63.refs_0_, f32[1024,512]{1,0:T(8,128)S(1)} %get-tuple-element.64.refs_1_, f32[1024,512]{1,0:T(8,128)S(1)} %get-tuple-element.65.refs_2_, ...), custom_call_target="tpu_custom_call" | custom-call | flops 805306368 | bytes 8388608 | tf_op jit(solution)/shard_map/decode/pallas_call | solution.py:556
  131.6 0.0 collective-permute-done.15.refs_8_
  131.6 4.0 %decode.5 = bf16[512,1024]{1,0:T(8,128)(2,1)} custom-call(s32[1]{0:T(128)S(6)} %sub.6.base_ref, bf16[1024,512]{1,0:T(8,128)(2,1)S(1)} %get-tuple-element.58.q_ref, f32[1024,512]{1,0:T(8,128)S(1)} %get-tuple-element.63.refs_0_, f32[1024,512]{1,0:T(8,128)S(1)} %get-tuple-element.64.refs_1_, f32[1024,512]{1,0:T(8,128)S(1)} %get-tuple-element.65.refs_2_, ...), custom_call_target="tpu_custom_call" | custom-call | flops 805306368 | bytes 8388608 | tf_op jit(solution)/shard_map/decode/pallas_call | solution.py:556
  (2 shorter events, 0.0 us)
Async XLA Ops:
  0.0 11.0 %copy-start = (bf16[1024,1024]{1,0:T(8,128)(2,1)S(1)}, bf16[1024,1024]{1,0:T(8,128)(2,1)}, u32[]{:S(2)}) copy-start(bf16[1024,1024]{1,0:T(8,128)(2,1)} %param.12) | copy-start | bytes 6291460
  2.5 18.6 %all-to-all-start = ((bf16[16,32,512]{2,1,0:T(8,128)(2,1)}), bf16[16,32,512]{2,1,0:T(8,128)(2,1)S(1)}, u32[]{:S(2)}, u32[]{:S(2)}) async-start(bf16[16,32,512]{2,1,0:T(8,128)(2,1)} %spread.1), calls=%async_computation | async-start | bytes 1048576 | tf_op jit(solution)/shard_map/all_to_all | solution.py:597
  18.0 9.7 %copy-start.1 = (s32[8]{0:T(128)S(1)}, s32[8]{0:T(128)}, u32[]{:S(2)}) copy-start(s32[8]{0:T(128)} %valid_ref.11) | copy-start | bytes 100
  21.2 9.6 %collective-permute-start = (bf16[512,512]{1,0:T(8,128)(2,1)S(1)}, bf16[512,512]{1,0:T(8,128)(2,1)S(1)}, u32[]{:S(2)}, u32[]{:S(2)}) collective-permute-start(bf16[512,512]{1,0:T(8,128)(2,1)S(1)} %bitcast.10), channel_id=1, source_target_pairs={{0,32},{1,9},{2,34},{3,11},{4,36},{5,13},{6,38},{7,15},{8,40},{9,1... | collective-permute-start | bytes 1572872 | tf_op jit(solution)/shard_map/ppermute | solution.py:600
  22.3 15.3 %collective-permute-start.1 = (bf16[512,512]{1,0:T(8,128)(2,1)S(1)}, bf16[512,512]{1,0:T(8,128)(2,1)S(1)}, u32[]{:S(2)}, u32[]{:S(2)}) collective-permute-start(bf16[512,512]{1,0:T(8,128)(2,1)S(1)} %bitcast.11), channel_id=1, source_target_pairs={{0,64},{1,17},{2,66},{3,19},{4,68},{5,21},{6,70},{7,23},{8,72},{9,... | collective-permute-start | bytes 1572872 | tf_op jit(solution)/shard_map/ppermute | solution.py:600
  25.1 20.7 %collective-permute-start.2 = (bf16[512,512]{1,0:T(8,128)(2,1)S(1)}, bf16[512,512]{1,0:T(8,128)(2,1)S(1)}, u32[]{:S(2)}, u32[]{:S(2)}) collective-permute-start(bf16[512,512]{1,0:T(8,128)(2,1)S(1)} %bitcast.12), channel_id=1, source_target_pairs={{0,96},{1,25},{2,98},{3,27},{4,100},{5,29},{6,102},{7,31},{8,104},... | collective-permute-start | bytes 1572872 | tf_op jit(solution)/shard_map/ppermute | solution.py:600
  41.5 15.4 %collective-permute-start.4 = (bf16[16,144,128]{2,1,0:T(8,128)(2,1)S(1)}, bf16[16,144,128]{2,1,0:T(8,128)(2,1)S(1)}, u32[]{:S(2)}, u32[]{:S(2)}) collective-permute-start(bf16[16,144,128]{2,1,0:T(8,128)(2,1)S(1)} %cross.8), channel_id=1, source_target_pairs={{0,64},{1,17},{2,66},{3,19},{4,68},{5,21},{6,70},{7,23},{8,72},{9,... | collective-permute-start | bytes 1769480 | tf_op jit(solution)/shard_map/ppermute | solution.py:600
  45.9 11.0 %collective-permute-start.3 = (bf16[16,144,128]{2,1,0:T(8,128)(2,1)S(1)}, bf16[16,144,128]{2,1,0:T(8,128)(2,1)S(1)}, u32[]{:S(2)}, u32[]{:S(2)}) collective-permute-start(bf16[16,144,128]{2,1,0:T(8,128)(2,1)S(1)} %cross.7), channel_id=1, source_target_pairs={{0,96},{1,25},{2,98},{3,27},{4,100},{5,29},{6,102},{7,31},{8,104},... | collective-permute-start | bytes 1769480 | tf_op jit(solution)/shard_map/ppermute | solution.py:600
  50.3 4.4 %copy-start.2 = (bf16[1024,512]{1,0:T(8,128)(2,1)S(1)}, bf16[1024,512]{1,0:T(8,128)(2,1)}, u32[]{:S(2)}) copy-start(bf16[1024,512]{1,0:T(8,128)(2,1)} %param.22) | copy-start | bytes 3145732
  50.3 7.9 %collective-permute-start.6 = (bf16[8,144,128]{2,1,0:T(8,128)(2,1)S(1)}, bf16[8,144,128]{2,1,0:T(8,128)(2,1)S(1)}, u32[]{:S(2)}, u32[]{:S(2)}) collective-permute-start(bf16[8,144,128]{2,1,0:T(8,128)(2,1)S(1)} %cross.10), channel_id=1, source_target_pairs={{0,32},{1,9},{2,34},{3,11},{4,36},{5,13},{6,38},{7,15},{8,40},{9,1... | collective-permute-start | bytes 884744 | tf_op jit(solution)/shard_map/ppermute | solution.py:600
  51.8 8.8 %collective-permute-start.5 = (bf16[8,144,128]{2,1,0:T(8,128)(2,1)S(1)}, bf16[8,144,128]{2,1,0:T(8,128)(2,1)S(1)}, u32[]{:S(2)}, u32[]{:S(2)}) collective-permute-start(bf16[8,144,128]{2,1,0:T(8,128)(2,1)S(1)} %cross.9), channel_id=1, source_target_pairs={{0,32},{1,9},{2,34},{3,11},{4,36},{5,13},{6,38},{7,15},{8,40},{9,1... | collective-permute-start | bytes 884744 | tf_op jit(solution)/shard_map/ppermute | solution.py:600
  77.6 5.1 %collective-permute-start.7 = (bf16[16,1024]{1,0:T(8,128)(2,1)S(1)}, bf16[16,1024]{1,0:T(8,128)(2,1)S(1)}, u32[]{:S(2)}, u32[]{:S(2)}) collective-permute-start(bf16[16,1024]{1,0:T(8,128)(2,1)S(1)} %get-tuple-element.55), channel_id=1, source_target_pairs={{0,1},{1,0},{2,3},{3,2},{4,5},{5,4},{6,7},{7,6},{8,9},{9,8},{10,11... | collective-permute-start | bytes 98312 | tf_op jit(solution)/shard_map/ppermute | solution.py:629
  97.6 3.3 %collective-permute-start.8 = (bf16[256,1024]{1,0:T(8,128)(2,1)S(1)}, bf16[256,1024]{1,0:T(8,128)(2,1)S(1)}, u32[]{:S(2)}, u32[]{:S(2)}) collective-permute-start(bf16[256,1024]{1,0:T(8,128)(2,1)S(1)} %bitcast.15), channel_id=1, source_target_pairs={{0,1},{1,0},{2,3},{3,2},{4,5},{5,4},{6,7},{7,6},{8,9},{9,8},{10,11... | collective-permute-start | bytes 1572872 | tf_op jit(solution)/shard_map/ppermute | solution.py:636
  98.0 13.4 %collective-permute-start.10 = (bf16[256,1024]{1,0:T(8,128)(2,1)S(1)}, bf16[256,1024]{1,0:T(8,128)(2,1)S(1)}, u32[]{:S(2)}, u32[]{:S(2)}) collective-permute-start(bf16[256,1024]{1,0:T(8,128)(2,1)S(1)} %bitcast.16), channel_id=1, source_target_pairs={{0,96},{1,25},{2,98},{3,27},{4,100},{5,29},{6,102},{7,31},{8,104},... | collective-permute-start | bytes 1572872 | tf_op jit(solution)/shard_map/ppermute | solution.py:600
  99.6 15.2 %collective-permute-start.9 = (bf16[256,1024]{1,0:T(8,128)(2,1)S(1)}, bf16[256,1024]{1,0:T(8,128)(2,1)S(1)}, u32[]{:S(2)}, u32[]{:S(2)}) collective-permute-start(bf16[256,1024]{1,0:T(8,128)(2,1)S(1)} %bitcast.17), channel_id=1, source_target_pairs={{0,32},{1,9},{2,34},{3,11},{4,36},{5,13},{6,38},{7,15},{8,40},{9,1... | collective-permute-start | bytes 1572872 | tf_op jit(solution)/shard_map/ppermute | solution.py:600
  99.7 16.4 %collective-permute-start.11 = (bf16[256,1024]{1,0:T(8,128)(2,1)S(1)}, bf16[256,1024]{1,0:T(8,128)(2,1)S(1)}, u32[]{:S(2)}, u32[]{:S(2)}) collective-permute-start(bf16[256,1024]{1,0:T(8,128)(2,1)S(1)} %bitcast.18), channel_id=1, source_target_pairs={{0,64},{1,17},{2,66},{3,19},{4,68},{5,21},{6,70},{7,23},{8,72},{9,... | collective-permute-start | bytes 1572872 | tf_op jit(solution)/shard_map/ppermute | solution.py:600
  116.1 3.5 %collective-permute-start.14 = (bf16[256,1024]{1,0:T(8,128)(2,1)S(1)}, bf16[256,1024]{1,0:T(8,128)(2,1)S(1)}, u32[]{:S(2)}, u32[]{:S(2)}) collective-permute-start(bf16[256,1024]{1,0:T(8,128)(2,1)S(1)} %collective-permute-done.11.refs_0_), channel_id=1, source_target_pairs={{0,1},{1,0},{2,3},{3,2},{4,5},{5,4},{6,7},{7,6},{8,9},{9,8},{10,11... | collective-permute-start | bytes 1572872 | tf_op jit(solution)/shard_map/ppermute | solution.py:646
  118.0 2.8 %collective-permute-start.12 = (bf16[256,1024]{1,0:T(8,128)(2,1)S(1)}, bf16[256,1024]{1,0:T(8,128)(2,1)S(1)}, u32[]{:S(2)}, u32[]{:S(2)}) collective-permute-start(bf16[256,1024]{1,0:T(8,128)(2,1)S(1)} %collective-permute-done.9.refs_0_), channel_id=1, source_target_pairs={{0,1},{1,0},{2,3},{3,2},{4,5},{5,4},{6,7},{7,6},{8,9},{9,8},{10,11... | collective-permute-start | bytes 1572872 | tf_op jit(solution)/shard_map/ppermute | solution.py:643
  118.1 2.9 %collective-permute-start.13 = (bf16[256,1024]{1,0:T(8,128)(2,1)S(1)}, bf16[256,1024]{1,0:T(8,128)(2,1)S(1)}, u32[]{:S(2)}, u32[]{:S(2)}) collective-permute-start(bf16[256,1024]{1,0:T(8,128)(2,1)S(1)} %collective-permute-done.10.refs_1_), channel_id=1, source_target_pairs={{0,1},{1,0},{2,3},{3,2},{4,5},{5,4},{6,7},{7,6},{8,9},{9,8},{10,11... | collective-permute-start | bytes 1572872 | tf_op jit(solution)/shard_map/ppermute | solution.py:643
  128.2 3.4 %collective-permute-start.15 = (bf16[512,1024]{1,0:T(8,128)(2,1)S(1)}, bf16[512,1024]{1,0:T(8,128)(2,1)S(1)}, u32[]{:S(2)}, u32[]{:S(2)}) collective-permute-start(bf16[512,1024]{1,0:T(8,128)(2,1)S(1)} %decode.4), channel_id=1, source_target_pairs={{0,1},{1,0},{2,3},{3,2},{4,5},{5,4},{6,7},{7,6},{8,9},{9,8},{10,11... | collective-permute-start | bytes 3145736 | tf_op jit(solution)/shard_map/ppermute | solution.py:652
